TPU v7x, 256 devices: a whole 4x4x8 slice. The times are simulated.
256 devices in a mesh: ctx: 64 (over z, x_hi, y), head: 4 (over x_lo, core).
Axes of the slice: x: 4 (x_hi: 2, x_lo: 2; x = x_hi * 2 + x_lo), y: 4, z: 8, core: 2. Of those that a mesh axis runs over, the one named last changes fastest.
Arguments:
- queries: bfloat16 [16384, 5120], P('ctx', 'head'), parts along dimension 1, may hold values from -6 to 6
- query_tangents: bfloat16 [16384, 5120], P('ctx', 'head'), parts along dimension 1, may hold values from -6 to 6
- keys: bfloat16 [16384, 5120], P('ctx', 'head'), parts along dimension 1, may hold values from -6 to 6
- key_tangents: bfloat16 [16384, 5120], P('ctx', 'head'), parts along dimension 1, may hold values from -6 to 6
- values: bfloat16 [16384, 5120], P('ctx', 'head'), parts along dimension 1, may hold values from -6 to 6
- value_tangents: bfloat16 [16384, 5120], P('ctx', 'head'), parts along dimension 1, may hold values from -6 to 6
- selection: int32 [128, 14], P('ctx'), may hold values from 0 to 1, as said below
Outputs:
- attention_out: bfloat16 [16384, 5120], P('ctx', 'head'), parts along dimension 1
- attention_tangent: bfloat16 [16384, 5120], P('ctx', 'head'), parts along dimension 1
There are 4 independent parts, one for each index of `head`. A program takes and returns all parts, laid end to end along the dimension named above; an argument that names none is the same for every part. Nothing has to cross between parts.
Inputs may be any that keep to these rules, and one draw needn't show every extreme that they name: `selection`: column 6 + b mod 2 of row b, the query block's own block, is always 1.
All inputs are finite; a program needn't handle non-finite values.
Results may differ from a plain program's by a relative error of at most 0.012.
Values may be sent and summed in bfloat16 or wider, within the bound.
No kernel may reach another device: no remote copies, remote signals or barrier semaphores. Data moves between devices by JAX's collectives and lax.ppermute only.
A program may use at most 128 MiB of HBM per device.

v0:
```python
import jax
import jax.numpy as jnp
from jax import lax
from jax.sharding import PartitionSpec as P

HEADS = 10
HEAD_DIM = 128
BLK = 128
REACH = 3


big_negative = -1e30


def from_behind(array, axis, by):
    devices = lax.axis_size(axis)
    return lax.ppermute(array, axis, [(i, (i + by) % devices) for i in range(devices)])


def heads_view(flat_array):
    return flat_array.reshape(flat_array.shape[0], HEADS, HEAD_DIM)


def tile_update(accumulators, query_pieces, key_pieces):
    score_scale = HEAD_DIM ** (-0.5)
    query_block, query_tangent = query_pieces
    key_block, key_tangent, value_block, value_tangent = key_pieces
    running, weight_total, tangent_total, mixed_sum, mixed_tangent = accumulators
    scores = (
        jnp.einsum("qhd,khd->qhk", query_block, key_block, preferred_element_type=jnp.float32)
        * score_scale
    )
    score_tangents = (
        jnp.einsum("qhd,khd->qhk", query_tangent, key_block, preferred_element_type=jnp.float32)
        + jnp.einsum("qhd,khd->qhk", query_block, key_tangent, preferred_element_type=jnp.float32)
    ) * score_scale
    highest = jnp.maximum(running, scores.max(axis=2))
    factor = jnp.exp(running - highest)
    weights = jnp.exp(scores - highest[:, :, None])
    weighted = weights * score_tangents
    weight_total = factor * weight_total + weights.sum(axis=2)
    tangent_total = factor * tangent_total + weighted.sum(axis=2)
    rounded_weights = weights.astype(jnp.bfloat16)
    rounded_tangent = weighted.astype(jnp.bfloat16)
    mixed_sum = factor[:, :, None] * mixed_sum + jnp.einsum(
        "qhk,khd->qhd", rounded_weights, value_block, preferred_element_type=jnp.float32
    )
    mixed_tangent = (
        factor[:, :, None] * mixed_tangent
        + jnp.einsum(
            "qhk,khd->qhd", rounded_tangent, value_block, preferred_element_type=jnp.float32
        )
        + jnp.einsum(
            "qhk,khd->qhd", rounded_weights, value_tangent, preferred_element_type=jnp.float32
        )
    )
    return (highest, weight_total, tangent_total, mixed_sum, mixed_tangent)


def sweep(accumulators, query_pair, chosen_rows, key_pack, column_base):
    per_device = chosen_rows.shape[0]

    def visit(tile_index, carried):
        query_index = tile_index // per_device
        key_index = tile_index % per_device
        picked = chosen_rows[query_index, column_base + key_index] != 0

        def apply(carried_state):
            first_row = query_index * BLK
            pieces = tuple(
                (
                    lax.dynamic_slice_in_dim(full_array, first_row, BLK, 0)
                    for full_array in carried_state
                )
            )
            query_pieces = tuple(
                (
                    lax.dynamic_slice_in_dim(full_array, first_row, BLK, 0)
                    for full_array in query_pair
                )
            )
            key_pieces = tuple(
                (
                    lax.dynamic_slice_in_dim(full_array, key_index * BLK, BLK, 0)
                    for full_array in key_pack
                )
            )
            updated = tile_update(pieces, query_pieces, key_pieces)
            return tuple(
                (
                    lax.dynamic_update_slice_in_dim(full_array, new_piece, first_row, 0)
                    for full_array, new_piece in zip(carried_state, updated)
                )
            )

        return lax.cond(picked, apply, lambda unchanged: unchanged, carried)

    return lax.fori_loop(0, per_device * per_device, visit, tuple(accumulators))


def finish(accumulators):
    running, weight_total, tangent_total, mixed_sum, mixed_tangent = accumulators
    token_count = mixed_sum.shape[0]
    output = mixed_sum / weight_total[:, :, None]
    tangent = (mixed_tangent - output * tangent_total[:, :, None]) / weight_total[:, :, None]
    return (
        output.reshape(token_count, HEADS * HEAD_DIM).astype(jnp.bfloat16),
        tangent.reshape(token_count, HEADS * HEAD_DIM).astype(jnp.bfloat16),
    )


def body(queries, query_tangents, keys, key_tangents, values, value_tangents, selection):
    token_count = queries.shape[0]
    per_device = token_count // BLK
    query_pair = (heads_view(queries), heads_view(query_tangents))
    key_pack = (
        heads_view(keys),
        heads_view(key_tangents),
        heads_view(values),
        heads_view(value_tangents),
    )
    initial = (
        jnp.full((token_count, HEADS), big_negative, jnp.float32),
        jnp.zeros((token_count, HEADS), jnp.float32),
        jnp.zeros((token_count, HEADS), jnp.float32),
        jnp.zeros((token_count, HEADS, HEAD_DIM), jnp.float32),
        jnp.zeros((token_count, HEADS, HEAD_DIM), jnp.float32),
    )
    at_home = sweep(initial, query_pair, selection, key_pack, REACH * per_device)
    accumulators = at_home
    rising = key_pack
    falling = key_pack
    for offset in range(1, REACH + 1):
        rising = from_behind((rising[0], rising[1], rising[2], rising[3]), "ctx", -1)
        accumulators = sweep(
            accumulators, query_pair, selection, rising, (REACH + offset) * per_device
        )
        falling = from_behind((falling[0], falling[1], falling[2], falling[3]), "ctx", 1)
        accumulators = sweep(
            accumulators, query_pair, selection, falling, (REACH - offset) * per_device
        )
    return finish(accumulators)


def solution(mesh):
    placed = (
        P("ctx", "head"),
        P("ctx", "head"),
        P("ctx", "head"),
        P("ctx", "head"),
        P("ctx", "head"),
        P("ctx", "head"),
        P("ctx", None),
    )
    return jax.shard_map(
        body,
        mesh=mesh,
        in_specs=placed,
        out_specs=(P("ctx", "head"), P("ctx", "head")),
        check_vma=False,
    )
```

profile of v0, /device:TPU:110, one launch (start us, length us, event | category | flops | bytes accessed | tf_op | source)
XLA Modules:
  0.0 395.6 jit_solution(12332529258552161207)
XLA Ops:
  0.7 2.3 copy.55
  4.4 3.9 collective-permute-start.1
  11.7 9.1 %collective-permute-done = bf16[256,10,128]{0,2,1:T(8,128)(2,1)} collective-permute-done((bf16[256,10,128]{0,2,1:T(8,128)(2,1)}, bf16[256,10,128]{0,2,1:T(8,128)(2,1)}, u32[]{:S(2)}, u32[]{:S(2)}) %collective-permute-start) | collective-permute-done | bytes 655392 | tf_op jit(solution)/shard_map/ppermute | solution.py:17
  22.4 12.5 %collective-permute-done.1 = bf16[256,10,128]{0,2,1:T(8,128)(2,1)} collective-permute-done((bf16[256,10,128]{0,2,1:T(8,128)(2,1)}, bf16[256,10,128]{0,2,1:T(8,128)(2,1)}, u32[]{:S(2)}, u32[]{:S(2)}) %collective-permute-start.1) | collective-permute-done | bytes 655392 | tf_op jit(solution)/shard_map/ppermute | solution.py:17
  36.5 12.4 %collective-permute-done.2 = bf16[256,10,128]{0,2,1:T(8,128)(2,1)S(1)} collective-permute-done((bf16[256,10,128]{0,2,1:T(8,128)(2,1)S(1)}, bf16[256,10,128]{0,2,1:T(8,128)(2,1)S(1)}, u32[]{:S(2)}, u32[]{:S(2)}) %collective-permute-start.2) | collective-permute-done | bytes 655392 | tf_op jit(solution)/shard_map/ppermute | solution.py:17
  50.4 11.3 %collective-permute-done.3 = bf16[256,10,128]{0,2,1:T(8,128)(2,1)S(1)} collective-permute-done((bf16[256,10,128]{0,2,1:T(8,128)(2,1)S(1)}, bf16[256,10,128]{0,2,1:T(8,128)(2,1)S(1)}, u32[]{:S(2)}, u32[]{:S(2)}) %collective-permute-start.3) | collective-permute-done | bytes 655392 | tf_op jit(solution)/shard_map/ppermute | solution.py:17
  63.6 6.1 %collective-permute-start.9 = (bf16[256,10,128]{0,2,1:T(8,128)(2,1)}, bf16[256,10,128]{0,2,1:T(8,128)(2,1)S(1)}, u32[]{:S(2)}, u32[]{:S(2)}) collective-permute-start(bf16[256,10,128]{0,2,1:T(8,128)(2,1)} %collective-permute-done.1), channel_id=1, source_target_pairs={{0,252},{4,0},{8,4},{12,8},{16,12},{20,16},{24,20},{28,24},{32,28}... | collective-permute-start | bytes 1966088 | tf_op jit(solution)/shard_map/ppermute | solution.py:17
  71.8 7.8 %collective-permute-done.8 = bf16[256,10,128]{0,2,1:T(8,128)(2,1)S(1)} collective-permute-done((bf16[256,10,128]{0,2,1:T(8,128)(2,1)}, bf16[256,10,128]{0,2,1:T(8,128)(2,1)S(1)}, u32[]{:S(2)}, u32[]{:S(2)}) %collective-permute-start.8) | collective-permute-done | bytes 655392 | tf_op jit(solution)/shard_map/ppermute | solution.py:17
  79.6 6.6 %collective-permute-start.13 = (bf16[256,10,128]{0,2,1:T(8,128)(2,1)S(1)}, bf16[256,10,128]{0,2,1:T(8,128)(2,1)}, u32[]{:S(2)}, u32[]{:S(2)}) collective-permute-start(bf16[256,10,128]{0,2,1:T(8,128)(2,1)S(1)} %collective-permute-done.5), channel_id=1, source_target_pairs={{0,4},{4,8},{8,12},{12,16},{16,20},{20,24},{24,28},{28,32},{32,36}... | collective-permute-start | bytes 1966088 | tf_op jit(solution)/shard_map/ppermute | solution.py:17
  86.2 7.5 %collective-permute-done.9 = bf16[256,10,128]{0,2,1:T(8,128)(2,1)S(1)} collective-permute-done((bf16[256,10,128]{0,2,1:T(8,128)(2,1)}, bf16[256,10,128]{0,2,1:T(8,128)(2,1)S(1)}, u32[]{:S(2)}, u32[]{:S(2)}) %collective-permute-start.9) | collective-permute-done | bytes 655392 | tf_op jit(solution)/shard_map/ppermute | solution.py:17
  93.7 6.6 %collective-permute-start.14 = (bf16[256,10,128]{0,2,1:T(8,128)(2,1)S(1)}, bf16[256,10,128]{0,2,1:T(8,128)(2,1)}, u32[]{:S(2)}, u32[]{:S(2)}) collective-permute-start(bf16[256,10,128]{0,2,1:T(8,128)(2,1)S(1)} %collective-permute-done.6), channel_id=1, source_target_pairs={{0,4},{4,8},{8,12},{12,16},{16,20},{20,24},{24,28},{28,32},{32,36}... | collective-permute-start | bytes 1966088 | tf_op jit(solution)/shard_map/ppermute | solution.py:17
  100.2 7.6 %collective-permute-done.10 = bf16[256,10,128]{0,2,1:T(8,128)(2,1)} collective-permute-done((bf16[256,10,128]{0,2,1:T(8,128)(2,1)S(1)}, bf16[256,10,128]{0,2,1:T(8,128)(2,1)}, u32[]{:S(2)}, u32[]{:S(2)}) %collective-permute-start.10) | collective-permute-done | bytes 655392 | tf_op jit(solution)/shard_map/ppermute | solution.py:17
  107.8 6.6 %collective-permute-start.15 = (bf16[256,10,128]{0,2,1:T(8,128)(2,1)S(1)}, bf16[256,10,128]{0,2,1:T(8,128)(2,1)}, u32[]{:S(2)}, u32[]{:S(2)}) collective-permute-start(bf16[256,10,128]{0,2,1:T(8,128)(2,1)S(1)} %collective-permute-done.7), channel_id=1, source_target_pairs={{0,4},{4,8},{8,12},{12,16},{16,20},{20,24},{24,28},{28,32},{32,36}... | collective-permute-start | bytes 1966088 | tf_op jit(solution)/shard_map/ppermute | solution.py:17
  114.4 5.4 %collective-permute-done.11 = bf16[256,10,128]{0,2,1:T(8,128)(2,1)} collective-permute-done((bf16[256,10,128]{0,2,1:T(8,128)(2,1)S(1)}, bf16[256,10,128]{0,2,1:T(8,128)(2,1)}, u32[]{:S(2)}, u32[]{:S(2)}) %collective-permute-start.11) | collective-permute-done | bytes 655392 | tf_op jit(solution)/shard_map/ppermute | solution.py:17
  119.8 5.3 %collective-permute-start.16 = (bf16[256,10,128]{0,2,1:T(8,128)(2,1)S(1)}, bf16[256,10,128]{0,2,1:T(8,128)(2,1)}, u32[]{:S(2)}, u32[]{:S(2)}) collective-permute-start(bf16[256,10,128]{0,2,1:T(8,128)(2,1)S(1)} %collective-permute-done.8), channel_id=1, source_target_pairs={{0,252},{4,0},{8,4},{12,8},{16,12},{20,16},{24,20},{28,24},{32,28}... | collective-permute-start | bytes 1966088 | tf_op jit(solution)/shard_map/ppermute | solution.py:17
  125.1 6.2 %collective-permute-start.17 = (bf16[256,10,128]{0,2,1:T(8,128)(2,1)S(1)}, bf16[256,10,128]{0,2,1:T(8,128)(2,1)}, u32[]{:S(2)}, u32[]{:S(2)}) collective-permute-start(bf16[256,10,128]{0,2,1:T(8,128)(2,1)S(1)} %collective-permute-done.9), channel_id=1, source_target_pairs={{0,252},{4,0},{8,4},{12,8},{16,12},{20,16},{24,20},{28,24},{32,28}... | collective-permute-start | bytes 1966088 | tf_op jit(solution)/shard_map/ppermute | solution.py:17
  131.3 2.9 collective-permute-start.21
  134.3 8.1 %collective-permute-done.16 = bf16[256,10,128]{0,2,1:T(8,128)(2,1)} collective-permute-done((bf16[256,10,128]{0,2,1:T(8,128)(2,1)S(1)}, bf16[256,10,128]{0,2,1:T(8,128)(2,1)}, u32[]{:S(2)}, u32[]{:S(2)}) %collective-permute-start.16) | collective-permute-done | bytes 655392 | tf_op jit(solution)/shard_map/ppermute | solution.py:17
  142.4 4.1 %collective-permute-start.19 = (bf16[256,10,128]{0,2,1:T(8,128)(2,1)}, bf16[256,10,128]{0,2,1:T(8,128)(2,1)}, u32[]{:S(2)}, u32[]{:S(2)}) collective-permute-start(bf16[256,10,128]{0,2,1:T(8,128)(2,1)} %collective-permute-done.11), channel_id=1, source_target_pairs={{0,252},{4,0},{8,4},{12,8},{16,12},{20,16},{24,20},{28,24},{32,28}... | collective-permute-start | bytes 1966088 | tf_op jit(solution)/shard_map/ppermute | solution.py:17
  146.5 9.9 %collective-permute-done.17 = bf16[256,10,128]{0,2,1:T(8,128)(2,1)} collective-permute-done((bf16[256,10,128]{0,2,1:T(8,128)(2,1)S(1)}, bf16[256,10,128]{0,2,1:T(8,128)(2,1)}, u32[]{:S(2)}, u32[]{:S(2)}) %collective-permute-start.17) | collective-permute-done | bytes 655392 | tf_op jit(solution)/shard_map/ppermute | solution.py:17
  156.4 7.5 %collective-permute-start.22 = (bf16[256,10,128]{0,2,1:T(8,128)(2,1)}, bf16[256,10,128]{0,2,1:T(8,128)(2,1)}, u32[]{:S(2)}, u32[]{:S(2)}) collective-permute-start(bf16[256,10,128]{0,2,1:T(8,128)(2,1)} %collective-permute-done.14), channel_id=1, source_target_pairs={{0,4},{4,8},{8,12},{12,16},{16,20},{20,24},{24,28},{28,32},{32,36}... | collective-permute-start | bytes 1966088 | tf_op jit(solution)/shard_map/ppermute | solution.py:17
  163.9 7.8 %collective-permute-start.23 = (bf16[256,10,128]{0,2,1:T(8,128)(2,1)}, bf16[256,10,128]{0,2,1:T(8,128)(2,1)}, u32[]{:S(2)}, u32[]{:S(2)}) collective-permute-start(bf16[256,10,128]{0,2,1:T(8,128)(2,1)} %collective-permute-done.15), channel_id=1, source_target_pairs={{0,4},{4,8},{8,12},{12,16},{16,20},{20,24},{24,28},{28,32},{32,36}... | collective-permute-start | bytes 1966088 | tf_op jit(solution)/shard_map/ppermute | solution.py:17
  173.9 2.2 copy.64
  179.8 22.2 %while.161 = (s32[]{:T(128)}, f32[256,10]{0,1:T(8,128)S(1)}, f32[256,10]{0,1:T(8,128)S(1)}, f32[256,10]{0,1:T(8,128)S(1)}, f32[256,10,128]{0,2,1:T(8,128)S(1)}, ...) while((s32[]{:T(128)}, f32[256,10]{0,1:T(8,128)S(1)}, ...), condition=%wide.region_6.7_spmd, body=%wide.region_0.6_spmd.sunk | while | flops 254775056 | bytes 25449332 | solution.py:98
  181.2 4.2 %conditional.14 = ((f32[256,10]{0,1:T(8,128)S(1)}, f32[256,10]{0,1:T(8,128)S(1)}, f32[256,10]{0,1:T(8,128)S(1)}, f32[256,10,128]{0,2,1:T(8,128)S(1)}, f32[256,10,128]{0,2,1:T(8,128)S(1)})) conditional(s32[]{:T(128)} %bitcast.183, (f32[256,10]{0,1:T(8,128)S(1)}, f32[256,10]{0,1:T(8,128)S(1)}, f32[256,10]{0,1:T(8,128)S(1)}, ...), branch_computations={%region_1.1_spmd, %region_2.5_spmd} | conditional | flops 254775040 | bytes 25448788 | solution.py:96
  186.8 4.2 %conditional.14 = ((f32[256,10]{0,1:T(8,128)S(1)}, f32[256,10]{0,1:T(8,128)S(1)}, f32[256,10]{0,1:T(8,128)S(1)}, f32[256,10,128]{0,2,1:T(8,128)S(1)}, f32[256,10,128]{0,2,1:T(8,128)S(1)})) conditional(s32[]{:T(128)} %bitcast.183, (f32[256,10]{0,1:T(8,128)S(1)}, f32[256,10]{0,1:T(8,128)S(1)}, f32[256,10]{0,1:T(8,128)S(1)}, ...), branch_computations={%region_1.1_spmd, %region_2.5_spmd} | conditional | flops 254775040 | bytes 25448788 | solution.py:96
  192.3 4.2 %conditional.14 = ((f32[256,10]{0,1:T(8,128)S(1)}, f32[256,10]{0,1:T(8,128)S(1)}, f32[256,10]{0,1:T(8,128)S(1)}, f32[256,10,128]{0,2,1:T(8,128)S(1)}, f32[256,10,128]{0,2,1:T(8,128)S(1)})) conditional(s32[]{:T(128)} %bitcast.183, (f32[256,10]{0,1:T(8,128)S(1)}, f32[256,10]{0,1:T(8,128)S(1)}, f32[256,10]{0,1:T(8,128)S(1)}, ...), branch_computations={%region_1.1_spmd, %region_2.5_spmd} | conditional | flops 254775040 | bytes 25448788 | solution.py:96
  197.9 4.2 %conditional.14 = ((f32[256,10]{0,1:T(8,128)S(1)}, f32[256,10]{0,1:T(8,128)S(1)}, f32[256,10]{0,1:T(8,128)S(1)}, f32[256,10,128]{0,2,1:T(8,128)S(1)}, f32[256,10,128]{0,2,1:T(8,128)S(1)})) conditional(s32[]{:T(128)} %bitcast.183, (f32[256,10]{0,1:T(8,128)S(1)}, f32[256,10]{0,1:T(8,128)S(1)}, f32[256,10]{0,1:T(8,128)S(1)}, ...), branch_computations={%region_1.1_spmd, %region_2.5_spmd} | conditional | flops 254775040 | bytes 25448788 | solution.py:96
  202.1 2.2 copy.65
  210.7 21.4 %while.162 = (s32[]{:T(128)}, f32[256,10]{0,1:T(8,128)S(1)}, f32[256,10]{0,1:T(8,128)S(1)}, f32[256,10]{0,1:T(8,128)S(1)}, f32[256,10,128]{0,2,1:T(8,128)S(1)}, ...) while((s32[]{:T(128)}, f32[256,10]{0,1:T(8,128)S(1)}, ...), condition=%wide.region_13.14_spmd, body=%wide.region_7.13_spmd.sunk | while | flops 254775056 | bytes 25449332 | solution.py:98
  211.9 4.2 %conditional.15 = ((f32[256,10]{0,1:T(8,128)S(1)}, f32[256,10]{0,1:T(8,128)S(1)}, f32[256,10]{0,1:T(8,128)S(1)}, f32[256,10,128]{0,2,1:T(8,128)S(1)}, f32[256,10,128]{0,2,1:T(8,128)S(1)})) conditional(s32[]{:T(128)} %bitcast.184, (f32[256,10]{0,1:T(8,128)S(1)}, f32[256,10]{0,1:T(8,128)S(1)}, f32[256,10]{0,1:T(8,128)S(1)}, ...), branch_computations={%region_8.8_spmd, %region_9.12_spmd} | conditional | flops 254775040 | bytes 25448788 | solution.py:96
  217.3 4.2 %conditional.15 = ((f32[256,10]{0,1:T(8,128)S(1)}, f32[256,10]{0,1:T(8,128)S(1)}, f32[256,10]{0,1:T(8,128)S(1)}, f32[256,10,128]{0,2,1:T(8,128)S(1)}, f32[256,10,128]{0,2,1:T(8,128)S(1)})) conditional(s32[]{:T(128)} %bitcast.184, (f32[256,10]{0,1:T(8,128)S(1)}, f32[256,10]{0,1:T(8,128)S(1)}, f32[256,10]{0,1:T(8,128)S(1)}, ...), branch_computations={%region_8.8_spmd, %region_9.12_spmd} | conditional | flops 254775040 | bytes 25448788 | solution.py:96
  222.6 4.2 %conditional.15 = ((f32[256,10]{0,1:T(8,128)S(1)}, f32[256,10]{0,1:T(8,128)S(1)}, f32[256,10]{0,1:T(8,128)S(1)}, f32[256,10,128]{0,2,1:T(8,128)S(1)}, f32[256,10,128]{0,2,1:T(8,128)S(1)})) conditional(s32[]{:T(128)} %bitcast.184, (f32[256,10]{0,1:T(8,128)S(1)}, f32[256,10]{0,1:T(8,128)S(1)}, f32[256,10]{0,1:T(8,128)S(1)}, ...), branch_computations={%region_8.8_spmd, %region_9.12_spmd} | conditional | flops 254775040 | bytes 25448788 | solution.py:96
  228.0 4.2 %conditional.15 = ((f32[256,10]{0,1:T(8,128)S(1)}, f32[256,10]{0,1:T(8,128)S(1)}, f32[256,10]{0,1:T(8,128)S(1)}, f32[256,10,128]{0,2,1:T(8,128)S(1)}, f32[256,10,128]{0,2,1:T(8,128)S(1)})) conditional(s32[]{:T(128)} %bitcast.184, (f32[256,10]{0,1:T(8,128)S(1)}, f32[256,10]{0,1:T(8,128)S(1)}, f32[256,10]{0,1:T(8,128)S(1)}, ...), branch_computations={%region_8.8_spmd, %region_9.12_spmd} | conditional | flops 254775040 | bytes 25448788 | solution.py:96
  232.2 21.7 %while.163 = (s32[]{:T(128)}, f32[256,10]{0,1:T(8,128)S(1)}, f32[256,10]{0,1:T(8,128)S(1)}, f32[256,10]{0,1:T(8,128)S(1)}, f32[256,10,128]{0,2,1:T(8,128)S(1)}, ...) while((s32[]{:T(128)}, f32[256,10]{0,1:T(8,128)S(1)}, ...), condition=%wide.region_20.21_spmd, body=%wide.region_14.20_spmd.sunk | while | flops 254775056 | bytes 25449332 | solution.py:98
  233.4 4.2 %conditional.16 = ((f32[256,10]{0,1:T(8,128)S(1)}, f32[256,10]{0,1:T(8,128)S(1)}, f32[256,10]{0,1:T(8,128)S(1)}, f32[256,10,128]{0,2,1:T(8,128)S(1)}, f32[256,10,128]{0,2,1:T(8,128)S(1)})) conditional(s32[]{:T(128)} %bitcast.185, (f32[256,10]{0,1:T(8,128)S(1)}, f32[256,10]{0,1:T(8,128)S(1)}, f32[256,10]{0,1:T(8,128)S(1)}, ...), branch_computations={%region_15.15_spmd, %region_16.19_spmd} | conditional | flops 254775040 | bytes 25448788 | solution.py:96
  238.9 4.2 %conditional.16 = ((f32[256,10]{0,1:T(8,128)S(1)}, f32[256,10]{0,1:T(8,128)S(1)}, f32[256,10]{0,1:T(8,128)S(1)}, f32[256,10,128]{0,2,1:T(8,128)S(1)}, f32[256,10,128]{0,2,1:T(8,128)S(1)})) conditional(s32[]{:T(128)} %bitcast.185, (f32[256,10]{0,1:T(8,128)S(1)}, f32[256,10]{0,1:T(8,128)S(1)}, f32[256,10]{0,1:T(8,128)S(1)}, ...), branch_computations={%region_15.15_spmd, %region_16.19_spmd} | conditional | flops 254775040 | bytes 25448788 | solution.py:96
  244.3 4.2 %conditional.16 = ((f32[256,10]{0,1:T(8,128)S(1)}, f32[256,10]{0,1:T(8,128)S(1)}, f32[256,10]{0,1:T(8,128)S(1)}, f32[256,10,128]{0,2,1:T(8,128)S(1)}, f32[256,10,128]{0,2,1:T(8,128)S(1)})) conditional(s32[]{:T(128)} %bitcast.185, (f32[256,10]{0,1:T(8,128)S(1)}, f32[256,10]{0,1:T(8,128)S(1)}, f32[256,10]{0,1:T(8,128)S(1)}, ...), branch_computations={%region_15.15_spmd, %region_16.19_spmd} | conditional | flops 254775040 | bytes 25448788 | solution.py:96
  249.7 4.2 %conditional.16 = ((f32[256,10]{0,1:T(8,128)S(1)}, f32[256,10]{0,1:T(8,128)S(1)}, f32[256,10]{0,1:T(8,128)S(1)}, f32[256,10,128]{0,2,1:T(8,128)S(1)}, f32[256,10,128]{0,2,1:T(8,128)S(1)})) conditional(s32[]{:T(128)} %bitcast.185, (f32[256,10]{0,1:T(8,128)S(1)}, f32[256,10]{0,1:T(8,128)S(1)}, f32[256,10]{0,1:T(8,128)S(1)}, ...), branch_computations={%region_15.15_spmd, %region_16.19_spmd} | conditional | flops 254775040 | bytes 25448788 | solution.py:96
  258.2 2.2 copy.77
  260.4 2.2 copy.80
  262.6 29.6 %while.164 = (s32[]{:T(128)}, f32[256,10]{0,1:T(8,128)S(1)}, f32[256,10]{0,1:T(8,128)S(1)}, f32[256,10]{0,1:T(8,128)S(1)}, f32[256,10,128]{0,2,1:T(8,128)S(1)}, ...) while((s32[]{:T(128)}, f32[256,10]{0,1:T(8,128)S(1)}, ...), condition=%wide.region_27.28_spmd, body=%wide.region_21.27_spmd.sunk | while | flops 254775056 | bytes 20203324 | solution.py:98
  263.7 6.2 %conditional.17 = ((f32[256,10]{0,1:T(8,128)S(1)}, f32[256,10]{0,1:T(8,128)S(1)}, f32[256,10]{0,1:T(8,128)S(1)}, f32[256,10,128]{0,2,1:T(8,128)S(1)}, f32[256,10,128]{0,2,1:T(8,128)S(1)})) conditional(s32[]{:T(128)} %bitcast.186, (f32[256,10]{0,1:T(8,128)S(1)}, f32[256,10]{0,1:T(8,128)S(1)}, f32[256,10]{0,1:T(8,128)S(1)}, ...), branch_computations={%region_22.22_spmd, %region_23.26_spmd} | conditional | flops 254775040 | bytes 20202780 | solution.py:96
  271.2 6.2 %conditional.17 = ((f32[256,10]{0,1:T(8,128)S(1)}, f32[256,10]{0,1:T(8,128)S(1)}, f32[256,10]{0,1:T(8,128)S(1)}, f32[256,10,128]{0,2,1:T(8,128)S(1)}, f32[256,10,128]{0,2,1:T(8,128)S(1)})) conditional(s32[]{:T(128)} %bitcast.186, (f32[256,10]{0,1:T(8,128)S(1)}, f32[256,10]{0,1:T(8,128)S(1)}, f32[256,10]{0,1:T(8,128)S(1)}, ...), branch_computations={%region_22.22_spmd, %region_23.26_spmd} | conditional | flops 254775040 | bytes 20202780 | solution.py:96
  278.6 6.2 %conditional.17 = ((f32[256,10]{0,1:T(8,128)S(1)}, f32[256,10]{0,1:T(8,128)S(1)}, f32[256,10]{0,1:T(8,128)S(1)}, f32[256,10,128]{0,2,1:T(8,128)S(1)}, f32[256,10,128]{0,2,1:T(8,128)S(1)})) conditional(s32[]{:T(128)} %bitcast.186, (f32[256,10]{0,1:T(8,128)S(1)}, f32[256,10]{0,1:T(8,128)S(1)}, f32[256,10]{0,1:T(8,128)S(1)}, ...), branch_computations={%region_22.22_spmd, %region_23.26_spmd} | conditional | flops 254775040 | bytes 20202780 | solution.py:96
  286.0 6.2 %conditional.17 = ((f32[256,10]{0,1:T(8,128)S(1)}, f32[256,10]{0,1:T(8,128)S(1)}, f32[256,10]{0,1:T(8,128)S(1)}, f32[256,10,128]{0,2,1:T(8,128)S(1)}, f32[256,10,128]{0,2,1:T(8,128)S(1)})) conditional(s32[]{:T(128)} %bitcast.186, (f32[256,10]{0,1:T(8,128)S(1)}, f32[256,10]{0,1:T(8,128)S(1)}, f32[256,10]{0,1:T(8,128)S(1)}, ...), branch_computations={%region_22.22_spmd, %region_23.26_spmd} | conditional | flops 254775040 | bytes 20202780 | solution.py:96
  292.2 30.1 %while.165 = (s32[]{:T(128)}, f32[256,10]{0,1:T(8,128)S(1)}, f32[256,10]{0,1:T(8,128)S(1)}, f32[256,10]{0,1:T(8,128)S(1)}, f32[256,10,128]{0,2,1:T(8,128)S(1)}, ...) while((s32[]{:T(128)}, f32[256,10]{0,1:T(8,128)S(1)}, ...), condition=%wide.region_34.35_spmd, body=%wide.region_28.34_spmd.sunk | while | flops 254775056 | bytes 20203316 | solution.py:98
  293.5 6.2 %conditional.18 = ((f32[256,10]{0,1:T(8,128)S(1)}, f32[256,10]{0,1:T(8,128)S(1)}, f32[256,10]{0,1:T(8,128)S(1)}, f32[256,10,128]{0,2,1:T(8,128)S(1)}, f32[256,10,128]{0,2,1:T(8,128)S(1)})) conditional(s32[]{:T(128)} %bitcast.187, (f32[256,10]{0,1:T(8,128)S(1)}, f32[256,10]{0,1:T(8,128)S(1)}, f32[256,10]{0,1:T(8,128)S(1)}, ...), branch_computations={%region_29.29_spmd, %region_30.33_spmd} | conditional | flops 254775040 | bytes 20202780 | solution.py:96
  301.0 6.2 %conditional.18 = ((f32[256,10]{0,1:T(8,128)S(1)}, f32[256,10]{0,1:T(8,128)S(1)}, f32[256,10]{0,1:T(8,128)S(1)}, f32[256,10,128]{0,2,1:T(8,128)S(1)}, f32[256,10,128]{0,2,1:T(8,128)S(1)})) conditional(s32[]{:T(128)} %bitcast.187, (f32[256,10]{0,1:T(8,128)S(1)}, f32[256,10]{0,1:T(8,128)S(1)}, f32[256,10]{0,1:T(8,128)S(1)}, ...), branch_computations={%region_29.29_spmd, %region_30.33_spmd} | conditional | flops 254775040 | bytes 20202780 | solution.py:96
  308.6 6.2 %conditional.18 = ((f32[256,10]{0,1:T(8,128)S(1)}, f32[256,10]{0,1:T(8,128)S(1)}, f32[256,10]{0,1:T(8,128)S(1)}, f32[256,10,128]{0,2,1:T(8,128)S(1)}, f32[256,10,128]{0,2,1:T(8,128)S(1)})) conditional(s32[]{:T(128)} %bitcast.187, (f32[256,10]{0,1:T(8,128)S(1)}, f32[256,10]{0,1:T(8,128)S(1)}, f32[256,10]{0,1:T(8,128)S(1)}, ...), branch_computations={%region_29.29_spmd, %region_30.33_spmd} | conditional | flops 254775040 | bytes 20202780 | solution.py:96
  316.1 6.2 %conditional.18 = ((f32[256,10]{0,1:T(8,128)S(1)}, f32[256,10]{0,1:T(8,128)S(1)}, f32[256,10]{0,1:T(8,128)S(1)}, f32[256,10,128]{0,2,1:T(8,128)S(1)}, f32[256,10,128]{0,2,1:T(8,128)S(1)})) conditional(s32[]{:T(128)} %bitcast.187, (f32[256,10]{0,1:T(8,128)S(1)}, f32[256,10]{0,1:T(8,128)S(1)}, f32[256,10]{0,1:T(8,128)S(1)}, ...), branch_computations={%region_29.29_spmd, %region_30.33_spmd} | conditional | flops 254775040 | bytes 20202780 | solution.py:96
  324.5 2.2 copy.84
  326.7 2.2 copy.85
  328.9 2.2 copy.88
  331.1 30.0 %while.166 = (s32[]{:T(128)}, f32[256,10]{0,1:T(8,128)S(1)}, f32[256,10]{0,1:T(8,128)S(1)}, f32[256,10]{0,1:T(8,128)S(1)}, f32[256,10,128]{0,2,1:T(8,128)S(1)}, ...) while((s32[]{:T(128)}, f32[256,10]{0,1:T(8,128)S(1)}, ...), condition=%wide.region_41.42_spmd, body=%wide.region_35.41_spmd.sunk | while | flops 254775056 | bytes 20203324 | solution.py:98
  332.3 6.2 %conditional.19 = ((f32[256,10]{0,1:T(8,128)S(1)}, f32[256,10]{0,1:T(8,128)S(1)}, f32[256,10]{0,1:T(8,128)S(1)}, f32[256,10,128]{0,2,1:T(8,128)S(1)}, f32[256,10,128]{0,2,1:T(8,128)S(1)})) conditional(s32[]{:T(128)} %bitcast.188, (f32[256,10]{0,1:T(8,128)S(1)}, f32[256,10]{0,1:T(8,128)S(1)}, f32[256,10]{0,1:T(8,128)S(1)}, ...), branch_computations={%region_36.36_spmd, %region_37.40_spmd} | conditional | flops 254775040 | bytes 20202780 | solution.py:96
  339.9 6.2 %conditional.19 = ((f32[256,10]{0,1:T(8,128)S(1)}, f32[256,10]{0,1:T(8,128)S(1)}, f32[256,10]{0,1:T(8,128)S(1)}, f32[256,10,128]{0,2,1:T(8,128)S(1)}, f32[256,10,128]{0,2,1:T(8,128)S(1)})) conditional(s32[]{:T(128)} %bitcast.188, (f32[256,10]{0,1:T(8,128)S(1)}, f32[256,10]{0,1:T(8,128)S(1)}, f32[256,10]{0,1:T(8,128)S(1)}, ...), branch_computations={%region_36.36_spmd, %region_37.40_spmd} | conditional | flops 254775040 | bytes 20202780 | solution.py:96
  347.4 6.2 %conditional.19 = ((f32[256,10]{0,1:T(8,128)S(1)}, f32[256,10]{0,1:T(8,128)S(1)}, f32[256,10]{0,1:T(8,128)S(1)}, f32[256,10,128]{0,2,1:T(8,128)S(1)}, f32[256,10,128]{0,2,1:T(8,128)S(1)})) conditional(s32[]{:T(128)} %bitcast.188, (f32[256,10]{0,1:T(8,128)S(1)}, f32[256,10]{0,1:T(8,128)S(1)}, f32[256,10]{0,1:T(8,128)S(1)}, ...), branch_computations={%region_36.36_spmd, %region_37.40_spmd} | conditional | flops 254775040 | bytes 20202780 | solution.py:96
  354.9 6.2 %conditional.19 = ((f32[256,10]{0,1:T(8,128)S(1)}, f32[256,10]{0,1:T(8,128)S(1)}, f32[256,10]{0,1:T(8,128)S(1)}, f32[256,10,128]{0,2,1:T(8,128)S(1)}, f32[256,10,128]{0,2,1:T(8,128)S(1)})) conditional(s32[]{:T(128)} %bitcast.188, (f32[256,10]{0,1:T(8,128)S(1)}, f32[256,10]{0,1:T(8,128)S(1)}, f32[256,10]{0,1:T(8,128)S(1)}, ...), branch_computations={%region_36.36_spmd, %region_37.40_spmd} | conditional | flops 254775040 | bytes 20202780 | solution.py:96
  361.1 30.1 %while.167 = (s32[]{:T(128)}, f32[256,10]{0,1:T(8,128)S(1)}, f32[256,10]{0,1:T(8,128)S(1)}, f32[256,10]{0,1:T(8,128)S(1)}, f32[256,10,128]{0,2,1:T(8,128)S(1)}, ...) while((s32[]{:T(128)}, f32[256,10]{0,1:T(8,128)S(1)}, ...), condition=%wide.region_48.49_spmd, body=%wide.region_42.48_spmd.sunk | while | flops 254775056 | bytes 20203304 | solution.py:98
  362.4 6.2 %conditional.20 = ((f32[256,10]{0,1:T(8,128)S(1)}, f32[256,10]{0,1:T(8,128)S(1)}, f32[256,10]{0,1:T(8,128)S(1)}, f32[256,10,128]{0,2,1:T(8,128)S(1)}, f32[256,10,128]{0,2,1:T(8,128)S(1)})) conditional(s32[]{:T(128)} %bitcast.189, (f32[256,10]{0,1:T(8,128)S(1)}, f32[256,10]{0,1:T(8,128)S(1)}, f32[256,10]{0,1:T(8,128)S(1)}, ...), branch_computations={%region_43.43_spmd, %region_44.47_spmd} | conditional | flops 254775040 | bytes 20202780 | solution.py:96
  370.0 6.2 %conditional.20 = ((f32[256,10]{0,1:T(8,128)S(1)}, f32[256,10]{0,1:T(8,128)S(1)}, f32[256,10]{0,1:T(8,128)S(1)}, f32[256,10,128]{0,2,1:T(8,128)S(1)}, f32[256,10,128]{0,2,1:T(8,128)S(1)})) conditional(s32[]{:T(128)} %bitcast.189, (f32[256,10]{0,1:T(8,128)S(1)}, f32[256,10]{0,1:T(8,128)S(1)}, f32[256,10]{0,1:T(8,128)S(1)}, ...), branch_computations={%region_43.43_spmd, %region_44.47_spmd} | conditional | flops 254775040 | bytes 20202780 | solution.py:96
  377.5 6.2 %conditional.20 = ((f32[256,10]{0,1:T(8,128)S(1)}, f32[256,10]{0,1:T(8,128)S(1)}, f32[256,10]{0,1:T(8,128)S(1)}, f32[256,10,128]{0,2,1:T(8,128)S(1)}, f32[256,10,128]{0,2,1:T(8,128)S(1)})) conditional(s32[]{:T(128)} %bitcast.189, (f32[256,10]{0,1:T(8,128)S(1)}, f32[256,10]{0,1:T(8,128)S(1)}, f32[256,10]{0,1:T(8,128)S(1)}, ...), branch_computations={%region_43.43_spmd, %region_44.47_spmd} | conditional | flops 254775040 | bytes 20202780 | solution.py:96
  385.0 6.2 %conditional.20 = ((f32[256,10]{0,1:T(8,128)S(1)}, f32[256,10]{0,1:T(8,128)S(1)}, f32[256,10]{0,1:T(8,128)S(1)}, f32[256,10,128]{0,2,1:T(8,128)S(1)}, f32[256,10,128]{0,2,1:T(8,128)S(1)})) conditional(s32[]{:T(128)} %bitcast.189, (f32[256,10]{0,1:T(8,128)S(1)}, f32[256,10]{0,1:T(8,128)S(1)}, f32[256,10]{0,1:T(8,128)S(1)}, ...), branch_computations={%region_43.43_spmd, %region_44.47_spmd} | conditional | flops 254775040 | bytes 20202780 | solution.py:96
  (661 shorter events, 199.1 us)
Async XLA Ops:
  0.6 2.7 copy-start.33
  0.6 7.7 %copy-start.34 = (bf16[256,1280]{1,0:T(8,128)(2,1)S(1)}, bf16[256,1280]{1,0:T(8,128)(2,1)}, u32[]{:S(2)}) copy-start(bf16[256,1280]{1,0:T(8,128)(2,1)} %param.39) | copy-start | bytes 1966084
  2.9 6.5 %copy-start.35 = (bf16[256,1280]{1,0:T(8,128)(2,1)S(1)}, bf16[256,1280]{1,0:T(8,128)(2,1)}, u32[]{:S(2)}) copy-start(bf16[256,1280]{1,0:T(8,128)(2,1)} %param.40) | copy-start | bytes 1966084
  2.9 17.9 %collective-permute-start = (bf16[256,10,128]{0,2,1:T(8,128)(2,1)}, bf16[256,10,128]{0,2,1:T(8,128)(2,1)}, u32[]{:S(2)}, u32[]{:S(2)}) collective-permute-start(bf16[256,10,128]{0,2,1:T(8,128)(2,1)} %bitcast.42), channel_id=1, source_target_pairs={{0,252},{4,0},{8,4},{12,8},{16,12},{20,16},{24,20},{28,24},{32,28}... | collective-permute-start | bytes 1966088 | tf_op jit(solution)/shard_map/ppermute | solution.py:17
  4.4 30.5 %collective-permute-start.1 = (bf16[256,10,128]{0,2,1:T(8,128)(2,1)}, bf16[256,10,128]{0,2,1:T(8,128)(2,1)}, u32[]{:S(2)}, u32[]{:S(2)}) collective-permute-start(bf16[256,10,128]{0,2,1:T(8,128)(2,1)} %bitcast.45), channel_id=1, source_target_pairs={{0,252},{4,0},{8,4},{12,8},{16,12},{20,16},{24,20},{28,24},{32,28}... | collective-permute-start | bytes 1966088 | tf_op jit(solution)/shard_map/ppermute | solution.py:17
  8.5 165.4 %copy-start.10 = (bf16[256,1280]{0,1:T(8,128)(2,1)}, bf16[256,1280]{0,1:T(8,128)(2,1)S(1)}, u32[]{:S(2)}) copy-start(bf16[256,1280]{0,1:T(8,128)(2,1)S(1)} %copy.59) | copy-start | bytes 1966084
  8.5 40.3 %collective-permute-start.2 = (bf16[256,10,128]{0,2,1:T(8,128)(2,1)S(1)}, bf16[256,10,128]{0,2,1:T(8,128)(2,1)S(1)}, u32[]{:S(2)}, u32[]{:S(2)}) collective-permute-start(bf16[256,10,128]{0,2,1:T(8,128)(2,1)S(1)} %bitcast.190), channel_id=1, source_target_pairs={{0,252},{4,0},{8,4},{12,8},{16,12},{20,16},{24,20},{28,24},{32,28}... | collective-permute-start | bytes 1966088 | tf_op jit(solution)/shard_map/ppermute | solution.py:17
  9.6 166.5 %copy-start.23 = (bf16[256,1280]{0,1:T(8,128)(2,1)}, bf16[256,1280]{0,1:T(8,128)(2,1)S(1)}, u32[]{:S(2)}) copy-start(bf16[256,1280]{0,1:T(8,128)(2,1)S(1)} %copy.60) | copy-start | bytes 1966084
  9.6 52.1 %collective-permute-start.3 = (bf16[256,10,128]{0,2,1:T(8,128)(2,1)S(1)}, bf16[256,10,128]{0,2,1:T(8,128)(2,1)S(1)}, u32[]{:S(2)}, u32[]{:S(2)}) collective-permute-start(bf16[256,10,128]{0,2,1:T(8,128)(2,1)S(1)} %bitcast.193), channel_id=1, source_target_pairs={{0,252},{4,0},{8,4},{12,8},{16,12},{20,16},{24,20},{28,24},{32,28}... | collective-permute-start | bytes 1966088 | tf_op jit(solution)/shard_map/ppermute | solution.py:17
  10.1 53.4 %collective-permute-start.4 = (bf16[256,10,128]{0,2,1:T(8,128)(2,1)}, bf16[256,10,128]{0,2,1:T(8,128)(2,1)S(1)}, u32[]{:S(2)}, u32[]{:S(2)}) collective-permute-start(bf16[256,10,128]{0,2,1:T(8,128)(2,1)} %bitcast.42), channel_id=1, source_target_pairs={{0,4},{4,8},{8,12},{12,16},{16,20},{20,24},{24,28},{28,32},{32,36}... | collective-permute-start | bytes 1966088 | tf_op jit(solution)/shard_map/ppermute | solution.py:17
  20.9 48.8 %collective-permute-start.5 = (bf16[256,10,128]{0,2,1:T(8,128)(2,1)}, bf16[256,10,128]{0,2,1:T(8,128)(2,1)S(1)}, u32[]{:S(2)}, u32[]{:S(2)}) collective-permute-start(bf16[256,10,128]{0,2,1:T(8,128)(2,1)} %bitcast.45), channel_id=1, source_target_pairs={{0,4},{4,8},{8,12},{12,16},{16,20},{20,24},{24,28},{28,32},{32,36}... | collective-permute-start | bytes 1966088 | tf_op jit(solution)/shard_map/ppermute | solution.py:17
  34.9 34.9 %collective-permute-start.6 = (bf16[256,10,128]{0,2,1:T(8,128)(2,1)S(1)}, bf16[256,10,128]{0,2,1:T(8,128)(2,1)S(1)}, u32[]{:S(2)}, u32[]{:S(2)}) collective-permute-start(bf16[256,10,128]{0,2,1:T(8,128)(2,1)S(1)} %bitcast.191), channel_id=1, source_target_pairs={{0,4},{4,8},{8,12},{12,16},{16,20},{20,24},{24,28},{28,32},{32,36}... | collective-permute-start | bytes 1966088 | tf_op jit(solution)/shard_map/ppermute | solution.py:17
  48.8 127.2 %copy-start.18 = (bf16[256,10,128]{0,2,1:T(8,128)(2,1)}, bf16[256,10,128]{0,2,1:T(8,128)(2,1)S(1)}, u32[]{:S(2)}) copy-start(bf16[256,10,128]{0,2,1:T(8,128)(2,1)S(1)} %collective-permute-done.2) | copy-start | bytes 1966084
  48.8 21.0 %collective-permute-start.7 = (bf16[256,10,128]{0,2,1:T(8,128)(2,1)S(1)}, bf16[256,10,128]{0,2,1:T(8,128)(2,1)S(1)}, u32[]{:S(2)}, u32[]{:S(2)}) collective-permute-start(bf16[256,10,128]{0,2,1:T(8,128)(2,1)S(1)} %bitcast.194), channel_id=1, source_target_pairs={{0,4},{4,8},{8,12},{12,16},{16,20},{20,24},{24,28},{28,32},{32,36}... | collective-permute-start | bytes 1966088 | tf_op jit(solution)/shard_map/ppermute | solution.py:17
  61.7 72.6 %copy-start.31 = (bf16[256,10,128]{0,2,1:T(8,128)(2,1)}, bf16[256,10,128]{0,2,1:T(8,128)(2,1)S(1)}, u32[]{:S(2)}) copy-start(bf16[256,10,128]{0,2,1:T(8,128)(2,1)S(1)} %collective-permute-done.3) | copy-start | bytes 1966084
  61.7 17.9 %collective-permute-start.8 = (bf16[256,10,128]{0,2,1:T(8,128)(2,1)}, bf16[256,10,128]{0,2,1:T(8,128)(2,1)S(1)}, u32[]{:S(2)}, u32[]{:S(2)}) collective-permute-start(bf16[256,10,128]{0,2,1:T(8,128)(2,1)} %collective-permute-done), channel_id=1, source_target_pairs={{0,252},{4,0},{8,4},{12,8},{16,12},{20,16},{24,20},{28,24},{32,28}... | collective-permute-start | bytes 1966088 | tf_op jit(solution)/shard_map/ppermute | solution.py:17
  63.6 100.3 %copy-start.40 = (bf16[256,10,128]{0,2,1:T(8,128)(2,1)}, bf16[256,10,128]{0,2,1:T(8,128)(2,1)S(1)}, u32[]{:S(2)}) copy-start(bf16[256,10,128]{0,2,1:T(8,128)(2,1)S(1)} %collective-permute-done.4) | copy-start | bytes 1966084
  63.6 30.1 %collective-permute-start.9 = (bf16[256,10,128]{0,2,1:T(8,128)(2,1)}, bf16[256,10,128]{0,2,1:T(8,128)(2,1)S(1)}, u32[]{:S(2)}, u32[]{:S(2)}) collective-permute-start(bf16[256,10,128]{0,2,1:T(8,128)(2,1)} %collective-permute-done.1), channel_id=1, source_target_pairs={{0,252},{4,0},{8,4},{12,8},{16,12},{20,16},{24,20},{28,24},{32,28}... | collective-permute-start | bytes 1966088 | tf_op jit(solution)/shard_map/ppermute | solution.py:17
  69.7 94.2 %copy-start.41 = (bf16[256,10,128]{0,2,1:T(8,128)(2,1)}, bf16[256,10,128]{0,2,1:T(8,128)(2,1)S(1)}, u32[]{:S(2)}) copy-start(bf16[256,10,128]{0,2,1:T(8,128)(2,1)S(1)} %collective-permute-done.5) | copy-start | bytes 1966084
  69.7 38.1 %collective-permute-start.10 = (bf16[256,10,128]{0,2,1:T(8,128)(2,1)S(1)}, bf16[256,10,128]{0,2,1:T(8,128)(2,1)}, u32[]{:S(2)}, u32[]{:S(2)}) collective-permute-start(bf16[256,10,128]{0,2,1:T(8,128)(2,1)S(1)} %collective-permute-done.2), channel_id=1, source_target_pairs={{0,252},{4,0},{8,4},{12,8},{16,12},{20,16},{24,20},{28,24},{32,28}... | collective-permute-start | bytes 1966088 | tf_op jit(solution)/shard_map/ppermute | solution.py:17
  69.8 106.3 %copy-start.16 = (bf16[256,10,128]{0,2,1:T(8,128)(2,1)}, bf16[256,10,128]{0,2,1:T(8,128)(2,1)S(1)}, u32[]{:S(2)}) copy-start(bf16[256,10,128]{0,2,1:T(8,128)(2,1)S(1)} %collective-permute-done.6) | copy-start | bytes 1966084
  69.8 50.0 %collective-permute-start.11 = (bf16[256,10,128]{0,2,1:T(8,128)(2,1)S(1)}, bf16[256,10,128]{0,2,1:T(8,128)(2,1)}, u32[]{:S(2)}, u32[]{:S(2)}) collective-permute-start(bf16[256,10,128]{0,2,1:T(8,128)(2,1)S(1)} %collective-permute-done.3), channel_id=1, source_target_pairs={{0,252},{4,0},{8,4},{12,8},{16,12},{20,16},{24,20},{28,24},{32,28}... | collective-permute-start | bytes 1966088 | tf_op jit(solution)/shard_map/ppermute | solution.py:17
  69.9 106.2 %copy-start.29 = (bf16[256,10,128]{0,2,1:T(8,128)(2,1)}, bf16[256,10,128]{0,2,1:T(8,128)(2,1)S(1)}, u32[]{:S(2)}) copy-start(bf16[256,10,128]{0,2,1:T(8,128)(2,1)S(1)} %collective-permute-done.7) | copy-start | bytes 1966084
  69.9 55.2 %collective-permute-start.12 = (bf16[256,10,128]{0,2,1:T(8,128)(2,1)S(1)}, bf16[256,10,128]{0,2,1:T(8,128)(2,1)S(1)}, u32[]{:S(2)}, u32[]{:S(2)}) collective-permute-start(bf16[256,10,128]{0,2,1:T(8,128)(2,1)S(1)} %collective-permute-done.4), channel_id=1, source_target_pairs={{0,4},{4,8},{8,12},{12,16},{16,20},{20,24},{24,28},{28,32},{32,36}... | collective-permute-start | bytes 1966088 | tf_op jit(solution)/shard_map/ppermute | solution.py:17
  79.6 54.7 %copy-start.37 = (bf16[256,10,128]{0,2,1:T(8,128)(2,1)}, bf16[256,10,128]{0,2,1:T(8,128)(2,1)S(1)}, u32[]{:S(2)}) copy-start(bf16[256,10,128]{0,2,1:T(8,128)(2,1)S(1)} %collective-permute-done.8) | copy-start | bytes 1966084
  79.6 51.7 %collective-permute-start.13 = (bf16[256,10,128]{0,2,1:T(8,128)(2,1)S(1)}, bf16[256,10,128]{0,2,1:T(8,128)(2,1)}, u32[]{:S(2)}, u32[]{:S(2)}) collective-permute-start(bf16[256,10,128]{0,2,1:T(8,128)(2,1)S(1)} %collective-permute-done.5), channel_id=1, source_target_pairs={{0,4},{4,8},{8,12},{12,16},{16,20},{20,24},{24,28},{28,32},{32,36}... | collective-permute-start | bytes 1966088 | tf_op jit(solution)/shard_map/ppermute | solution.py:17
  93.7 48.7 %copy-start.38 = (bf16[256,10,128]{0,2,1:T(8,128)(2,1)}, bf16[256,10,128]{0,2,1:T(8,128)(2,1)S(1)}, u32[]{:S(2)}) copy-start(bf16[256,10,128]{0,2,1:T(8,128)(2,1)S(1)} %collective-permute-done.9) | copy-start | bytes 1966084
  93.7 37.7 %collective-permute-start.14 = (bf16[256,10,128]{0,2,1:T(8,128)(2,1)S(1)}, bf16[256,10,128]{0,2,1:T(8,128)(2,1)}, u32[]{:S(2)}, u32[]{:S(2)}) collective-permute-start(bf16[256,10,128]{0,2,1:T(8,128)(2,1)S(1)} %collective-permute-done.6), channel_id=1, source_target_pairs={{0,4},{4,8},{8,12},{12,16},{16,20},{20,24},{24,28},{28,32},{32,36}... | collective-permute-start | bytes 1966088 | tf_op jit(solution)/shard_map/ppermute | solution.py:17
  107.8 26.5 %collective-permute-start.15 = (bf16[256,10,128]{0,2,1:T(8,128)(2,1)S(1)}, bf16[256,10,128]{0,2,1:T(8,128)(2,1)}, u32[]{:S(2)}, u32[]{:S(2)}) collective-permute-start(bf16[256,10,128]{0,2,1:T(8,128)(2,1)S(1)} %collective-permute-done.7), channel_id=1, source_target_pairs={{0,4},{4,8},{8,12},{12,16},{16,20},{20,24},{24,28},{28,32},{32,36}... | collective-permute-start | bytes 1966088 | tf_op jit(solution)/shard_map/ppermute | solution.py:17
  119.8 22.6 %collective-permute-start.16 = (bf16[256,10,128]{0,2,1:T(8,128)(2,1)S(1)}, bf16[256,10,128]{0,2,1:T(8,128)(2,1)}, u32[]{:S(2)}, u32[]{:S(2)}) collective-permute-start(bf16[256,10,128]{0,2,1:T(8,128)(2,1)S(1)} %collective-permute-done.8), channel_id=1, source_target_pairs={{0,252},{4,0},{8,4},{12,8},{16,12},{20,16},{24,20},{28,24},{32,28}... | collective-permute-start | bytes 1966088 | tf_op jit(solution)/shard_map/ppermute | solution.py:17
  125.1 31.3 %copy-start.39 = (bf16[256,10,128]{0,2,1:T(8,128)(2,1)}, bf16[256,10,128]{0,2,1:T(8,128)(2,1)S(1)}, u32[]{:S(2)}) copy-start(bf16[256,10,128]{0,2,1:T(8,128)(2,1)S(1)} %collective-permute-done.12) | copy-start | bytes 1966084
  125.1 31.3 %collective-permute-start.17 = (bf16[256,10,128]{0,2,1:T(8,128)(2,1)S(1)}, bf16[256,10,128]{0,2,1:T(8,128)(2,1)}, u32[]{:S(2)}, u32[]{:S(2)}) collective-permute-start(bf16[256,10,128]{0,2,1:T(8,128)(2,1)S(1)} %collective-permute-done.9), channel_id=1, source_target_pairs={{0,252},{4,0},{8,4},{12,8},{16,12},{20,16},{24,20},{28,24},{32,28}... | collective-permute-start | bytes 1966088 | tf_op jit(solution)/shard_map/ppermute | solution.py:17
  131.3 32.6 %collective-permute-start.20 = (bf16[256,10,128]{0,2,1:T(8,128)(2,1)S(1)}, bf16[256,10,128]{0,2,1:T(8,128)(2,1)}, u32[]{:S(2)}, u32[]{:S(2)}) collective-permute-start(bf16[256,10,128]{0,2,1:T(8,128)(2,1)S(1)} %collective-permute-done.12), channel_id=1, source_target_pairs={{0,4},{4,8},{8,12},{12,16},{16,20},{20,24},{24,28},{28,32},{32,36}... | collective-permute-start | bytes 1966088 | tf_op jit(solution)/shard_map/ppermute | solution.py:17
  131.3 197.6 %collective-permute-start.21 = (bf16[256,10,128]{0,2,1:T(8,128)(2,1)}, bf16[256,10,128]{0,2,1:T(8,128)(2,1)}, u32[]{:S(2)}, u32[]{:S(2)}) collective-permute-start(bf16[256,10,128]{0,2,1:T(8,128)(2,1)} %collective-permute-done.13), channel_id=1, source_target_pairs={{0,4},{4,8},{8,12},{12,16},{16,20},{20,24},{24,28},{28,32},{32,36}... | collective-permute-start | bytes 1966088 | tf_op jit(solution)/shard_map/ppermute | solution.py:17
  134.3 196.8 %collective-permute-start.18 = (bf16[256,10,128]{0,2,1:T(8,128)(2,1)}, bf16[256,10,128]{0,2,1:T(8,128)(2,1)}, u32[]{:S(2)}, u32[]{:S(2)}) collective-permute-start(bf16[256,10,128]{0,2,1:T(8,128)(2,1)} %collective-permute-done.10), channel_id=1, source_target_pairs={{0,252},{4,0},{8,4},{12,8},{16,12},{20,16},{24,20},{28,24},{32,28}... | collective-permute-start | bytes 1966088 | tf_op jit(solution)/shard_map/ppermute | solution.py:17
  142.4 188.7 %collective-permute-start.19 = (bf16[256,10,128]{0,2,1:T(8,128)(2,1)}, bf16[256,10,128]{0,2,1:T(8,128)(2,1)}, u32[]{:S(2)}, u32[]{:S(2)}) collective-permute-start(bf16[256,10,128]{0,2,1:T(8,128)(2,1)} %collective-permute-done.11), channel_id=1, source_target_pairs={{0,252},{4,0},{8,4},{12,8},{16,12},{20,16},{24,20},{28,24},{32,28}... | collective-permute-start | bytes 1966088 | tf_op jit(solution)/shard_map/ppermute | solution.py:17
  156.4 204.7 %collective-permute-start.22 = (bf16[256,10,128]{0,2,1:T(8,128)(2,1)}, bf16[256,10,128]{0,2,1:T(8,128)(2,1)}, u32[]{:S(2)}, u32[]{:S(2)}) collective-permute-start(bf16[256,10,128]{0,2,1:T(8,128)(2,1)} %collective-permute-done.14), channel_id=1, source_target_pairs={{0,4},{4,8},{8,12},{12,16},{16,20},{20,24},{24,28},{28,32},{32,36}... | collective-permute-start | bytes 1966088 | tf_op jit(solution)/shard_map/ppermute | solution.py:17
  163.9 197.2 %collective-permute-start.23 = (bf16[256,10,128]{0,2,1:T(8,128)(2,1)}, bf16[256,10,128]{0,2,1:T(8,128)(2,1)}, u32[]{:S(2)}, u32[]{:S(2)}) collective-permute-start(bf16[256,10,128]{0,2,1:T(8,128)(2,1)} %collective-permute-done.15), channel_id=1, source_target_pairs={{0,4},{4,8},{8,12},{12,16},{16,20},{20,24},{24,28},{28,32},{32,36}... | collective-permute-start | bytes 1966088 | tf_op jit(solution)/shard_map/ppermute | solution.py:17
  181.3 1.9 copy-start.25
  186.8 1.9 copy-start.25
  192.4 1.9 copy-start.25
  198.0 1.9 copy-start.25
  212.0 1.9 copy-start.27
  217.3 1.9 copy-start.27
  222.7 1.9 copy-start.27
  228.1 1.9 copy-start.27
  233.5 1.9 copy-start.21
  238.9 1.9 copy-start.21
  244.4 1.9 copy-start.21
  249.8 1.9 copy-start.21
  271.2 1.9 copy-start.28
  286.0 1.9 copy-start.28
  293.6 1.9 copy-start.22
  301.1 1.9 copy-start.22
  308.6 1.9 copy-start.22
  316.1 1.9 copy-start.22
  332.4 1.9 copy-start.26
  339.9 1.9 copy-start.26
  347.4 1.9 copy-start.26
  354.9 1.9 copy-start.26
  362.5 1.9 copy-start.20
  370.0 1.9 copy-start.20
  377.5 1.9 copy-start.20
  385.0 1.9 copy-start.20
  (84 other events, 119.5 us)
where the time goes:
time: 399 us; the launch traced here: 396 us
  matrix products  130 us (33%)
  waiting for transfers between devices  91.6 us (23%)
  starting transfers between devices  75.6 us (19%)
  local copies, waits for them, and re-layouts  69.5 us (17%)
  loops' own time  22.9 us (6%)
  other arithmetic  5.39 us (1%)
    ppermute x24, waiting for transfers between devices, from_behind(): lax.ppermute(array, axis, [(i, (i + by) % devices) for i in range(devices)])  91.6 us
    ppermute x24, starting transfers between devices, from_behind(): lax.ppermute(array, axis, [(i, (i + by) % devices) for i in range(devices)])  75.6 us
    dot_general x28, matrix products, tile_update(): jnp.einsum('qhd,khd->qhk', query_block, key_block, preferred_element_type...  41.4 us
    while x16, local copies, waits for them, and re-layouts, sweep(): return lax.fori_loop(0, per_device * per_device, visit, tuple(accumulators))  31.8 us
    dot_general x28, matrix products, tile_update(): jnp.einsum('qhk,khd->qhd', rounded_weights, value_block, preferred_elemen...  22.8 us
    dot_general x28, matrix products, tile_update(): jnp.einsum('qhk,khd->qhd', rounded_weights, value_tangent, preferred_elem...  22.6 us
    dot_general x28, matrix products, tile_update(): jnp.einsum('qhk,khd->qhd', rounded_tangent, value_block, preferred_elemen...  22.3 us
    another operation x7, loops' own time, sweep(): return lax.fori_loop(0, per_device * per_device, visit, tuple(accumulators))  18.5 us
  transfers between devices with their start and end apart: 24, of which 10 were waited for; matrix products, arithmetic and copies ran while one was open for 40% of the time, Pallas kernels for 0%

commit v1 on v0

v1 whole, which is shorter than its diff:
```python
import functools

import jax
import jax.numpy as jnp
from jax import lax
from jax.experimental import pallas as pl
from jax.experimental.pallas import tpu as pltpu
from jax.sharding import PartitionSpec as P

HEADS = 10
HEAD_DIM = 128
BLK = 128
REACH = 3
TOK = 256
WIN = 14
PLANE = 8
CHUNKS = 2 * REACH + 1
NEG = -1.0e30
LOG2E = 1.4426950408889634
SCALE = HEAD_DIM ** -0.5
MIB = 1 << 20

VMEM_SPEC = pl.BlockSpec(memory_space=pltpu.VMEM)
SMEM_SPEC = pl.BlockSpec(memory_space=pltpu.SMEM)


def pack_kernel(par_ref, q, qt, k, kt, v, vt, sel, kv_out, q_out, kv_same, kv_opp, q_same, q_opp):
    par = par_ref[0]
    for j in range(PLANE):
        cols = pl.ds(j * HEAD_DIM, HEAD_DIM)
        for n, ref in enumerate((k, kt, v, vt)):
            kv_out[j, :, n * HEAD_DIM:(n + 1) * HEAD_DIM] = ref[:, cols]
        for n, ref in enumerate((qt, q)):
            q_out[j, 0:TOK, n * HEAD_DIM:(n + 1) * HEAD_DIM] = ref[:, cols]
        q_out[j, TOK:TOK + 16, :] = sel[...]
    for which, kv_to, q_to in ((par, kv_same, q_same), (1 - par, kv_opp, q_opp)):
        cols = pl.ds(pl.multiple_of((PLANE + which) * HEAD_DIM, HEAD_DIM), HEAD_DIM)
        for n, ref in enumerate((k, kt, v, vt)):
            kv_to[:, n * HEAD_DIM:(n + 1) * HEAD_DIM] = ref[:, cols]
        for n, ref in enumerate((qt, q)):
            q_to[:, n * HEAD_DIM:(n + 1) * HEAD_DIM] = ref[:, cols]


def attend(sel_ref, row, base, qcat, kk, vv, s_scr, p_scr, t_scr):
    dims = (((1,), (1,)), ((), ()))
    query = qcat[:, HEAD_DIM:]
    peak = [None, None]
    for t in range(CHUNKS):
        keys = kk[pl.ds(base + t * TOK, TOK), :HEAD_DIM]
        s = lax.dot_general(query, keys, dims, preferred_element_type=jnp.float32)
        for qb in range(2):
            for kb in range(2):
                listed = sel_ref[row, qb * WIN + 2 * t + kb]
                bias = jnp.where(listed != 0, 0.0, NEG)
                piece = s[qb * BLK:(qb + 1) * BLK, kb * BLK:(kb + 1) * BLK] + bias
                s_scr[qb * BLK:(qb + 1) * BLK, t * TOK + kb * BLK:t * TOK + (kb + 1) * BLK] = piece
                peak[qb] = piece if peak[qb] is None else jnp.maximum(peak[qb], piece)
    factor = SCALE * LOG2E
    top = jnp.concatenate([jnp.max(p, axis=1, keepdims=True) for p in peak], axis=0) * factor
    total = jnp.zeros((TOK, BLK), jnp.float32)
    tangent_total = jnp.zeros((TOK, BLK), jnp.float32)
    for t in range(CHUNKS):
        both = kk[pl.ds(base + t * TOK, TOK), :]
        st = lax.dot_general(qcat, both, dims, preferred_element_type=jnp.float32)
        weights = jnp.exp2(s_scr[:, t * TOK:(t + 1) * TOK] * factor - top)
        weighted = weights * st
        total += weights[:, :BLK] + weights[:, BLK:]
        tangent_total += weighted[:, :BLK] + weighted[:, BLK:]
        p_scr[:, t * TOK:(t + 1) * TOK] = weights.astype(jnp.bfloat16)
        t_scr[:, t * TOK:(t + 1) * TOK] = weighted.astype(jnp.bfloat16)
    window = pl.ds(base, CHUNKS * TOK)
    first = jnp.dot(p_scr[...], vv[window, :], preferred_element_type=jnp.float32)
    second = jnp.dot(t_scr[...], vv[window, :HEAD_DIM], preferred_element_type=jnp.float32)
    inverse = 1.0 / jnp.sum(total, axis=1, keepdims=True)
    out = first[:, :HEAD_DIM] * inverse
    tangent_sum = jnp.sum(tangent_total, axis=1, keepdims=True)
    tangent = ((second - out * tangent_sum) * SCALE + first[:, HEAD_DIM:]) * inverse
    return jnp.concatenate([out.astype(jnp.bfloat16), tangent.astype(jnp.bfloat16)], axis=1)


def plane_kernel(sel_ref, q_ref, main, up, dn, o_ref, kk, vv, s_scr, p_scr, t_scr):
    half = 2 * HEAD_DIM
    for slot in range(PLANE + 2 * REACH):
        if slot < REACH:
            piece = up.at[slot]
        elif slot < REACH + PLANE:
            piece = main.at[slot - REACH]
        else:
            piece = dn.at[slot - REACH - PLANE]
        kk[slot * TOK:(slot + 1) * TOK, :] = piece[:, :half]
        vv[slot * TOK:(slot + 1) * TOK, :] = piece[:, half:]

    def step(i, carry):
        base = pl.multiple_of(i * TOK, TOK)
        o_ref[i] = attend(sel_ref, i, base, q_ref[i, :TOK, :], kk, vv, s_scr, p_scr, t_scr)
        return carry

    lax.fori_loop(0, PLANE, step, 0)


def pair_kernel(where_ref, sel_ref, q_own, q_other, a3, a2, a1, own, b1, b2, b3, far, o_own, o_other,
                kk, vv, s_scr, p_scr, t_scr):
    half = 2 * HEAD_DIM
    par, row = where_ref[0], where_ref[1]
    for place, piece in enumerate((a3, a2, a1, own, b1, b2, b3)):
        rows = pl.ds(pl.multiple_of((place + par) * TOK, TOK), TOK)
        kk[rows, :] = piece[:, :half]
        vv[rows, :] = piece[:, half:]
    rows = pl.ds(pl.multiple_of((1 - par) * CHUNKS * TOK, TOK), TOK)
    kk[rows, :] = far[:, :half]
    vv[rows, :] = far[:, half:]
    base = pl.multiple_of(par * TOK, TOK)
    o_own[...] = attend(sel_ref, row, base, q_own[...], kk, vv, s_scr, p_scr, t_scr)
    base = pl.multiple_of((1 - par) * TOK, TOK)
    o_other[...] = attend(sel_ref, row + 1 - 2 * par, base, q_other[...], kk, vv, s_scr, p_scr, t_scr)


def unpack_kernel(par_ref, mine, own, other, o_ref, t_ref):
    par = par_ref[0]
    for j in range(PLANE):
        cols = pl.ds(j * HEAD_DIM, HEAD_DIM)
        o_ref[:, cols] = mine[j, :, :HEAD_DIM]
        t_ref[:, cols] = mine[j, :, HEAD_DIM:]
    for which, piece in ((par, own), (1 - par, other)):
        cols = pl.ds(pl.multiple_of((PLANE + which) * HEAD_DIM, HEAD_DIM), HEAD_DIM)
        o_ref[:, cols] = piece[:, :HEAD_DIM]
        t_ref[:, cols] = piece[:, HEAD_DIM:]


def bf16(*shape):
    return jax.ShapeDtypeStruct(shape, jnp.bfloat16)


def scratch(slots):
    return [
        pltpu.VMEM((slots * TOK, 2 * HEAD_DIM), jnp.bfloat16),
        pltpu.VMEM((slots * TOK, 2 * HEAD_DIM), jnp.bfloat16),
        pltpu.VMEM((TOK, CHUNKS * TOK), jnp.float32),
        pltpu.VMEM((TOK, CHUNKS * TOK), jnp.bfloat16),
        pltpu.VMEM((TOK, CHUNKS * TOK), jnp.bfloat16),
    ]


def cost(positions):
    products = positions * CHUNKS * TOK * TOK
    return pl.CostEstimate(
        flops=10 * HEAD_DIM * products,
        bytes_accessed=(positions + 2 * REACH) * 4 * TOK * HEAD_DIM * 2 + positions * TOK * 4 * HEAD_DIM * 2,
        transcendentals=products,
    )


def body(queries, query_tangents, keys, key_tangents, values, value_tangents, selection):
    devices = lax.axis_size("ctx")
    me = lax.axis_index("ctx")
    par = (me % 2).astype(jnp.int32)
    where = jnp.stack([par, (me % PLANE).astype(jnp.int32)])
    planes = [[z * PLANE + i for i in range(PLANE)] for z in range(devices // PLANE)]


    def send(array, pairs):
        return lax.ppermute(array, "ctx", pairs)

    def shifted(by):
        return [(i, (i + by) % devices) for i in range(devices)]

    def exchange(array):
        return lax.all_to_all(array, "ctx", 0, 0, axis_index_groups=planes, tiled=True)

    sel_rows = jnp.pad(selection.astype(jnp.bfloat16).reshape(1, 2 * WIN), ((0, 15), (0, 2 * HEAD_DIM - 2 * WIN)))
    kv_out, q_out, kv_same, kv_opp, q_same, q_opp = pl.pallas_call(
        pack_kernel,
        out_shape=(bf16(PLANE, TOK, 512), bf16(PLANE, TOK + 16, 256), bf16(TOK, 512), bf16(TOK, 512),
                   bf16(TOK, 256), bf16(TOK, 256)),
        in_specs=[SMEM_SPEC] + [VMEM_SPEC] * 7,
        out_specs=(VMEM_SPEC,) * 6,
        compiler_params=pltpu.CompilerParams(vmem_limit_bytes=20 * MIB),
        name="pack",
    )(where, queries, query_tangents, keys, key_tangents, values, value_tangents, sel_rows)

    main = exchange(kv_out)
    up = send(main[PLANE - REACH:], shifted(PLANE))
    dn = send(main[:REACH], shifted(-PLANE))
    q_all = exchange(q_out)
    sel_all = q_all[:, TOK, :2 * WIN].astype(jnp.int32)

    swap = [(i, i ^ 1) for i in range(devices)]
    far_pairs = [(i, (i - 4) % devices) if i % 2 == 0 else (i, (i + 4) % devices) for i in range(devices)]
    a3 = send(kv_opp, shifted(3))
    b3 = send(kv_opp, shifted(-3))
    a2 = send(kv_same, shifted(2))
    b2 = send(kv_same, shifted(-2))
    a1 = send(kv_opp, shifted(1))
    b1 = send(kv_opp, shifted(-1))
    far = send(kv_same, far_pairs)
    q_other = send(q_opp, swap)

    mine = pl.pallas_call(
        plane_kernel,
        out_shape=bf16(PLANE, TOK, 256),
        in_specs=[SMEM_SPEC] + [VMEM_SPEC] * 4,
        out_specs=VMEM_SPEC,
        scratch_shapes=scratch(PLANE + 2 * REACH),
        compiler_params=pltpu.CompilerParams(vmem_limit_bytes=32 * MIB),
        cost_estimate=cost(PLANE),
        name="plane",
    )(sel_all, q_all, main, up, dn)
    back = exchange(mine)

    own, other = pl.pallas_call(
        pair_kernel,
        out_shape=(bf16(TOK, 256), bf16(TOK, 256)),
        in_specs=[SMEM_SPEC] * 2 + [VMEM_SPEC] * 10,
        out_specs=(VMEM_SPEC,) * 2,
        scratch_shapes=scratch(2 + 2 * REACH),
        compiler_params=pltpu.CompilerParams(vmem_limit_bytes=24 * MIB),
        cost_estimate=cost(2),
        name="pair",
    )(where, sel_all, q_same, q_other, a3, a2, a1, kv_same, b1, b2, b3, far)
    partner = send(other, swap)

    return pl.pallas_call(
        unpack_kernel,
        out_shape=(bf16(TOK, HEADS * HEAD_DIM), bf16(TOK, HEADS * HEAD_DIM)),
        in_specs=[SMEM_SPEC] + [VMEM_SPEC] * 3,
        out_specs=(VMEM_SPEC,) * 2,
        compiler_params=pltpu.CompilerParams(vmem_limit_bytes=12 * MIB),
        name="unpack",
    )(where, back, own, partner)


def solution(mesh):
    wide = P("ctx", "head")
    return jax.shard_map(
        body,
        mesh=mesh,
        in_specs=(wide,) * 6 + (P("ctx", None),),
        out_specs=(wide, wide),
        check_vma=False,
    )
```

time: 399 us -> 149 us (0.37)
  the two profiles are of different devices: /device:TPU:110 before, /device:TPU:4 now
where the time goes in v1:
time: 149 us; the launch traced here: 148 us
  waiting for transfers between devices  49.6 us (33%)
  starting transfers between devices  35.1 us (24%)
  blocking collectives  33 us (22%)
  Pallas kernels  20.3 us (14%)
  local copies, waits for them, and re-layouts  8.89 us (6%)
    ppermute x11, waiting for transfers between devices, send(): return lax.ppermute(array, 'ctx', pairs)  43.3 us
    all_to_all x1, blocking collectives, exchange(): lax.all_to_all(array, 'ctx', 0, 0, axis_index_groups=planes, tiled=True)  33 us
    ppermute x11, starting transfers between devices, send(): return lax.ppermute(array, 'ctx', pairs)  21.6 us
    pallas_call x1, Pallas kernels, body(): pl.pallas_call(plane_kernel, out_shape=bf16(PLANE, TOK, 256), in_specs=[S...  13.9 us
    all_to_all x2, starting transfers between devices, exchange(): lax.all_to_all(array, 'ctx', 0, 0, axis_index_groups=planes, tiled=True)  13.5 us
    unnamed x28, local copies, waits for them, and re-layouts  7.53 us
    all_to_all x2, waiting for transfers between devices, exchange(): lax.all_to_all(array, 'ctx', 0, 0, axis_index_groups=planes, tiled=True)  6.29 us
    pallas_call x1, Pallas kernels, body(): pl.pallas_call(pair_kernel, out_shape=(bf16(TOK, 256), bf16(TOK, 256)), i...  3.4 us
  transfers between devices with their start and end apart: 13, of which 7 were waited for; matrix products, arithmetic and copies ran while one was open for 1% of the time, Pallas kernels for 2%

profile of v1, /device:TPU:4, one launch (start us, length us, event | category | flops | bytes accessed | tf_op | source)
XLA Modules:
  0.0 148.4 jit_solution(7446408779777981944)
XLA Ops:
  0.6 0.7 convert_element_type.10
  1.3 0.1 reshape.9
  1.4 0.1 pad_add_fusion.par_ref.where_ref
  1.5 0.0 copy-start.2
  1.5 1.1 copy-done.2
  2.6 0.0 copy-start.3
  2.6 1.1 copy-done.3
  3.7 0.0 copy-start.4
  3.7 1.1 copy-done.4
  4.8 0.0 copy-start.5
  4.8 1.1 copy-done.5
  5.8 0.0 copy-start.6
  5.8 1.1 copy-done.6
  6.9 0.0 copy-start.7
  6.9 1.1 copy-done.7
  8.0 1.2 pack.1
  9.2 0.0 copy-start
  9.3 0.0 copy-start.8
  9.3 0.0 copy-start.10
  9.3 0.0 copy-start.12
  9.3 33.0 %all_to_all.15.main = bf16[8,256,512]{2,1,0:T(8,128)(2,1)S(1)} all-to-all(bf16[8,256,512]{2,1,0:T(8,128)(2,1)S(1)} %get-tuple-element.11), channel_id=1, replica_groups={{0,4,8,12,16,20,24,28},{32,36,40,44,48,52,56,60},{64,68,72,76,80,84,88,..., dimensions={0} | all-to-all | bytes 4194304 | tf_op jit(solution)/shard_map/all_to_all | solution.py:168
  42.3 0.0 copy-done
  42.3 0.0 copy-done.8
  42.3 0.0 copy-done.10
  42.3 0.0 copy-done.12
  42.3 6.1 %all-to-all-start = ((bf16[8,272,256]{2,1,0:T(8,128)(2,1)}), bf16[8,272,256]{2,1,0:T(8,128)(2,1)S(1)}, u32[]{:S(2)}, u32[]{:S(2)}) async-start(bf16[8,272,256]{2,1,0:T(8,128)(2,1)} %copy-done), calls=%async_computation | async-start | bytes 2228224 | tf_op jit(solution)/shard_map/all_to_all | solution.py:168
  48.4 1.3 fusion.1
  49.7 5.9 %collective-permute-start.1 = (bf16[3,256,512]{2,1,0:T(8,128)(2,1)}, bf16[3,256,512]{2,1,0:T(8,128)(2,1)}, u32[]{:S(2)}, u32[]{:S(2)}) collective-permute-start(bf16[3,256,512]{2,1,0:T(8,128)(2,1)} %get-tuple-element.18), channel_id=1, source_target_pairs={{0,224},{4,228},{8,232},{12,236},{16,240},{20,244},{24,248},{28,25... | collective-permute-start | bytes 2359304 | tf_op jit(solution)/shard_map/ppermute | solution.py:162
  55.5 0.0 collective-permute-start
  55.5 6.3 %all-to-all-done.q_ref = bf16[8,272,256]{2,1,0:T(8,128)(2,1)S(1)} async-done(((bf16[8,272,256]{2,1,0:T(8,128)(2,1)}), bf16[8,272,256]{2,1,0:T(8,128)(2,1)S(1)}, u32[]{:S(2)}, u32[]{:S(2)}) %all-to-all-start) | async-done | bytes 1114144 | tf_op jit(solution)/shard_map/all_to_all | solution.py:168
  61.8 8.7 %collective-permute-done.1.dn = bf16[3,256,512]{2,1,0:T(8,128)(2,1)} collective-permute-done((bf16[3,256,512]{2,1,0:T(8,128)(2,1)}, bf16[3,256,512]{2,1,0:T(8,128)(2,1)}, u32[]{:S(2)}, u32[]{:S(2)}) %collective-permute-start.1) | collective-permute-done | bytes 786464 | tf_op jit(solution)/shard_map/ppermute | solution.py:162
  70.5 3.4 %collective-permute-done.up = bf16[3,256,512]{2,1,0:T(8,128)(2,1)} collective-permute-done((bf16[3,256,512]{2,1,0:T(8,128)(2,1)}, bf16[3,256,512]{2,1,0:T(8,128)(2,1)}, u32[]{:S(2)}, u32[]{:S(2)}) %collective-permute-start) | collective-permute-done | bytes 786464 | tf_op jit(solution)/shard_map/ppermute | solution.py:162
  74.0 13.9 %plane.1 = bf16[8,256,256]{2,1,0:T(8,128)(2,1)S(1)} custom-call(s32[8,28]{1,0:T(8,128)S(1)} %fusion.sel_ref, bf16[8,272,256]{2,1,0:T(8,128)(2,1)S(1)} %all-to-all-done.q_ref, bf16[8,256,512]{2,1,0:T(8,128)(2,1)S(1)} %all_to_all.15.main, bf16[3,256,512]{2,1,0:T(8,128)(2,1)} %collective-permute-done.up, bf16[3,256,512]{2,1,0:T(8,128)(2,1)} %collective-permute-done.1.dn), custom_call_target="tpu_custom_call" | custom-call | flops 4697620480 | bytes 5767168 | tf_op jit(solution)/shard_map/plane/pallas_call | solution.py:198
  87.8 0.0 copy-start.1
  87.8 1.0 copy-done.1
  88.8 0.0 copy-start.9
  88.8 0.0 copy-start.13
  88.8 0.0 copy-start.11
  88.8 7.4 %all-to-all-start.2 = ((bf16[8,256,256]{2,1,0:T(8,128)(2,1)}), bf16[8,256,256]{2,1,0:T(8,128)(2,1)S(1)}, u32[]{:S(2)}, u32[]{:S(2)}) async-start(bf16[8,256,256]{2,1,0:T(8,128)(2,1)} %copy-done.1), calls=%async_computation.2 | async-start | bytes 2097152 | tf_op jit(solution)/shard_map/all_to_all | solution.py:168
  96.2 0.0 copy-done.9
  96.2 1.5 collective-permute-start.8
  97.7 1.3 collective-permute-start.6
  99.0 0.0 copy-done.13
  99.0 0.7 collective-permute-start.2
  99.7 1.3 collective-permute-start.5
  101.0 5.2 %collective-permute-start.3 = (bf16[256,512]{1,0:T(8,128)(2,1)S(1)}, bf16[256,512]{1,0:T(8,128)(2,1)S(1)}, u32[]{:S(2)}, u32[]{:S(2)}) collective-permute-start(bf16[256,512]{1,0:T(8,128)(2,1)S(1)} %copy-done.9), channel_id=1, source_target_pairs={{0,12},{4,16},{8,20},{12,24},{16,28},{20,32},{24,36},{28,40},{32,4... | collective-permute-start | bytes 786440 | tf_op jit(solution)/shard_map/ppermute | solution.py:162
  106.2 13.7 %collective-permute-done.2.q_other = bf16[256,256]{1,0:T(8,128)(2,1)S(1)} collective-permute-done((bf16[256,256]{1,0:T(8,128)(2,1)S(1)}, bf16[256,256]{1,0:T(8,128)(2,1)S(1)}, u32[]{:S(2)}, u32[]{:S(2)}) %collective-permute-start.2) | collective-permute-done | bytes 131104 | tf_op jit(solution)/shard_map/ppermute | solution.py:162
  119.9 0.6 collective-permute-start.9
  120.5 0.0 collective-permute-done.8.b3
  120.6 5.0 %collective-permute-start.7 = (bf16[256,512]{1,0:T(8,128)(2,1)S(1)}, bf16[256,512]{1,0:T(8,128)(2,1)S(1)}, u32[]{:S(2)}, u32[]{:S(2)}) collective-permute-start(bf16[256,512]{1,0:T(8,128)(2,1)S(1)} %get-tuple-element.15.own), channel_id=1, source_target_pairs={{0,248},{4,252},{8,0},{12,4},{16,8},{20,12},{24,16},{28,20},{32,24... | collective-permute-start | bytes 786440 | tf_op jit(solution)/shard_map/ppermute | solution.py:162
  125.6 0.0 collective-permute-done.6.b1
  125.6 0.0 collective-permute-start.4
  125.6 0.0 collective-permute-done.5.a1
  125.6 0.0 collective-permute-done.3.a3
  125.6 5.9 %collective-permute-done.9.far = bf16[256,512]{1,0:T(8,128)(2,1)S(1)} collective-permute-done((bf16[256,512]{1,0:T(8,128)(2,1)S(1)}, bf16[256,512]{1,0:T(8,128)(2,1)S(1)}, u32[]{:S(2)}, u32[]{:S(2)}) %collective-permute-start.9) | collective-permute-done | bytes 262176 | tf_op jit(solution)/shard_map/ppermute | solution.py:162
  131.5 0.0 collective-permute-done.7.b2
  131.5 6.7 %collective-permute-done.4.a2 = bf16[256,512]{1,0:T(8,128)(2,1)S(1)} collective-permute-done((bf16[256,512]{1,0:T(8,128)(2,1)S(1)}, bf16[256,512]{1,0:T(8,128)(2,1)S(1)}, u32[]{:S(2)}, u32[]{:S(2)}) %collective-permute-start.4) | collective-permute-done | bytes 262176 | tf_op jit(solution)/shard_map/ppermute | solution.py:162
  138.2 0.0 copy-done.11
  138.2 3.4 %pair.1 = (bf16[256,256]{1,0:T(8,128)(2,1)S(1)}, bf16[256,256]{1,0:T(8,128)(2,1)S(1)}) custom-call(s32[2]{0:T(128)S(1)} %pad_add_fusion.par_ref.where_ref, s32[8,28]{1,0:T(8,128)S(1)} %fusion.sel_ref, bf16[256,256]{1,0:T(8,128)(2,1)S(1)} %copy-done.11, bf16[256,256]{1,0:T(8,128)(2,1)S(1)} %collective-permute-done.2.q_other, ...), custom_call_target="tpu_custom_call" | custom-call | flops 1174405120 | bytes 2621440 | tf_op jit(solution)/shard_map/pair/pallas_call | solution.py:210
  141.6 0.1 collective-permute-start.10
  141.7 5.0 %collective-permute-done.10.other = bf16[256,256]{1,0:T(8,128)(2,1)S(1)} collective-permute-done((bf16[256,256]{1,0:T(8,128)(2,1)S(1)}, bf16[256,256]{1,0:T(8,128)(2,1)S(1)}, u32[]{:S(2)}, u32[]{:S(2)}) %collective-permute-start.10) | collective-permute-done | bytes 131104 | tf_op jit(solution)/shard_map/ppermute | solution.py:162
  146.6 0.0 all-to-all-done.2.mine
  146.6 1.8 %unpack.1 = (bf16[256,1280]{1,0:T(8,128)(2,1)}, bf16[256,1280]{1,0:T(8,128)(2,1)}) custom-call(s32[2]{0:T(128)S(1)} %pad_add_fusion.par_ref.where_ref, bf16[8,256,256]{2,1,0:T(8,128)(2,1)S(1)} %all-to-all-done.2.mine, bf16[256,256]{1,0:T(8,128)(2,1)S(1)} %get-tuple-element.16.own, bf16[256,256]{1,0:T(8,128)(2,1)S(1)} %collective-permute-done.10.other), custom_call_target="tpu_custom_call" | custom-call | tf_op jit(solution)/shard_map/unpack/pallas_call | solution.py:222
  (3 shorter events, 0.0 us)
Async XLA Ops:
  1.5 1.1 copy-start.2
  2.6 1.1 copy-start.3
  3.7 1.1 copy-start.4
  4.8 1.1 copy-start.5
  5.8 1.1 copy-start.6
  6.9 1.1 copy-start.7
  9.2 33.0 %copy-start = (bf16[8,272,256]{2,1,0:T(8,128)(2,1)}, bf16[8,272,256]{2,1,0:T(8,128)(2,1)S(1)}, u32[]{:S(2)}) copy-start(bf16[8,272,256]{2,1,0:T(8,128)(2,1)S(1)} %get-tuple-element.10) | copy-start | bytes 3342340
  9.3 33.0 %copy-start.8 = (bf16[256,512]{1,0:T(8,128)(2,1)}, bf16[256,512]{1,0:T(8,128)(2,1)S(1)}, u32[]{:S(2)}) copy-start(bf16[256,512]{1,0:T(8,128)(2,1)S(1)} %get-tuple-element.14) | copy-start | bytes 786436
  9.3 33.0 %copy-start.10 = (bf16[256,256]{1,0:T(8,128)(2,1)}, bf16[256,256]{1,0:T(8,128)(2,1)S(1)}, u32[]{:S(2)}) copy-start(bf16[256,256]{1,0:T(8,128)(2,1)S(1)} %get-tuple-element.12.q_own) | copy-start | bytes 393220
  9.3 33.0 %copy-start.12 = (bf16[256,256]{1,0:T(8,128)(2,1)}, bf16[256,256]{1,0:T(8,128)(2,1)S(1)}, u32[]{:S(2)}) copy-start(bf16[256,256]{1,0:T(8,128)(2,1)S(1)} %get-tuple-element.13) | copy-start | bytes 393220
  42.3 19.5 %all-to-all-start = ((bf16[8,272,256]{2,1,0:T(8,128)(2,1)}), bf16[8,272,256]{2,1,0:T(8,128)(2,1)S(1)}, u32[]{:S(2)}, u32[]{:S(2)}) async-start(bf16[8,272,256]{2,1,0:T(8,128)(2,1)} %copy-done), calls=%async_computation | async-start | bytes 2228224 | tf_op jit(solution)/shard_map/all_to_all | solution.py:168
  49.7 20.9 %collective-permute-start.1 = (bf16[3,256,512]{2,1,0:T(8,128)(2,1)}, bf16[3,256,512]{2,1,0:T(8,128)(2,1)}, u32[]{:S(2)}, u32[]{:S(2)}) collective-permute-start(bf16[3,256,512]{2,1,0:T(8,128)(2,1)} %get-tuple-element.18), channel_id=1, source_target_pairs={{0,224},{4,228},{8,232},{12,236},{16,240},{20,244},{24,248},{28,25... | collective-permute-start | bytes 2359304 | tf_op jit(solution)/shard_map/ppermute | solution.py:162
  55.5 18.4 %collective-permute-start = (bf16[3,256,512]{2,1,0:T(8,128)(2,1)}, bf16[3,256,512]{2,1,0:T(8,128)(2,1)}, u32[]{:S(2)}, u32[]{:S(2)}) collective-permute-start(bf16[3,256,512]{2,1,0:T(8,128)(2,1)} %get-tuple-element.19), channel_id=1, source_target_pairs={{0,32},{4,36},{8,40},{12,44},{16,48},{20,52},{24,56},{28,60},{32,6... | collective-permute-start | bytes 2359304 | tf_op jit(solution)/shard_map/ppermute | solution.py:162
  87.8 1.0 copy-start.1
  88.8 7.4 %copy-start.9 = (bf16[256,512]{1,0:T(8,128)(2,1)S(1)}, bf16[256,512]{1,0:T(8,128)(2,1)}, u32[]{:S(2)}) copy-start(bf16[256,512]{1,0:T(8,128)(2,1)} %copy-done.8) | copy-start | bytes 786436
  88.8 10.1 %copy-start.13 = (bf16[256,256]{1,0:T(8,128)(2,1)S(1)}, bf16[256,256]{1,0:T(8,128)(2,1)}, u32[]{:S(2)}) copy-start(bf16[256,256]{1,0:T(8,128)(2,1)} %copy-done.12) | copy-start | bytes 393220
  88.8 49.3 %copy-start.11 = (bf16[256,256]{1,0:T(8,128)(2,1)S(1)}, bf16[256,256]{1,0:T(8,128)(2,1)}, u32[]{:S(2)}) copy-start(bf16[256,256]{1,0:T(8,128)(2,1)} %copy-done.10) | copy-start | bytes 393220
  88.8 57.8 %all-to-all-start.2 = ((bf16[8,256,256]{2,1,0:T(8,128)(2,1)}), bf16[8,256,256]{2,1,0:T(8,128)(2,1)S(1)}, u32[]{:S(2)}, u32[]{:S(2)}) async-start(bf16[8,256,256]{2,1,0:T(8,128)(2,1)} %copy-done.1), calls=%async_computation.2 | async-start | bytes 2097152 | tf_op jit(solution)/shard_map/all_to_all | solution.py:168
  96.2 24.4 %collective-permute-start.8 = (bf16[256,512]{1,0:T(8,128)(2,1)S(1)}, bf16[256,512]{1,0:T(8,128)(2,1)S(1)}, u32[]{:S(2)}, u32[]{:S(2)}) collective-permute-start(bf16[256,512]{1,0:T(8,128)(2,1)S(1)} %copy-done.9), channel_id=1, source_target_pairs={{0,244},{4,248},{8,252},{12,0},{16,4},{20,8},{24,12},{28,16},{32,2... | collective-permute-start | bytes 786440 | tf_op jit(solution)/shard_map/ppermute | solution.py:162
  97.7 27.9 %collective-permute-start.6 = (bf16[256,512]{1,0:T(8,128)(2,1)S(1)}, bf16[256,512]{1,0:T(8,128)(2,1)S(1)}, u32[]{:S(2)}, u32[]{:S(2)}) collective-permute-start(bf16[256,512]{1,0:T(8,128)(2,1)S(1)} %copy-done.9), channel_id=1, source_target_pairs={{0,252},{4,0},{8,4},{12,8},{16,12},{20,16},{24,20},{28,24},{32,28}... | collective-permute-start | bytes 786440 | tf_op jit(solution)/shard_map/ppermute | solution.py:162
  99.0 21.0 %collective-permute-start.2 = (bf16[256,256]{1,0:T(8,128)(2,1)S(1)}, bf16[256,256]{1,0:T(8,128)(2,1)S(1)}, u32[]{:S(2)}, u32[]{:S(2)}) collective-permute-start(bf16[256,256]{1,0:T(8,128)(2,1)S(1)} %copy-done.13), channel_id=1, source_target_pairs={{0,4},{4,0},{8,12},{12,8},{16,20},{20,16},{24,28},{28,24},{32,36},... | collective-permute-start | bytes 393224 | tf_op jit(solution)/shard_map/ppermute | solution.py:162
  99.7 25.9 %collective-permute-start.5 = (bf16[256,512]{1,0:T(8,128)(2,1)S(1)}, bf16[256,512]{1,0:T(8,128)(2,1)S(1)}, u32[]{:S(2)}, u32[]{:S(2)}) collective-permute-start(bf16[256,512]{1,0:T(8,128)(2,1)S(1)} %copy-done.9), channel_id=1, source_target_pairs={{0,4},{4,8},{8,12},{12,16},{16,20},{20,24},{24,28},{28,32},{32,36}... | collective-permute-start | bytes 786440 | tf_op jit(solution)/shard_map/ppermute | solution.py:162
  101.0 24.6 %collective-permute-start.3 = (bf16[256,512]{1,0:T(8,128)(2,1)S(1)}, bf16[256,512]{1,0:T(8,128)(2,1)S(1)}, u32[]{:S(2)}, u32[]{:S(2)}) collective-permute-start(bf16[256,512]{1,0:T(8,128)(2,1)S(1)} %copy-done.9), channel_id=1, source_target_pairs={{0,12},{4,16},{8,20},{12,24},{16,28},{20,32},{24,36},{28,40},{32,4... | collective-permute-start | bytes 786440 | tf_op jit(solution)/shard_map/ppermute | solution.py:162
  119.9 11.5 %collective-permute-start.9 = (bf16[256,512]{1,0:T(8,128)(2,1)S(1)}, bf16[256,512]{1,0:T(8,128)(2,1)S(1)}, u32[]{:S(2)}, u32[]{:S(2)}) collective-permute-start(bf16[256,512]{1,0:T(8,128)(2,1)S(1)} %get-tuple-element.15.own), channel_id=1, source_target_pairs={{0,240},{4,20},{8,248},{12,28},{16,0},{20,36},{24,8},{28,44},{32,1... | collective-permute-start | bytes 786440 | tf_op jit(solution)/shard_map/ppermute | solution.py:162
  120.6 10.9 %collective-permute-start.7 = (bf16[256,512]{1,0:T(8,128)(2,1)S(1)}, bf16[256,512]{1,0:T(8,128)(2,1)S(1)}, u32[]{:S(2)}, u32[]{:S(2)}) collective-permute-start(bf16[256,512]{1,0:T(8,128)(2,1)S(1)} %get-tuple-element.15.own), channel_id=1, source_target_pairs={{0,248},{4,252},{8,0},{12,4},{16,8},{20,12},{24,16},{28,20},{32,24... | collective-permute-start | bytes 786440 | tf_op jit(solution)/shard_map/ppermute | solution.py:162
  125.6 12.6 %collective-permute-start.4 = (bf16[256,512]{1,0:T(8,128)(2,1)S(1)}, bf16[256,512]{1,0:T(8,128)(2,1)S(1)}, u32[]{:S(2)}, u32[]{:S(2)}) collective-permute-start(bf16[256,512]{1,0:T(8,128)(2,1)S(1)} %get-tuple-element.15.own), channel_id=1, source_target_pairs={{0,8},{4,12},{8,16},{12,20},{16,24},{20,28},{24,32},{28,36},{32,40... | collective-permute-start | bytes 786440 | tf_op jit(solution)/shard_map/ppermute | solution.py:162
  141.6 5.1 %collective-permute-start.10 = (bf16[256,256]{1,0:T(8,128)(2,1)S(1)}, bf16[256,256]{1,0:T(8,128)(2,1)S(1)}, u32[]{:S(2)}, u32[]{:S(2)}) collective-permute-start(bf16[256,256]{1,0:T(8,128)(2,1)S(1)} %get-tuple-element.17), channel_id=1, source_target_pairs={{0,4},{4,0},{8,12},{12,8},{16,20},{20,16},{24,28},{28,24},{32,36},... | collective-permute-start | bytes 393224 | tf_op jit(solution)/shard_map/ppermute | solution.py:162

commit v2 on v1

--- a/solution.py
+++ b/solution.py
@@ -1,5 +1,3 @@
-import functools
-
 import jax
 import jax.numpy as jnp
 from jax import lax
@@ -15,30 +13,42 @@
 WIN = 14
 PLANE = 8
 CHUNKS = 2 * REACH + 1
+SLOTS = PLANE + 2 * REACH
 NEG = -1.0e30
 LOG2E = 1.4426950408889634
 SCALE = HEAD_DIM ** -0.5
 MIB = 1 << 20
 
 VMEM_SPEC = pl.BlockSpec(memory_space=pltpu.VMEM)
+HBM_SPEC = pl.BlockSpec(memory_space=pltpu.HBM)
 SMEM_SPEC = pl.BlockSpec(memory_space=pltpu.SMEM)
 
 
-def pack_kernel(par_ref, q, qt, k, kt, v, vt, sel, kv_out, q_out, kv_same, kv_opp, q_same, q_opp):
-    par = par_ref[0]
-    for j in range(PLANE):
-        cols = pl.ds(j * HEAD_DIM, HEAD_DIM)
-        for n, ref in enumerate((k, kt, v, vt)):
-            kv_out[j, :, n * HEAD_DIM:(n + 1) * HEAD_DIM] = ref[:, cols]
-        for n, ref in enumerate((qt, q)):
-            q_out[j, 0:TOK, n * HEAD_DIM:(n + 1) * HEAD_DIM] = ref[:, cols]
-        q_out[j, TOK:TOK + 16, :] = sel[...]
-    for which, kv_to, q_to in ((par, kv_same, q_same), (1 - par, kv_opp, q_opp)):
+def run_copies(pairs, sem):
+    copies = [pltpu.make_async_copy(source, target, sem.at[n]) for n, (source, target) in enumerate(pairs)]
+    for copy in copies:
+        copy.start()
+    for copy in copies:
+        copy.wait()
+
+
+def lanes(n):
+    return pl.ds(n * HEAD_DIM, HEAD_DIM)
+
+
+def cut_keys_kernel(k, kt, v, vt, out, sem):
+    run_copies([(ref.at[:, lanes(j)], out.at[j, :, lanes(n)])
+                for j in range(PLANE) for n, ref in enumerate((k, kt, v, vt))], sem)
+
+
+def cut_rest_kernel(row_ref, q, qt, k, kt, v, vt, q_out, q_same, q_opp, kv_same, kv_opp, sem):
+    pairs = [(ref.at[:, lanes(j)], q_out.at[j, 0:TOK, lanes(n)]) for j in range(PLANE) for n, ref in enumerate((qt, q))]
+    par = row_ref[0] % 2
+    for which, q_to, kv_to in ((par, q_same, kv_same), (1 - par, q_opp, kv_opp)):
         cols = pl.ds(pl.multiple_of((PLANE + which) * HEAD_DIM, HEAD_DIM), HEAD_DIM)
-        for n, ref in enumerate((k, kt, v, vt)):
-            kv_to[:, n * HEAD_DIM:(n + 1) * HEAD_DIM] = ref[:, cols]
-        for n, ref in enumerate((qt, q)):
-            q_to[:, n * HEAD_DIM:(n + 1) * HEAD_DIM] = ref[:, cols]
+        pairs += [(ref.at[:, cols], q_to.at[:, lanes(n)]) for n, ref in enumerate((qt, q))]
+        pairs += [(ref.at[:, cols], kv_to.at[:, lanes(n)]) for n, ref in enumerate((k, kt, v, vt))]
+    run_copies(pairs, sem)
 
 
 def attend(sel_ref, row, base, qcat, kk, vv, s_scr, p_scr, t_scr):
@@ -80,7 +90,7 @@
 
 def plane_kernel(sel_ref, q_ref, main, up, dn, o_ref, kk, vv, s_scr, p_scr, t_scr):
     half = 2 * HEAD_DIM
-    for slot in range(PLANE + 2 * REACH):
+    for slot in range(SLOTS):
         if slot < REACH:
             piece = up.at[slot]
         elif slot < REACH + PLANE:
@@ -98,10 +108,11 @@
     lax.fori_loop(0, PLANE, step, 0)
 
 
-def pair_kernel(where_ref, sel_ref, q_own, q_other, a3, a2, a1, own, b1, b2, b3, far, o_own, o_other,
+def pair_kernel(row_ref, sel_ref, q_own, q_other, a3, a2, a1, own, b1, b2, b3, far, o_own, o_other,
                 kk, vv, s_scr, p_scr, t_scr):
     half = 2 * HEAD_DIM
-    par, row = where_ref[0], where_ref[1]
+    row = row_ref[0]
+    par = row % 2
     for place, piece in enumerate((a3, a2, a1, own, b1, b2, b3)):
         rows = pl.ds(pl.multiple_of((place + par) * TOK, TOK), TOK)
         kk[rows, :] = piece[:, :half]
@@ -109,14 +120,13 @@
     rows = pl.ds(pl.multiple_of((1 - par) * CHUNKS * TOK, TOK), TOK)
     kk[rows, :] = far[:, :half]
     vv[rows, :] = far[:, half:]
-    base = pl.multiple_of(par * TOK, TOK)
-    o_own[...] = attend(sel_ref, row, base, q_own[...], kk, vv, s_scr, p_scr, t_scr)
-    base = pl.multiple_of((1 - par) * TOK, TOK)
-    o_other[...] = attend(sel_ref, row + 1 - 2 * par, base, q_other[...], kk, vv, s_scr, p_scr, t_scr)
+    for q_ref, at, place, o_ref in ((q_own, row, par, o_own), (q_other, row + 1 - 2 * par, 1 - par, o_other)):
+        base = pl.multiple_of(place * TOK, TOK)
+        o_ref[...] = attend(sel_ref, at, base, q_ref[...], kk, vv, s_scr, p_scr, t_scr)
 
 
 def unpack_kernel(par_ref, mine, own, other, o_ref, t_ref):
-    par = par_ref[0]
+    par = par_ref[0] % 2
     for j in range(PLANE):
         cols = pl.ds(j * HEAD_DIM, HEAD_DIM)
         o_ref[:, cols] = mine[j, :, :HEAD_DIM]
@@ -152,59 +162,65 @@
 
 def body(queries, query_tangents, keys, key_tangents, values, value_tangents, selection):
     devices = lax.axis_size("ctx")
-    me = lax.axis_index("ctx")
-    par = (me % 2).astype(jnp.int32)
-    where = jnp.stack([par, (me % PLANE).astype(jnp.int32)])
+    row = (lax.axis_index("ctx") % PLANE).astype(jnp.int32)[None]
     planes = [[z * PLANE + i for i in range(PLANE)] for z in range(devices // PLANE)]
 
-
-    def send(array, pairs):
-        return lax.ppermute(array, "ctx", pairs)
-
-    def shifted(by):
-        return [(i, (i + by) % devices) for i in range(devices)]
+    def send(array, by):
+        return lax.ppermute(array, "ctx", [(i, (i + by) % devices) for i in range(devices)])
+
+    def swapped(array):
+        return lax.ppermute(array, "ctx", [(i, i ^ 1) for i in range(devices)])
 
     def exchange(array):
         return lax.all_to_all(array, "ctx", 0, 0, axis_index_groups=planes, tiled=True)
 
-    sel_rows = jnp.pad(selection.astype(jnp.bfloat16).reshape(1, 2 * WIN), ((0, 15), (0, 2 * HEAD_DIM - 2 * WIN)))
-    kv_out, q_out, kv_same, kv_opp, q_same, q_opp = pl.pallas_call(
-        pack_kernel,
-        out_shape=(bf16(PLANE, TOK, 512), bf16(PLANE, TOK + 16, 256), bf16(TOK, 512), bf16(TOK, 512),
-                   bf16(TOK, 256), bf16(TOK, 256)),
-        in_specs=[SMEM_SPEC] + [VMEM_SPEC] * 7,
-        out_specs=(VMEM_SPEC,) * 6,
-        compiler_params=pltpu.CompilerParams(vmem_limit_bytes=20 * MIB),
-        name="pack",
-    )(where, queries, query_tangents, keys, key_tangents, values, value_tangents, sel_rows)
+    wide = [pltpu.with_memory_space_constraint(array, pltpu.HBM) for array in
+            (queries, query_tangents, keys, key_tangents, values, value_tangents)]
+    kv_out = pl.pallas_call(
+        cut_keys_kernel,
+        out_shape=bf16(PLANE, TOK, 512),
+        in_specs=[HBM_SPEC] * 4,
+        out_specs=VMEM_SPEC,
+        scratch_shapes=[pltpu.SemaphoreType.DMA((4 * PLANE,))],
+        compiler_params=pltpu.CompilerParams(vmem_limit_bytes=8 * MIB),
+        name="cut_keys",
+    )(*wide[2:])
+    q_out, q_same, q_opp, kv_same, kv_opp = pl.pallas_call(
+        cut_rest_kernel,
+        out_shape=(bf16(PLANE, TOK, 256), bf16(TOK, 256), bf16(TOK, 256), bf16(TOK, 512), bf16(TOK, 512)),
+        in_specs=[SMEM_SPEC] + [HBM_SPEC] * 6,
+        out_specs=(VMEM_SPEC,) * 5,
+        scratch_shapes=[pltpu.SemaphoreType.DMA((2 * PLANE + 12,))],
+        compiler_params=pltpu.CompilerParams(vmem_limit_bytes=8 * MIB),
+        name="cut_rest",
+    )(row, *wide)
+    sel_rows = jnp.pad(selection.astype(jnp.bfloat16).reshape(1, 1, 2 * WIN), ((0, 0), (0, 15), (0, 256 - 2 * WIN)))
+    q_out = jnp.concatenate([q_out, jnp.broadcast_to(sel_rows, (PLANE, 16, 256))], axis=1)
 
     main = exchange(kv_out)
-    up = send(main[PLANE - REACH:], shifted(PLANE))
-    dn = send(main[:REACH], shifted(-PLANE))
+    main, q_out, kv_same, kv_opp, q_opp = lax.optimization_barrier((main, q_out, kv_same, kv_opp, q_opp))
+    up = send(main[PLANE - REACH:], PLANE)
+    dn = send(main[:REACH], -PLANE)
     q_all = exchange(q_out)
+    a3, b3, a2 = send(kv_opp, 3), send(kv_opp, -3), send(kv_same, 2)
+    q_all, up, dn, a3, b3, a2, kv_same, kv_opp, q_opp = lax.optimization_barrier(
+        (q_all, up, dn, a3, b3, a2, kv_same, kv_opp, q_opp))
+    b2, a1, b1 = send(kv_same, -2), send(kv_opp, 1), send(kv_opp, -1)
+    far = lax.ppermute(kv_same, "ctx", [(i, (i - 4 + 8 * (i % 2)) % devices) for i in range(devices)])
+    q_other = swapped(q_opp)
     sel_all = q_all[:, TOK, :2 * WIN].astype(jnp.int32)
-
-    swap = [(i, i ^ 1) for i in range(devices)]
-    far_pairs = [(i, (i - 4) % devices) if i % 2 == 0 else (i, (i + 4) % devices) for i in range(devices)]
-    a3 = send(kv_opp, shifted(3))
-    b3 = send(kv_opp, shifted(-3))
-    a2 = send(kv_same, shifted(2))
-    b2 = send(kv_same, shifted(-2))
-    a1 = send(kv_opp, shifted(1))
-    b1 = send(kv_opp, shifted(-1))
-    far = send(kv_same, far_pairs)
-    q_other = send(q_opp, swap)
 
     mine = pl.pallas_call(
         plane_kernel,
         out_shape=bf16(PLANE, TOK, 256),
         in_specs=[SMEM_SPEC] + [VMEM_SPEC] * 4,
         out_specs=VMEM_SPEC,
-        scratch_shapes=scratch(PLANE + 2 * REACH),
-        compiler_params=pltpu.CompilerParams(vmem_limit_bytes=32 * MIB),
+        scratch_shapes=scratch(SLOTS),
+        compiler_params=pltpu.CompilerParams(vmem_limit_bytes=16 * MIB),
         cost_estimate=cost(PLANE),
         name="plane",
     )(sel_all, q_all, main, up, dn)
+    mine, b2, a1, b1, far, q_other = lax.optimization_barrier((mine, b2, a1, b1, far, q_other))
     back = exchange(mine)
 
     own, other = pl.pallas_call(
@@ -213,11 +229,11 @@
         in_specs=[SMEM_SPEC] * 2 + [VMEM_SPEC] * 10,
         out_specs=(VMEM_SPEC,) * 2,
         scratch_shapes=scratch(2 + 2 * REACH),
-        compiler_params=pltpu.CompilerParams(vmem_limit_bytes=24 * MIB),
+        compiler_params=pltpu.CompilerParams(vmem_limit_bytes=12 * MIB),
         cost_estimate=cost(2),
         name="pair",
-    )(where, sel_all, q_same, q_other, a3, a2, a1, kv_same, b1, b2, b3, far)
-    partner = send(other, swap)
+    )(row, sel_all, q_same, q_other, a3, a2, a1, kv_same, b1, b2, b3, far)
+    partner = swapped(other)
 
     return pl.pallas_call(
         unpack_kernel,
@@ -226,7 +242,7 @@
         out_specs=(VMEM_SPEC,) * 2,
         compiler_params=pltpu.CompilerParams(vmem_limit_bytes=12 * MIB),
         name="unpack",
-    )(where, back, own, partner)
+    )(row, back, own, partner)
 
 
 def solution(mesh):

time: 149 us -> 135 us (0.906)
  the two profiles are of different devices: /device:TPU:4 before, /device:TPU:1 now
where the time goes in v2:
time: 135 us; the launch traced here: 133 us
  waiting for transfers between devices  51.5 us (38%)
  starting transfers between devices  43.5 us (32%)
  Pallas kernels  22.9 us (17%)
  local copies, waits for them, and re-layouts  12.9 us (10%)
    ppermute x8, waiting for transfers between devices, send(): lax.ppermute(array, 'ctx', [(i, (i + by) % devices) for i in range(device...  22.7 us
    ppermute x8, starting transfers between devices, send(): lax.ppermute(array, 'ctx', [(i, (i + by) % devices) for i in range(device...  21.9 us
    all_to_all x3, waiting for transfers between devices, exchange(): lax.all_to_all(array, 'ctx', 0, 0, axis_index_groups=planes, tiled=True)  21.2 us
    all_to_all x3, starting transfers between devices, exchange(): lax.all_to_all(array, 'ctx', 0, 0, axis_index_groups=planes, tiled=True)  19.4 us
    pallas_call x1, Pallas kernels, body(): pl.pallas_call(plane_kernel, out_shape=bf16(PLANE, TOK, 256), in_specs=[S...  13.1 us
    unnamed x56, local copies, waits for them, and re-layouts  12.3 us
    ppermute x2, waiting for transfers between devices, swapped(): return lax.ppermute(array, 'ctx', [(i, i ^ 1) for i in range(devices)])  7.51 us
    pallas_call x1, Pallas kernels, body(): pl.pallas_call(pair_kernel, out_shape=(bf16(TOK, 256), bf16(TOK, 256)), i...  3.45 us
  transfers between devices with their start and end apart: 14, of which 5 were waited for; matrix products, arithmetic and copies ran while one was open for 1% of the time, Pallas kernels for 14%

profile of v2, /device:TPU:1, one launch (start us, length us, event | category | flops | bytes accessed | tf_op | source)
XLA Modules:
  0.0 132.6 jit_solution(11339353628384262242)
XLA Ops:
  0.6 3.2 %cut_keys.1 = bf16[8,256,512]{2,1,0:T(8,128)(2,1)} custom-call(bf16[256,1280]{1,0:T(8,128)(2,1)} %k.3, bf16[256,1280]{1,0:T(8,128)(2,1)} %kt.3, bf16[256,1280]{1,0:T(8,128)(2,1)} %v.3, bf16[256,1280]{1,0:T(8,128)(2,1)} %vt.3), custom_call_target="tpu_custom_call" | custom-call | tf_op jit(solution)/shard_map/cut_keys/pallas_call | solution.py:179
  3.9 0.0 copy-start.27
  3.9 7.5 %all-to-all-start = ((bf16[8,256,512]{2,1,0:T(8,128)(2,1)}), bf16[8,256,512]{2,1,0:T(8,128)(2,1)S(1)}, u32[]{:S(2)}, u32[]{:S(2)}) async-start(bf16[8,256,512]{2,1,0:T(8,128)(2,1)} %cut_keys.1), calls=%async_computation | async-start | bytes 4194304 | tf_op jit(solution)/shard_map/all_to_all | solution.py:175
  11.4 0.0 copy-done.27
  11.4 0.1 reshape.9
  11.5 1.8 %cut_rest.1 = (bf16[8,256,256]{2,1,0:T(8,128)(2,1)S(1)}, bf16[256,256]{1,0:T(8,128)(2,1)S(1)}, bf16[256,256]{1,0:T(8,128)(2,1)S(1)}, bf16[256,512]{1,0:T(8,128)(2,1)S(1)}, bf16[256,512]{1,0:T(8,128)(2,1)S(1)}) custom-call(s32[1]{0:T(128)} %bitcast.row_ref.par_ref, bf16[256,1280]{1,0:T(8,128)(2,1)} %q.1, bf16[256,1280]{1,0:T(8,128)(2,1)} %qt.1, ...), custom_call_target="tpu_custom_call" | custom-call | tf_op jit(solution)/shard_map/cut_rest/pallas_call | solution.py:188
  13.3 0.0 copy-start.5
  13.3 0.7 copy-done.5
  14.0 0.7 copy-done.21
  14.6 0.7 copy-done.23
  15.3 1.1 pad_maximum_fusion
  16.3 21.2 %all-to-all-done.main = bf16[8,256,512]{2,1,0:T(8,128)(2,1)S(1)} async-done(((bf16[8,256,512]{2,1,0:T(8,128)(2,1)}), bf16[8,256,512]{2,1,0:T(8,128)(2,1)S(1)}, u32[]{:S(2)}, u32[]{:S(2)}) %all-to-all-start) | async-done | bytes 2097184 | tf_op jit(solution)/shard_map/all_to_all | solution.py:175
  37.5 5.2 %all-to-all-start.1 = ((bf16[8,272,256]{2,1,0:T(8,128)(2,1)}), bf16[8,272,256]{2,1,0:T(8,128)(2,1)S(1)}, u32[]{:S(2)}, u32[]{:S(2)}) async-start(bf16[8,272,256]{2,1,0:T(8,128)(2,1)} %pad_maximum_fusion), calls=%async_computation.1 | async-start | bytes 2228224 | tf_op jit(solution)/shard_map/all_to_all | solution.py:175
  42.7 0.1 fusion.1
  42.9 1.7 %collective-permute-start = (bf16[3,256,512]{2,1,0:T(8,128)(2,1)S(1)}, bf16[3,256,512]{2,1,0:T(8,128)(2,1)S(1)}, u32[]{:S(2)}, u32[]{:S(2)}) collective-permute-start(bf16[3,256,512]{2,1,0:T(8,128)(2,1)S(1)} %get-tuple-element.57), channel_id=1, source_target_pairs={{0,32},{4,36},{8,40},{12,44},{16,48},{20,52},{24,56},{28,60},{32,6... | collective-permute-start | bytes 2359304 | tf_op jit(solution)/shard_map/ppermute | solution.py:169
  44.6 4.0 %collective-permute-start.1 = (bf16[3,256,512]{2,1,0:T(8,128)(2,1)S(1)}, bf16[3,256,512]{2,1,0:T(8,128)(2,1)S(1)}, u32[]{:S(2)}, u32[]{:S(2)}) collective-permute-start(bf16[3,256,512]{2,1,0:T(8,128)(2,1)S(1)} %get-tuple-element.56), channel_id=1, source_target_pairs={{0,224},{4,228},{8,232},{12,236},{16,240},{20,244},{24,248},{28,25... | collective-permute-start | bytes 2359304 | tf_op jit(solution)/shard_map/ppermute | solution.py:169
  48.6 0.0 copy-done.6
  48.6 2.7 %collective-permute-start.2 = (bf16[256,512]{1,0:T(8,128)(2,1)S(1)}, bf16[256,512]{1,0:T(8,128)(2,1)S(1)}, u32[]{:S(2)}, u32[]{:S(2)}) collective-permute-start(bf16[256,512]{1,0:T(8,128)(2,1)S(1)} %copy-done.6), channel_id=1, source_target_pairs={{0,12},{4,16},{8,20},{12,24},{16,28},{20,32},{24,36},{28,40},{32,4... | collective-permute-start | bytes 786440 | tf_op jit(solution)/shard_map/ppermute | solution.py:169
  51.3 3.3 %collective-permute-start.3 = (bf16[256,512]{1,0:T(8,128)(2,1)S(1)}, bf16[256,512]{1,0:T(8,128)(2,1)S(1)}, u32[]{:S(2)}, u32[]{:S(2)}) collective-permute-start(bf16[256,512]{1,0:T(8,128)(2,1)S(1)} %copy-done.6), channel_id=1, source_target_pairs={{0,244},{4,248},{8,252},{12,0},{16,4},{20,8},{24,12},{28,16},{32,2... | collective-permute-start | bytes 786440 | tf_op jit(solution)/shard_map/ppermute | solution.py:169
  54.6 3.0 %collective-permute-start.4 = (bf16[256,512]{1,0:T(8,128)(2,1)S(1)}, bf16[256,512]{1,0:T(8,128)(2,1)S(1)}, u32[]{:S(2)}, u32[]{:S(2)}) collective-permute-start(bf16[256,512]{1,0:T(8,128)(2,1)S(1)} %get-tuple-element.41.own), channel_id=1, source_target_pairs={{0,8},{4,12},{8,16},{12,20},{16,24},{20,28},{24,32},{28,36},{32,40... | collective-permute-start | bytes 786440 | tf_op jit(solution)/shard_map/ppermute | solution.py:169
  57.5 17.0 %collective-permute-done.2.a3 = bf16[256,512]{1,0:T(8,128)(2,1)S(1)} collective-permute-done((bf16[256,512]{1,0:T(8,128)(2,1)S(1)}, bf16[256,512]{1,0:T(8,128)(2,1)S(1)}, u32[]{:S(2)}, u32[]{:S(2)}) %collective-permute-start.2) | collective-permute-done | bytes 262176 | tf_op jit(solution)/shard_map/ppermute | solution.py:169
  74.5 0.7 copy-done.7
  75.2 0.0 collective-permute-done.3.b3
  75.2 0.7 copy-done.9
  75.9 5.7 %collective-permute-done.4.a2 = bf16[256,512]{1,0:T(8,128)(2,1)S(1)} collective-permute-done((bf16[256,512]{1,0:T(8,128)(2,1)S(1)}, bf16[256,512]{1,0:T(8,128)(2,1)S(1)}, u32[]{:S(2)}, u32[]{:S(2)}) %collective-permute-start.4) | collective-permute-done | bytes 262176 | tf_op jit(solution)/shard_map/ppermute | solution.py:169
  81.7 0.7 copy-done.11
  82.4 0.0 collective-permute-done.up
  82.4 0.9 copy-done.1
  83.3 0.0 collective-permute-done.1.dn
  83.3 0.9 copy-done.3
  84.2 0.0 all-to-all-done.1.q_ref
  84.2 0.4 collective-permute-start.6
  84.5 6.9 %collective-permute-start.7 = (bf16[256,512]{1,0:T(8,128)(2,1)}, bf16[256,512]{1,0:T(8,128)(2,1)S(1)}, u32[]{:S(2)}, u32[]{:S(2)}) collective-permute-start(bf16[256,512]{1,0:T(8,128)(2,1)} %copy-done.5), channel_id=1, source_target_pairs={{0,252},{4,0},{8,4},{12,8},{16,12},{20,16},{24,20},{28,24},{32,28}... | collective-permute-start | bytes 786440 | tf_op jit(solution)/shard_map/ppermute | solution.py:169
  91.4 0.0 collective-permute-start.5
  91.4 0.0 collective-permute-start.8
  91.5 0.4 copy.11
  91.8 0.0 copy-done.24
  91.8 0.7 collective-permute-start.9
  92.5 0.0 copy-done.2
  92.5 0.0 copy-done.4
  92.5 13.1 %plane.1 = bf16[8,256,256]{2,1,0:T(8,128)(2,1)S(1)} custom-call(s32[8,28]{1,0:T(8,128)S(1)} %fusion.sel_ref, bf16[8,272,256]{2,1,0:T(8,128)(2,1)S(1)} %all-to-all-done.1.q_ref, bf16[8,256,512]{2,1,0:T(8,128)(2,1)S(1)} %all-to-all-done.main, bf16[3,256,512]{2,1,0:T(8,128)(2,1)S(1)} %copy-done.2, bf16[3,256,512]{2,1,0:T(8,128)(2,1)S(1)} %copy-done.4), custom_call_target="tpu_custom_call" | custom-call | flops 4697620480 | bytes 5767168 | tf_op jit(solution)/shard_map/plane/pallas_call | solution.py:213
  105.6 0.0 copy-start
  105.6 1.0 copy-done
  106.6 0.0 collective-permute-done.9.q_other
  106.7 0.0 copy-start.25
  106.7 0.6 copy-done.25
  107.3 0.0 collective-permute-done.5.b2
  107.3 0.7 copy-done.17
  108.0 0.0 collective-permute-done.6.a1
  108.0 0.7 copy-done.13
  108.7 0.0 collective-permute-done.7.b1
  108.8 0.7 copy-done.15
  109.5 0.1 collective-permute-done.8.far
  109.5 0.7 copy-done.19
  110.2 6.7 %all-to-all-start.2 = ((bf16[8,256,256]{2,1,0:T(8,128)(2,1)}), bf16[8,256,256]{2,1,0:T(8,128)(2,1)S(1)}, u32[]{:S(2)}, u32[]{:S(2)}) async-start(bf16[8,256,256]{2,1,0:T(8,128)(2,1)} %copy-done), calls=%async_computation.2 | async-start | bytes 2097152 | tf_op jit(solution)/shard_map/all_to_all | solution.py:175
  116.9 0.0 copy-done.8
  116.9 0.0 copy-done.10
  117.0 0.9 copy-done.20
  118.0 0.9 copy-done.26
  118.9 3.4 %pair.1 = (bf16[256,256]{1,0:T(8,128)(2,1)S(1)}, bf16[256,256]{1,0:T(8,128)(2,1)S(1)}) custom-call(s32[1]{0:T(128)} %bitcast.row_ref.par_ref, s32[8,28]{1,0:T(8,128)S(1)} %fusion.sel_ref, bf16[256,256]{1,0:T(8,128)(2,1)S(1)} %copy-done.22, bf16[256,256]{1,0:T(8,128)(2,1)S(1)} %copy-done.26, bf16[256,512]{1,0:T(8,128)(2,1)S(1)} %copy-done.8, ...), custom_call_target="tpu_custom_call" | custom-call | flops 1174405120 | bytes 2621440 | tf_op jit(solution)/shard_map/pair/pallas_call | solution.py:226
  122.3 1.5 %collective-permute-start.10 = (bf16[256,256]{1,0:T(8,128)(2,1)S(1)}, bf16[256,256]{1,0:T(8,128)(2,1)S(1)}, u32[]{:S(2)}, u32[]{:S(2)}) collective-permute-start(bf16[256,256]{1,0:T(8,128)(2,1)S(1)} %get-tuple-element.55), channel_id=1, source_target_pairs={{0,4},{4,0},{8,12},{12,8},{16,20},{20,16},{24,28},{28,24},{32,36},... | collective-permute-start | bytes 393224 | tf_op jit(solution)/shard_map/ppermute | solution.py:172
  123.8 7.5 %collective-permute-done.10.other = bf16[256,256]{1,0:T(8,128)(2,1)S(1)} collective-permute-done((bf16[256,256]{1,0:T(8,128)(2,1)S(1)}, bf16[256,256]{1,0:T(8,128)(2,1)S(1)}, u32[]{:S(2)}, u32[]{:S(2)}) %collective-permute-start.10) | collective-permute-done | bytes 131104 | tf_op jit(solution)/shard_map/ppermute | solution.py:172
  131.4 0.0 all-to-all-done.2.mine
  131.4 1.3 unpack.1
  (33 shorter events, 0.1 us)
Async XLA Ops:
  3.9 7.5 %copy-start.27 = (s32[2,14]{1,0:T(2,128)S(1)}, s32[2,14]{1,0:T(2,128)}, u32[]{:S(2)}) copy-start(s32[2,14]{1,0:T(2,128)} %param.13) | copy-start | bytes 340
  3.9 33.6 %all-to-all-start = ((bf16[8,256,512]{2,1,0:T(8,128)(2,1)}), bf16[8,256,512]{2,1,0:T(8,128)(2,1)S(1)}, u32[]{:S(2)}, u32[]{:S(2)}) async-start(bf16[8,256,512]{2,1,0:T(8,128)(2,1)} %cut_keys.1), calls=%async_computation | async-start | bytes 4194304 | tf_op jit(solution)/shard_map/all_to_all | solution.py:175
  13.3 0.7 copy-start.5
  14.0 0.7 copy-start.21
  14.6 0.7 copy-start.23
  37.5 46.6 %all-to-all-start.1 = ((bf16[8,272,256]{2,1,0:T(8,128)(2,1)}), bf16[8,272,256]{2,1,0:T(8,128)(2,1)S(1)}, u32[]{:S(2)}, u32[]{:S(2)}) async-start(bf16[8,272,256]{2,1,0:T(8,128)(2,1)} %pad_maximum_fusion), calls=%async_computation.1 | async-start | bytes 2228224 | tf_op jit(solution)/shard_map/all_to_all | solution.py:175
  42.7 5.9 %copy-start.6 = (bf16[256,512]{1,0:T(8,128)(2,1)S(1)}, bf16[256,512]{1,0:T(8,128)(2,1)}, u32[]{:S(2)}) copy-start(bf16[256,512]{1,0:T(8,128)(2,1)} %copy-done.5) | copy-start | bytes 786436
  42.9 39.5 %collective-permute-start = (bf16[3,256,512]{2,1,0:T(8,128)(2,1)S(1)}, bf16[3,256,512]{2,1,0:T(8,128)(2,1)S(1)}, u32[]{:S(2)}, u32[]{:S(2)}) collective-permute-start(bf16[3,256,512]{2,1,0:T(8,128)(2,1)S(1)} %get-tuple-element.57), channel_id=1, source_target_pairs={{0,32},{4,36},{8,40},{12,44},{16,48},{20,52},{24,56},{28,60},{32,6... | collective-permute-start | bytes 2359304 | tf_op jit(solution)/shard_map/ppermute | solution.py:169
  44.6 38.7 %collective-permute-start.1 = (bf16[3,256,512]{2,1,0:T(8,128)(2,1)S(1)}, bf16[3,256,512]{2,1,0:T(8,128)(2,1)S(1)}, u32[]{:S(2)}, u32[]{:S(2)}) collective-permute-start(bf16[3,256,512]{2,1,0:T(8,128)(2,1)S(1)} %get-tuple-element.56), channel_id=1, source_target_pairs={{0,224},{4,228},{8,232},{12,236},{16,240},{20,244},{24,248},{28,25... | collective-permute-start | bytes 2359304 | tf_op jit(solution)/shard_map/ppermute | solution.py:169
  48.6 25.9 %collective-permute-start.2 = (bf16[256,512]{1,0:T(8,128)(2,1)S(1)}, bf16[256,512]{1,0:T(8,128)(2,1)S(1)}, u32[]{:S(2)}, u32[]{:S(2)}) collective-permute-start(bf16[256,512]{1,0:T(8,128)(2,1)S(1)} %copy-done.6), channel_id=1, source_target_pairs={{0,12},{4,16},{8,20},{12,24},{16,28},{20,32},{24,36},{28,40},{32,4... | collective-permute-start | bytes 786440 | tf_op jit(solution)/shard_map/ppermute | solution.py:169
  51.3 24.0 %collective-permute-start.3 = (bf16[256,512]{1,0:T(8,128)(2,1)S(1)}, bf16[256,512]{1,0:T(8,128)(2,1)S(1)}, u32[]{:S(2)}, u32[]{:S(2)}) collective-permute-start(bf16[256,512]{1,0:T(8,128)(2,1)S(1)} %copy-done.6), channel_id=1, source_target_pairs={{0,244},{4,248},{8,252},{12,0},{16,4},{20,8},{24,12},{28,16},{32,2... | collective-permute-start | bytes 786440 | tf_op jit(solution)/shard_map/ppermute | solution.py:169
  54.6 27.1 %collective-permute-start.4 = (bf16[256,512]{1,0:T(8,128)(2,1)S(1)}, bf16[256,512]{1,0:T(8,128)(2,1)S(1)}, u32[]{:S(2)}, u32[]{:S(2)}) collective-permute-start(bf16[256,512]{1,0:T(8,128)(2,1)S(1)} %get-tuple-element.41.own), channel_id=1, source_target_pairs={{0,8},{4,12},{8,16},{12,20},{16,24},{20,28},{24,32},{28,36},{32,40... | collective-permute-start | bytes 786440 | tf_op jit(solution)/shard_map/ppermute | solution.py:169
  74.5 0.7 copy-start.7
  75.2 0.7 copy-start.9
  81.7 0.7 copy-start.11
  82.4 0.9 copy-start.1
  83.3 0.9 copy-start.3
  84.2 7.7 %copy-start.24 = (bf16[256,256]{1,0:T(8,128)(2,1)S(1)}, bf16[256,256]{1,0:T(8,128)(2,1)}, u32[]{:S(2)}) copy-start(bf16[256,256]{1,0:T(8,128)(2,1)} %copy-done.23) | copy-start | bytes 393220
  84.2 8.3 %copy-start.2 = (bf16[3,256,512]{2,1,0:T(8,128)(2,1)S(1)}, bf16[3,256,512]{2,1,0:T(8,128)(2,1)}, u32[]{:S(2)}) copy-start(bf16[3,256,512]{2,1,0:T(8,128)(2,1)} %copy-done.1) | copy-start | bytes 2359300
  84.2 8.3 %copy-start.4 = (bf16[3,256,512]{2,1,0:T(8,128)(2,1)S(1)}, bf16[3,256,512]{2,1,0:T(8,128)(2,1)}, u32[]{:S(2)}) copy-start(bf16[3,256,512]{2,1,0:T(8,128)(2,1)} %copy-done.3) | copy-start | bytes 2359300
  84.2 23.9 %collective-permute-start.6 = (bf16[256,512]{1,0:T(8,128)(2,1)}, bf16[256,512]{1,0:T(8,128)(2,1)S(1)}, u32[]{:S(2)}, u32[]{:S(2)}) collective-permute-start(bf16[256,512]{1,0:T(8,128)(2,1)} %copy-done.5), channel_id=1, source_target_pairs={{0,4},{4,8},{8,12},{12,16},{16,20},{20,24},{24,28},{28,32},{32,36}... | collective-permute-start | bytes 786440 | tf_op jit(solution)/shard_map/ppermute | solution.py:169
  84.5 24.2 %collective-permute-start.7 = (bf16[256,512]{1,0:T(8,128)(2,1)}, bf16[256,512]{1,0:T(8,128)(2,1)S(1)}, u32[]{:S(2)}, u32[]{:S(2)}) collective-permute-start(bf16[256,512]{1,0:T(8,128)(2,1)} %copy-done.5), channel_id=1, source_target_pairs={{0,252},{4,0},{8,4},{12,8},{16,12},{20,16},{24,20},{28,24},{32,28}... | collective-permute-start | bytes 786440 | tf_op jit(solution)/shard_map/ppermute | solution.py:169
  91.4 15.9 %collective-permute-start.5 = (bf16[256,512]{1,0:T(8,128)(2,1)S(1)}, bf16[256,512]{1,0:T(8,128)(2,1)S(1)}, u32[]{:S(2)}, u32[]{:S(2)}) collective-permute-start(bf16[256,512]{1,0:T(8,128)(2,1)S(1)} %get-tuple-element.41.own), channel_id=1, source_target_pairs={{0,248},{4,252},{8,0},{12,4},{16,8},{20,12},{24,16},{28,20},{32,24... | collective-permute-start | bytes 786440 | tf_op jit(solution)/shard_map/ppermute | solution.py:169
  91.4 18.1 %collective-permute-start.8 = (bf16[256,512]{1,0:T(8,128)(2,1)S(1)}, bf16[256,512]{1,0:T(8,128)(2,1)S(1)}, u32[]{:S(2)}, u32[]{:S(2)}) collective-permute-start(bf16[256,512]{1,0:T(8,128)(2,1)S(1)} %get-tuple-element.41.own), channel_id=1, source_target_pairs={{0,240},{4,20},{8,248},{12,28},{16,0},{20,36},{24,8},{28,44},{32,1... | collective-permute-start | bytes 786440 | tf_op jit(solution)/shard_map/ppermute | solution.py:209
  91.8 14.8 %collective-permute-start.9 = (bf16[256,256]{1,0:T(8,128)(2,1)S(1)}, bf16[256,256]{1,0:T(8,128)(2,1)S(1)}, u32[]{:S(2)}, u32[]{:S(2)}) collective-permute-start(bf16[256,256]{1,0:T(8,128)(2,1)S(1)} %copy-done.24), channel_id=1, source_target_pairs={{0,4},{4,0},{8,12},{12,8},{16,20},{20,16},{24,28},{28,24},{32,36},... | collective-permute-start | bytes 393224 | tf_op jit(solution)/shard_map/ppermute | solution.py:172
  105.6 1.0 copy-start
  106.6 10.3 %copy-start.8 = (bf16[256,512]{1,0:T(8,128)(2,1)S(1)}, bf16[256,512]{1,0:T(8,128)(2,1)}, u32[]{:S(2)}) copy-start(bf16[256,512]{1,0:T(8,128)(2,1)} %copy-done.7) | copy-start | bytes 786436
  106.6 10.3 %copy-start.10 = (bf16[256,512]{1,0:T(8,128)(2,1)S(1)}, bf16[256,512]{1,0:T(8,128)(2,1)}, u32[]{:S(2)}) copy-start(bf16[256,512]{1,0:T(8,128)(2,1)} %copy-done.9) | copy-start | bytes 786436
  106.6 10.3 %copy-start.12 = (bf16[256,512]{1,0:T(8,128)(2,1)S(1)}, bf16[256,512]{1,0:T(8,128)(2,1)}, u32[]{:S(2)}) copy-start(bf16[256,512]{1,0:T(8,128)(2,1)} %copy-done.11) | copy-start | bytes 786436
  106.6 10.3 %copy-start.22 = (bf16[256,256]{1,0:T(8,128)(2,1)S(1)}, bf16[256,256]{1,0:T(8,128)(2,1)}, u32[]{:S(2)}) copy-start(bf16[256,256]{1,0:T(8,128)(2,1)} %copy-done.21) | copy-start | bytes 393220
  106.7 0.6 copy-start.25
  107.3 0.7 copy-start.17
  108.0 0.7 copy-start.13
  108.7 8.2 %copy-start.18 = (bf16[256,512]{1,0:T(8,128)(2,1)S(1)}, bf16[256,512]{1,0:T(8,128)(2,1)}, u32[]{:S(2)}) copy-start(bf16[256,512]{1,0:T(8,128)(2,1)} %copy-done.17) | copy-start | bytes 786436
  108.8 0.7 copy-start.15
  109.5 7.5 %copy-start.14 = (bf16[256,512]{1,0:T(8,128)(2,1)S(1)}, bf16[256,512]{1,0:T(8,128)(2,1)}, u32[]{:S(2)}) copy-start(bf16[256,512]{1,0:T(8,128)(2,1)} %copy-done.13) | copy-start | bytes 786436
  109.5 0.7 copy-start.19
  110.2 6.8 %copy-start.16 = (bf16[256,512]{1,0:T(8,128)(2,1)S(1)}, bf16[256,512]{1,0:T(8,128)(2,1)}, u32[]{:S(2)}) copy-start(bf16[256,512]{1,0:T(8,128)(2,1)} %copy-done.15) | copy-start | bytes 786436
  110.2 21.1 %all-to-all-start.2 = ((bf16[8,256,256]{2,1,0:T(8,128)(2,1)}), bf16[8,256,256]{2,1,0:T(8,128)(2,1)S(1)}, u32[]{:S(2)}, u32[]{:S(2)}) async-start(bf16[8,256,256]{2,1,0:T(8,128)(2,1)} %copy-done), calls=%async_computation.2 | async-start | bytes 2097152 | tf_op jit(solution)/shard_map/all_to_all | solution.py:175
  117.0 1.0 copy-start.20
  118.0 0.9 copy-start.26
  122.3 9.1 %collective-permute-start.10 = (bf16[256,256]{1,0:T(8,128)(2,1)S(1)}, bf16[256,256]{1,0:T(8,128)(2,1)S(1)}, u32[]{:S(2)}, u32[]{:S(2)}) collective-permute-start(bf16[256,256]{1,0:T(8,128)(2,1)S(1)} %get-tuple-element.55), channel_id=1, source_target_pairs={{0,4},{4,0},{8,12},{12,8},{16,20},{20,16},{24,28},{28,24},{32,36},... | collective-permute-start | bytes 393224 | tf_op jit(solution)/shard_map/ppermute | solution.py:172

commit v3 on v2

v3 whole, which is shorter than its diff:
```python
import jax
import jax.numpy as jnp
from jax import lax
from jax.experimental import pallas as pl
from jax.experimental.pallas import tpu as pltpu
from jax.sharding import PartitionSpec as P

HEADS = 10
HEAD_DIM = 128
BLK = 128
REACH = 3
TOK = 256
WIN = 14
PLANE = 8
CHUNKS = 2 * REACH + 1
NEG = -1.0e30
LOG2E = 1.4426950408889634
SCALE = HEAD_DIM ** -0.5
FACTOR = SCALE * LOG2E
MIB = 1 << 20

VMEM_SPEC = pl.BlockSpec(memory_space=pltpu.VMEM)
HBM_SPEC = pl.BlockSpec(memory_space=pltpu.HBM)
ANY_SPEC = pl.BlockSpec(memory_space=pl.ANY)
SMEM_SPEC = pl.BlockSpec(memory_space=pltpu.SMEM)


def run_copies(pairs, sem):
    copies = [pltpu.make_async_copy(source, target, sem.at[n]) for n, (source, target) in enumerate(pairs)]
    for copy in copies:
        copy.start()
    for copy in copies:
        copy.wait()


def lanes(n):
    return pl.ds(n * HEAD_DIM, HEAD_DIM)


def cut_keys_kernel(k, kt, v, vt, out, sem):
    run_copies([(ref.at[:, lanes(j)], out.at[j, :, lanes(n)])
                for j in range(PLANE) for n, ref in enumerate((k, kt, v, vt))], sem)


def cut_rest_kernel(row_ref, sel, q, qt, k, kt, v, vt, q_out, same, opp, sem):
    pairs = [(ref.at[:, lanes(j)], q_out.at[j, 0:TOK, lanes(n)]) for j in range(PLANE) for n, ref in enumerate((qt, q))]
    par = row_ref[0] % 2
    for which, target in ((par, same), (1 - par, opp)):
        cols = pl.ds(pl.multiple_of((PLANE + which) * HEAD_DIM, HEAD_DIM), HEAD_DIM)
        pairs += [(ref.at[:, cols], target.at[:, lanes(n)]) for n, ref in enumerate((k, kt, v, vt, qt, q))]
    for j in range(PLANE):
        q_out[j, TOK:, :] = sel[...]
    run_copies(pairs, sem)


def weigh(sel_ref, row, first, count, chunk, qcat, floor, s_scr, p_scr, t_scr):
    dims = (((1,), (1,)), ((), ()))
    query = qcat[:, HEAD_DIM:]
    peak = [None, None]
    for u in range(count):
        s = lax.dot_general(query, chunk(u)[:, :HEAD_DIM], dims, preferred_element_type=jnp.float32)
        for qb in range(2):
            for kb in range(2):
                listed = sel_ref[row, qb * WIN + 2 * (first + u) + kb]
                piece = s[qb * BLK:(qb + 1) * BLK, kb * BLK:(kb + 1) * BLK] + jnp.where(listed != 0, 0.0, NEG)
                s_scr[qb * BLK:(qb + 1) * BLK, u * TOK + kb * BLK:u * TOK + (kb + 1) * BLK] = piece
                peak[qb] = piece if peak[qb] is None else jnp.maximum(peak[qb], piece)
    top = jnp.concatenate([jnp.max(p, axis=1, keepdims=True) for p in peak], axis=0) * FACTOR
    if floor is not None:
        top = jnp.maximum(top, floor)
    total = jnp.zeros((TOK, BLK), jnp.float32)
    tangent_total = jnp.zeros((TOK, BLK), jnp.float32)
    for u in range(count):
        st = lax.dot_general(qcat, chunk(u), dims, preferred_element_type=jnp.float32)
        weights = jnp.exp2(s_scr[:, u * TOK:(u + 1) * TOK] * FACTOR - top)
        weighted = weights * st
        total += weights[:, :BLK] + weights[:, BLK:]
        tangent_total += weighted[:, :BLK] + weighted[:, BLK:]
        p_scr[:, u * TOK:(u + 1) * TOK] = weights.astype(jnp.bfloat16)
        t_scr[:, u * TOK:(u + 1) * TOK] = weighted.astype(jnp.bfloat16)
    return top, total, tangent_total


def finish(total, tangent_total, first, second):
    inverse = 1.0 / jnp.sum(total, axis=1, keepdims=True)
    out = first[:, :HEAD_DIM] * inverse
    tangent_sum = jnp.sum(tangent_total, axis=1, keepdims=True)
    tangent = ((second - out * tangent_sum) * SCALE + first[:, HEAD_DIM:]) * inverse
    return jnp.concatenate([out.astype(jnp.bfloat16), tangent.astype(jnp.bfloat16)], axis=1)


def mix(p_scr, t_scr, width, values):
    first = jnp.dot(p_scr[:, :width], values, preferred_element_type=jnp.float32)
    second = jnp.dot(t_scr[:, :width], values[:, :HEAD_DIM], preferred_element_type=jnp.float32)
    return first, second


def inner_kernel(sel_ref, q_ref, main, gate, o_ref, stats, first_ref, second_ref, s_scr, p_scr, t_scr):
    del gate

    def position(i, count, final):
        base = pl.multiple_of(jnp.maximum(i - REACH, 0) * TOK, TOK)
        top, total, tangent_total = weigh(
            sel_ref, i, jnp.maximum(REACH - i, 0), count,
            lambda u: main[pl.ds(base + u * TOK, TOK), :2 * HEAD_DIM], q_ref[i, :TOK, :], None, s_scr, p_scr, t_scr)
        first, second = mix(p_scr, t_scr, count * TOK, main[pl.ds(base, count * TOK), 2 * HEAD_DIM:])
        if final:
            o_ref[i - REACH] = finish(total, tangent_total, first, second)
        else:
            stats[i, 0] = jnp.broadcast_to(top, (TOK, BLK))
            stats[i, 1] = total
            stats[i, 2] = tangent_total
            first_ref[i] = first
            second_ref[i] = second

    def step(n, carry):
        for low in range(REACH + 1):
            position(low + n * (PLANE - 1 - 2 * low), low + REACH + 1, low == REACH)
        return carry

    lax.fori_loop(0, 2, step, 0)


def outer_kernel(sel_ref, q_ref, up, dn, mid, stats, first_ref, second_ref, gate_a, gate_b, o_ref, s_scr, p_scr, t_scr):
    del gate_a, gate_b
    for i in (3, 4):
        o_ref[i] = mid[i - REACH]
    for i in (0, 1, 2, 5, 6, 7):
        low = i < REACH
        halo, skip, at = (up, i, 0) if low else (dn, 0, PLANE + REACH - i)
        count = REACH - i if low else i - REACH - 1
        before = stats[i, 0][:, :1]
        top, total, tangent_total = weigh(
            sel_ref, i, at, count, lambda u: halo[skip + u, :, :2 * HEAD_DIM], q_ref[i, :TOK, :], before,
            s_scr, p_scr, t_scr)
        shrink = jnp.exp2(before - top)
        first, second = first_ref[i] * shrink, second_ref[i] * shrink
        for u in range(count):
            more = mix(p_scr.at[:, u * TOK:(u + 1) * TOK], t_scr.at[:, u * TOK:(u + 1) * TOK], TOK,
                       halo[skip + u, :, 2 * HEAD_DIM:])
            first, second = first + more[0], second + more[1]
        o_ref[i] = finish(stats[i, 1] * shrink + total, stats[i, 2] * shrink + tangent_total, first, second)


def join_kernel(row_ref, same, other, gate, both, even, odd):
    del gate
    par = row_ref[0] % 2
    both[par] = same[:, :4 * HEAD_DIM]
    both[1 - par] = other[:, :4 * HEAD_DIM]
    even[...] = both[0]
    odd[...] = both[1]


def pair_kernel(row_ref, sel_ref, same, other, a4, a2, both, b2, b4, o_own, o_other, kv, s_scr, p_scr, t_scr):
    row = row_ref[0]
    par = row % 2
    places = [a4] + [ref.at[n] for ref in (a2, both, b2) for n in range(2)] + [b4]
    for n, ref in enumerate(places):
        kv[n * TOK:(n + 1) * TOK, :] = ref[...]
    for ref, at, place, o_ref in ((same, row, par, o_own), (other, row + 1 - 2 * par, 1 - par, o_other)):
        base = pl.multiple_of(place * TOK, TOK)
        _, total, tangent_total = weigh(
            sel_ref, at, 0, CHUNKS, lambda u: kv[pl.ds(base + u * TOK, TOK), :2 * HEAD_DIM],
            ref[:, 4 * HEAD_DIM:], None, s_scr, p_scr, t_scr)
        first, second = mix(p_scr, t_scr, CHUNKS * TOK, kv[pl.ds(base, CHUNKS * TOK), 2 * HEAD_DIM:])
        o_ref[...] = finish(total, tangent_total, first, second)


def unpack_kernel(par_ref, mine, own, other, o_ref, t_ref):
    par = par_ref[0] % 2
    for j in range(PLANE):
        cols = pl.ds(j * HEAD_DIM, HEAD_DIM)
        o_ref[:, cols] = mine[j, :, :HEAD_DIM]
        t_ref[:, cols] = mine[j, :, HEAD_DIM:]
    for which, piece in ((par, own), (1 - par, other)):
        cols = pl.ds(pl.multiple_of((PLANE + which) * HEAD_DIM, HEAD_DIM), HEAD_DIM)
        o_ref[:, cols] = piece[:, :HEAD_DIM]
        t_ref[:, cols] = piece[:, HEAD_DIM:]


def bf16(*shape):
    return jax.ShapeDtypeStruct(shape, jnp.bfloat16)


def f32(*shape):
    return jax.ShapeDtypeStruct(shape, jnp.float32)


def scratch(chunks):
    return [
        pltpu.VMEM((TOK, chunks * TOK), jnp.float32),
        pltpu.VMEM((TOK, chunks * TOK), jnp.bfloat16),
        pltpu.VMEM((TOK, chunks * TOK), jnp.bfloat16),
    ]


def cost(chunks):
    products = chunks * TOK * TOK
    return pl.CostEstimate(flops=10 * HEAD_DIM * products, bytes_accessed=chunks * 2 * TOK * 4 * HEAD_DIM,
                           transcendentals=products)


def params(mib):
    return pltpu.CompilerParams(vmem_limit_bytes=mib * MIB)


def body(queries, query_tangents, keys, key_tangents, values, value_tangents, selection):
    devices = lax.axis_size("ctx")
    row = (lax.axis_index("ctx") % PLANE).astype(jnp.int32)[None]
    planes = [[z * PLANE + i for i in range(PLANE)] for z in range(devices // PLANE)]

    def send(array, by):
        return lax.ppermute(array, "ctx", [(i, (i + by) % devices) for i in range(devices)])

    def swapped(array):
        return lax.ppermute(array, "ctx", [(i, i ^ 1) for i in range(devices)])

    def exchange(array):
        return lax.all_to_all(array, "ctx", 0, 0, axis_index_groups=planes, tiled=True)

    wide = [pltpu.with_memory_space_constraint(array, pltpu.HBM) for array in
            (queries, query_tangents, keys, key_tangents, values, value_tangents)]
    kv_out = pl.pallas_call(
        cut_keys_kernel,
        out_shape=bf16(PLANE, TOK, 512),
        in_specs=[HBM_SPEC] * 4,
        out_specs=ANY_SPEC,
        scratch_shapes=[pltpu.SemaphoreType.DMA((4 * PLANE,))],
        compiler_params=params(4),
        name="cut_keys",
    )(*wide[2:])
    sel_rows = jnp.pad(selection.astype(jnp.bfloat16).reshape(1, 2 * WIN), ((0, 15), (0, 256 - 2 * WIN)))
    q_out, same, opp = pl.pallas_call(
        cut_rest_kernel,
        out_shape=(bf16(PLANE, TOK + 16, 256), bf16(TOK, 768), bf16(TOK, 768)),
        in_specs=[SMEM_SPEC, VMEM_SPEC] + [HBM_SPEC] * 6,
        out_specs=(VMEM_SPEC,) * 3,
        scratch_shapes=[pltpu.SemaphoreType.DMA((2 * PLANE + 12,))],
        compiler_params=params(8),
        name="cut_rest",
    )(row, sel_rows, *wide)

    other = swapped(opp)
    main = exchange(kv_out)
    up, dn = send(main[PLANE - REACH:], PLANE), send(main[:REACH], -PLANE)
    q_all = exchange(q_out)
    sel_all = q_all[:, TOK, :2 * WIN].astype(jnp.int32)

    both, even, odd = pl.pallas_call(
        join_kernel,
        out_shape=(bf16(2, TOK, 512), bf16(TOK, 512), bf16(TOK, 512)),
        in_specs=[SMEM_SPEC] + [VMEM_SPEC] * 2 + [ANY_SPEC],
        out_specs=(VMEM_SPEC,) * 3,
        compiler_params=params(4),
        name="join",
    )(row, same, other, q_all)
    a2, b2, a4, b4 = send(both, 2), send(both, -2), send(odd, 4), send(even, -4)

    mid, stats, first, second = pl.pallas_call(
        inner_kernel,
        out_shape=(bf16(2, TOK, 256), f32(PLANE, 3, TOK, BLK), f32(PLANE, TOK, 256), f32(PLANE, TOK, BLK)),
        in_specs=[SMEM_SPEC] + [VMEM_SPEC] * 2 + [ANY_SPEC],
        out_specs=(VMEM_SPEC,) * 4,
        scratch_shapes=scratch(CHUNKS),
        compiler_params=params(20),
        cost_estimate=cost(44),
        name="inner",
    )(sel_all, q_all, main.reshape(PLANE * TOK, 512), both)
    mine = pl.pallas_call(
        outer_kernel,
        out_shape=bf16(PLANE, TOK, 256),
        in_specs=[SMEM_SPEC] + [VMEM_SPEC] * 7 + [ANY_SPEC] * 2,
        out_specs=VMEM_SPEC,
        scratch_shapes=scratch(REACH),
        compiler_params=params(20),
        cost_estimate=cost(12),
        name="outer",
    )(sel_all, q_all, up, dn, mid, stats, first, second, a2, b2)
    back = exchange(mine)

    own, lent = pl.pallas_call(
        pair_kernel,
        out_shape=(bf16(TOK, 256), bf16(TOK, 256)),
        in_specs=[SMEM_SPEC] * 2 + [VMEM_SPEC] * 7,
        out_specs=(VMEM_SPEC,) * 2,
        scratch_shapes=[pltpu.VMEM((8 * TOK, 512), jnp.bfloat16)] + scratch(CHUNKS),
        compiler_params=params(12),
        cost_estimate=cost(14),
        name="pair",
    )(row, sel_all, same, other, a4, a2, both, b2, b4)
    partner = swapped(lent)

    return pl.pallas_call(
        unpack_kernel,
        out_shape=(bf16(TOK, HEADS * HEAD_DIM), bf16(TOK, HEADS * HEAD_DIM)),
        in_specs=[SMEM_SPEC] + [VMEM_SPEC] * 3,
        out_specs=(VMEM_SPEC,) * 2,
        compiler_params=params(6),
        name="unpack",
    )(row, back, own, partner)


def solution(mesh):
    wide = P("ctx", "head")
    return jax.shard_map(
        body,
        mesh=mesh,
        in_specs=(wide,) * 6 + (P("ctx", None),),
        out_specs=(wide, wide),
        check_vma=False,
    )
```

time: 135 us -> 210 us (1.56)
  Pallas kernels: 22.9 us -> 86.7 us
  waiting for transfers between devices: 51.5 us -> 63.9 us
  starting transfers between devices: 43.5 us -> 46 us
    pallas_call x1, Pallas kernels: 3.24 us -> 64.9 us  [body(): pl.pallas_call(cut_keys_kernel, out_shape=bf16(PLANE, TOK, 512), in_specs...]
    ppermute x2, waiting for transfers between devices: 7.51 us -> 16.4 us  [swapped(): return lax.ppermute(array, 'ctx', [(i, i ^ 1) for i in range(devices)])]
    ppermute x8 -> x6, starting transfers between devices: 21.9 us -> 25.4 us  [send(): lax.ppermute(array, 'ctx', [(i, (i + by) % devices) for i in range(device...]
    ppermute x8 -> x6, waiting for transfers between devices: 22.7 us -> 25.7 us  [send(): lax.ppermute(array, 'ctx', [(i, (i + by) % devices) for i in range(device...]
    unnamed x56 -> x34, local copies, waits for them, and re-layouts: 12.3 us -> 9.61 us
    pallas_call x2 -> x4, Pallas kernels: 14.9 us -> 17.1 us  [the longest x1 9.13 us: body(): pl.pallas_call(inner_kernel, out_shape=(bf16(2, TOK, 256), f32(PLANE, 3,...]
  transfers between devices with their start and end apart: 14 -> 11, of which waited for: 5 -> 7; matrix products, arithmetic and copies ran while one was open for 1% -> 1% of each run, Pallas kernels for 14% -> 7%
where the time goes in v3:
time: 210 us; the launch traced here: 208 us
  Pallas kernels  86.7 us (41%)
  waiting for transfers between devices  63.9 us (30%)
  starting transfers between devices  46 us (22%)
  local copies, waits for them, and re-layouts  11 us (5%)
    pallas_call x1, Pallas kernels, body(): pl.pallas_call(cut_keys_kernel, out_shape=bf16(PLANE, TOK, 512), in_specs...  64.9 us
    ppermute x6, waiting for transfers between devices, send(): lax.ppermute(array, 'ctx', [(i, (i + by) % devices) for i in range(device...  25.7 us
    ppermute x6, starting transfers between devices, send(): lax.ppermute(array, 'ctx', [(i, (i + by) % devices) for i in range(device...  25.4 us
    all_to_all x3, waiting for transfers between devices, exchange(): lax.all_to_all(array, 'ctx', 0, 0, axis_index_groups=planes, tiled=True)  21.8 us
    all_to_all x3, starting transfers between devices, exchange(): lax.all_to_all(array, 'ctx', 0, 0, axis_index_groups=planes, tiled=True)  17.8 us
    ppermute x2, waiting for transfers between devices, swapped(): return lax.ppermute(array, 'ctx', [(i, i ^ 1) for i in range(devices)])  16.4 us
    unnamed x34, local copies, waits for them, and re-layouts  9.61 us
    pallas_call x1, Pallas kernels, body(): pl.pallas_call(inner_kernel, out_shape=(bf16(2, TOK, 256), f32(PLANE, 3,...  9.13 us
  transfers between devices with their start and end apart: 11, of which 7 were waited for; matrix products, arithmetic and copies ran while one was open for 1% of the time, Pallas kernels for 7%

profile of v3, /device:TPU:1, one launch (start us, length us, event | category | flops | bytes accessed | tf_op | source)
XLA Modules:
  0.0 208.4 jit_solution(4151269518992352227)
XLA Ops:
  0.6 64.9 %cut_keys.1 = bf16[8,256,512]{2,1,0:T(8,128)(2,1)} custom-call(bf16[256,1280]{1,0:T(8,128)(2,1)} %k.3, bf16[256,1280]{1,0:T(8,128)(2,1)} %kt.3, bf16[256,1280]{1,0:T(8,128)(2,1)} %v.3, bf16[256,1280]{1,0:T(8,128)(2,1)} %vt.3), custom_call_target="tpu_custom_call" | custom-call | tf_op jit(solution)/shard_map/cut_keys/pallas_call | solution.py:223
  65.6 0.0 copy-start.16
  65.6 7.5 %all-to-all-start.1 = ((bf16[8,256,512]{2,1,0:T(8,128)(2,1)}), bf16[8,256,512]{2,1,0:T(8,128)(2,1)S(1)}, u32[]{:S(2)}, u32[]{:S(2)}) async-start(bf16[8,256,512]{2,1,0:T(8,128)(2,1)} %cut_keys.1), calls=%async_computation.1 | async-start | bytes 4194304 | tf_op jit(solution)/shard_map/all_to_all | solution.py:219
  73.1 0.0 copy-done.16
  73.1 0.1 reshape.12
  73.2 1.8 cut_rest.1
  75.0 0.0 copy-start
  75.0 1.0 copy-done
  76.0 0.0 copy-start.5
  76.0 0.7 copy-done.5
  76.7 0.0 copy-start.13
  76.7 0.7 copy-done.13
  77.5 21.8 %all-to-all-done.1 = bf16[8,256,512]{2,1,0:T(8,128)(2,1)S(1)} async-done(((bf16[8,256,512]{2,1,0:T(8,128)(2,1)}), bf16[8,256,512]{2,1,0:T(8,128)(2,1)S(1)}, u32[]{:S(2)}, u32[]{:S(2)}) %all-to-all-start.1) | async-done | bytes 2097184 | tf_op jit(solution)/shard_map/all_to_all | solution.py:219
  99.2 5.2 %all-to-all-start = ((bf16[8,272,256]{2,1,0:T(8,128)(2,1)}), bf16[8,272,256]{2,1,0:T(8,128)(2,1)S(1)}, u32[]{:S(2)}, u32[]{:S(2)}) async-start(bf16[8,272,256]{2,1,0:T(8,128)(2,1)} %copy-done), calls=%async_computation | async-start | bytes 2228224 | tf_op jit(solution)/shard_map/all_to_all | solution.py:219
  104.4 1.5 collective-permute-start.2
  105.9 1.3 fusion.1
  107.2 1.6 collective-permute-start
  108.8 3.9 %collective-permute-start.1 = (bf16[3,256,512]{2,1,0:T(8,128)(2,1)}, bf16[3,256,512]{2,1,0:T(8,128)(2,1)}, u32[]{:S(2)}, u32[]{:S(2)}) collective-permute-start(bf16[3,256,512]{2,1,0:T(8,128)(2,1)} %get-tuple-element.26), channel_id=1, source_target_pairs={{0,224},{4,228},{8,232},{12,236},{16,240},{20,244},{24,248},{28,25... | collective-permute-start | bytes 2359304 | tf_op jit(solution)/shard_map/ppermute | solution.py:213
  112.7 13.8 %collective-permute-done.2.other = bf16[256,768]{1,0:T(8,128)(2,1)S(1)} collective-permute-done((bf16[256,768]{1,0:T(8,128)(2,1)}, bf16[256,768]{1,0:T(8,128)(2,1)S(1)}, u32[]{:S(2)}, u32[]{:S(2)}) %collective-permute-start.2) | collective-permute-done | bytes 393248 | tf_op jit(solution)/shard_map/ppermute | solution.py:216
  126.5 0.0 copy-start.8
  126.5 0.7 copy-done.8
  127.3 0.0 all-to-all-done.gate.q_ref
  127.3 0.0 copy-start.6
  127.3 1.0 copy-done.6
  128.3 0.0 copy-start.9
  128.3 1.0 copy-done.9
  129.3 0.1 join.1
  129.4 0.0 copy-start.14
  129.4 0.7 copy-done.14
  130.1 0.0 copy-start.11
  130.1 2.4 %collective-permute-start.3 = (bf16[2,256,512]{2,1,0:T(8,128)(2,1)S(1)}, bf16[2,256,512]{2,1,0:T(8,128)(2,1)S(1)}, u32[]{:S(2)}, u32[]{:S(2)}) collective-permute-start(bf16[2,256,512]{2,1,0:T(8,128)(2,1)S(1)} %get-tuple-element.17.gate.both), channel_id=1, source_target_pairs={{0,8},{4,12},{8,16},{12,20},{16,24},{20,28},{24,32},{28,36},{32,40... | collective-permute-start | bytes 1572872 | tf_op jit(solution)/shard_map/ppermute | solution.py:213
  132.5 8.9 %collective-permute-start.4 = (bf16[2,256,512]{2,1,0:T(8,128)(2,1)S(1)}, bf16[2,256,512]{2,1,0:T(8,128)(2,1)S(1)}, u32[]{:S(2)}, u32[]{:S(2)}) collective-permute-start(bf16[2,256,512]{2,1,0:T(8,128)(2,1)S(1)} %get-tuple-element.17.gate.both), channel_id=1, source_target_pairs={{0,248},{4,252},{8,0},{12,4},{16,8},{20,12},{24,16},{28,20},{32,24... | collective-permute-start | bytes 1572872 | tf_op jit(solution)/shard_map/ppermute | solution.py:213
  141.3 9.1 %inner.1 = (bf16[2,256,256]{2,1,0:T(8,128)(2,1)S(1)}, f32[8,3,256,128]{3,2,1,0:T(8,128)S(1)}, f32[8,256,256]{2,1,0:T(8,128)S(1)}, f32[8,256,128]{2,1,0:T(8,128)S(1)}) custom-call(s32[8,28]{1,0:T(8,128)S(1)} %fusion.sel_ref, bf16[8,272,256]{2,1,0:T(8,128)(2,1)S(1)} %all-to-all-done.gate.q_ref, bf16[2048,512]{1,0:T(8,128)(2,1)S(1)} %bitcast.7, ...), custom_call_target="tpu_custom_call" | custom-call | flops 3690987520 | bytes 11534336 | tf_op jit(solution)/shard_map/inner/pallas_call | solution.py:259
  150.5 0.0 copy-done.11
  150.5 2.9 %collective-permute-done.3.gate_a.a2 = bf16[2,256,512]{2,1,0:T(8,128)(2,1)S(1)} collective-permute-done((bf16[2,256,512]{2,1,0:T(8,128)(2,1)S(1)}, bf16[2,256,512]{2,1,0:T(8,128)(2,1)S(1)}, u32[]{:S(2)}, u32[]{:S(2)}) %collective-permute-start.3) | collective-permute-done | bytes 524320 | tf_op jit(solution)/shard_map/ppermute | solution.py:213
  153.4 5.8 %collective-permute-done.4.gate_b.b2 = bf16[2,256,512]{2,1,0:T(8,128)(2,1)S(1)} collective-permute-done((bf16[2,256,512]{2,1,0:T(8,128)(2,1)S(1)}, bf16[2,256,512]{2,1,0:T(8,128)(2,1)S(1)}, u32[]{:S(2)}, u32[]{:S(2)}) %collective-permute-start.4) | collective-permute-done | bytes 524320 | tf_op jit(solution)/shard_map/ppermute | solution.py:213
  159.2 0.0 collective-permute-done.up
  159.2 0.0 collective-permute-done.1.dn
  159.2 6.1 %outer.1 = bf16[8,256,256]{2,1,0:T(8,128)(2,1)} custom-call(s32[8,28]{1,0:T(8,128)S(1)} %fusion.sel_ref, bf16[8,272,256]{2,1,0:T(8,128)(2,1)S(1)} %all-to-all-done.gate.q_ref, bf16[3,256,512]{2,1,0:T(8,128)(2,1)} %collective-permute-done.up, bf16[3,256,512]{2,1,0:T(8,128)(2,1)} %collective-permute-done.1.dn, bf16[2,256,256]{2,1,0:T(8,128)(2,1)S(1)} %get-tuple-element.18.mid, ...), custom_call_target="tpu_custom_call" | custom-call | flops 1006632960 | bytes 3145728 | tf_op jit(solution)/shard_map/outer/pallas_call | solution.py:269
  165.3 0.0 copy-start.1
  165.3 0.8 copy-done.1
  166.1 0.0 copy-start.3
  166.1 0.8 copy-done.3
  166.9 0.0 copy-start.15
  166.9 0.0 copy-start.7
  166.9 0.0 copy-start.10
  166.9 0.0 copy-start.12
  166.9 5.1 %all-to-all-start.2 = ((bf16[8,256,256]{2,1,0:T(8,128)(2,1)}), bf16[8,256,256]{2,1,0:T(8,128)(2,1)S(1)}, u32[]{:S(2)}, u32[]{:S(2)}) async-start(bf16[8,256,256]{2,1,0:T(8,128)(2,1)} %outer.1), calls=%async_computation.2 | async-start | bytes 2097152 | tf_op jit(solution)/shard_map/all_to_all | solution.py:219
  172.0 0.0 copy-done.15
  172.0 3.0 %collective-permute-start.5 = (bf16[256,512]{1,0:T(8,128)(2,1)S(1)}, bf16[256,512]{1,0:T(8,128)(2,1)S(1)}, u32[]{:S(2)}, u32[]{:S(2)}) collective-permute-start(bf16[256,512]{1,0:T(8,128)(2,1)S(1)} %copy-done.15), channel_id=1, source_target_pairs={{0,16},{4,20},{8,24},{12,28},{16,32},{20,36},{24,40},{28,44},{32,4... | collective-permute-start | bytes 786440 | tf_op jit(solution)/shard_map/ppermute | solution.py:213
  175.0 5.6 %collective-permute-start.6 = (bf16[256,512]{1,0:T(8,128)(2,1)S(1)}, bf16[256,512]{1,0:T(8,128)(2,1)S(1)}, u32[]{:S(2)}, u32[]{:S(2)}) collective-permute-start(bf16[256,512]{1,0:T(8,128)(2,1)S(1)} %get-tuple-element.23), channel_id=1, source_target_pairs={{0,240},{4,244},{8,248},{12,252},{16,0},{20,4},{24,8},{28,12},{32,... | collective-permute-start | bytes 786440 | tf_op jit(solution)/shard_map/ppermute | solution.py:213
  180.6 13.7 %collective-permute-done.5.a4 = bf16[256,512]{1,0:T(8,128)(2,1)S(1)} collective-permute-done((bf16[256,512]{1,0:T(8,128)(2,1)S(1)}, bf16[256,512]{1,0:T(8,128)(2,1)S(1)}, u32[]{:S(2)}, u32[]{:S(2)}) %collective-permute-start.5) | collective-permute-done | bytes 262176 | tf_op jit(solution)/shard_map/ppermute | solution.py:213
  194.2 3.4 %collective-permute-done.6.b4 = bf16[256,512]{1,0:T(8,128)(2,1)S(1)} collective-permute-done((bf16[256,512]{1,0:T(8,128)(2,1)S(1)}, bf16[256,512]{1,0:T(8,128)(2,1)S(1)}, u32[]{:S(2)}, u32[]{:S(2)}) %collective-permute-start.6) | collective-permute-done | bytes 262176 | tf_op jit(solution)/shard_map/ppermute | solution.py:213
  197.6 0.0 copy-done.7
  197.6 0.0 copy-done.10
  197.6 0.0 copy-done.12
  197.6 0.0 copy-start.2
  197.6 1.0 copy-done.2
  198.7 1.0 copy-done.4
  199.7 3.5 %pair.1 = (bf16[256,256]{1,0:T(8,128)(2,1)S(1)}, bf16[256,256]{1,0:T(8,128)(2,1)S(1)}) custom-call(s32[1]{0:T(128)} %bitcast.row_ref.par_ref, s32[8,28]{1,0:T(8,128)S(1)} %fusion.sel_ref, bf16[256,768]{1,0:T(8,128)(2,1)S(1)} %copy-done.7, bf16[256,768]{1,0:T(8,128)(2,1)S(1)} %copy-done.10, bf16[256,512]{1,0:T(8,128)(2,1)S(1)} %collective-permute-done.5.a4, ...), custom_call_target="tpu_custom_call" | custom-call | flops 1174405120 | bytes 3670016 | tf_op jit(solution)/shard_map/pair/pallas_call | solution.py:281
  203.2 1.3 collective-permute-start.7
  204.5 2.6 %collective-permute-done.7.other = bf16[256,256]{1,0:T(8,128)(2,1)S(1)} collective-permute-done((bf16[256,256]{1,0:T(8,128)(2,1)S(1)}, bf16[256,256]{1,0:T(8,128)(2,1)S(1)}, u32[]{:S(2)}, u32[]{:S(2)}) %collective-permute-start.7) | collective-permute-done | bytes 131104 | tf_op jit(solution)/shard_map/ppermute | solution.py:216
  207.1 0.0 all-to-all-done.2.mine
  207.1 1.3 unpack.1
  (5 shorter events, 0.0 us)
Async XLA Ops:
  65.6 7.5 %copy-start.16 = (s32[2,14]{1,0:T(2,128)S(1)}, s32[2,14]{1,0:T(2,128)}, u32[]{:S(2)}) copy-start(s32[2,14]{1,0:T(2,128)} %param.13) | copy-start | bytes 340
  65.6 33.6 %all-to-all-start.1 = ((bf16[8,256,512]{2,1,0:T(8,128)(2,1)}), bf16[8,256,512]{2,1,0:T(8,128)(2,1)S(1)}, u32[]{:S(2)}, u32[]{:S(2)}) async-start(bf16[8,256,512]{2,1,0:T(8,128)(2,1)} %cut_keys.1), calls=%async_computation.1 | async-start | bytes 4194304 | tf_op jit(solution)/shard_map/all_to_all | solution.py:219
  75.0 1.0 copy-start
  76.0 0.7 copy-start.5
  76.7 0.7 copy-start.13
  99.2 28.1 %all-to-all-start = ((bf16[8,272,256]{2,1,0:T(8,128)(2,1)}), bf16[8,272,256]{2,1,0:T(8,128)(2,1)S(1)}, u32[]{:S(2)}, u32[]{:S(2)}) async-start(bf16[8,272,256]{2,1,0:T(8,128)(2,1)} %copy-done), calls=%async_computation | async-start | bytes 2228224 | tf_op jit(solution)/shard_map/all_to_all | solution.py:219
  104.4 22.1 %collective-permute-start.2 = (bf16[256,768]{1,0:T(8,128)(2,1)}, bf16[256,768]{1,0:T(8,128)(2,1)S(1)}, u32[]{:S(2)}, u32[]{:S(2)}) collective-permute-start(bf16[256,768]{1,0:T(8,128)(2,1)} %copy-done.13), channel_id=1, source_target_pairs={{0,4},{4,0},{8,12},{12,8},{16,20},{20,16},{24,28},{28,24},{32,36},... | collective-permute-start | bytes 1179656 | tf_op jit(solution)/shard_map/ppermute | solution.py:216
  107.2 52.0 %collective-permute-start = (bf16[3,256,512]{2,1,0:T(8,128)(2,1)}, bf16[3,256,512]{2,1,0:T(8,128)(2,1)}, u32[]{:S(2)}, u32[]{:S(2)}) collective-permute-start(bf16[3,256,512]{2,1,0:T(8,128)(2,1)} %get-tuple-element.27), channel_id=1, source_target_pairs={{0,32},{4,36},{8,40},{12,44},{16,48},{20,52},{24,56},{28,60},{32,6... | collective-permute-start | bytes 2359304 | tf_op jit(solution)/shard_map/ppermute | solution.py:213
  108.8 50.4 %collective-permute-start.1 = (bf16[3,256,512]{2,1,0:T(8,128)(2,1)}, bf16[3,256,512]{2,1,0:T(8,128)(2,1)}, u32[]{:S(2)}, u32[]{:S(2)}) collective-permute-start(bf16[3,256,512]{2,1,0:T(8,128)(2,1)} %get-tuple-element.26), channel_id=1, source_target_pairs={{0,224},{4,228},{8,232},{12,236},{16,240},{20,244},{24,248},{28,25... | collective-permute-start | bytes 2359304 | tf_op jit(solution)/shard_map/ppermute | solution.py:213
  126.5 0.8 copy-start.8
  127.3 1.0 copy-start.6
  128.3 1.0 copy-start.9
  129.4 0.7 copy-start.14
  130.1 20.4 %copy-start.11 = (bf16[2,256,512]{2,1,0:T(8,128)(2,1)}, bf16[2,256,512]{2,1,0:T(8,128)(2,1)S(1)}, u32[]{:S(2)}) copy-start(bf16[2,256,512]{2,1,0:T(8,128)(2,1)S(1)} %get-tuple-element.17.gate.both) | copy-start | bytes 1572868
  130.1 23.3 %collective-permute-start.3 = (bf16[2,256,512]{2,1,0:T(8,128)(2,1)S(1)}, bf16[2,256,512]{2,1,0:T(8,128)(2,1)S(1)}, u32[]{:S(2)}, u32[]{:S(2)}) collective-permute-start(bf16[2,256,512]{2,1,0:T(8,128)(2,1)S(1)} %get-tuple-element.17.gate.both), channel_id=1, source_target_pairs={{0,8},{4,12},{8,16},{12,20},{16,24},{20,28},{24,32},{28,36},{32,40... | collective-permute-start | bytes 1572872 | tf_op jit(solution)/shard_map/ppermute | solution.py:213
  132.5 26.7 %collective-permute-start.4 = (bf16[2,256,512]{2,1,0:T(8,128)(2,1)S(1)}, bf16[2,256,512]{2,1,0:T(8,128)(2,1)S(1)}, u32[]{:S(2)}, u32[]{:S(2)}) collective-permute-start(bf16[2,256,512]{2,1,0:T(8,128)(2,1)S(1)} %get-tuple-element.17.gate.both), channel_id=1, source_target_pairs={{0,248},{4,252},{8,0},{12,4},{16,8},{20,12},{24,16},{28,20},{32,24... | collective-permute-start | bytes 1572872 | tf_op jit(solution)/shard_map/ppermute | solution.py:213
  165.3 0.8 copy-start.1
  166.1 0.8 copy-start.3
  166.9 5.1 %copy-start.15 = (bf16[256,512]{1,0:T(8,128)(2,1)S(1)}, bf16[256,512]{1,0:T(8,128)(2,1)}, u32[]{:S(2)}) copy-start(bf16[256,512]{1,0:T(8,128)(2,1)} %copy-done.14) | copy-start | bytes 786436
  166.9 30.7 %copy-start.7 = (bf16[256,768]{1,0:T(8,128)(2,1)S(1)}, bf16[256,768]{1,0:T(8,128)(2,1)}, u32[]{:S(2)}) copy-start(bf16[256,768]{1,0:T(8,128)(2,1)} %copy-done.5) | copy-start | bytes 1179652
  166.9 30.7 %copy-start.10 = (bf16[256,768]{1,0:T(8,128)(2,1)S(1)}, bf16[256,768]{1,0:T(8,128)(2,1)}, u32[]{:S(2)}) copy-start(bf16[256,768]{1,0:T(8,128)(2,1)} %copy-done.8) | copy-start | bytes 1179652
  166.9 30.8 %copy-start.12 = (bf16[2,256,512]{2,1,0:T(8,128)(2,1)S(1)}, bf16[2,256,512]{2,1,0:T(8,128)(2,1)}, u32[]{:S(2)}) copy-start(bf16[2,256,512]{2,1,0:T(8,128)(2,1)} %copy-done.11) | copy-start | bytes 1572868
  166.9 40.2 %all-to-all-start.2 = ((bf16[8,256,256]{2,1,0:T(8,128)(2,1)}), bf16[8,256,256]{2,1,0:T(8,128)(2,1)S(1)}, u32[]{:S(2)}, u32[]{:S(2)}) async-start(bf16[8,256,256]{2,1,0:T(8,128)(2,1)} %outer.1), calls=%async_computation.2 | async-start | bytes 2097152 | tf_op jit(solution)/shard_map/all_to_all | solution.py:219
  172.0 22.2 %collective-permute-start.5 = (bf16[256,512]{1,0:T(8,128)(2,1)S(1)}, bf16[256,512]{1,0:T(8,128)(2,1)S(1)}, u32[]{:S(2)}, u32[]{:S(2)}) collective-permute-start(bf16[256,512]{1,0:T(8,128)(2,1)S(1)} %copy-done.15), channel_id=1, source_target_pairs={{0,16},{4,20},{8,24},{12,28},{16,32},{20,36},{24,40},{28,44},{32,4... | collective-permute-start | bytes 786440 | tf_op jit(solution)/shard_map/ppermute | solution.py:213
  175.0 22.6 %collective-permute-start.6 = (bf16[256,512]{1,0:T(8,128)(2,1)S(1)}, bf16[256,512]{1,0:T(8,128)(2,1)S(1)}, u32[]{:S(2)}, u32[]{:S(2)}) collective-permute-start(bf16[256,512]{1,0:T(8,128)(2,1)S(1)} %get-tuple-element.23), channel_id=1, source_target_pairs={{0,240},{4,244},{8,248},{12,252},{16,0},{20,4},{24,8},{28,12},{32,... | collective-permute-start | bytes 786440 | tf_op jit(solution)/shard_map/ppermute | solution.py:213
  197.6 1.0 copy-start.2
  198.7 1.0 copy-start.4
  203.2 3.9 %collective-permute-start.7 = (bf16[256,256]{1,0:T(8,128)(2,1)S(1)}, bf16[256,256]{1,0:T(8,128)(2,1)S(1)}, u32[]{:S(2)}, u32[]{:S(2)}) collective-permute-start(bf16[256,256]{1,0:T(8,128)(2,1)S(1)} %get-tuple-element.25), channel_id=1, source_target_pairs={{0,4},{4,0},{8,12},{12,8},{16,20},{20,16},{24,28},{28,24},{32,36},... | collective-permute-start | bytes 393224 | tf_op jit(solution)/shard_map/ppermute | solution.py:216

commit v4 on v3

v4 whole, which is shorter than its diff:
```python
import jax
import jax.numpy as jnp
from jax import lax
from jax.experimental import pallas as pl
from jax.experimental.pallas import tpu as pltpu
from jax.sharding import PartitionSpec as P

HEADS = 10
HEAD_DIM = 128
BLK = 128
REACH = 3
TOK = 256
WIN = 14
PLANE = 8
CHUNKS = 2 * REACH + 1
EXTRA = 8
NEG = -1.0e30
LOG2E = 1.4426950408889634
SCALE = HEAD_DIM ** -0.5
FACTOR = SCALE * LOG2E
MIB = 1 << 20

VMEM_SPEC = pl.BlockSpec(memory_space=pltpu.VMEM)
HBM_SPEC = pl.BlockSpec(memory_space=pltpu.HBM)
ANY_SPEC = pl.BlockSpec(memory_space=pl.ANY)
SMEM_SPEC = pl.BlockSpec(memory_space=pltpu.SMEM)


def run_copies(pairs, sem):
    copies = [pltpu.make_async_copy(source, target, sem.at[n]) for n, (source, target) in enumerate(pairs)]
    for copy in copies:
        copy.start()
    for copy in copies:
        copy.wait()


def lanes(n):
    return pl.ds(n * HEAD_DIM, HEAD_DIM)


def cut_keys_kernel(k, kt, v, vt, out):
    for n, ref in enumerate((k, kt, v, vt)):
        out[0, :, n * HEAD_DIM:(n + 1) * HEAD_DIM] = ref[...]


def cut_rest_kernel(row_ref, sel, q, qt, k, kt, v, vt, q_out, kv_same, kv_opp, near, q_same, sem):
    pairs = [(ref.at[:, lanes(j)], q_out.at[j, 0:TOK, lanes(n)]) for j in range(PLANE) for n, ref in enumerate((qt, q))]
    par = row_ref[0] % 2
    own, opp = [pl.ds(pl.multiple_of((PLANE + which) * HEAD_DIM, HEAD_DIM), HEAD_DIM) for which in (par, 1 - par)]
    for n, ref in enumerate((k, kt, v, vt)):
        pairs += [(ref.at[:, own], kv_same.at[:, lanes(n)]), (ref.at[:, opp], kv_opp.at[:, lanes(n)]),
                  (ref.at[:, opp], near.at[:, lanes(n)])]
    for n, ref in enumerate((qt, q)):
        pairs += [(ref.at[:, own], q_same.at[:, lanes(n)]), (ref.at[:, opp], near.at[:, lanes(n + 4)])]
    for j in range(PLANE):
        q_out[j, TOK:, :] = sel[...]
    run_copies(pairs, sem)


def weigh(sel_ref, row, first, count, chunk, qcat, floor, s_scr, p_scr, t_scr):
    dims = (((1,), (1,)), ((), ()))
    query = qcat[:, HEAD_DIM:]
    peak = [None, None]
    for u in range(count):
        s = lax.dot_general(query, chunk(u)[:, :HEAD_DIM], dims, preferred_element_type=jnp.float32)
        for qb in range(2):
            for kb in range(2):
                listed = sel_ref[row, qb * WIN + 2 * (first + u) + kb]
                piece = s[qb * BLK:(qb + 1) * BLK, kb * BLK:(kb + 1) * BLK] + jnp.where(listed != 0, 0.0, NEG)
                s_scr[qb * BLK:(qb + 1) * BLK, u * TOK + kb * BLK:u * TOK + (kb + 1) * BLK] = piece
                peak[qb] = piece if peak[qb] is None else jnp.maximum(peak[qb], piece)
    top = jnp.concatenate([jnp.max(p, axis=1, keepdims=True) for p in peak], axis=0) * FACTOR
    if floor is not None:
        top = jnp.maximum(top, floor)
    total = jnp.zeros((TOK, BLK), jnp.float32)
    tangent_total = jnp.zeros((TOK, BLK), jnp.float32)
    for u in range(count):
        st = lax.dot_general(qcat, chunk(u), dims, preferred_element_type=jnp.float32)
        weights = jnp.exp2(s_scr[:, u * TOK:(u + 1) * TOK] * FACTOR - top)
        weighted = weights * st
        total += weights[:, :BLK] + weights[:, BLK:]
        tangent_total += weighted[:, :BLK] + weighted[:, BLK:]
        p_scr[:, u * TOK:(u + 1) * TOK] = weights.astype(jnp.bfloat16)
        t_scr[:, u * TOK:(u + 1) * TOK] = weighted.astype(jnp.bfloat16)
    return top, total, tangent_total


def finish(total, tangent_total, first, second):
    inverse = 1.0 / jnp.sum(total, axis=1, keepdims=True)
    out = first[:, :HEAD_DIM] * inverse
    tangent_sum = jnp.sum(tangent_total, axis=1, keepdims=True)
    tangent = ((second - out * tangent_sum) * SCALE + first[:, HEAD_DIM:]) * inverse
    return jnp.concatenate([out.astype(jnp.bfloat16), tangent.astype(jnp.bfloat16)], axis=1)


def mix(p_scr, t_scr, width, values):
    first = jnp.dot(p_scr[:, :width], values, preferred_element_type=jnp.float32)
    second = jnp.dot(t_scr[:, :width], values[:, :HEAD_DIM], preferred_element_type=jnp.float32)
    return first, second


def whole(sel_ref, row, base, qcat, kv, s_scr, p_scr, t_scr):
    _, total, tangent_total = weigh(
        sel_ref, row, 0, CHUNKS, lambda u: kv[pl.ds(base + u * TOK, TOK), :2 * HEAD_DIM], qcat, None,
        s_scr, p_scr, t_scr)
    first, second = mix(p_scr, t_scr, CHUNKS * TOK, kv[pl.ds(base, CHUNKS * TOK), 2 * HEAD_DIM:])
    return finish(total, tangent_total, first, second)


def plane_kernel(sel_ref, q_ref, main, up, dn, o_ref, kv, s_scr, p_scr, t_scr):
    for slot in range(PLANE + 2 * REACH):
        if slot < REACH:
            piece = up.at[slot]
        elif slot < REACH + PLANE:
            piece = main.at[slot - REACH]
        else:
            piece = dn.at[slot - REACH - PLANE]
        kv[slot * TOK:(slot + 1) * TOK, :] = piece[...]

    def step(i, carry):
        base = pl.multiple_of(i * TOK, TOK)
        o_ref[i] = whole(sel_ref, i, base, q_ref[i, :TOK, :], kv, s_scr, p_scr, t_scr)
        return carry

    lax.fori_loop(0, PLANE, step, 0)


def pair_kernel(row_ref, sel_ref, q_own, a3, a2, a1, own, b1, b2, b3, far, gate, o_own, o_other,
                kv, s_scr, p_scr, t_scr):
    del gate
    row = row_ref[0]
    par = row % 2
    for place, piece in enumerate((a3, a2, a1, own, b1, b2, b3)):
        kv[pl.ds(pl.multiple_of((place + par) * TOK, TOK), TOK), :] = piece[:, :512]
    kv[pl.ds(pl.multiple_of((1 - par) * CHUNKS * TOK, TOK), TOK), :] = far[...]
    q_other = jnp.where(par == 1, a1[:, 512:], b1[:, 512:])
    for qcat, at, place, o_ref in ((q_own[...], row, par, o_own), (q_other, row + 1 - 2 * par, 1 - par, o_other)):
        base = pl.multiple_of(place * TOK, TOK)
        o_ref[...] = whole(sel_ref, at, base, qcat, kv, s_scr, p_scr, t_scr)


def after_kernel(*refs):
    del refs


def after(array, *others):
    return pl.pallas_call(
        after_kernel,
        out_shape=jax.ShapeDtypeStruct(array.shape, array.dtype),
        in_specs=[ANY_SPEC] + [VMEM_SPEC] * len(others),
        out_specs=ANY_SPEC,
        input_output_aliases={0: 0},
        compiler_params=params(1),
        name="after",
    )(array, *others)


def unpack_kernel(par_ref, mine, own, other, o_ref, t_ref):
    par = par_ref[0] % 2
    for j in range(PLANE):
        cols = pl.ds(j * HEAD_DIM, HEAD_DIM)
        o_ref[:, cols] = mine[j, :, :HEAD_DIM]
        t_ref[:, cols] = mine[j, :, HEAD_DIM:]
    for which, piece in ((par, own), (1 - par, other)):
        cols = pl.ds(pl.multiple_of((PLANE + which) * HEAD_DIM, HEAD_DIM), HEAD_DIM)
        o_ref[:, cols] = piece[:, :HEAD_DIM]
        t_ref[:, cols] = piece[:, HEAD_DIM:]


def bf16(*shape):
    return jax.ShapeDtypeStruct(shape, jnp.bfloat16)


def f32(*shape):
    return jax.ShapeDtypeStruct(shape, jnp.float32)


def scratch(chunks):
    return [
        pltpu.VMEM((TOK, chunks * TOK), jnp.float32),
        pltpu.VMEM((TOK, chunks * TOK), jnp.bfloat16),
        pltpu.VMEM((TOK, chunks * TOK), jnp.bfloat16),
    ]


def cost(chunks):
    products = chunks * TOK * TOK
    return pl.CostEstimate(flops=10 * HEAD_DIM * products, bytes_accessed=chunks * 2 * TOK * 4 * HEAD_DIM,
                           transcendentals=products)


def params(mib):
    return pltpu.CompilerParams(vmem_limit_bytes=mib * MIB)


def body(queries, query_tangents, keys, key_tangents, values, value_tangents, selection):
    devices = lax.axis_size("ctx")
    row = (lax.axis_index("ctx") % PLANE).astype(jnp.int32)[None]
    planes = [[z * PLANE + i for i in range(PLANE)] for z in range(devices // PLANE)]

    def send(array, by):
        return lax.ppermute(array, "ctx", [(i, (i + by) % devices) for i in range(devices)])

    def swapped(array):
        return lax.ppermute(array, "ctx", [(i, i ^ 1) for i in range(devices)])

    def exchange(array):
        return lax.all_to_all(array, "ctx", 0, 0, axis_index_groups=planes, tiled=True)

    wide = [pltpu.with_memory_space_constraint(array, pltpu.HBM) for array in
            (queries, query_tangents, keys, key_tangents, values, value_tangents)]
    kv_out = pl.pallas_call(
        cut_keys_kernel,
        grid=(PLANE,),
        out_shape=pltpu.HBM((PLANE, TOK, 512), jnp.bfloat16),
        in_specs=[pl.BlockSpec((TOK, HEAD_DIM), lambda j: (0, j))] * 4,
        out_specs=pl.BlockSpec((1, TOK, 512), lambda j: (j, 0, 0)),
        compiler_params=params(8),
        name="cut_keys",
    )(*wide[2:])
    sel_rows = jnp.pad(selection.astype(jnp.bfloat16).reshape(1, 2 * WIN), ((0, EXTRA - 1), (0, 256 - 2 * WIN)))
    q_out, kv_same, kv_opp, near, q_same = pl.pallas_call(
        cut_rest_kernel,
        out_shape=(bf16(PLANE, TOK + EXTRA, 256), bf16(TOK, 512), bf16(TOK, 512), bf16(TOK, 768), bf16(TOK, 256)),
        in_specs=[SMEM_SPEC, VMEM_SPEC] + [HBM_SPEC] * 6,
        out_specs=(VMEM_SPEC,) * 5,
        scratch_shapes=[pltpu.SemaphoreType.DMA((2 * PLANE + 16,))],
        compiler_params=params(8),
        name="cut_rest",
    )(row, sel_rows, *wide)

    main = exchange(kv_out)
    up, dn = send(main[PLANE - REACH:], PLANE), send(main[:REACH], -PLANE)
    q_all = exchange(after(q_out, main))
    sel_all = q_all[:, TOK, :2 * WIN].astype(jnp.int32)

    near = after(near, main)
    a1, b1 = send(near, 1), send(near, -1)
    kv_same, kv_opp = after(kv_same, sel_all, a1, b1), after(kv_opp, sel_all, a1, b1)
    a2, b2, a3, b3 = send(kv_same, 2), send(kv_same, -2), send(kv_opp, 3), send(kv_opp, -3)
    far = lax.ppermute(kv_same, "ctx", [(i, (i - 4 + 8 * (i % 2)) % devices) for i in range(devices)])

    mine = pl.pallas_call(
        plane_kernel,
        out_shape=bf16(PLANE, TOK, 256),
        in_specs=[SMEM_SPEC] + [VMEM_SPEC] * 4,
        out_specs=VMEM_SPEC,
        scratch_shapes=[pltpu.VMEM(((PLANE + 2 * REACH) * TOK, 512), jnp.bfloat16)] + scratch(CHUNKS),
        compiler_params=params(16),
        cost_estimate=cost(56),
        name="plane",
    )(sel_all, q_all, main, up, dn)
    own, other = pl.pallas_call(
        pair_kernel,
        out_shape=(bf16(TOK, 256), bf16(TOK, 256)),
        in_specs=[SMEM_SPEC] * 2 + [VMEM_SPEC] * 10,
        out_specs=(VMEM_SPEC,) * 2,
        scratch_shapes=[pltpu.VMEM((8 * TOK, 512), jnp.bfloat16)] + scratch(CHUNKS),
        compiler_params=params(12),
        cost_estimate=cost(14),
        name="pair",
    )(row, sel_all, q_same, a3, a2, a1, kv_same, b1, b2, b3, far, mine)
    partner = swapped(other)
    back = exchange(after(mine, other))

    return pl.pallas_call(
        unpack_kernel,
        out_shape=(bf16(TOK, HEADS * HEAD_DIM), bf16(TOK, HEADS * HEAD_DIM)),
        in_specs=[SMEM_SPEC] + [VMEM_SPEC] * 3,
        out_specs=(VMEM_SPEC,) * 2,
        compiler_params=params(6),
        name="unpack",
    )(row, back, own, partner)


def solution(mesh):
    wide = P("ctx", "head")
    return jax.shard_map(
        body,
        mesh=mesh,
        in_specs=(wide,) * 6 + (P("ctx", None),),
        out_specs=(wide, wide),
        check_vma=False,
    )
```

time: 210 us -> 139 us (0.66)
  Pallas kernels: 86.7 us -> 29.3 us
  local copies, waits for them, and re-layouts: 11 us -> 3.84 us
  waiting for transfers between devices: 63.9 us -> 58.4 us
    pallas_call x5 -> x8, Pallas kernels: 82 us -> 23.9 us  [the longest x1 15.2 us: body(): pl.pallas_call(plane_kernel, out_shape=bf16(PLANE, TOK, 256), in_specs=[S...]
    unnamed x34 -> x14, local copies, waits for them, and re-layouts: 9.61 us -> 1.68 us
    ppermute x6 -> x8, waiting for transfers between devices: 25.7 us -> 21.6 us  [send(): lax.ppermute(array, 'ctx', [(i, (i + by) % devices) for i in range(device...]
    ppermute x2 -> x1, waiting for transfers between devices: 16.4 us -> 13 us  [swapped(): return lax.ppermute(array, 'ctx', [(i, i ^ 1) for i in range(devices)])]
    ppermute x6 -> x8, starting transfers between devices: 25.4 us -> 26.2 us  [send(): lax.ppermute(array, 'ctx', [(i, (i + by) % devices) for i in range(device...]
  transfers between devices with their start and end apart: 11 -> 13, of which waited for: 7 -> 4; matrix products, arithmetic and copies ran while one was open for 1% -> 2% of each run, Pallas kernels for 7% -> 13%
where the time goes in v4:
time: 139 us; the launch traced here: 137 us
  waiting for transfers between devices  58.4 us (42%)
  starting transfers between devices  44.8 us (32%)
  Pallas kernels  29.3 us (21%)
  local copies, waits for them, and re-layouts  3.84 us (3%)
    ppermute x8, starting transfers between devices, send(): lax.ppermute(array, 'ctx', [(i, (i + by) % devices) for i in range(device...  26.2 us
    all_to_all x3, waiting for transfers between devices, exchange(): lax.all_to_all(array, 'ctx', 0, 0, axis_index_groups=planes, tiled=True)  23.8 us
    ppermute x8, waiting for transfers between devices, send(): lax.ppermute(array, 'ctx', [(i, (i + by) % devices) for i in range(device...  21.6 us
    all_to_all x3, starting transfers between devices, exchange(): lax.all_to_all(array, 'ctx', 0, 0, axis_index_groups=planes, tiled=True)  17.1 us
    pallas_call x1, Pallas kernels, body(): pl.pallas_call(plane_kernel, out_shape=bf16(PLANE, TOK, 256), in_specs=[S...  15.2 us
    ppermute x1, waiting for transfers between devices, swapped(): return lax.ppermute(array, 'ctx', [(i, i ^ 1) for i in range(devices)])  13 us
    pallas_call x1, Pallas kernels, body(): pl.pallas_call(cut_keys_kernel, grid=(PLANE,), out_shape=pltpu.HBM((PLANE...  5.78 us
    pallas_call x1, Pallas kernels, body(): pl.pallas_call(pair_kernel, out_shape=(bf16(TOK, 256), bf16(TOK, 256)), i...  4.13 us
  transfers between devices with their start and end apart: 13, of which 4 were waited for; matrix products, arithmetic and copies ran while one was open for 2% of the time, Pallas kernels for 13%

profile of v4, /device:TPU:1, one launch (start us, length us, event | category | flops | bytes accessed | tf_op | source)
XLA Modules:
  0.0 137.1 jit_solution(12799884659987577042)
XLA Ops:
  0.6 5.8 %cut_keys.1 = bf16[8,256,512]{2,1,0:T(8,128)(2,1)} custom-call(bf16[256,1280]{1,0:T(8,128)(2,1)} %k.3, bf16[256,1280]{1,0:T(8,128)(2,1)} %kt.3, bf16[256,1280]{1,0:T(8,128)(2,1)} %v.3, bf16[256,1280]{1,0:T(8,128)(2,1)} %vt.3), custom_call_target="tpu_custom_call" | custom-call | tf_op jit(solution)/shard_map/cut_keys/pallas_call | solution.py:212
  6.4 0.0 copy-start.6
  6.4 7.6 %all-to-all-start = ((bf16[8,256,512]{2,1,0:T(8,128)(2,1)}), bf16[8,256,512]{2,1,0:T(8,128)(2,1)S(1)}, u32[]{:S(2)}, u32[]{:S(2)}) async-start(bf16[8,256,512]{2,1,0:T(8,128)(2,1)} %cut_keys.1), calls=%async_computation | async-start | bytes 4194304 | tf_op jit(solution)/shard_map/all_to_all | solution.py:208
  14.0 0.0 copy-done.6
  14.0 0.1 reshape.9
  14.1 2.9 %cut_rest.1 = (bf16[8,264,256]{2,1,0:T(8,128)(2,1)}, bf16[256,512]{1,0:T(8,128)(2,1)S(1)}, bf16[256,512]{1,0:T(8,128)(2,1)S(1)}, bf16[256,768]{1,0:T(8,128)(2,1)S(1)}, bf16[256,256]{1,0:T(8,128)(2,1)S(1)}) custom-call(s32[1]{0:T(128)} %bitcast.row_ref.par_ref, bf16[8,256]{1,0:T(8,128)(2,1)S(1)} %pad.4.sel, bf16[256,1280]{1,0:T(8,128)(2,1)} %q.1, ...), custom_call_target="tpu_custom_call" | custom-call | tf_op jit(solution)/shard_map/cut_rest/pallas_call | solution.py:222
  17.0 0.0 copy-start
  17.0 0.0 copy-start.4
  17.0 23.1 %all-to-all-done.refs_1_.main = bf16[8,256,512]{2,1,0:T(8,128)(2,1)S(1)} async-done(((bf16[8,256,512]{2,1,0:T(8,128)(2,1)}), bf16[8,256,512]{2,1,0:T(8,128)(2,1)S(1)}, u32[]{:S(2)}, u32[]{:S(2)}) %all-to-all-start) | async-done | bytes 2097184 | tf_op jit(solution)/shard_map/all_to_all | solution.py:208
  40.2 0.0 copy-done
  40.2 0.0 copy-done.4
  40.2 5.2 %all-to-all-start.1 = ((bf16[8,264,256]{2,1,0:T(8,128)(2,1)}), bf16[8,264,256]{2,1,0:T(8,128)(2,1)}, u32[]{:S(2)}, u32[]{:S(2)}) async-start(bf16[8,264,256]{2,1,0:T(8,128)(2,1)} %after.5), calls=%async_computation.1 | async-start | bytes 2162688 | tf_op jit(solution)/shard_map/all_to_all | solution.py:208
  45.4 1.3 fusion.1
  46.7 1.6 %collective-permute-start = (bf16[3,256,512]{2,1,0:T(8,128)(2,1)}, bf16[3,256,512]{2,1,0:T(8,128)(2,1)}, u32[]{:S(2)}, u32[]{:S(2)}) collective-permute-start(bf16[3,256,512]{2,1,0:T(8,128)(2,1)} %get-tuple-element.17), channel_id=1, source_target_pairs={{0,32},{4,36},{8,40},{12,44},{16,48},{20,52},{24,56},{28,60},{32,6... | collective-permute-start | bytes 2359304 | tf_op jit(solution)/shard_map/ppermute | solution.py:202
  48.4 3.9 %collective-permute-start.1 = (bf16[3,256,512]{2,1,0:T(8,128)(2,1)}, bf16[3,256,512]{2,1,0:T(8,128)(2,1)}, u32[]{:S(2)}, u32[]{:S(2)}) collective-permute-start(bf16[3,256,512]{2,1,0:T(8,128)(2,1)} %get-tuple-element.16), channel_id=1, source_target_pairs={{0,224},{4,228},{8,232},{12,236},{16,240},{20,244},{24,248},{28,25... | collective-permute-start | bytes 2359304 | tf_op jit(solution)/shard_map/ppermute | solution.py:202
  52.3 1.5 %collective-permute-start.2 = (bf16[256,768]{1,0:T(8,128)(2,1)S(1)}, bf16[256,768]{1,0:T(8,128)(2,1)S(1)}, u32[]{:S(2)}, u32[]{:S(2)}) collective-permute-start(bf16[256,768]{1,0:T(8,128)(2,1)S(1)} %after.6), channel_id=1, source_target_pairs={{0,4},{4,8},{8,12},{12,16},{16,20},{20,24},{24,28},{28,32},{32,36}... | collective-permute-start | bytes 1179656 | tf_op jit(solution)/shard_map/ppermute | solution.py:202
  53.8 5.7 %collective-permute-start.3 = (bf16[256,768]{1,0:T(8,128)(2,1)S(1)}, bf16[256,768]{1,0:T(8,128)(2,1)S(1)}, u32[]{:S(2)}, u32[]{:S(2)}) collective-permute-start(bf16[256,768]{1,0:T(8,128)(2,1)S(1)} %after.6), channel_id=1, source_target_pairs={{0,252},{4,0},{8,4},{12,8},{16,12},{20,16},{24,20},{28,24},{32,28}... | collective-permute-start | bytes 1179656 | tf_op jit(solution)/shard_map/ppermute | solution.py:202
  59.5 0.7 all-to-all-done.1.q_ref
  60.2 0.7 slice.12
  61.0 21.6 %collective-permute-done.2.refs_2_.a1 = bf16[256,768]{1,0:T(8,128)(2,1)S(1)} collective-permute-done((bf16[256,768]{1,0:T(8,128)(2,1)S(1)}, bf16[256,768]{1,0:T(8,128)(2,1)S(1)}, u32[]{:S(2)}, u32[]{:S(2)}) %collective-permute-start.2) | collective-permute-done | bytes 393248 | tf_op jit(solution)/shard_map/ppermute | solution.py:202
  82.6 0.0 collective-permute-done.3.refs_3_.b1
  82.6 0.0 copy-start.1
  82.6 0.9 copy-done.1
  83.5 0.0 copy-start.2
  83.5 0.7 copy-done.2
  84.2 0.0 collective-permute-start.5
  84.2 7.5 %collective-permute-start.6 = (bf16[256,512]{1,0:T(8,128)(2,1)}, bf16[256,512]{1,0:T(8,128)(2,1)S(1)}, u32[]{:S(2)}, u32[]{:S(2)}) collective-permute-start(bf16[256,512]{1,0:T(8,128)(2,1)} %copy-done.2), channel_id=1, source_target_pairs={{0,248},{4,252},{8,0},{12,4},{16,8},{20,12},{24,16},{28,20},{32,24... | collective-permute-start | bytes 786440 | tf_op jit(solution)/shard_map/ppermute | solution.py:202
  91.7 0.0 copy-start.3
  91.7 0.0 copy-start.5
  91.7 0.0 collective-permute-start.4
  91.7 0.0 collective-permute-done.up
  91.7 6.0 %collective-permute-start.7 = (bf16[256,512]{1,0:T(8,128)(2,1)S(1)}, bf16[256,512]{1,0:T(8,128)(2,1)S(1)}, u32[]{:S(2)}, u32[]{:S(2)}) collective-permute-start(bf16[256,512]{1,0:T(8,128)(2,1)S(1)} %after.7), channel_id=1, source_target_pairs={{0,244},{4,248},{8,252},{12,0},{16,4},{20,8},{24,12},{28,16},{32,2... | collective-permute-start | bytes 786440 | tf_op jit(solution)/shard_map/ppermute | solution.py:202
  97.7 0.0 collective-permute-done.1.dn
  97.7 0.0 collective-permute-start.8
  97.7 15.2 %plane.1.gate.refs_0_ = bf16[8,256,256]{2,1,0:T(8,128)(2,1)} custom-call(s32[8,28]{1,0:T(8,128)S(1)} %fusion.sel_ref.refs_1_, bf16[8,264,256]{2,1,0:T(8,128)(2,1)} %all-to-all-done.1.q_ref, bf16[8,256,512]{2,1,0:T(8,128)(2,1)S(1)} %all-to-all-done.refs_1_.main, bf16[3,256,512]{2,1,0:T(8,128)(2,1)} %collective-permute-done.up, ...), custom_call_target="tpu_custom_call" | custom-call | flops 4697620480 | bytes 14680064 | tf_op jit(solution)/shard_map/plane/pallas_call | solution.py:243
  112.9 0.0 collective-permute-done.4.a3
  112.9 0.0 collective-permute-done.5.a2
  112.9 0.0 collective-permute-done.6.b2
  112.9 0.0 collective-permute-done.7.b3
  112.9 0.0 collective-permute-done.8.far
  113.0 0.0 copy-done.3
  113.0 0.0 copy-done.5
  113.0 4.1 %pair.1 = (bf16[256,256]{1,0:T(8,128)(2,1)S(1)}, bf16[256,256]{1,0:T(8,128)(2,1)S(1)}) custom-call(s32[1]{0:T(128)} %bitcast.row_ref.par_ref, s32[8,28]{1,0:T(8,128)S(1)} %fusion.sel_ref.refs_1_, bf16[256,256]{1,0:T(8,128)(2,1)S(1)} %copy-done.5, bf16[256,512]{1,0:T(8,128)(2,1)S(1)} %collective-permute-done.4.a3, ...), custom_call_target="tpu_custom_call" | custom-call | flops 1174405120 | bytes 3670016 | tf_op jit(solution)/shard_map/pair/pallas_call | solution.py:253
  117.1 4.3 %all-to-all-start.2 = ((bf16[8,256,256]{2,1,0:T(8,128)(2,1)}), bf16[8,256,256]{2,1,0:T(8,128)(2,1)S(1)}, u32[]{:S(2)}, u32[]{:S(2)}) async-start(bf16[8,256,256]{2,1,0:T(8,128)(2,1)} %after.9), calls=%async_computation.2 | async-start | bytes 2097152 | tf_op jit(solution)/shard_map/all_to_all | solution.py:208
  121.4 1.5 %collective-permute-start.9 = (bf16[256,256]{1,0:T(8,128)(2,1)S(1)}, bf16[256,256]{1,0:T(8,128)(2,1)S(1)}, u32[]{:S(2)}, u32[]{:S(2)}) collective-permute-start(bf16[256,256]{1,0:T(8,128)(2,1)S(1)} %get-tuple-element.14.refs_1_), channel_id=1, source_target_pairs={{0,4},{4,0},{8,12},{12,8},{16,20},{20,16},{24,28},{28,24},{32,36},... | collective-permute-start | bytes 393224 | tf_op jit(solution)/shard_map/ppermute | solution.py:205
  122.8 13.0 %collective-permute-done.9.other = bf16[256,256]{1,0:T(8,128)(2,1)S(1)} collective-permute-done((bf16[256,256]{1,0:T(8,128)(2,1)S(1)}, bf16[256,256]{1,0:T(8,128)(2,1)S(1)}, u32[]{:S(2)}, u32[]{:S(2)}) %collective-permute-start.9) | collective-permute-done | bytes 131104 | tf_op jit(solution)/shard_map/ppermute | solution.py:205
  135.8 0.0 all-to-all-done.2.mine
  135.8 1.3 unpack.1
  (8 shorter events, 0.0 us)
Async XLA Ops:
  6.4 7.6 %copy-start.6 = (s32[2,14]{1,0:T(2,128)S(1)}, s32[2,14]{1,0:T(2,128)}, u32[]{:S(2)}) copy-start(s32[2,14]{1,0:T(2,128)} %param.13) | copy-start | bytes 340
  6.4 33.8 %all-to-all-start = ((bf16[8,256,512]{2,1,0:T(8,128)(2,1)}), bf16[8,256,512]{2,1,0:T(8,128)(2,1)S(1)}, u32[]{:S(2)}, u32[]{:S(2)}) async-start(bf16[8,256,512]{2,1,0:T(8,128)(2,1)} %cut_keys.1), calls=%async_computation | async-start | bytes 4194304 | tf_op jit(solution)/shard_map/all_to_all | solution.py:208
  17.0 23.2 %copy-start = (bf16[256,512]{1,0:T(8,128)(2,1)}, bf16[256,512]{1,0:T(8,128)(2,1)S(1)}, u32[]{:S(2)}) copy-start(bf16[256,512]{1,0:T(8,128)(2,1)S(1)} %get-tuple-element.13.refs_0_) | copy-start | bytes 786436
  17.0 23.1 %copy-start.4 = (bf16[256,256]{1,0:T(8,128)(2,1)}, bf16[256,256]{1,0:T(8,128)(2,1)S(1)}, u32[]{:S(2)}) copy-start(bf16[256,256]{1,0:T(8,128)(2,1)S(1)} %get-tuple-element.10.q_own) | copy-start | bytes 393220
  40.2 20.1 %all-to-all-start.1 = ((bf16[8,264,256]{2,1,0:T(8,128)(2,1)}), bf16[8,264,256]{2,1,0:T(8,128)(2,1)}, u32[]{:S(2)}, u32[]{:S(2)}) async-start(bf16[8,264,256]{2,1,0:T(8,128)(2,1)} %after.5), calls=%async_computation.1 | async-start | bytes 2162688 | tf_op jit(solution)/shard_map/all_to_all | solution.py:208
  46.7 45.0 %collective-permute-start = (bf16[3,256,512]{2,1,0:T(8,128)(2,1)}, bf16[3,256,512]{2,1,0:T(8,128)(2,1)}, u32[]{:S(2)}, u32[]{:S(2)}) collective-permute-start(bf16[3,256,512]{2,1,0:T(8,128)(2,1)} %get-tuple-element.17), channel_id=1, source_target_pairs={{0,32},{4,36},{8,40},{12,44},{16,48},{20,52},{24,56},{28,60},{32,6... | collective-permute-start | bytes 2359304 | tf_op jit(solution)/shard_map/ppermute | solution.py:202
  48.4 49.3 %collective-permute-start.1 = (bf16[3,256,512]{2,1,0:T(8,128)(2,1)}, bf16[3,256,512]{2,1,0:T(8,128)(2,1)}, u32[]{:S(2)}, u32[]{:S(2)}) collective-permute-start(bf16[3,256,512]{2,1,0:T(8,128)(2,1)} %get-tuple-element.16), channel_id=1, source_target_pairs={{0,224},{4,228},{8,232},{12,236},{16,240},{20,244},{24,248},{28,25... | collective-permute-start | bytes 2359304 | tf_op jit(solution)/shard_map/ppermute | solution.py:202
  52.3 30.3 %collective-permute-start.2 = (bf16[256,768]{1,0:T(8,128)(2,1)S(1)}, bf16[256,768]{1,0:T(8,128)(2,1)S(1)}, u32[]{:S(2)}, u32[]{:S(2)}) collective-permute-start(bf16[256,768]{1,0:T(8,128)(2,1)S(1)} %after.6), channel_id=1, source_target_pairs={{0,4},{4,8},{8,12},{12,16},{16,20},{20,24},{24,28},{28,32},{32,36}... | collective-permute-start | bytes 1179656 | tf_op jit(solution)/shard_map/ppermute | solution.py:202
  53.8 28.8 %collective-permute-start.3 = (bf16[256,768]{1,0:T(8,128)(2,1)S(1)}, bf16[256,768]{1,0:T(8,128)(2,1)S(1)}, u32[]{:S(2)}, u32[]{:S(2)}) collective-permute-start(bf16[256,768]{1,0:T(8,128)(2,1)S(1)} %after.6), channel_id=1, source_target_pairs={{0,252},{4,0},{8,4},{12,8},{16,12},{20,16},{24,20},{28,24},{32,28}... | collective-permute-start | bytes 1179656 | tf_op jit(solution)/shard_map/ppermute | solution.py:202
  82.6 1.0 copy-start.1
  83.5 0.7 copy-start.2
  84.2 28.7 %collective-permute-start.5 = (bf16[256,512]{1,0:T(8,128)(2,1)}, bf16[256,512]{1,0:T(8,128)(2,1)S(1)}, u32[]{:S(2)}, u32[]{:S(2)}) collective-permute-start(bf16[256,512]{1,0:T(8,128)(2,1)} %copy-done.2), channel_id=1, source_target_pairs={{0,8},{4,12},{8,16},{12,20},{16,24},{20,28},{24,32},{28,36},{32,40... | collective-permute-start | bytes 786440 | tf_op jit(solution)/shard_map/ppermute | solution.py:202
  84.2 28.7 %collective-permute-start.6 = (bf16[256,512]{1,0:T(8,128)(2,1)}, bf16[256,512]{1,0:T(8,128)(2,1)S(1)}, u32[]{:S(2)}, u32[]{:S(2)}) collective-permute-start(bf16[256,512]{1,0:T(8,128)(2,1)} %copy-done.2), channel_id=1, source_target_pairs={{0,248},{4,252},{8,0},{12,4},{16,8},{20,12},{24,16},{28,20},{32,24... | collective-permute-start | bytes 786440 | tf_op jit(solution)/shard_map/ppermute | solution.py:202
  91.7 21.2 %copy-start.3 = (bf16[256,512]{1,0:T(8,128)(2,1)S(1)}, bf16[256,512]{1,0:T(8,128)(2,1)}, u32[]{:S(2)}) copy-start(bf16[256,512]{1,0:T(8,128)(2,1)} %copy-done.2) | copy-start | bytes 786436
  91.7 21.3 %copy-start.5 = (bf16[256,256]{1,0:T(8,128)(2,1)S(1)}, bf16[256,256]{1,0:T(8,128)(2,1)}, u32[]{:S(2)}) copy-start(bf16[256,256]{1,0:T(8,128)(2,1)} %copy-done.4) | copy-start | bytes 393220
  91.7 21.2 %collective-permute-start.4 = (bf16[256,512]{1,0:T(8,128)(2,1)S(1)}, bf16[256,512]{1,0:T(8,128)(2,1)S(1)}, u32[]{:S(2)}, u32[]{:S(2)}) collective-permute-start(bf16[256,512]{1,0:T(8,128)(2,1)S(1)} %after.7), channel_id=1, source_target_pairs={{0,12},{4,16},{8,20},{12,24},{16,28},{20,32},{24,36},{28,40},{32,4... | collective-permute-start | bytes 786440 | tf_op jit(solution)/shard_map/ppermute | solution.py:202
  91.7 21.2 %collective-permute-start.7 = (bf16[256,512]{1,0:T(8,128)(2,1)S(1)}, bf16[256,512]{1,0:T(8,128)(2,1)S(1)}, u32[]{:S(2)}, u32[]{:S(2)}) collective-permute-start(bf16[256,512]{1,0:T(8,128)(2,1)S(1)} %after.7), channel_id=1, source_target_pairs={{0,244},{4,248},{8,252},{12,0},{16,4},{20,8},{24,12},{28,16},{32,2... | collective-permute-start | bytes 786440 | tf_op jit(solution)/shard_map/ppermute | solution.py:202
  97.7 15.2 %collective-permute-start.8 = (bf16[256,512]{1,0:T(8,128)(2,1)}, bf16[256,512]{1,0:T(8,128)(2,1)S(1)}, u32[]{:S(2)}, u32[]{:S(2)}) collective-permute-start(bf16[256,512]{1,0:T(8,128)(2,1)} %copy-done.2), channel_id=1, source_target_pairs={{0,240},{4,20},{8,248},{12,28},{16,0},{20,36},{24,8},{28,44},{32,1... | collective-permute-start | bytes 786440 | tf_op jit(solution)/shard_map/ppermute | solution.py:241
  117.1 18.7 %all-to-all-start.2 = ((bf16[8,256,256]{2,1,0:T(8,128)(2,1)}), bf16[8,256,256]{2,1,0:T(8,128)(2,1)S(1)}, u32[]{:S(2)}, u32[]{:S(2)}) async-start(bf16[8,256,256]{2,1,0:T(8,128)(2,1)} %after.9), calls=%async_computation.2 | async-start | bytes 2097152 | tf_op jit(solution)/shard_map/all_to_all | solution.py:208
  121.4 14.4 %collective-permute-start.9 = (bf16[256,256]{1,0:T(8,128)(2,1)S(1)}, bf16[256,256]{1,0:T(8,128)(2,1)S(1)}, u32[]{:S(2)}, u32[]{:S(2)}) collective-permute-start(bf16[256,256]{1,0:T(8,128)(2,1)S(1)} %get-tuple-element.14.refs_1_), channel_id=1, source_target_pairs={{0,4},{4,0},{8,12},{12,8},{16,20},{20,16},{24,28},{28,24},{32,36},... | collective-permute-start | bytes 393224 | tf_op jit(solution)/shard_map/ppermute | solution.py:205

commit v5 on v3

--- a/solution.py
+++ b/solution.py
@@ -13,6 +13,10 @@
 WIN = 14
 PLANE = 8
 CHUNKS = 2 * REACH + 1
+EXTRA = 8
+KV = 4 * HEAD_DIM
+ALL = 6 * HEAD_DIM
+CROSSING = (((7, 2), (6, 0), (5, 1)), ((7, 3), (6, 1), (5, 0)), ((7, 0),), ((7, 1),))
 NEG = -1.0e30
 LOG2E = 1.4426950408889634
 SCALE = HEAD_DIM ** -0.5
@@ -37,20 +41,43 @@
     return pl.ds(n * HEAD_DIM, HEAD_DIM)
 
 
-def cut_keys_kernel(k, kt, v, vt, out, sem):
-    run_copies([(ref.at[:, lanes(j)], out.at[j, :, lanes(n)])
-                for j in range(PLANE) for n, ref in enumerate((k, kt, v, vt))], sem)
-
-
-def cut_rest_kernel(row_ref, sel, q, qt, k, kt, v, vt, q_out, same, opp, sem):
-    pairs = [(ref.at[:, lanes(j)], q_out.at[j, 0:TOK, lanes(n)]) for j in range(PLANE) for n, ref in enumerate((qt, q))]
-    par = row_ref[0] % 2
-    for which, target in ((par, same), (1 - par, opp)):
-        cols = pl.ds(pl.multiple_of((PLANE + which) * HEAD_DIM, HEAD_DIM), HEAD_DIM)
-        pairs += [(ref.at[:, cols], target.at[:, lanes(n)]) for n, ref in enumerate((k, kt, v, vt, qt, q))]
+def cut_plane_kernel(sel, q, qt, k, kt, v, vt, out, buf, in_sem, out_sem):
+    arrays = (k, kt, v, vt, qt, q)
+    ins = [[pltpu.make_async_copy(ref.at[:, lanes(j)], buf.at[j, 0:TOK, lanes(n)], in_sem.at[j, n])
+            for n, ref in enumerate(arrays)] for j in range(PLANE)]
+    outs = [pltpu.make_async_copy(buf.at[j], out.at[j], out_sem.at[j]) for j in range(PLANE)]
+    for chunk in ins:
+        for copy in chunk:
+            copy.start()
     for j in range(PLANE):
-        q_out[j, TOK:, :] = sel[...]
-    run_copies(pairs, sem)
+        buf[j, TOK:, :] = sel[...]
+        for copy in ins[j]:
+            copy.wait()
+        outs[j].start()
+    for copy in outs:
+        copy.wait()
+
+
+def cut_pair_kernel(row_ref, q, qt, k, kt, v, vt, rest, first, second, q_same, q_opp, buf, in_sem, out_sem):
+    arrays = (k, kt, v, vt, qt, q)
+    ins = [pltpu.make_async_copy(ref.at[:, lanes(PLANE + h)], buf.at[h, :, lanes(n)], in_sem.at[h, n])
+           for h in range(2) for n, ref in enumerate(arrays)]
+    outs = [pltpu.make_async_copy(buf.at[j % 2, :, 0:KV], rest.at[j], out_sem.at[j]) for j in range(PLANE)]
+    for copy in ins:
+        copy.start()
+    for copy in ins:
+        copy.wait()
+    for copy in outs:
+        copy.start()
+    row = row_ref[0]
+    par = row % 2
+    bit = jnp.where(jnp.logical_or(row < 2, row == 5), 1, 0)
+    first[...] = buf[bit, :, :KV]
+    second[...] = buf[1 - bit, :, :KV]
+    q_same[...] = buf[par, :, KV:]
+    q_opp[...] = buf[1 - par, :, KV:]
+    for copy in outs:
+        copy.wait()
 
 
 def weigh(sel_ref, row, first, count, chunk, qcat, floor, s_scr, p_scr, t_scr):
@@ -95,15 +122,17 @@
     return first, second
 
 
-def inner_kernel(sel_ref, q_ref, main, gate, o_ref, stats, first_ref, second_ref, s_scr, p_scr, t_scr):
-    del gate
+def inner_kernel(sel_ref, main, o_ref, stats, first_ref, second_ref, vv, s_scr, p_scr, t_scr):
+    for c in range(PLANE):
+        vv[c * TOK:(c + 1) * TOK, :] = main[c, :TOK, 2 * HEAD_DIM:KV]
 
     def position(i, count, final):
-        base = pl.multiple_of(jnp.maximum(i - REACH, 0) * TOK, TOK)
+        begin = jnp.maximum(i - REACH, 0)
+        base = pl.multiple_of(begin * TOK, TOK)
         top, total, tangent_total = weigh(
-            sel_ref, i, jnp.maximum(REACH - i, 0), count,
-            lambda u: main[pl.ds(base + u * TOK, TOK), :2 * HEAD_DIM], q_ref[i, :TOK, :], None, s_scr, p_scr, t_scr)
-        first, second = mix(p_scr, t_scr, count * TOK, main[pl.ds(base, count * TOK), 2 * HEAD_DIM:])
+            sel_ref, i, jnp.maximum(REACH - i, 0), count, lambda u: main[begin + u, :TOK, :2 * HEAD_DIM],
+            main[i, :TOK, KV:], None, s_scr, p_scr, t_scr)
+        first, second = mix(p_scr, t_scr, count * TOK, vv[pl.ds(base, count * TOK), :])
         if final:
             o_ref[i - REACH] = finish(total, tangent_total, first, second)
         else:
@@ -121,8 +150,7 @@
     lax.fori_loop(0, 2, step, 0)
 
 
-def outer_kernel(sel_ref, q_ref, up, dn, mid, stats, first_ref, second_ref, gate_a, gate_b, o_ref, s_scr, p_scr, t_scr):
-    del gate_a, gate_b
+def outer_kernel(sel_ref, main, up, dn, mid, stats, first_ref, second_ref, o_ref, s_scr, p_scr, t_scr):
     for i in (3, 4):
         o_ref[i] = mid[i - REACH]
     for i in (0, 1, 2, 5, 6, 7):
@@ -131,7 +159,7 @@
         count = REACH - i if low else i - REACH - 1
         before = stats[i, 0][:, :1]
         top, total, tangent_total = weigh(
-            sel_ref, i, at, count, lambda u: halo[skip + u, :, :2 * HEAD_DIM], q_ref[i, :TOK, :], before,
+            sel_ref, i, at, count, lambda u: halo[skip + u, :, :2 * HEAD_DIM], main[i, :TOK, KV:], before,
             s_scr, p_scr, t_scr)
         shrink = jnp.exp2(before - top)
         first, second = first_ref[i] * shrink, second_ref[i] * shrink
@@ -142,28 +170,50 @@
         o_ref[i] = finish(stats[i, 1] * shrink + total, stats[i, 2] * shrink + tangent_total, first, second)
 
 
-def join_kernel(row_ref, same, other, gate, both, even, odd):
-    del gate
-    par = row_ref[0] % 2
-    both[par] = same[:, :4 * HEAD_DIM]
-    both[1 - par] = other[:, :4 * HEAD_DIM]
-    even[...] = both[0]
-    odd[...] = both[1]
-
-
-def pair_kernel(row_ref, sel_ref, same, other, a4, a2, both, b2, b4, o_own, o_other, kv, s_scr, p_scr, t_scr):
+def crossing_places():
+    unused = PLANE + 2 * REACH
+    tables = []
+    for pairs in CROSSING:
+        table = [unused] * PLANE
+        for source, target in pairs:
+            table[target] = source - (PLANE - REACH)
+            table[PLANE - 1 - target] = PLANE + REACH + PLANE - 1 - source
+        tables.append(table)
+    return tables
+
+
+def pair_kernel(row_ref, sel_ref, q_own, q_other, main, c0, c1, c2, c3, o_own, o_other, kv, s_scr, p_scr, t_scr):
     row = row_ref[0]
-    par = row % 2
-    places = [a4] + [ref.at[n] for ref in (a2, both, b2) for n in range(2)] + [b4]
-    for n, ref in enumerate(places):
-        kv[n * TOK:(n + 1) * TOK, :] = ref[...]
-    for ref, at, place, o_ref in ((same, row, par, o_own), (other, row + 1 - 2 * par, 1 - par, o_other)):
-        base = pl.multiple_of(place * TOK, TOK)
+    for c in range(PLANE):
+        kv[(c + REACH) * TOK:(c + REACH + 1) * TOK, :] = main[c]
+    for ref, table in zip((c0, c1, c2, c3), crossing_places()):
+        place = jnp.int32(table[0])
+        for d in range(1, PLANE):
+            place = jnp.where(row == d, table[d], place)
+        kv[pl.ds(pl.multiple_of(place * TOK, TOK), TOK), :] = ref[...]
+    for ref, at, o_ref in ((q_own, row, o_own), (q_other, row + 1 - 2 * (row % 2), o_other)):
+        base = pl.multiple_of(at * TOK, TOK)
         _, total, tangent_total = weigh(
-            sel_ref, at, 0, CHUNKS, lambda u: kv[pl.ds(base + u * TOK, TOK), :2 * HEAD_DIM],
-            ref[:, 4 * HEAD_DIM:], None, s_scr, p_scr, t_scr)
+            sel_ref, at, 0, CHUNKS, lambda u: kv[pl.ds(base + u * TOK, TOK), :2 * HEAD_DIM], ref[...], None,
+            s_scr, p_scr, t_scr)
         first, second = mix(p_scr, t_scr, CHUNKS * TOK, kv[pl.ds(base, CHUNKS * TOK), 2 * HEAD_DIM:])
         o_ref[...] = finish(total, tangent_total, first, second)
+
+
+def after_kernel(*refs):
+    del refs
+
+
+def after(array, *others):
+    return pl.pallas_call(
+        after_kernel,
+        out_shape=pltpu.HBM(array.shape, array.dtype),
+        in_specs=[HBM_SPEC] + [ANY_SPEC] * len(others),
+        out_specs=HBM_SPEC,
+        input_output_aliases={0: 0},
+        compiler_params=params(1),
+        name="after",
+    )(pltpu.with_memory_space_constraint(array, pltpu.HBM), *others)
 
 
 def unpack_kernel(par_ref, mine, own, other, o_ref, t_ref):
@@ -215,79 +265,81 @@
     def swapped(array):
         return lax.ppermute(array, "ctx", [(i, i ^ 1) for i in range(devices)])
 
+    def cross(array, pairs):
+        last = PLANE - 1
+        moves = [(z * PLANE + a, (z * PLANE + PLANE + b) % devices) for z in range(devices // PLANE) for a, b in pairs]
+        moves += [(z * PLANE + last - a, (z * PLANE - PLANE + last - b) % devices)
+                  for z in range(devices // PLANE) for a, b in pairs]
+        return lax.ppermute(array, "ctx", moves)
+
     def exchange(array):
         return lax.all_to_all(array, "ctx", 0, 0, axis_index_groups=planes, tiled=True)
 
     wide = [pltpu.with_memory_space_constraint(array, pltpu.HBM) for array in
             (queries, query_tangents, keys, key_tangents, values, value_tangents)]
-    kv_out = pl.pallas_call(
-        cut_keys_kernel,
-        out_shape=bf16(PLANE, TOK, 512),
-        in_specs=[HBM_SPEC] * 4,
+    sel_rows = jnp.pad(selection.astype(jnp.bfloat16).reshape(1, 2 * WIN), ((0, EXTRA - 1), (0, ALL - 2 * WIN)))
+    plane_out = pl.pallas_call(
+        cut_plane_kernel,
+        out_shape=pltpu.HBM((PLANE, TOK + EXTRA, ALL), jnp.bfloat16),
+        in_specs=[VMEM_SPEC] + [HBM_SPEC] * 6,
         out_specs=ANY_SPEC,
-        scratch_shapes=[pltpu.SemaphoreType.DMA((4 * PLANE,))],
-        compiler_params=params(4),
-        name="cut_keys",
-    )(*wide[2:])
-    sel_rows = jnp.pad(selection.astype(jnp.bfloat16).reshape(1, 2 * WIN), ((0, 15), (0, 256 - 2 * WIN)))
-    q_out, same, opp = pl.pallas_call(
-        cut_rest_kernel,
-        out_shape=(bf16(PLANE, TOK + 16, 256), bf16(TOK, 768), bf16(TOK, 768)),
-        in_specs=[SMEM_SPEC, VMEM_SPEC] + [HBM_SPEC] * 6,
-        out_specs=(VMEM_SPEC,) * 3,
-        scratch_shapes=[pltpu.SemaphoreType.DMA((2 * PLANE + 12,))],
+        scratch_shapes=[pltpu.VMEM((PLANE, TOK + EXTRA, ALL), jnp.bfloat16),
+                        pltpu.SemaphoreType.DMA((PLANE, 6)), pltpu.SemaphoreType.DMA((PLANE,))],
         compiler_params=params(8),
-        name="cut_rest",
-    )(row, sel_rows, *wide)
-
-    other = swapped(opp)
-    main = exchange(kv_out)
-    up, dn = send(main[PLANE - REACH:], PLANE), send(main[:REACH], -PLANE)
-    q_all = exchange(q_out)
-    sel_all = q_all[:, TOK, :2 * WIN].astype(jnp.int32)
-
-    both, even, odd = pl.pallas_call(
-        join_kernel,
-        out_shape=(bf16(2, TOK, 512), bf16(TOK, 512), bf16(TOK, 512)),
-        in_specs=[SMEM_SPEC] + [VMEM_SPEC] * 2 + [ANY_SPEC],
-        out_specs=(VMEM_SPEC,) * 3,
-        compiler_params=params(4),
-        name="join",
-    )(row, same, other, q_all)
-    a2, b2, a4, b4 = send(both, 2), send(both, -2), send(odd, 4), send(even, -4)
+        name="cut_plane",
+    )(sel_rows, *wide)
+    rest_out, first_out, second_out, q_same, q_opp = pl.pallas_call(
+        cut_pair_kernel,
+        out_shape=(pltpu.HBM((PLANE, TOK, KV), jnp.bfloat16), bf16(TOK, KV), bf16(TOK, KV), bf16(TOK, 256), bf16(TOK, 256)),
+        in_specs=[SMEM_SPEC] + [HBM_SPEC] * 6,
+        out_specs=(ANY_SPEC,) + (VMEM_SPEC,) * 4,
+        scratch_shapes=[pltpu.VMEM((2, TOK, ALL), jnp.bfloat16),
+                        pltpu.SemaphoreType.DMA((2, 6)), pltpu.SemaphoreType.DMA((PLANE,))],
+        compiler_params=params(8),
+        name="cut_pair",
+    )(row, *wide)
+
+    crossed = [cross(array, pairs) for array, pairs in zip((first_out, second_out) * 2, CROSSING)]
+    q_other = swapped(q_opp)
+
+    main = exchange(plane_out)
+    sel_all = main[:, TOK, :2 * WIN].astype(jnp.int32)
+    edge_up, edge_dn = main[PLANE - REACH:, :TOK, :KV], main[:REACH, :TOK, :KV]
+    up, dn = send(edge_up, PLANE), send(edge_dn, -PLANE)
+    rest = exchange(after(rest_out, sel_all, q_other, *crossed))
 
     mid, stats, first, second = pl.pallas_call(
         inner_kernel,
         out_shape=(bf16(2, TOK, 256), f32(PLANE, 3, TOK, BLK), f32(PLANE, TOK, 256), f32(PLANE, TOK, BLK)),
-        in_specs=[SMEM_SPEC] + [VMEM_SPEC] * 2 + [ANY_SPEC],
+        in_specs=[SMEM_SPEC, VMEM_SPEC],
         out_specs=(VMEM_SPEC,) * 4,
-        scratch_shapes=scratch(CHUNKS),
-        compiler_params=params(20),
+        scratch_shapes=[pltpu.VMEM((PLANE * TOK, 2 * HEAD_DIM), jnp.bfloat16)] + scratch(CHUNKS),
+        compiler_params=params(16),
         cost_estimate=cost(44),
         name="inner",
-    )(sel_all, q_all, main.reshape(PLANE * TOK, 512), both)
+    )(sel_all, main)
     mine = pl.pallas_call(
         outer_kernel,
         out_shape=bf16(PLANE, TOK, 256),
-        in_specs=[SMEM_SPEC] + [VMEM_SPEC] * 7 + [ANY_SPEC] * 2,
+        in_specs=[SMEM_SPEC] + [VMEM_SPEC] * 7,
         out_specs=VMEM_SPEC,
         scratch_shapes=scratch(REACH),
-        compiler_params=params(20),
+        compiler_params=params(16),
         cost_estimate=cost(12),
         name="outer",
-    )(sel_all, q_all, up, dn, mid, stats, first, second, a2, b2)
-    back = exchange(mine)
+    )(sel_all, main, up, dn, mid, stats, first, second)
+    back = exchange(after(mine, rest))
 
     own, lent = pl.pallas_call(
         pair_kernel,
         out_shape=(bf16(TOK, 256), bf16(TOK, 256)),
         in_specs=[SMEM_SPEC] * 2 + [VMEM_SPEC] * 7,
         out_specs=(VMEM_SPEC,) * 2,
-        scratch_shapes=[pltpu.VMEM((8 * TOK, 512), jnp.bfloat16)] + scratch(CHUNKS),
-        compiler_params=params(12),
+        scratch_shapes=[pltpu.VMEM(((PLANE + 2 * REACH + 1) * TOK, KV), jnp.bfloat16)] + scratch(CHUNKS),
+        compiler_params=params(14),
         cost_estimate=cost(14),
         name="pair",
-    )(row, sel_all, same, other, a4, a2, both, b2, b4)
+    )(row, sel_all, q_same, q_other, rest, *crossed)
     partner = swapped(lent)
 
     return pl.pallas_call(

time: 210 us -> 134 us (0.64)
  Pallas kernels: 86.7 us -> 27.6 us
  waiting for transfers between devices: 63.9 us -> 51.1 us
  local copies, waits for them, and re-layouts: 11 us -> 1.85 us
  starting transfers between devices: 46 us -> 50.2 us
    pallas_call x3 -> x4, Pallas kernels: 66.8 us -> 6.94 us  [the longest x1 3.47 us: body(): pl.pallas_call(cut_pair_kernel, out_shape=(pltpu.HBM((PLANE, TOK, KV), jn...]
    ppermute x0 -> x4, starting transfers between devices: none -> 25 us  [cross(): return lax.ppermute(array, 'ctx', moves)]
    ppermute x6 -> x2, starting transfers between devices: 25.4 us -> 4.78 us  [send(): lax.ppermute(array, 'ctx', [(i, (i + by) % devices) for i in range(device...]
    ppermute x6 -> x2, waiting for transfers between devices: 25.7 us -> 6.8 us  [send(): lax.ppermute(array, 'ctx', [(i, (i + by) % devices) for i in range(device...]
    all_to_all x3, waiting for transfers between devices: 21.8 us -> 36 us  [exchange(): lax.all_to_all(array, 'ctx', 0, 0, axis_index_groups=planes, tiled=True)]
    ppermute x2, waiting for transfers between devices: 16.4 us -> 8.3 us  [swapped(): return lax.ppermute(array, 'ctx', [(i, i ^ 1) for i in range(devices)])]
    unnamed x34 -> x6, local copies, waits for them, and re-layouts: 9.61 us -> 1.62 us
  transfers between devices with their start and end apart: 11 -> 11, of which waited for: 7 -> 3; matrix products, arithmetic and copies ran while one was open for 1% -> 0% of each run, Pallas kernels for 7% -> 16%
where the time goes in v5:
time: 134 us; the launch traced here: 132 us
  waiting for transfers between devices  51.1 us (38%)
  starting transfers between devices  50.2 us (37%)
  Pallas kernels  27.6 us (21%)
  local copies, waits for them, and re-layouts  1.85 us (1%)
    all_to_all x3, waiting for transfers between devices, exchange(): lax.all_to_all(array, 'ctx', 0, 0, axis_index_groups=planes, tiled=True)  36 us
    ppermute x4, starting transfers between devices, cross(): return lax.ppermute(array, 'ctx', moves)  25 us
    all_to_all x3, starting transfers between devices, exchange(): lax.all_to_all(array, 'ctx', 0, 0, axis_index_groups=planes, tiled=True)  18.9 us
    pallas_call x1, Pallas kernels, body(): pl.pallas_call(inner_kernel, out_shape=(bf16(2, TOK, 256), f32(PLANE, 3,...  9.19 us
    ppermute x2, waiting for transfers between devices, swapped(): return lax.ppermute(array, 'ctx', [(i, i ^ 1) for i in range(devices)])  8.3 us
    ppermute x2, waiting for transfers between devices, send(): lax.ppermute(array, 'ctx', [(i, (i + by) % devices) for i in range(device...  6.8 us
    ppermute x2, starting transfers between devices, send(): lax.ppermute(array, 'ctx', [(i, (i + by) % devices) for i in range(device...  4.78 us
    pallas_call x1, Pallas kernels, body(): pl.pallas_call(pair_kernel, out_shape=(bf16(TOK, 256), bf16(TOK, 256)), i...  4.69 us
  transfers between devices with their start and end apart: 11, of which 3 were waited for; matrix products, arithmetic and copies ran while one was open for 0% of the time, Pallas kernels for 16%

profile of v5, /device:TPU:1, one launch (start us, length us, event | category | flops | bytes accessed | tf_op | source)
XLA Modules:
  0.0 132.3 jit_solution(1619685689848319055)
XLA Ops:
  0.6 0.7 convert_element_type.10
  1.3 0.1 reshape.9
  1.4 3.5 %cut_plane.1 = bf16[8,264,768]{2,1,0:T(8,128)(2,1)} custom-call(bf16[8,768]{1,0:T(8,128)(2,1)S(1)} %pad.4.sel, bf16[256,1280]{1,0:T(8,128)(2,1)} %q.3, bf16[256,1280]{1,0:T(8,128)(2,1)} %qt.3, bf16[256,1280]{1,0:T(8,128)(2,1)} %k.3, bf16[256,1280]{1,0:T(8,128)(2,1)} %kt.3, bf16[256,1280]{1,0:T(8,128)(2,1)} %v.3, bf16[256,1280]{1,0:T(8,128)(2,1)} %vt.3), custom_call_target="tpu_custom_call" | custom-call | tf_op jit(solution)/shard_map/cut_plane/pallas_call | solution.py:281
  4.9 7.5 %all-to-all-start = ((bf16[8,264,768]{2,1,0:T(8,128)(2,1)}), bf16[8,264,768]{2,1,0:T(8,128)(2,1)S(1)}, u32[]{:S(2)}, u32[]{:S(2)}) async-start(bf16[8,264,768]{2,1,0:T(8,128)(2,1)} %cut_plane.1), calls=%async_computation | async-start | bytes 6488064 | tf_op jit(solution)/shard_map/all_to_all | solution.py:276
  12.4 3.5 %cut_pair.1 = (bf16[8,256,512]{2,1,0:T(8,128)(2,1)}, bf16[256,512]{1,0:T(8,128)(2,1)}, bf16[256,512]{1,0:T(8,128)(2,1)}, bf16[256,256]{1,0:T(8,128)(2,1)S(1)}, bf16[256,256]{1,0:T(8,128)(2,1)}) custom-call(s32[1]{0:T(128)} %bitcast.row_ref.par_ref, bf16[256,1280]{1,0:T(8,128)(2,1)} %q.3, bf16[256,1280]{1,0:T(8,128)(2,1)} %qt.3, bf16[256,1280]{1,0:T(8,128)(2,1)} %k.3, ...), custom_call_target="tpu_custom_call" | custom-call | tf_op jit(solution)/shard_map/cut_pair/pallas_call | solution.py:291
  15.9 0.0 copy-start.1
  15.9 0.6 copy-done.1
  16.5 11.1 %collective-permute-start.3 = (bf16[256,512]{1,0:T(8,128)(2,1)}, bf16[256,512]{1,0:T(8,128)(2,1)S(1)}, u32[]{:S(2)}, u32[]{:S(2)}) collective-permute-start(bf16[256,512]{1,0:T(8,128)(2,1)} %get-tuple-element.19), channel_id=1, source_target_pairs={{28,40},{24,32},{20,36},{60,72},{56,64},{52,68},{92,104},{88,96},{... | collective-permute-start | bytes 786440 | tf_op jit(solution)/shard_map/ppermute | solution.py:273
  27.6 1.9 %collective-permute-start.4 = (bf16[256,512]{1,0:T(8,128)(2,1)}, bf16[256,512]{1,0:T(8,128)(2,1)}, u32[]{:S(2)}, u32[]{:S(2)}) collective-permute-start(bf16[256,512]{1,0:T(8,128)(2,1)} %get-tuple-element.20), channel_id=1, source_target_pairs={{28,44},{24,36},{20,32},{60,76},{56,68},{52,64},{92,108},{88,100},... | collective-permute-start | bytes 786440 | tf_op jit(solution)/shard_map/ppermute | solution.py:273
  29.5 3.1 %collective-permute-start.5 = (bf16[256,512]{1,0:T(8,128)(2,1)}, bf16[256,512]{1,0:T(8,128)(2,1)}, u32[]{:S(2)}, u32[]{:S(2)}) collective-permute-start(bf16[256,512]{1,0:T(8,128)(2,1)} %get-tuple-element.19), channel_id=1, source_target_pairs={{28,32},{60,64},{92,96},{124,128},{156,160},{188,192},{220,224},{2... | collective-permute-start | bytes 786440 | tf_op jit(solution)/shard_map/ppermute | solution.py:273
  32.6 8.9 %collective-permute-start.6 = (bf16[256,512]{1,0:T(8,128)(2,1)}, bf16[256,512]{1,0:T(8,128)(2,1)}, u32[]{:S(2)}, u32[]{:S(2)}) collective-permute-start(bf16[256,512]{1,0:T(8,128)(2,1)} %get-tuple-element.20), channel_id=1, source_target_pairs={{28,36},{60,68},{92,100},{124,132},{156,164},{188,196},{220,228},{... | collective-permute-start | bytes 786440 | tf_op jit(solution)/shard_map/ppermute | solution.py:273
  41.5 0.0 collective-permute-start.2
  41.5 36.0 %all-to-all-done.main = bf16[8,264,768]{2,1,0:T(8,128)(2,1)S(1)} async-done(((bf16[8,264,768]{2,1,0:T(8,128)(2,1)}), bf16[8,264,768]{2,1,0:T(8,128)(2,1)S(1)}, u32[]{:S(2)}, u32[]{:S(2)}) %all-to-all-start) | async-done | bytes 3244064 | tf_op jit(solution)/shard_map/all_to_all | solution.py:276
  77.6 0.0 collective-permute-done.2.refs_2_.q_other
  77.6 0.0 collective-permute-done.3.refs_3_.c0
  77.6 0.0 collective-permute-done.4.refs_4_.c1
  77.6 0.0 collective-permute-done.5.refs_5_.c2
  77.6 0.0 collective-permute-done.6.refs_6_.c3
  77.6 4.9 %all-to-all-start.1 = ((bf16[8,256,512]{2,1,0:T(8,128)(2,1)}), bf16[8,256,512]{2,1,0:T(8,128)(2,1)}, u32[]{:S(2)}, u32[]{:S(2)}) async-start(bf16[8,256,512]{2,1,0:T(8,128)(2,1)} %after.2), calls=%async_computation.1 | async-start | bytes 4194304 | tf_op jit(solution)/shard_map/all_to_all | solution.py:276
  82.5 0.1 fusion.1
  82.6 1.7 %collective-permute-start = (bf16[3,256,512]{2,1,0:T(8,128)(2,1)S(1)}, bf16[3,256,512]{2,1,0:T(8,128)(2,1)S(1)}, u32[]{:S(2)}, u32[]{:S(2)}) collective-permute-start(bf16[3,256,512]{2,1,0:T(8,128)(2,1)S(1)} %get-tuple-element.25), channel_id=1, source_target_pairs={{0,32},{4,36},{8,40},{12,44},{16,48},{20,52},{24,56},{28,60},{32,6... | collective-permute-start | bytes 2359304 | tf_op jit(solution)/shard_map/ppermute | solution.py:263
  84.4 3.1 %collective-permute-start.1 = (bf16[3,256,512]{2,1,0:T(8,128)(2,1)S(1)}, bf16[3,256,512]{2,1,0:T(8,128)(2,1)S(1)}, u32[]{:S(2)}, u32[]{:S(2)}) collective-permute-start(bf16[3,256,512]{2,1,0:T(8,128)(2,1)S(1)} %get-tuple-element.24), channel_id=1, source_target_pairs={{0,224},{4,228},{8,232},{12,236},{16,240},{20,244},{24,248},{28,25... | collective-permute-start | bytes 2359304 | tf_op jit(solution)/shard_map/ppermute | solution.py:263
  87.4 9.2 %inner.1 = (bf16[2,256,256]{2,1,0:T(8,128)(2,1)S(1)}, f32[8,3,256,128]{3,2,1,0:T(8,128)S(1)}, f32[8,256,256]{2,1,0:T(8,128)S(1)}, f32[8,256,128]{2,1,0:T(8,128)S(1)}) custom-call(s32[8,28]{1,0:T(8,128)S(1)} %fusion.sel_ref.refs_1_, bf16[8,264,768]{2,1,0:T(8,128)(2,1)S(1)} %all-to-all-done.main), custom_call_target="tpu_custom_call" | custom-call | flops 3690987520 | bytes 11534336 | tf_op jit(solution)/shard_map/inner/pallas_call | solution.py:311
  96.6 6.8 %collective-permute-done.up = bf16[3,256,512]{2,1,0:T(8,128)(2,1)S(1)} collective-permute-done((bf16[3,256,512]{2,1,0:T(8,128)(2,1)S(1)}, bf16[3,256,512]{2,1,0:T(8,128)(2,1)S(1)}, u32[]{:S(2)}, u32[]{:S(2)}) %collective-permute-start) | collective-permute-done | bytes 786464 | tf_op jit(solution)/shard_map/ppermute | solution.py:263
  103.4 0.0 collective-permute-done.1.dn
  103.4 4.3 %outer.1.refs_0_ = bf16[8,256,256]{2,1,0:T(8,128)(2,1)S(1)} custom-call(s32[8,28]{1,0:T(8,128)S(1)} %fusion.sel_ref.refs_1_, bf16[8,264,768]{2,1,0:T(8,128)(2,1)S(1)} %all-to-all-done.main, bf16[3,256,512]{2,1,0:T(8,128)(2,1)S(1)} %collective-permute-done.up, bf16[3,256,512]{2,1,0:T(8,128)(2,1)S(1)} %collective-permute-done.1.dn, ...), custom_call_target="tpu_custom_call" | custom-call | flops 1006632960 | bytes 3145728 | tf_op jit(solution)/shard_map/outer/pallas_call | solution.py:321
  107.7 0.0 copy-start
  107.7 1.0 copy-done
  108.7 0.0 copy-start.2
  108.7 0.0 all-to-all-done.1.refs_1_.main
  108.7 6.5 %all-to-all-start.2 = ((bf16[8,256,256]{2,1,0:T(8,128)(2,1)}), bf16[8,256,256]{2,1,0:T(8,128)(2,1)}, u32[]{:S(2)}, u32[]{:S(2)}) async-start(bf16[8,256,256]{2,1,0:T(8,128)(2,1)} %after.3), calls=%async_computation.2 | async-start | bytes 2097152 | tf_op jit(solution)/shard_map/all_to_all | solution.py:276
  115.2 0.0 copy-done.2
  115.2 4.7 %pair.1 = (bf16[256,256]{1,0:T(8,128)(2,1)S(1)}, bf16[256,256]{1,0:T(8,128)(2,1)S(1)}) custom-call(s32[1]{0:T(128)} %bitcast.row_ref.par_ref, s32[8,28]{1,0:T(8,128)S(1)} %fusion.sel_ref.refs_1_, bf16[256,256]{1,0:T(8,128)(2,1)S(1)} %copy-done.2, bf16[256,256]{1,0:T(8,128)(2,1)} %collective-permute-done.2.refs_2_.q_other, ...), custom_call_target="tpu_custom_call" | custom-call | flops 1174405120 | bytes 3670016 | tf_op jit(solution)/shard_map/pair/pallas_call | solution.py:333
  119.9 1.5 %collective-permute-start.7 = (bf16[256,256]{1,0:T(8,128)(2,1)S(1)}, bf16[256,256]{1,0:T(8,128)(2,1)S(1)}, u32[]{:S(2)}, u32[]{:S(2)}) collective-permute-start(bf16[256,256]{1,0:T(8,128)(2,1)S(1)} %get-tuple-element.23), channel_id=1, source_target_pairs={{0,4},{4,0},{8,12},{12,8},{16,20},{20,16},{24,28},{28,24},{32,36},... | collective-permute-start | bytes 393224 | tf_op jit(solution)/shard_map/ppermute | solution.py:266
  121.5 8.3 %collective-permute-done.7.other = bf16[256,256]{1,0:T(8,128)(2,1)S(1)} collective-permute-done((bf16[256,256]{1,0:T(8,128)(2,1)S(1)}, bf16[256,256]{1,0:T(8,128)(2,1)S(1)}, u32[]{:S(2)}, u32[]{:S(2)}) %collective-permute-start.7) | collective-permute-done | bytes 131104 | tf_op jit(solution)/shard_map/ppermute | solution.py:266
  129.8 0.0 all-to-all-done.2.mine
  129.8 2.5 %unpack.1 = (bf16[256,1280]{1,0:T(8,128)(2,1)}, bf16[256,1280]{1,0:T(8,128)(2,1)}) custom-call(s32[1]{0:T(128)} %bitcast.row_ref.par_ref, bf16[8,256,256]{2,1,0:T(8,128)(2,1)} %all-to-all-done.2.mine, bf16[256,256]{1,0:T(8,128)(2,1)S(1)} %get-tuple-element.22.own, bf16[256,256]{1,0:T(8,128)(2,1)S(1)} %collective-permute-done.7.other), custom_call_target="tpu_custom_call" | custom-call | tf_op jit(solution)/shard_map/unpack/pallas_call | solution.py:345
  (5 shorter events, 0.0 us)
Async XLA Ops:
  4.9 72.7 %all-to-all-start = ((bf16[8,264,768]{2,1,0:T(8,128)(2,1)}), bf16[8,264,768]{2,1,0:T(8,128)(2,1)S(1)}, u32[]{:S(2)}, u32[]{:S(2)}) async-start(bf16[8,264,768]{2,1,0:T(8,128)(2,1)} %cut_plane.1), calls=%async_computation | async-start | bytes 6488064 | tf_op jit(solution)/shard_map/all_to_all | solution.py:276
  15.9 0.6 copy-start.1
  16.5 61.1 %collective-permute-start.3 = (bf16[256,512]{1,0:T(8,128)(2,1)}, bf16[256,512]{1,0:T(8,128)(2,1)S(1)}, u32[]{:S(2)}, u32[]{:S(2)}) collective-permute-start(bf16[256,512]{1,0:T(8,128)(2,1)} %get-tuple-element.19), channel_id=1, source_target_pairs={{28,40},{24,32},{20,36},{60,72},{56,64},{52,68},{92,104},{88,96},{... | collective-permute-start | bytes 786440 | tf_op jit(solution)/shard_map/ppermute | solution.py:273
  27.6 50.0 %collective-permute-start.4 = (bf16[256,512]{1,0:T(8,128)(2,1)}, bf16[256,512]{1,0:T(8,128)(2,1)}, u32[]{:S(2)}, u32[]{:S(2)}) collective-permute-start(bf16[256,512]{1,0:T(8,128)(2,1)} %get-tuple-element.20), channel_id=1, source_target_pairs={{28,44},{24,36},{20,32},{60,76},{56,68},{52,64},{92,108},{88,100},... | collective-permute-start | bytes 786440 | tf_op jit(solution)/shard_map/ppermute | solution.py:273
  29.5 48.1 %collective-permute-start.5 = (bf16[256,512]{1,0:T(8,128)(2,1)}, bf16[256,512]{1,0:T(8,128)(2,1)}, u32[]{:S(2)}, u32[]{:S(2)}) collective-permute-start(bf16[256,512]{1,0:T(8,128)(2,1)} %get-tuple-element.19), channel_id=1, source_target_pairs={{28,32},{60,64},{92,96},{124,128},{156,160},{188,192},{220,224},{2... | collective-permute-start | bytes 786440 | tf_op jit(solution)/shard_map/ppermute | solution.py:273
  32.6 45.0 %collective-permute-start.6 = (bf16[256,512]{1,0:T(8,128)(2,1)}, bf16[256,512]{1,0:T(8,128)(2,1)}, u32[]{:S(2)}, u32[]{:S(2)}) collective-permute-start(bf16[256,512]{1,0:T(8,128)(2,1)} %get-tuple-element.20), channel_id=1, source_target_pairs={{28,36},{60,68},{92,100},{124,132},{156,164},{188,196},{220,228},{... | collective-permute-start | bytes 786440 | tf_op jit(solution)/shard_map/ppermute | solution.py:273
  41.5 36.0 %collective-permute-start.2 = (bf16[256,256]{1,0:T(8,128)(2,1)}, bf16[256,256]{1,0:T(8,128)(2,1)}, u32[]{:S(2)}, u32[]{:S(2)}) collective-permute-start(bf16[256,256]{1,0:T(8,128)(2,1)} %get-tuple-element.18), channel_id=1, source_target_pairs={{0,4},{4,0},{8,12},{12,8},{16,20},{20,16},{24,28},{28,24},{32,36},... | collective-permute-start | bytes 393224 | tf_op jit(solution)/shard_map/ppermute | solution.py:266
  77.6 31.1 %all-to-all-start.1 = ((bf16[8,256,512]{2,1,0:T(8,128)(2,1)}), bf16[8,256,512]{2,1,0:T(8,128)(2,1)}, u32[]{:S(2)}, u32[]{:S(2)}) async-start(bf16[8,256,512]{2,1,0:T(8,128)(2,1)} %after.2), calls=%async_computation.1 | async-start | bytes 4194304 | tf_op jit(solution)/shard_map/all_to_all | solution.py:276
  82.6 20.8 %collective-permute-start = (bf16[3,256,512]{2,1,0:T(8,128)(2,1)S(1)}, bf16[3,256,512]{2,1,0:T(8,128)(2,1)S(1)}, u32[]{:S(2)}, u32[]{:S(2)}) collective-permute-start(bf16[3,256,512]{2,1,0:T(8,128)(2,1)S(1)} %get-tuple-element.25), channel_id=1, source_target_pairs={{0,32},{4,36},{8,40},{12,44},{16,48},{20,52},{24,56},{28,60},{32,6... | collective-permute-start | bytes 2359304 | tf_op jit(solution)/shard_map/ppermute | solution.py:263
  84.4 19.1 %collective-permute-start.1 = (bf16[3,256,512]{2,1,0:T(8,128)(2,1)S(1)}, bf16[3,256,512]{2,1,0:T(8,128)(2,1)S(1)}, u32[]{:S(2)}, u32[]{:S(2)}) collective-permute-start(bf16[3,256,512]{2,1,0:T(8,128)(2,1)S(1)} %get-tuple-element.24), channel_id=1, source_target_pairs={{0,224},{4,228},{8,232},{12,236},{16,240},{20,244},{24,248},{28,25... | collective-permute-start | bytes 2359304 | tf_op jit(solution)/shard_map/ppermute | solution.py:263
  107.7 1.0 copy-start
  108.7 6.5 %copy-start.2 = (bf16[256,256]{1,0:T(8,128)(2,1)S(1)}, bf16[256,256]{1,0:T(8,128)(2,1)}, u32[]{:S(2)}) copy-start(bf16[256,256]{1,0:T(8,128)(2,1)} %copy-done.1) | copy-start | bytes 393220
  108.7 21.0 %all-to-all-start.2 = ((bf16[8,256,256]{2,1,0:T(8,128)(2,1)}), bf16[8,256,256]{2,1,0:T(8,128)(2,1)}, u32[]{:S(2)}, u32[]{:S(2)}) async-start(bf16[8,256,256]{2,1,0:T(8,128)(2,1)} %after.3), calls=%async_computation.2 | async-start | bytes 2097152 | tf_op jit(solution)/shard_map/all_to_all | solution.py:276
  119.9 9.8 %collective-permute-start.7 = (bf16[256,256]{1,0:T(8,128)(2,1)S(1)}, bf16[256,256]{1,0:T(8,128)(2,1)S(1)}, u32[]{:S(2)}, u32[]{:S(2)}) collective-permute-start(bf16[256,256]{1,0:T(8,128)(2,1)S(1)} %get-tuple-element.23), channel_id=1, source_target_pairs={{0,4},{4,0},{8,12},{12,8},{16,20},{20,16},{24,28},{28,24},{32,36},... | collective-permute-start | bytes 393224 | tf_op jit(solution)/shard_map/ppermute | solution.py:266

commit v6 on v5

--- a/solution.py
+++ b/solution.py
@@ -16,7 +16,6 @@
 EXTRA = 8
 KV = 4 * HEAD_DIM
 ALL = 6 * HEAD_DIM
-CROSSING = (((7, 2), (6, 0), (5, 1)), ((7, 3), (6, 1), (5, 0)), ((7, 0),), ((7, 1),))
 NEG = -1.0e30
 LOG2E = 1.4426950408889634
 SCALE = HEAD_DIM ** -0.5
@@ -58,7 +57,7 @@
         copy.wait()
 
 
-def cut_pair_kernel(row_ref, q, qt, k, kt, v, vt, rest, first, second, q_same, q_opp, buf, in_sem, out_sem):
+def cut_pair_kernel(row_ref, q, qt, k, kt, v, vt, rest, q_same, q_opp, buf, in_sem, out_sem):
     arrays = (k, kt, v, vt, qt, q)
     ins = [pltpu.make_async_copy(ref.at[:, lanes(PLANE + h)], buf.at[h, :, lanes(n)], in_sem.at[h, n])
            for h in range(2) for n, ref in enumerate(arrays)]
@@ -69,11 +68,7 @@
         copy.wait()
     for copy in outs:
         copy.start()
-    row = row_ref[0]
-    par = row % 2
-    bit = jnp.where(jnp.logical_or(row < 2, row == 5), 1, 0)
-    first[...] = buf[bit, :, :KV]
-    second[...] = buf[1 - bit, :, :KV]
+    par = row_ref[0] % 2
     q_same[...] = buf[par, :, KV:]
     q_opp[...] = buf[1 - par, :, KV:]
     for copy in outs:
@@ -150,7 +145,8 @@
     lax.fori_loop(0, 2, step, 0)
 
 
-def outer_kernel(sel_ref, main, up, dn, mid, stats, first_ref, second_ref, o_ref, s_scr, p_scr, t_scr):
+def outer_kernel(sel_ref, main, up, dn, mid, stats, first_ref, second_ref, o_ref, done, s_scr, p_scr, t_scr):
+    done[...] = jnp.zeros_like(done)
     for i in (3, 4):
         o_ref[i] = mid[i - REACH]
     for i in (0, 1, 2, 5, 6, 7):
@@ -170,28 +166,21 @@
         o_ref[i] = finish(stats[i, 1] * shrink + total, stats[i, 2] * shrink + tangent_total, first, second)
 
 
-def crossing_places():
-    unused = PLANE + 2 * REACH
-    tables = []
-    for pairs in CROSSING:
-        table = [unused] * PLANE
-        for source, target in pairs:
-            table[target] = source - (PLANE - REACH)
-            table[PLANE - 1 - target] = PLANE + REACH + PLANE - 1 - source
-        tables.append(table)
-    return tables
-
-
-def pair_kernel(row_ref, sel_ref, q_own, q_other, main, c0, c1, c2, c3, o_own, o_other, kv, s_scr, p_scr, t_scr):
-    row = row_ref[0]
+def edge_kernel(task_ref, main, gate, edge):
+    del gate
+    begin = jnp.where(task_ref[0] < PLANE // 2, PLANE - REACH, 0)
+    for n in range(REACH):
+        edge[n] = main[begin + n]
+
+
+def pair_kernel(task_ref, sel_ref, q_first, q_second, main, halo, o_first, o_second, kv, s_scr, p_scr, t_scr):
+    task = task_ref[0]
     for c in range(PLANE):
         kv[(c + REACH) * TOK:(c + REACH + 1) * TOK, :] = main[c]
-    for ref, table in zip((c0, c1, c2, c3), crossing_places()):
-        place = jnp.int32(table[0])
-        for d in range(1, PLANE):
-            place = jnp.where(row == d, table[d], place)
-        kv[pl.ds(pl.multiple_of(place * TOK, TOK), TOK), :] = ref[...]
-    for ref, at, o_ref in ((q_own, row, o_own), (q_other, row + 1 - 2 * (row % 2), o_other)):
+    begin = jnp.where(task < PLANE // 2, 0, REACH + PLANE)
+    for n in range(REACH):
+        kv[pl.ds(pl.multiple_of((begin + n) * TOK, TOK), TOK), :] = halo[n]
+    for ref, at, o_ref in ((q_first, task, o_first), (q_second, task + 1 - 2 * (task % 2), o_second)):
         base = pl.multiple_of(at * TOK, TOK)
         _, total, tangent_total = weigh(
             sel_ref, at, 0, CHUNKS, lambda u: kv[pl.ds(base + u * TOK, TOK), :2 * HEAD_DIM], ref[...], None,
@@ -256,21 +245,23 @@
 
 def body(queries, query_tangents, keys, key_tangents, values, value_tangents, selection):
     devices = lax.axis_size("ctx")
+    columns = lax.axis_size("head")
     row = (lax.axis_index("ctx") % PLANE).astype(jnp.int32)[None]
+    task = row ^ (4 * (lax.axis_index("head") % 2).astype(jnp.int32))
     planes = [[z * PLANE + i for i in range(PLANE)] for z in range(devices // PLANE)]
 
     def send(array, by):
         return lax.ppermute(array, "ctx", [(i, (i + by) % devices) for i in range(devices)])
 
-    def swapped(array):
-        return lax.ppermute(array, "ctx", [(i, i ^ 1) for i in range(devices)])
-
-    def cross(array, pairs):
-        last = PLANE - 1
-        moves = [(z * PLANE + a, (z * PLANE + PLANE + b) % devices) for z in range(devices // PLANE) for a, b in pairs]
-        moves += [(z * PLANE + last - a, (z * PLANE - PLANE + last - b) % devices)
-                  for z in range(devices // PLANE) for a, b in pairs]
-        return lax.ppermute(array, "ctx", moves)
+    def spread(array, target):
+        pairs = [(i * columns + h, target(i, h % 2) * columns + h) for i in range(devices) for h in range(columns)]
+        return lax.ppermute(array, ("ctx", "head"), pairs)
+
+    def to_first(array):
+        return spread(array, lambda i, core: i ^ (4 * core))
+
+    def to_second(array):
+        return spread(array, lambda i, core: i ^ (4 * core) ^ 1)
 
     def exchange(array):
         return lax.all_to_all(array, "ctx", 0, 0, axis_index_groups=planes, tiled=True)
@@ -288,25 +279,24 @@
         compiler_params=params(8),
         name="cut_plane",
     )(sel_rows, *wide)
-    rest_out, first_out, second_out, q_same, q_opp = pl.pallas_call(
+    rest_out, q_same, q_opp = pl.pallas_call(
         cut_pair_kernel,
-        out_shape=(pltpu.HBM((PLANE, TOK, KV), jnp.bfloat16), bf16(TOK, KV), bf16(TOK, KV), bf16(TOK, 256), bf16(TOK, 256)),
+        out_shape=(pltpu.HBM((PLANE, TOK, KV), jnp.bfloat16), bf16(TOK, 256), bf16(TOK, 256)),
         in_specs=[SMEM_SPEC] + [HBM_SPEC] * 6,
-        out_specs=(ANY_SPEC,) + (VMEM_SPEC,) * 4,
+        out_specs=(ANY_SPEC,) + (VMEM_SPEC,) * 2,
         scratch_shapes=[pltpu.VMEM((2, TOK, ALL), jnp.bfloat16),
                         pltpu.SemaphoreType.DMA((2, 6)), pltpu.SemaphoreType.DMA((PLANE,))],
         compiler_params=params(8),
         name="cut_pair",
     )(row, *wide)
 
-    crossed = [cross(array, pairs) for array, pairs in zip((first_out, second_out) * 2, CROSSING)]
-    q_other = swapped(q_opp)
+    q_first, q_second = to_first(q_same), to_second(q_opp)
 
     main = exchange(plane_out)
     sel_all = main[:, TOK, :2 * WIN].astype(jnp.int32)
     edge_up, edge_dn = main[PLANE - REACH:, :TOK, :KV], main[:REACH, :TOK, :KV]
     up, dn = send(edge_up, PLANE), send(edge_dn, -PLANE)
-    rest = exchange(after(rest_out, sel_all, q_other, *crossed))
+    rest = exchange(after(rest_out, sel_all, q_first, q_second))
 
     mid, stats, first, second = pl.pallas_call(
         inner_kernel,
@@ -318,29 +308,38 @@
         cost_estimate=cost(44),
         name="inner",
     )(sel_all, main)
-    mine = pl.pallas_call(
+    mine, done = pl.pallas_call(
         outer_kernel,
-        out_shape=bf16(PLANE, TOK, 256),
+        out_shape=(bf16(PLANE, TOK, 256), f32(8, BLK)),
         in_specs=[SMEM_SPEC] + [VMEM_SPEC] * 7,
-        out_specs=VMEM_SPEC,
+        out_specs=(VMEM_SPEC,) * 2,
         scratch_shapes=scratch(REACH),
         compiler_params=params(16),
         cost_estimate=cost(12),
         name="outer",
     )(sel_all, main, up, dn, mid, stats, first, second)
-    back = exchange(after(mine, rest))
+    edge = pl.pallas_call(
+        edge_kernel,
+        out_shape=bf16(REACH, TOK, KV),
+        in_specs=[SMEM_SPEC, VMEM_SPEC, ANY_SPEC],
+        out_specs=VMEM_SPEC,
+        compiler_params=params(4),
+        name="edge",
+    )(task, rest, done)
+    halo = spread(edge, lambda i, core: (i + (PLANE if (i ^ (4 * core)) % PLANE < PLANE // 2 else -PLANE)) % devices)
+    back = exchange(after(mine, edge))
 
     own, lent = pl.pallas_call(
         pair_kernel,
         out_shape=(bf16(TOK, 256), bf16(TOK, 256)),
-        in_specs=[SMEM_SPEC] * 2 + [VMEM_SPEC] * 7,
+        in_specs=[SMEM_SPEC] * 2 + [VMEM_SPEC] * 4,
         out_specs=(VMEM_SPEC,) * 2,
-        scratch_shapes=[pltpu.VMEM(((PLANE + 2 * REACH + 1) * TOK, KV), jnp.bfloat16)] + scratch(CHUNKS),
+        scratch_shapes=[pltpu.VMEM(((PLANE + 2 * REACH) * TOK, KV), jnp.bfloat16)] + scratch(CHUNKS),
         compiler_params=params(14),
         cost_estimate=cost(14),
         name="pair",
-    )(row, sel_all, q_same, q_other, rest, *crossed)
-    partner = swapped(lent)
+    )(task, sel_all, q_first, q_second, rest, halo)
+    own, partner = to_first(own), to_second(lent)
 
     return pl.pallas_call(
         unpack_kernel,

time: 134 us -> 125 us (0.933)
  starting transfers between devices: 50.2 us -> 37.6 us
  local copies, waits for them, and re-layouts: 1.85 us -> 4.42 us
  Pallas kernels: 27.6 us -> 29.2 us
    ppermute x6 -> x5, starting transfers between devices: 26.5 us -> 15.6 us  [spread(): return lax.ppermute(array, ('ctx', 'head'), pairs)]
    all_to_all x3, waiting for transfers between devices: 36 us -> 28.9 us  [exchange(): lax.all_to_all(array, 'ctx', 0, 0, axis_index_groups=planes, tiled=True)]
    ppermute x6 -> x5, waiting for transfers between devices: 8.31 us -> 14.3 us  [spread(): return lax.ppermute(array, ('ctx', 'head'), pairs)]
    all_to_all x3, starting transfers between devices: 18.9 us -> 16.4 us  [exchange(): lax.all_to_all(array, 'ctx', 0, 0, axis_index_groups=planes, tiled=True)]
    pallas_call x1 -> x2, Pallas kernels: 4.31 us -> 6.75 us  [the longest x1 5.11 us: body(): pl.pallas_call(outer_kernel, out_shape=(bf16(PLANE, TOK, 256), f32(8, BLK...]
    unnamed x6, local copies, waits for them, and re-layouts: 1.62 us -> 2.98 us
    ppermute x2, waiting for transfers between devices: 6.8 us -> 8.16 us  [send(): lax.ppermute(array, 'ctx', [(i, (i + by) % devices) for i in range(device...]
  transfers between devices with their start and end apart: 11 -> 10, of which waited for: 3 -> 7; matrix products, arithmetic and copies ran while one was open for 0% -> 1% of each run, Pallas kernels for 16% -> 18%
where the time goes in v6:
time: 125 us; the launch traced here: 124 us
  waiting for transfers between devices  51.4 us (41%)
  starting transfers between devices  37.6 us (30%)
  Pallas kernels  29.2 us (23%)
  local copies, waits for them, and re-layouts  4.42 us (4%)
    all_to_all x3, waiting for transfers between devices, exchange(): lax.all_to_all(array, 'ctx', 0, 0, axis_index_groups=planes, tiled=True)  28.9 us
    all_to_all x3, starting transfers between devices, exchange(): lax.all_to_all(array, 'ctx', 0, 0, axis_index_groups=planes, tiled=True)  16.4 us
    ppermute x5, starting transfers between devices, spread(): return lax.ppermute(array, ('ctx', 'head'), pairs)  15.6 us
    ppermute x5, waiting for transfers between devices, spread(): return lax.ppermute(array, ('ctx', 'head'), pairs)  14.3 us
    pallas_call x1, Pallas kernels, body(): pl.pallas_call(inner_kernel, out_shape=(bf16(2, TOK, 256), f32(PLANE, 3,...  9.18 us
    ppermute x2, waiting for transfers between devices, send(): lax.ppermute(array, 'ctx', [(i, (i + by) % devices) for i in range(device...  8.16 us
    ppermute x2, starting transfers between devices, send(): lax.ppermute(array, 'ctx', [(i, (i + by) % devices) for i in range(device...  5.58 us
    pallas_call x1, Pallas kernels, body(): pl.pallas_call(pair_kernel, out_shape=(bf16(TOK, 256), bf16(TOK, 256)), i...  5.14 us
  transfers between devices with their start and end apart: 10, of which 7 were waited for; matrix products, arithmetic and copies ran while one was open for 1% of the time, Pallas kernels for 18%

profile of v6, /device:TPU:1, one launch (start us, length us, event | category | flops | bytes accessed | tf_op | source)
XLA Modules:
  0.0 124.0 jit_solution(14777190085820498604)
XLA Ops:
  0.6 0.7 convert_element_type.10
  1.3 0.1 reshape.9
  1.4 3.5 %cut_plane.1 = bf16[8,264,768]{2,1,0:T(8,128)(2,1)} custom-call(bf16[8,768]{1,0:T(8,128)(2,1)S(1)} %pad.4.sel, bf16[256,1280]{1,0:T(8,128)(2,1)} %q.3, bf16[256,1280]{1,0:T(8,128)(2,1)} %qt.3, bf16[256,1280]{1,0:T(8,128)(2,1)} %k.3, bf16[256,1280]{1,0:T(8,128)(2,1)} %kt.3, bf16[256,1280]{1,0:T(8,128)(2,1)} %v.3, bf16[256,1280]{1,0:T(8,128)(2,1)} %vt.3), custom_call_target="tpu_custom_call" | custom-call | tf_op jit(solution)/shard_map/cut_plane/pallas_call | solution.py:272
  4.9 7.5 %all-to-all-start = ((bf16[8,264,768]{2,1,0:T(8,128)(2,1)}), bf16[8,264,768]{2,1,0:T(8,128)(2,1)S(1)}, u32[]{:S(2)}, u32[]{:S(2)}) async-start(bf16[8,264,768]{2,1,0:T(8,128)(2,1)} %cut_plane.1), calls=%async_computation | async-start | bytes 6488064 | tf_op jit(solution)/shard_map/all_to_all | solution.py:267
  12.4 3.4 %cut_pair.1 = (bf16[8,256,512]{2,1,0:T(8,128)(2,1)}, bf16[256,256]{1,0:T(8,128)(2,1)}, bf16[256,256]{1,0:T(8,128)(2,1)}) custom-call(s32[1]{0:T(128)} %bitcast.row_ref.par_ref, bf16[256,1280]{1,0:T(8,128)(2,1)} %q.3, bf16[256,1280]{1,0:T(8,128)(2,1)} %qt.3, bf16[256,1280]{1,0:T(8,128)(2,1)} %k.3, bf16[256,1280]{1,0:T(8,128)(2,1)} %kt.3, ...), custom_call_target="tpu_custom_call" | custom-call | tf_op jit(solution)/shard_map/cut_pair/pallas_call | solution.py:282
  15.7 4.9 %collective-permute-start.2 = (bf16[256,256]{1,0:T(8,128)(2,1)}, bf16[256,256]{1,0:T(8,128)(2,1)S(1)}, u32[]{:S(2)}, u32[]{:S(2)}) collective-permute-start(bf16[256,256]{1,0:T(8,128)(2,1)} %get-tuple-element.19), channel_id=1, source_target_pairs={{0,0},{1,17},{2,2},{3,19},{4,4},{5,21},{6,6},{7,23},{8,8},{9,25},{... | collective-permute-start | bytes 393224 | tf_op jit(solution)/shard_map/ppermute | solution.py:258
  20.6 1.3 %collective-permute-start.3 = (bf16[256,256]{1,0:T(8,128)(2,1)}, bf16[256,256]{1,0:T(8,128)(2,1)S(1)}, u32[]{:S(2)}, u32[]{:S(2)}) collective-permute-start(bf16[256,256]{1,0:T(8,128)(2,1)} %get-tuple-element.20), channel_id=1, source_target_pairs={{0,4},{1,21},{2,6},{3,23},{4,0},{5,17},{6,2},{7,19},{8,12},{9,29},... | collective-permute-start | bytes 393224 | tf_op jit(solution)/shard_map/ppermute | solution.py:258
  21.9 28.9 %all-to-all-done.main = bf16[8,264,768]{2,1,0:T(8,128)(2,1)S(1)} async-done(((bf16[8,264,768]{2,1,0:T(8,128)(2,1)}), bf16[8,264,768]{2,1,0:T(8,128)(2,1)S(1)}, u32[]{:S(2)}, u32[]{:S(2)}) %all-to-all-start) | async-done | bytes 3244064 | tf_op jit(solution)/shard_map/all_to_all | solution.py:267
  50.8 2.1 %collective-permute-done.2.refs_2_.q_first = bf16[256,256]{1,0:T(8,128)(2,1)S(1)} collective-permute-done((bf16[256,256]{1,0:T(8,128)(2,1)}, bf16[256,256]{1,0:T(8,128)(2,1)S(1)}, u32[]{:S(2)}, u32[]{:S(2)}) %collective-permute-start.2) | collective-permute-done | bytes 131104 | tf_op jit(solution)/shard_map/ppermute | solution.py:258
  52.9 2.2 %collective-permute-done.3.refs_3_.q_second = bf16[256,256]{1,0:T(8,128)(2,1)S(1)} collective-permute-done((bf16[256,256]{1,0:T(8,128)(2,1)}, bf16[256,256]{1,0:T(8,128)(2,1)S(1)}, u32[]{:S(2)}, u32[]{:S(2)}) %collective-permute-start.3) | collective-permute-done | bytes 131104 | tf_op jit(solution)/shard_map/ppermute | solution.py:258
  55.1 4.3 %all-to-all-start.1 = ((bf16[8,256,512]{2,1,0:T(8,128)(2,1)}), bf16[8,256,512]{2,1,0:T(8,128)(2,1)}, u32[]{:S(2)}, u32[]{:S(2)}) async-start(bf16[8,256,512]{2,1,0:T(8,128)(2,1)} %after.2), calls=%async_computation.1 | async-start | bytes 4194304 | tf_op jit(solution)/shard_map/all_to_all | solution.py:267
  59.4 1.3 %fusion.1 = (bf16[3,256,512]{2,1,0:T(8,128)(2,1)}, bf16[3,256,512]{2,1,0:T(8,128)(2,1)}) fusion(bf16[8,264,768]{2,1,0:T(8,128)(2,1)S(1)} %all-to-all-done.main), kind=kLoop, calls=%fused_computation.2 | loop fusion | bytes 3145728 | tf_op jit(solution)/shard_map/slice | solution.py:297
  60.8 1.6 %collective-permute-start = (bf16[3,256,512]{2,1,0:T(8,128)(2,1)}, bf16[3,256,512]{2,1,0:T(8,128)(2,1)}, u32[]{:S(2)}, u32[]{:S(2)}) collective-permute-start(bf16[3,256,512]{2,1,0:T(8,128)(2,1)} %get-tuple-element.25), channel_id=1, source_target_pairs={{0,32},{4,36},{8,40},{12,44},{16,48},{20,52},{24,56},{28,60},{32,6... | collective-permute-start | bytes 2359304 | tf_op jit(solution)/shard_map/ppermute | solution.py:254
  62.4 3.9 %collective-permute-start.1 = (bf16[3,256,512]{2,1,0:T(8,128)(2,1)}, bf16[3,256,512]{2,1,0:T(8,128)(2,1)}, u32[]{:S(2)}, u32[]{:S(2)}) collective-permute-start(bf16[3,256,512]{2,1,0:T(8,128)(2,1)} %get-tuple-element.24), channel_id=1, source_target_pairs={{0,224},{4,228},{8,232},{12,236},{16,240},{20,244},{24,248},{28,25... | collective-permute-start | bytes 2359304 | tf_op jit(solution)/shard_map/ppermute | solution.py:254
  66.4 9.2 %inner.1 = (bf16[2,256,256]{2,1,0:T(8,128)(2,1)S(1)}, f32[8,3,256,128]{3,2,1,0:T(8,128)S(1)}, f32[8,256,256]{2,1,0:T(8,128)S(1)}, f32[8,256,128]{2,1,0:T(8,128)S(1)}) custom-call(s32[8,28]{1,0:T(8,128)S(1)} %fusion.sel_ref.refs_1_, bf16[8,264,768]{2,1,0:T(8,128)(2,1)S(1)} %all-to-all-done.main), custom_call_target="tpu_custom_call" | custom-call | flops 3690987520 | bytes 11534336 | tf_op jit(solution)/shard_map/inner/pallas_call | solution.py:301
  75.5 8.2 %collective-permute-done.up = bf16[3,256,512]{2,1,0:T(8,128)(2,1)} collective-permute-done((bf16[3,256,512]{2,1,0:T(8,128)(2,1)}, bf16[3,256,512]{2,1,0:T(8,128)(2,1)}, u32[]{:S(2)}, u32[]{:S(2)}) %collective-permute-start) | collective-permute-done | bytes 786464 | tf_op jit(solution)/shard_map/ppermute | solution.py:254
  83.7 0.0 collective-permute-done.1.dn
  83.7 5.1 %outer.1 = (bf16[8,256,256]{2,1,0:T(8,128)(2,1)S(1)}, f32[8,128]{1,0:T(8,128)S(1)}) custom-call(s32[8,28]{1,0:T(8,128)S(1)} %fusion.sel_ref.refs_1_, bf16[8,264,768]{2,1,0:T(8,128)(2,1)S(1)} %all-to-all-done.main, bf16[3,256,512]{2,1,0:T(8,128)(2,1)} %collective-permute-done.up, bf16[3,256,512]{2,1,0:T(8,128)(2,1)} %collective-permute-done.1.dn, ...), custom_call_target="tpu_custom_call" | custom-call | flops 1006632960 | bytes 3145728 | tf_op jit(solution)/shard_map/outer/pallas_call | solution.py:311
  88.8 0.0 copy-start
  88.8 1.0 copy-done
  89.8 0.0 all-to-all-done.1.main
  89.8 1.6 %edge.1.refs_1_ = bf16[3,256,512]{2,1,0:T(8,128)(2,1)S(1)} custom-call(s32[1]{0:T(128)S(6)} %xor.7.task_ref, bf16[8,256,512]{2,1,0:T(8,128)(2,1)} %all-to-all-done.1.main, f32[8,128]{1,0:T(8,128)S(1)} %get-tuple-element.21.gate), custom_call_target="tpu_custom_call" | custom-call | tf_op jit(solution)/shard_map/edge/pallas_call | solution.py:321
  91.4 3.0 %collective-permute-start.4 = (bf16[3,256,512]{2,1,0:T(8,128)(2,1)S(1)}, bf16[3,256,512]{2,1,0:T(8,128)(2,1)S(1)}, u32[]{:S(2)}, u32[]{:S(2)}) collective-permute-start(bf16[3,256,512]{2,1,0:T(8,128)(2,1)S(1)} %edge.1.refs_1_), channel_id=1, source_target_pairs={{0,32},{1,225},{2,34},{3,227},{4,36},{5,229},{6,38},{7,231},{8,40}... | collective-permute-start | bytes 2359304 | tf_op jit(solution)/shard_map/ppermute | solution.py:258
  94.5 4.5 %all-to-all-start.2 = ((bf16[8,256,256]{2,1,0:T(8,128)(2,1)}), bf16[8,256,256]{2,1,0:T(8,128)(2,1)S(1)}, u32[]{:S(2)}, u32[]{:S(2)}) async-start(bf16[8,256,256]{2,1,0:T(8,128)(2,1)} %after.3), calls=%async_computation.2 | async-start | bytes 2097152 | tf_op jit(solution)/shard_map/all_to_all | solution.py:267
  99.0 4.4 %collective-permute-done.4.halo = bf16[3,256,512]{2,1,0:T(8,128)(2,1)S(1)} collective-permute-done((bf16[3,256,512]{2,1,0:T(8,128)(2,1)S(1)}, bf16[3,256,512]{2,1,0:T(8,128)(2,1)S(1)}, u32[]{:S(2)}, u32[]{:S(2)}) %collective-permute-start.4) | collective-permute-done | bytes 786464 | tf_op jit(solution)/shard_map/ppermute | solution.py:258
  103.4 0.0 copy-start.1
  103.4 0.9 copy-done.1
  104.3 0.0 copy-start.2
  104.3 1.1 copy-done.2
  105.4 5.1 %pair.1 = (bf16[256,256]{1,0:T(8,128)(2,1)}, bf16[256,256]{1,0:T(8,128)(2,1)}) custom-call(s32[1]{0:T(128)S(6)} %xor.7.task_ref, s32[8,28]{1,0:T(8,128)S(1)} %fusion.sel_ref.refs_1_, bf16[256,256]{1,0:T(8,128)(2,1)S(1)} %collective-permute-done.2.refs_2_.q_first, bf16[256,256]{1,0:T(8,128)(2,1)S(1)} %collective-permute-done.3.refs_3_.q_second, ...), custom_call_target="tpu_custom_call" | custom-call | flops 1174405120 | bytes 3670016 | tf_op jit(solution)/shard_map/pair/pallas_call | solution.py:332
  110.6 5.6 %collective-permute-start.5 = (bf16[256,256]{1,0:T(8,128)(2,1)}, bf16[256,256]{1,0:T(8,128)(2,1)S(1)}, u32[]{:S(2)}, u32[]{:S(2)}) collective-permute-start(bf16[256,256]{1,0:T(8,128)(2,1)} %get-tuple-element.22), channel_id=1, source_target_pairs={{0,0},{1,17},{2,2},{3,19},{4,4},{5,21},{6,6},{7,23},{8,8},{9,25},{... | collective-permute-start | bytes 393224 | tf_op jit(solution)/shard_map/ppermute | solution.py:258
  116.2 0.8 collective-permute-start.6
  117.0 0.0 all-to-all-done.2.mine
  117.0 1.7 %collective-permute-done.5.own = bf16[256,256]{1,0:T(8,128)(2,1)S(1)} collective-permute-done((bf16[256,256]{1,0:T(8,128)(2,1)}, bf16[256,256]{1,0:T(8,128)(2,1)S(1)}, u32[]{:S(2)}, u32[]{:S(2)}) %collective-permute-start.5) | collective-permute-done | bytes 131104 | tf_op jit(solution)/shard_map/ppermute | solution.py:258
  118.7 4.0 %collective-permute-done.6.other = bf16[256,256]{1,0:T(8,128)(2,1)S(1)} collective-permute-done((bf16[256,256]{1,0:T(8,128)(2,1)}, bf16[256,256]{1,0:T(8,128)(2,1)S(1)}, u32[]{:S(2)}, u32[]{:S(2)}) %collective-permute-start.6) | collective-permute-done | bytes 131104 | tf_op jit(solution)/shard_map/ppermute | solution.py:258
  122.7 1.3 %unpack.1 = (bf16[256,1280]{1,0:T(8,128)(2,1)}, bf16[256,1280]{1,0:T(8,128)(2,1)}) custom-call(s32[1]{0:T(128)} %bitcast.row_ref.par_ref, bf16[8,256,256]{2,1,0:T(8,128)(2,1)S(1)} %all-to-all-done.2.mine, bf16[256,256]{1,0:T(8,128)(2,1)S(1)} %collective-permute-done.5.own, bf16[256,256]{1,0:T(8,128)(2,1)S(1)} %collective-permute-done.6.other), custom_call_target="tpu_custom_call" | custom-call | tf_op jit(solution)/shard_map/unpack/pallas_call | solution.py:344
  (5 shorter events, 0.0 us)
Async XLA Ops:
  4.9 45.9 %all-to-all-start = ((bf16[8,264,768]{2,1,0:T(8,128)(2,1)}), bf16[8,264,768]{2,1,0:T(8,128)(2,1)S(1)}, u32[]{:S(2)}, u32[]{:S(2)}) async-start(bf16[8,264,768]{2,1,0:T(8,128)(2,1)} %cut_plane.1), calls=%async_computation | async-start | bytes 6488064 | tf_op jit(solution)/shard_map/all_to_all | solution.py:267
  15.7 37.2 %collective-permute-start.2 = (bf16[256,256]{1,0:T(8,128)(2,1)}, bf16[256,256]{1,0:T(8,128)(2,1)S(1)}, u32[]{:S(2)}, u32[]{:S(2)}) collective-permute-start(bf16[256,256]{1,0:T(8,128)(2,1)} %get-tuple-element.19), channel_id=1, source_target_pairs={{0,0},{1,17},{2,2},{3,19},{4,4},{5,21},{6,6},{7,23},{8,8},{9,25},{... | collective-permute-start | bytes 393224 | tf_op jit(solution)/shard_map/ppermute | solution.py:258
  20.6 34.5 %collective-permute-start.3 = (bf16[256,256]{1,0:T(8,128)(2,1)}, bf16[256,256]{1,0:T(8,128)(2,1)S(1)}, u32[]{:S(2)}, u32[]{:S(2)}) collective-permute-start(bf16[256,256]{1,0:T(8,128)(2,1)} %get-tuple-element.20), channel_id=1, source_target_pairs={{0,4},{1,21},{2,6},{3,23},{4,0},{5,17},{6,2},{7,19},{8,12},{9,29},... | collective-permute-start | bytes 393224 | tf_op jit(solution)/shard_map/ppermute | solution.py:258
  55.1 34.7 %all-to-all-start.1 = ((bf16[8,256,512]{2,1,0:T(8,128)(2,1)}), bf16[8,256,512]{2,1,0:T(8,128)(2,1)}, u32[]{:S(2)}, u32[]{:S(2)}) async-start(bf16[8,256,512]{2,1,0:T(8,128)(2,1)} %after.2), calls=%async_computation.1 | async-start | bytes 4194304 | tf_op jit(solution)/shard_map/all_to_all | solution.py:267
  60.8 22.9 %collective-permute-start = (bf16[3,256,512]{2,1,0:T(8,128)(2,1)}, bf16[3,256,512]{2,1,0:T(8,128)(2,1)}, u32[]{:S(2)}, u32[]{:S(2)}) collective-permute-start(bf16[3,256,512]{2,1,0:T(8,128)(2,1)} %get-tuple-element.25), channel_id=1, source_target_pairs={{0,32},{4,36},{8,40},{12,44},{16,48},{20,52},{24,56},{28,60},{32,6... | collective-permute-start | bytes 2359304 | tf_op jit(solution)/shard_map/ppermute | solution.py:254
  62.4 21.3 %collective-permute-start.1 = (bf16[3,256,512]{2,1,0:T(8,128)(2,1)}, bf16[3,256,512]{2,1,0:T(8,128)(2,1)}, u32[]{:S(2)}, u32[]{:S(2)}) collective-permute-start(bf16[3,256,512]{2,1,0:T(8,128)(2,1)} %get-tuple-element.24), channel_id=1, source_target_pairs={{0,224},{4,228},{8,232},{12,236},{16,240},{20,244},{24,248},{28,25... | collective-permute-start | bytes 2359304 | tf_op jit(solution)/shard_map/ppermute | solution.py:254
  88.8 1.0 copy-start
  91.4 12.0 %collective-permute-start.4 = (bf16[3,256,512]{2,1,0:T(8,128)(2,1)S(1)}, bf16[3,256,512]{2,1,0:T(8,128)(2,1)S(1)}, u32[]{:S(2)}, u32[]{:S(2)}) collective-permute-start(bf16[3,256,512]{2,1,0:T(8,128)(2,1)S(1)} %edge.1.refs_1_), channel_id=1, source_target_pairs={{0,32},{1,225},{2,34},{3,227},{4,36},{5,229},{6,38},{7,231},{8,40}... | collective-permute-start | bytes 2359304 | tf_op jit(solution)/shard_map/ppermute | solution.py:258
  94.5 22.5 %all-to-all-start.2 = ((bf16[8,256,256]{2,1,0:T(8,128)(2,1)}), bf16[8,256,256]{2,1,0:T(8,128)(2,1)S(1)}, u32[]{:S(2)}, u32[]{:S(2)}) async-start(bf16[8,256,256]{2,1,0:T(8,128)(2,1)} %after.3), calls=%async_computation.2 | async-start | bytes 2097152 | tf_op jit(solution)/shard_map/all_to_all | solution.py:267
  103.4 0.9 copy-start.1
  104.3 1.1 copy-start.2
  110.6 8.2 %collective-permute-start.5 = (bf16[256,256]{1,0:T(8,128)(2,1)}, bf16[256,256]{1,0:T(8,128)(2,1)S(1)}, u32[]{:S(2)}, u32[]{:S(2)}) collective-permute-start(bf16[256,256]{1,0:T(8,128)(2,1)} %get-tuple-element.22), channel_id=1, source_target_pairs={{0,0},{1,17},{2,2},{3,19},{4,4},{5,21},{6,6},{7,23},{8,8},{9,25},{... | collective-permute-start | bytes 393224 | tf_op jit(solution)/shard_map/ppermute | solution.py:258
  116.2 6.5 %collective-permute-start.6 = (bf16[256,256]{1,0:T(8,128)(2,1)}, bf16[256,256]{1,0:T(8,128)(2,1)S(1)}, u32[]{:S(2)}, u32[]{:S(2)}) collective-permute-start(bf16[256,256]{1,0:T(8,128)(2,1)} %get-tuple-element.23), channel_id=1, source_target_pairs={{0,4},{1,21},{2,6},{3,23},{4,0},{5,17},{6,2},{7,19},{8,12},{9,29},... | collective-permute-start | bytes 393224 | tf_op jit(solution)/shard_map/ppermute | solution.py:258

commit v7 on v6

--- a/solution.py
+++ b/solution.py
@@ -48,8 +48,9 @@
     for chunk in ins:
         for copy in chunk:
             copy.start()
+    listed = sel[...].astype(jnp.float32).astype(jnp.bfloat16)
     for j in range(PLANE):
-        buf[j, TOK:, :] = sel[...]
+        buf[j, TOK:TOK + 2, :WIN] = listed
         for copy in ins[j]:
             copy.wait()
         outs[j].start()
@@ -145,10 +146,17 @@
     lax.fori_loop(0, 2, step, 0)
 
 
-def outer_kernel(sel_ref, main, up, dn, mid, stats, first_ref, second_ref, o_ref, done, s_scr, p_scr, t_scr):
+def outer_kernel(sel_ref, main, up, dn, mid, stats, first_ref, second_ref, o_ref, done, buf, sem, s_scr, p_scr, t_scr):
     done[...] = jnp.zeros_like(done)
+    copies = []
+
+    def leave(i, value):
+        buf[i] = value
+        copies.append(pltpu.make_async_copy(buf.at[i], o_ref.at[i], sem.at[i]))
+        copies[-1].start()
+
     for i in (3, 4):
-        o_ref[i] = mid[i - REACH]
+        leave(i, mid[i - REACH])
     for i in (0, 1, 2, 5, 6, 7):
         low = i < REACH
         halo, skip, at = (up, i, 0) if low else (dn, 0, PLANE + REACH - i)
@@ -163,7 +171,16 @@
             more = mix(p_scr.at[:, u * TOK:(u + 1) * TOK], t_scr.at[:, u * TOK:(u + 1) * TOK], TOK,
                        halo[skip + u, :, 2 * HEAD_DIM:])
             first, second = first + more[0], second + more[1]
-        o_ref[i] = finish(stats[i, 1] * shrink + total, stats[i, 2] * shrink + tangent_total, first, second)
+        leave(i, finish(stats[i, 1] * shrink + total, stats[i, 2] * shrink + tangent_total, first, second))
+    for copy in copies:
+        copy.wait()
+
+
+def edges_kernel(main, gate_a, gate_b, up, dn):
+    del gate_a, gate_b
+    for n in range(REACH):
+        up[n] = main[PLANE - REACH + n, :TOK, :KV]
+        dn[n] = main[n, :TOK, :KV]
 
 
 def edge_kernel(task_ref, main, gate, edge):
@@ -173,13 +190,12 @@
         edge[n] = main[begin + n]
 
 
-def pair_kernel(task_ref, sel_ref, q_first, q_second, main, halo, o_first, o_second, kv, s_scr, p_scr, t_scr):
+def pair_kernel(task_ref, sel_ref, q_first, q_second, main, halo, o_first, o_second, kv, s_scr, p_scr, t_scr, sem):
     task = task_ref[0]
-    for c in range(PLANE):
-        kv[(c + REACH) * TOK:(c + REACH + 1) * TOK, :] = main[c]
     begin = jnp.where(task < PLANE // 2, 0, REACH + PLANE)
-    for n in range(REACH):
-        kv[pl.ds(pl.multiple_of((begin + n) * TOK, TOK), TOK), :] = halo[n]
+    pairs = [(main.at[c], kv.at[pl.ds((c + REACH) * TOK, TOK), :]) for c in range(PLANE)]
+    pairs += [(halo.at[n], kv.at[pl.ds(pl.multiple_of((begin + n) * TOK, TOK), TOK), :]) for n in range(REACH)]
+    run_copies(pairs, sem)
     for ref, at, o_ref in ((q_first, task, o_first), (q_second, task + 1 - 2 * (task % 2), o_second)):
         base = pl.multiple_of(at * TOK, TOK)
         _, total, tangent_total = weigh(
@@ -268,7 +284,6 @@
 
     wide = [pltpu.with_memory_space_constraint(array, pltpu.HBM) for array in
             (queries, query_tangents, keys, key_tangents, values, value_tangents)]
-    sel_rows = jnp.pad(selection.astype(jnp.bfloat16).reshape(1, 2 * WIN), ((0, EXTRA - 1), (0, ALL - 2 * WIN)))
     plane_out = pl.pallas_call(
         cut_plane_kernel,
         out_shape=pltpu.HBM((PLANE, TOK + EXTRA, ALL), jnp.bfloat16),
@@ -278,7 +293,7 @@
                         pltpu.SemaphoreType.DMA((PLANE, 6)), pltpu.SemaphoreType.DMA((PLANE,))],
         compiler_params=params(8),
         name="cut_plane",
-    )(sel_rows, *wide)
+    )(selection, *wide)
     rest_out, q_same, q_opp = pl.pallas_call(
         cut_pair_kernel,
         out_shape=(pltpu.HBM((PLANE, TOK, KV), jnp.bfloat16), bf16(TOK, 256), bf16(TOK, 256)),
@@ -293,8 +308,15 @@
     q_first, q_second = to_first(q_same), to_second(q_opp)
 
     main = exchange(plane_out)
-    sel_all = main[:, TOK, :2 * WIN].astype(jnp.int32)
-    edge_up, edge_dn = main[PLANE - REACH:, :TOK, :KV], main[:REACH, :TOK, :KV]
+    sel_all = main[:, TOK:TOK + 2, :WIN].astype(jnp.int32).reshape(PLANE, 2 * WIN)
+    edge_up, edge_dn = pl.pallas_call(
+        edges_kernel,
+        out_shape=(bf16(REACH, TOK, KV),) * 2,
+        in_specs=[VMEM_SPEC] + [ANY_SPEC] * 2,
+        out_specs=(VMEM_SPEC,) * 2,
+        compiler_params=params(4),
+        name="edges",
+    )(main, q_first, q_second)
     up, dn = send(edge_up, PLANE), send(edge_dn, -PLANE)
     rest = exchange(after(rest_out, sel_all, q_first, q_second))
 
@@ -305,17 +327,17 @@
         out_specs=(VMEM_SPEC,) * 4,
         scratch_shapes=[pltpu.VMEM((PLANE * TOK, 2 * HEAD_DIM), jnp.bfloat16)] + scratch(CHUNKS),
         compiler_params=params(16),
-        cost_estimate=cost(44),
+        cost_estimate=cost(2),
         name="inner",
     )(sel_all, main)
     mine, done = pl.pallas_call(
         outer_kernel,
-        out_shape=(bf16(PLANE, TOK, 256), f32(8, BLK)),
+        out_shape=(pltpu.HBM((PLANE, TOK, 256), jnp.bfloat16), f32(8, BLK)),
         in_specs=[SMEM_SPEC] + [VMEM_SPEC] * 7,
-        out_specs=(VMEM_SPEC,) * 2,
-        scratch_shapes=scratch(REACH),
+        out_specs=(ANY_SPEC, VMEM_SPEC),
+        scratch_shapes=[pltpu.VMEM((PLANE, TOK, 256), jnp.bfloat16), pltpu.SemaphoreType.DMA((PLANE,))] + scratch(REACH),
         compiler_params=params(16),
-        cost_estimate=cost(12),
+        cost_estimate=cost(276),
         name="outer",
     )(sel_all, main, up, dn, mid, stats, first, second)
     edge = pl.pallas_call(
@@ -332,13 +354,13 @@
     own, lent = pl.pallas_call(
         pair_kernel,
         out_shape=(bf16(TOK, 256), bf16(TOK, 256)),
-        in_specs=[SMEM_SPEC] * 2 + [VMEM_SPEC] * 4,
+        in_specs=[SMEM_SPEC] * 2 + [VMEM_SPEC] * 2 + [ANY_SPEC, HBM_SPEC],
         out_specs=(VMEM_SPEC,) * 2,
-        scratch_shapes=[pltpu.VMEM(((PLANE + 2 * REACH) * TOK, KV), jnp.bfloat16)] + scratch(CHUNKS),
+        scratch_shapes=[pltpu.VMEM(((PLANE + 2 * REACH) * TOK, KV), jnp.bfloat16)] + scratch(CHUNKS) + [pltpu.SemaphoreType.DMA((PLANE + REACH,))],
         compiler_params=params(14),
         cost_estimate=cost(14),
         name="pair",
-    )(task, sel_all, q_first, q_second, rest, halo)
+    )(task, sel_all, q_first, q_second, rest, pltpu.with_memory_space_constraint(halo, pltpu.HBM))
     own, partner = to_first(own), to_second(lent)
 
     return pl.pallas_call(

time: 125 us -> 125 us (level)
  waiting for transfers between devices: 51.4 us -> 56.1 us
  local copies, waits for them, and re-layouts: 4.42 us -> 1.64 us
  starting transfers between devices: 37.6 us -> 35.6 us
  Pallas kernels: 29.2 us -> 30.5 us
    ppermute x5, waiting for transfers between devices: 14.3 us -> 44.8 us  [spread(): return lax.ppermute(array, ('ctx', 'head'), pairs)]
    all_to_all x3, waiting for transfers between devices: 28.9 us -> 7.88 us  [exchange(): lax.all_to_all(array, 'ctx', 0, 0, axis_index_groups=planes, tiled=True)]
    ppermute x2, waiting for transfers between devices: 8.16 us -> 3.36 us  [send(): lax.ppermute(array, 'ctx', [(i, (i + by) % devices) for i in range(device...]
    pallas_call x1 -> x2, Pallas kernels: 5.11 us -> 7.1 us  [the longest x1 5.85 us: body(): pl.pallas_call(outer_kernel, out_shape=(pltpu.HBM((PLANE, TOK, 256), jnp....]
    ppermute x5, starting transfers between devices: 15.6 us -> 14.2 us  [spread(): return lax.ppermute(array, ('ctx', 'head'), pairs)]
    unnamed x6 -> x4, local copies, waits for them, and re-layouts: 2.98 us -> 1.55 us
    slice x2 -> x0, local copies, waits for them, and re-layouts: 1.34 us -> none  [the longest x1 1.34 us: body(): main[:REACH, :TOK, :KV]]
  transfers between devices with their start and end apart: 10 -> 10, of which waited for: 7 -> 7; matrix products, arithmetic and copies ran while one was open for 1% -> 0% of each run, Pallas kernels for 18% -> 18%
where the time goes in v7:
time: 125 us; the launch traced here: 124 us
  waiting for transfers between devices  56.1 us (45%)
  starting transfers between devices  35.6 us (28%)
  Pallas kernels  30.5 us (24%)
  local copies, waits for them, and re-layouts  1.64 us (1%)
    ppermute x5, waiting for transfers between devices, spread(): return lax.ppermute(array, ('ctx', 'head'), pairs)  44.8 us
    all_to_all x3, starting transfers between devices, exchange(): lax.all_to_all(array, 'ctx', 0, 0, axis_index_groups=planes, tiled=True)  15.8 us
    ppermute x5, starting transfers between devices, spread(): return lax.ppermute(array, ('ctx', 'head'), pairs)  14.2 us
    pallas_call x1, Pallas kernels, body(): pl.pallas_call(inner_kernel, out_shape=(bf16(2, TOK, 256), f32(PLANE, 3,...  9.19 us
    all_to_all x3, waiting for transfers between devices, exchange(): lax.all_to_all(array, 'ctx', 0, 0, axis_index_groups=planes, tiled=True)  7.88 us
    pallas_call x1, Pallas kernels, body(): pl.pallas_call(outer_kernel, out_shape=(pltpu.HBM((PLANE, TOK, 256), jnp....  5.85 us
    ppermute x2, starting transfers between devices, send(): lax.ppermute(array, 'ctx', [(i, (i + by) % devices) for i in range(device...  5.58 us
    pallas_call x1, Pallas kernels, body(): pl.pallas_call(pair_kernel, out_shape=(bf16(TOK, 256), bf16(TOK, 256)), i...  5.13 us
  transfers between devices with their start and end apart: 10, of which 7 were waited for; matrix products, arithmetic and copies ran while one was open for 0% of the time, Pallas kernels for 18%

profile of v7, /device:TPU:1, one launch (start us, length us, event | category | flops | bytes accessed | tf_op | source)
XLA Modules:
  0.0 124.5 jit_solution(17111828106490740167)
XLA Ops:
  0.6 0.0 copy-start
  0.6 0.7 copy-done
  1.3 3.5 %cut_plane.1 = bf16[8,264,768]{2,1,0:T(8,128)(2,1)} custom-call(s32[2,14]{1,0:T(2,128)S(1)} %copy-done, bf16[256,1280]{1,0:T(8,128)(2,1)} %q.3, bf16[256,1280]{1,0:T(8,128)(2,1)} %qt.3, bf16[256,1280]{1,0:T(8,128)(2,1)} %k.3, bf16[256,1280]{1,0:T(8,128)(2,1)} %kt.3, bf16[256,1280]{1,0:T(8,128)(2,1)} %v.3, bf16[256,1280]{1,0:T(8,128)(2,1)} %vt.3), custom_call_target="tpu_custom_call" | custom-call | tf_op jit(solution)/shard_map/cut_plane/pallas_call | solution.py:287
  4.8 7.5 %all-to-all-start = ((bf16[8,264,768]{2,1,0:T(8,128)(2,1)}), bf16[8,264,768]{2,1,0:T(8,128)(2,1)S(1)}, u32[]{:S(2)}, u32[]{:S(2)}) async-start(bf16[8,264,768]{2,1,0:T(8,128)(2,1)} %cut_plane.1), calls=%async_computation | async-start | bytes 6488064 | tf_op jit(solution)/shard_map/all_to_all | solution.py:283
  12.3 2.7 %cut_pair.1 = (bf16[8,256,512]{2,1,0:T(8,128)(2,1)}, bf16[256,256]{1,0:T(8,128)(2,1)S(1)}, bf16[256,256]{1,0:T(8,128)(2,1)S(1)}) custom-call(s32[1]{0:T(128)} %bitcast.row_ref.par_ref, bf16[256,1280]{1,0:T(8,128)(2,1)} %q.3, bf16[256,1280]{1,0:T(8,128)(2,1)} %qt.3, bf16[256,1280]{1,0:T(8,128)(2,1)} %k.3, bf16[256,1280]{1,0:T(8,128)(2,1)} %kt.3, ...), custom_call_target="tpu_custom_call" | custom-call | tf_op jit(solution)/shard_map/cut_pair/pallas_call | solution.py:297
  15.0 4.9 %collective-permute-start = (bf16[256,256]{1,0:T(8,128)(2,1)S(1)}, bf16[256,256]{1,0:T(8,128)(2,1)S(1)}, u32[]{:S(2)}, u32[]{:S(2)}) collective-permute-start(bf16[256,256]{1,0:T(8,128)(2,1)S(1)} %get-tuple-element.15), channel_id=1, source_target_pairs={{0,0},{1,17},{2,2},{3,19},{4,4},{5,21},{6,6},{7,23},{8,8},{9,25},{... | collective-permute-start | bytes 393224 | tf_op jit(solution)/shard_map/ppermute | solution.py:274
  19.9 1.3 %collective-permute-start.1 = (bf16[256,256]{1,0:T(8,128)(2,1)S(1)}, bf16[256,256]{1,0:T(8,128)(2,1)S(1)}, u32[]{:S(2)}, u32[]{:S(2)}) collective-permute-start(bf16[256,256]{1,0:T(8,128)(2,1)S(1)} %get-tuple-element.16), channel_id=1, source_target_pairs={{0,4},{1,21},{2,6},{3,23},{4,0},{5,17},{6,2},{7,19},{8,12},{9,29},... | collective-permute-start | bytes 393224 | tf_op jit(solution)/shard_map/ppermute | solution.py:274
  21.1 31.7 %collective-permute-done.gate_a.refs_2_.q_first = bf16[256,256]{1,0:T(8,128)(2,1)S(1)} collective-permute-done((bf16[256,256]{1,0:T(8,128)(2,1)S(1)}, bf16[256,256]{1,0:T(8,128)(2,1)S(1)}, u32[]{:S(2)}, u32[]{:S(2)}) %collective-permute-start) | collective-permute-done | bytes 131104 | tf_op jit(solution)/shard_map/ppermute | solution.py:274
  52.8 2.2 %collective-permute-done.1.gate_b.refs_3_.q_second = bf16[256,256]{1,0:T(8,128)(2,1)S(1)} collective-permute-done((bf16[256,256]{1,0:T(8,128)(2,1)S(1)}, bf16[256,256]{1,0:T(8,128)(2,1)S(1)}, u32[]{:S(2)}, u32[]{:S(2)}) %collective-permute-start.1) | collective-permute-done | bytes 131104 | tf_op jit(solution)/shard_map/ppermute | solution.py:274
  55.0 0.0 all-to-all-done.main
  55.0 1.3 %edges.1 = (bf16[3,256,512]{2,1,0:T(8,128)(2,1)}, bf16[3,256,512]{2,1,0:T(8,128)(2,1)}) custom-call(bf16[8,264,768]{2,1,0:T(8,128)(2,1)S(1)} %all-to-all-done.main, bf16[256,256]{1,0:T(8,128)(2,1)S(1)} %collective-permute-done.gate_a.refs_2_.q_first, bf16[256,256]{1,0:T(8,128)(2,1)S(1)} %collective-permute-done.1.gate_b.refs_3_.q_second), custom_call_target="tpu_custom_call" | custom-call | tf_op jit(solution)/shard_map/edges/pallas_call | solution.py:312
  56.3 1.6 %collective-permute-start.2 = (bf16[3,256,512]{2,1,0:T(8,128)(2,1)}, bf16[3,256,512]{2,1,0:T(8,128)(2,1)}, u32[]{:S(2)}, u32[]{:S(2)}) collective-permute-start(bf16[3,256,512]{2,1,0:T(8,128)(2,1)} %get-tuple-element.17), channel_id=1, source_target_pairs={{0,32},{4,36},{8,40},{12,44},{16,48},{20,52},{24,56},{28,60},{32,6... | collective-permute-start | bytes 2359304 | tf_op jit(solution)/shard_map/ppermute | solution.py:270
  57.9 3.9 %collective-permute-start.3 = (bf16[3,256,512]{2,1,0:T(8,128)(2,1)}, bf16[3,256,512]{2,1,0:T(8,128)(2,1)}, u32[]{:S(2)}, u32[]{:S(2)}) collective-permute-start(bf16[3,256,512]{2,1,0:T(8,128)(2,1)} %get-tuple-element.18), channel_id=1, source_target_pairs={{0,224},{4,228},{8,232},{12,236},{16,240},{20,244},{24,248},{28,25... | collective-permute-start | bytes 2359304 | tf_op jit(solution)/shard_map/ppermute | solution.py:270
  61.9 0.1 reshape.12.sel_ref.refs_1_
  61.9 4.3 %all-to-all-start.1 = ((bf16[8,256,512]{2,1,0:T(8,128)(2,1)}), bf16[8,256,512]{2,1,0:T(8,128)(2,1)}, u32[]{:S(2)}, u32[]{:S(2)}) async-start(bf16[8,256,512]{2,1,0:T(8,128)(2,1)} %after.2), calls=%async_computation.1 | async-start | bytes 4194304 | tf_op jit(solution)/shard_map/all_to_all | solution.py:283
  66.3 9.2 %inner.1 = (bf16[2,256,256]{2,1,0:T(8,128)(2,1)S(1)}, f32[8,3,256,128]{3,2,1,0:T(8,128)S(1)}, f32[8,256,256]{2,1,0:T(8,128)S(1)}, f32[8,256,128]{2,1,0:T(8,128)S(1)}) custom-call(s32[8,28]{1,0:T(8,128)S(1)} %reshape.12.sel_ref.refs_1_, bf16[8,264,768]{2,1,0:T(8,128)(2,1)S(1)} %all-to-all-done.main), custom_call_target="tpu_custom_call" | custom-call | flops 167772160 | bytes 524288 | tf_op jit(solution)/shard_map/inner/pallas_call | solution.py:323
  75.5 3.4 %collective-permute-done.2.up = bf16[3,256,512]{2,1,0:T(8,128)(2,1)} collective-permute-done((bf16[3,256,512]{2,1,0:T(8,128)(2,1)}, bf16[3,256,512]{2,1,0:T(8,128)(2,1)}, u32[]{:S(2)}, u32[]{:S(2)}) %collective-permute-start.2) | collective-permute-done | bytes 786464 | tf_op jit(solution)/shard_map/ppermute | solution.py:270
  78.8 0.0 collective-permute-done.3.dn
  78.8 5.8 %outer.1 = (bf16[8,256,256]{2,1,0:T(8,128)(2,1)}, f32[8,128]{1,0:T(8,128)S(1)}) custom-call(s32[8,28]{1,0:T(8,128)S(1)} %reshape.12.sel_ref.refs_1_, bf16[8,264,768]{2,1,0:T(8,128)(2,1)S(1)} %all-to-all-done.main, bf16[3,256,512]{2,1,0:T(8,128)(2,1)} %collective-permute-done.2.up, bf16[3,256,512]{2,1,0:T(8,128)(2,1)} %collective-permute-done.3.dn, ...), custom_call_target="tpu_custom_call" | custom-call | flops 23152558080 | bytes 72351744 | tf_op jit(solution)/shard_map/outer/pallas_call | solution.py:333
  84.7 7.9 %all-to-all-done.1.main = bf16[8,256,512]{2,1,0:T(8,128)(2,1)} async-done(((bf16[8,256,512]{2,1,0:T(8,128)(2,1)}), bf16[8,256,512]{2,1,0:T(8,128)(2,1)}, u32[]{:S(2)}, u32[]{:S(2)}) %all-to-all-start.1) | async-done | bytes 2097184 | tf_op jit(solution)/shard_map/all_to_all | solution.py:283
  92.6 1.6 %edge.1.refs_1_ = bf16[3,256,512]{2,1,0:T(8,128)(2,1)S(1)} custom-call(s32[1]{0:T(128)S(6)} %xor.7.task_ref, bf16[8,256,512]{2,1,0:T(8,128)(2,1)} %all-to-all-done.1.main, f32[8,128]{1,0:T(8,128)S(1)} %get-tuple-element.25.gate), custom_call_target="tpu_custom_call" | custom-call | tf_op jit(solution)/shard_map/edge/pallas_call | solution.py:343
  94.2 1.9 %collective-permute-start.4 = (bf16[3,256,512]{2,1,0:T(8,128)(2,1)S(1)}, bf16[3,256,512]{2,1,0:T(8,128)(2,1)S(1)}, u32[]{:S(2)}, u32[]{:S(2)}) collective-permute-start(bf16[3,256,512]{2,1,0:T(8,128)(2,1)S(1)} %edge.1.refs_1_), channel_id=1, source_target_pairs={{0,32},{1,225},{2,34},{3,227},{4,36},{5,229},{6,38},{7,231},{8,40}... | collective-permute-start | bytes 2359304 | tf_op jit(solution)/shard_map/ppermute | solution.py:274
  96.2 4.0 %all-to-all-start.2 = ((bf16[8,256,256]{2,1,0:T(8,128)(2,1)}), bf16[8,256,256]{2,1,0:T(8,128)(2,1)S(1)}, u32[]{:S(2)}, u32[]{:S(2)}) async-start(bf16[8,256,256]{2,1,0:T(8,128)(2,1)} %after.3), calls=%async_computation.2 | async-start | bytes 2097152 | tf_op jit(solution)/shard_map/all_to_all | solution.py:283
  100.1 5.3 %collective-permute-done.4.halo = bf16[3,256,512]{2,1,0:T(8,128)(2,1)S(1)} collective-permute-done((bf16[3,256,512]{2,1,0:T(8,128)(2,1)S(1)}, bf16[3,256,512]{2,1,0:T(8,128)(2,1)S(1)}, u32[]{:S(2)}, u32[]{:S(2)}) %collective-permute-start.4) | collective-permute-done | bytes 786464 | tf_op jit(solution)/shard_map/ppermute | solution.py:274
  105.4 0.0 copy-start.1
  105.4 0.9 copy-done.1
  106.3 5.1 %pair.1 = (bf16[256,256]{1,0:T(8,128)(2,1)S(1)}, bf16[256,256]{1,0:T(8,128)(2,1)S(1)}) custom-call(s32[1]{0:T(128)S(6)} %xor.7.task_ref, s32[8,28]{1,0:T(8,128)S(1)} %reshape.12.sel_ref.refs_1_, bf16[256,256]{1,0:T(8,128)(2,1)S(1)} %collective-permute-done.gate_a.refs_2_.q_first, bf16[256,256]{1,0:T(8,128)(2,1)S(1)} %collective-permute-done.1.gate_b.refs_3_.q_second, ...), custom_call_target="tpu_custom_call" | custom-call | flops 1174405120 | bytes 3670016 | tf_op jit(solution)/shard_map/pair/pallas_call | solution.py:354
  111.4 5.4 %collective-permute-start.5 = (bf16[256,256]{1,0:T(8,128)(2,1)S(1)}, bf16[256,256]{1,0:T(8,128)(2,1)S(1)}, u32[]{:S(2)}, u32[]{:S(2)}) collective-permute-start(bf16[256,256]{1,0:T(8,128)(2,1)S(1)} %get-tuple-element.26), channel_id=1, source_target_pairs={{0,0},{1,17},{2,2},{3,19},{4,4},{5,21},{6,6},{7,23},{8,8},{9,25},{... | collective-permute-start | bytes 393224 | tf_op jit(solution)/shard_map/ppermute | solution.py:274
  116.9 0.6 collective-permute-start.6
  117.5 0.0 all-to-all-done.2.mine
  117.5 1.7 %collective-permute-done.5.own = bf16[256,256]{1,0:T(8,128)(2,1)S(1)} collective-permute-done((bf16[256,256]{1,0:T(8,128)(2,1)S(1)}, bf16[256,256]{1,0:T(8,128)(2,1)S(1)}, u32[]{:S(2)}, u32[]{:S(2)}) %collective-permute-start.5) | collective-permute-done | bytes 131104 | tf_op jit(solution)/shard_map/ppermute | solution.py:274
  119.2 4.0 %collective-permute-done.6.other = bf16[256,256]{1,0:T(8,128)(2,1)S(1)} collective-permute-done((bf16[256,256]{1,0:T(8,128)(2,1)S(1)}, bf16[256,256]{1,0:T(8,128)(2,1)S(1)}, u32[]{:S(2)}, u32[]{:S(2)}) %collective-permute-start.6) | collective-permute-done | bytes 131104 | tf_op jit(solution)/shard_map/ppermute | solution.py:274
  123.2 1.3 %unpack.1 = (bf16[256,1280]{1,0:T(8,128)(2,1)}, bf16[256,1280]{1,0:T(8,128)(2,1)}) custom-call(s32[1]{0:T(128)} %bitcast.row_ref.par_ref, bf16[8,256,256]{2,1,0:T(8,128)(2,1)S(1)} %all-to-all-done.2.mine, bf16[256,256]{1,0:T(8,128)(2,1)S(1)} %collective-permute-done.5.own, bf16[256,256]{1,0:T(8,128)(2,1)S(1)} %collective-permute-done.6.other), custom_call_target="tpu_custom_call" | custom-call | tf_op jit(solution)/shard_map/unpack/pallas_call | solution.py:366
  (3 shorter events, 0.0 us)
Async XLA Ops:
  0.6 0.7 copy-start
  4.8 50.2 %all-to-all-start = ((bf16[8,264,768]{2,1,0:T(8,128)(2,1)}), bf16[8,264,768]{2,1,0:T(8,128)(2,1)S(1)}, u32[]{:S(2)}, u32[]{:S(2)}) async-start(bf16[8,264,768]{2,1,0:T(8,128)(2,1)} %cut_plane.1), calls=%async_computation | async-start | bytes 6488064 | tf_op jit(solution)/shard_map/all_to_all | solution.py:283
  15.0 37.9 %collective-permute-start = (bf16[256,256]{1,0:T(8,128)(2,1)S(1)}, bf16[256,256]{1,0:T(8,128)(2,1)S(1)}, u32[]{:S(2)}, u32[]{:S(2)}) collective-permute-start(bf16[256,256]{1,0:T(8,128)(2,1)S(1)} %get-tuple-element.15), channel_id=1, source_target_pairs={{0,0},{1,17},{2,2},{3,19},{4,4},{5,21},{6,6},{7,23},{8,8},{9,25},{... | collective-permute-start | bytes 393224 | tf_op jit(solution)/shard_map/ppermute | solution.py:274
  19.9 35.1 %collective-permute-start.1 = (bf16[256,256]{1,0:T(8,128)(2,1)S(1)}, bf16[256,256]{1,0:T(8,128)(2,1)S(1)}, u32[]{:S(2)}, u32[]{:S(2)}) collective-permute-start(bf16[256,256]{1,0:T(8,128)(2,1)S(1)} %get-tuple-element.16), channel_id=1, source_target_pairs={{0,4},{1,21},{2,6},{3,23},{4,0},{5,17},{6,2},{7,19},{8,12},{9,29},... | collective-permute-start | bytes 393224 | tf_op jit(solution)/shard_map/ppermute | solution.py:274
  56.3 22.6 %collective-permute-start.2 = (bf16[3,256,512]{2,1,0:T(8,128)(2,1)}, bf16[3,256,512]{2,1,0:T(8,128)(2,1)}, u32[]{:S(2)}, u32[]{:S(2)}) collective-permute-start(bf16[3,256,512]{2,1,0:T(8,128)(2,1)} %get-tuple-element.17), channel_id=1, source_target_pairs={{0,32},{4,36},{8,40},{12,44},{16,48},{20,52},{24,56},{28,60},{32,6... | collective-permute-start | bytes 2359304 | tf_op jit(solution)/shard_map/ppermute | solution.py:270
  57.9 20.9 %collective-permute-start.3 = (bf16[3,256,512]{2,1,0:T(8,128)(2,1)}, bf16[3,256,512]{2,1,0:T(8,128)(2,1)}, u32[]{:S(2)}, u32[]{:S(2)}) collective-permute-start(bf16[3,256,512]{2,1,0:T(8,128)(2,1)} %get-tuple-element.18), channel_id=1, source_target_pairs={{0,224},{4,228},{8,232},{12,236},{16,240},{20,244},{24,248},{28,25... | collective-permute-start | bytes 2359304 | tf_op jit(solution)/shard_map/ppermute | solution.py:270
  61.9 30.6 %all-to-all-start.1 = ((bf16[8,256,512]{2,1,0:T(8,128)(2,1)}), bf16[8,256,512]{2,1,0:T(8,128)(2,1)}, u32[]{:S(2)}, u32[]{:S(2)}) async-start(bf16[8,256,512]{2,1,0:T(8,128)(2,1)} %after.2), calls=%async_computation.1 | async-start | bytes 4194304 | tf_op jit(solution)/shard_map/all_to_all | solution.py:283
  94.2 11.2 %collective-permute-start.4 = (bf16[3,256,512]{2,1,0:T(8,128)(2,1)S(1)}, bf16[3,256,512]{2,1,0:T(8,128)(2,1)S(1)}, u32[]{:S(2)}, u32[]{:S(2)}) collective-permute-start(bf16[3,256,512]{2,1,0:T(8,128)(2,1)S(1)} %edge.1.refs_1_), channel_id=1, source_target_pairs={{0,32},{1,225},{2,34},{3,227},{4,36},{5,229},{6,38},{7,231},{8,40}... | collective-permute-start | bytes 2359304 | tf_op jit(solution)/shard_map/ppermute | solution.py:274
  96.2 21.4 %all-to-all-start.2 = ((bf16[8,256,256]{2,1,0:T(8,128)(2,1)}), bf16[8,256,256]{2,1,0:T(8,128)(2,1)S(1)}, u32[]{:S(2)}, u32[]{:S(2)}) async-start(bf16[8,256,256]{2,1,0:T(8,128)(2,1)} %after.3), calls=%async_computation.2 | async-start | bytes 2097152 | tf_op jit(solution)/shard_map/all_to_all | solution.py:283
  105.4 0.9 copy-start.1
  111.4 7.8 %collective-permute-start.5 = (bf16[256,256]{1,0:T(8,128)(2,1)S(1)}, bf16[256,256]{1,0:T(8,128)(2,1)S(1)}, u32[]{:S(2)}, u32[]{:S(2)}) collective-permute-start(bf16[256,256]{1,0:T(8,128)(2,1)S(1)} %get-tuple-element.26), channel_id=1, source_target_pairs={{0,0},{1,17},{2,2},{3,19},{4,4},{5,21},{6,6},{7,23},{8,8},{9,25},{... | collective-permute-start | bytes 393224 | tf_op jit(solution)/shard_map/ppermute | solution.py:274
  116.9 6.3 %collective-permute-start.6 = (bf16[256,256]{1,0:T(8,128)(2,1)S(1)}, bf16[256,256]{1,0:T(8,128)(2,1)S(1)}, u32[]{:S(2)}, u32[]{:S(2)}) collective-permute-start(bf16[256,256]{1,0:T(8,128)(2,1)S(1)} %get-tuple-element.27), channel_id=1, source_target_pairs={{0,4},{1,21},{2,6},{3,23},{4,0},{5,17},{6,2},{7,19},{8,12},{9,29},... | collective-permute-start | bytes 393224 | tf_op jit(solution)/shard_map/ppermute | solution.py:274

commit v8 on v7

--- a/solution.py
+++ b/solution.py
@@ -15,6 +15,8 @@
 CHUNKS = 2 * REACH + 1
 EXTRA = 8
 KV = 4 * HEAD_DIM
+EARLY = 4
+GATES = 3
 ALL = 6 * HEAD_DIM
 NEG = -1.0e30
 LOG2E = 1.4426950408889634
@@ -146,17 +148,10 @@
     lax.fori_loop(0, 2, step, 0)
 
 
-def outer_kernel(sel_ref, main, up, dn, mid, stats, first_ref, second_ref, o_ref, done, buf, sem, s_scr, p_scr, t_scr):
-    done[...] = jnp.zeros_like(done)
-    copies = []
-
-    def leave(i, value):
-        buf[i] = value
-        copies.append(pltpu.make_async_copy(buf.at[i], o_ref.at[i], sem.at[i]))
-        copies[-1].start()
-
+def outer_kernel(row_ref, sel_ref, main, up, dn, mid, stats, first_ref, second_ref, *rest):
+    outs, (buf, sem, s_scr, p_scr, t_scr) = rest[:PLANE], rest[PLANE:]
     for i in (3, 4):
-        leave(i, mid[i - REACH])
+        buf[i] = mid[i - REACH]
     for i in (0, 1, 2, 5, 6, 7):
         low = i < REACH
         halo, skip, at = (up, i, 0) if low else (dn, 0, PLANE + REACH - i)
@@ -171,9 +166,8 @@
             more = mix(p_scr.at[:, u * TOK:(u + 1) * TOK], t_scr.at[:, u * TOK:(u + 1) * TOK], TOK,
                        halo[skip + u, :, 2 * HEAD_DIM:])
             first, second = first + more[0], second + more[1]
-        leave(i, finish(stats[i, 1] * shrink + total, stats[i, 2] * shrink + tangent_total, first, second))
-    for copy in copies:
-        copy.wait()
+        buf[i] = finish(stats[i, 1] * shrink + total, stats[i, 2] * shrink + tangent_total, first, second)
+    run_copies([(buf.at[row_ref[0] ^ k], outs[k]) for k in range(PLANE)], sem)
 
 
 def edges_kernel(main, gate_a, gate_b, up, dn):
@@ -183,14 +177,15 @@
         dn[n] = main[n, :TOK, :KV]
 
 
-def edge_kernel(task_ref, main, gate, edge):
-    del gate
+def edge_kernel(task_ref, main, *rest):
+    edge = rest[-1]
     begin = jnp.where(task_ref[0] < PLANE // 2, PLANE - REACH, 0)
     for n in range(REACH):
         edge[n] = main[begin + n]
 
 
-def pair_kernel(task_ref, sel_ref, q_first, q_second, main, halo, o_first, o_second, kv, s_scr, p_scr, t_scr, sem):
+def pair_kernel(task_ref, sel_ref, q_first, q_second, main, halo, *rest):
+    o_first, o_second, kv, s_scr, p_scr, t_scr, sem = rest[GATES:]
     task = task_ref[0]
     begin = jnp.where(task < PLANE // 2, 0, REACH + PLANE)
     pairs = [(main.at[c], kv.at[pl.ds((c + REACH) * TOK, TOK), :]) for c in range(PLANE)]
@@ -221,14 +216,13 @@
     )(pltpu.with_memory_space_constraint(array, pltpu.HBM), *others)
 
 
-def unpack_kernel(par_ref, mine, own, other, o_ref, t_ref):
-    par = par_ref[0] % 2
-    for j in range(PLANE):
-        cols = pl.ds(j * HEAD_DIM, HEAD_DIM)
-        o_ref[:, cols] = mine[j, :, :HEAD_DIM]
-        t_ref[:, cols] = mine[j, :, HEAD_DIM:]
-    for which, piece in ((par, own), (1 - par, other)):
-        cols = pl.ds(pl.multiple_of((PLANE + which) * HEAD_DIM, HEAD_DIM), HEAD_DIM)
+def unpack_kernel(row_ref, *refs):
+    pieces, (own, other, o_ref, t_ref) = refs[:PLANE], refs[PLANE:]
+    row = row_ref[0]
+    heads = [(row ^ k, piece) for k, piece in enumerate(pieces)]
+    heads += [(PLANE + row % 2, own), (PLANE + 1 - row % 2, other)]
+    for head, piece in heads:
+        cols = pl.ds(pl.multiple_of(head * HEAD_DIM, HEAD_DIM), HEAD_DIM)
         o_ref[:, cols] = piece[:, :HEAD_DIM]
         t_ref[:, cols] = piece[:, HEAD_DIM:]
 
@@ -330,47 +324,47 @@
         cost_estimate=cost(2),
         name="inner",
     )(sel_all, main)
-    mine, done = pl.pallas_call(
+    mine = pl.pallas_call(
         outer_kernel,
-        out_shape=(pltpu.HBM((PLANE, TOK, 256), jnp.bfloat16), f32(8, BLK)),
-        in_specs=[SMEM_SPEC] + [VMEM_SPEC] * 7,
-        out_specs=(ANY_SPEC, VMEM_SPEC),
+        out_shape=(pltpu.HBM((TOK, 256), jnp.bfloat16),) * PLANE,
+        in_specs=[SMEM_SPEC] * 2 + [VMEM_SPEC] * 7,
+        out_specs=(ANY_SPEC,) * PLANE,
         scratch_shapes=[pltpu.VMEM((PLANE, TOK, 256), jnp.bfloat16), pltpu.SemaphoreType.DMA((PLANE,))] + scratch(REACH),
         compiler_params=params(16),
         cost_estimate=cost(276),
         name="outer",
-    )(sel_all, main, up, dn, mid, stats, first, second)
+    )(row, sel_all, main, up, dn, mid, stats, first, second)
+    back = [mine[0]] + [lax.ppermute(mine[k], "ctx", [(i, i ^ k) for i in range(devices)]) for k in range(1, PLANE)]
     edge = pl.pallas_call(
         edge_kernel,
         out_shape=bf16(REACH, TOK, KV),
-        in_specs=[SMEM_SPEC, VMEM_SPEC, ANY_SPEC],
+        in_specs=[SMEM_SPEC, VMEM_SPEC] + [ANY_SPEC] * EARLY,
         out_specs=VMEM_SPEC,
         compiler_params=params(4),
         name="edge",
-    )(task, rest, done)
+    )(task, rest, *back[1:1 + EARLY])
     halo = spread(edge, lambda i, core: (i + (PLANE if (i ^ (4 * core)) % PLANE < PLANE // 2 else -PLANE)) % devices)
-    back = exchange(after(mine, edge))
 
     own, lent = pl.pallas_call(
         pair_kernel,
         out_shape=(bf16(TOK, 256), bf16(TOK, 256)),
-        in_specs=[SMEM_SPEC] * 2 + [VMEM_SPEC] * 2 + [ANY_SPEC, HBM_SPEC],
+        in_specs=[SMEM_SPEC] * 2 + [VMEM_SPEC] * 2 + [ANY_SPEC, HBM_SPEC] + [ANY_SPEC] * GATES,
         out_specs=(VMEM_SPEC,) * 2,
         scratch_shapes=[pltpu.VMEM(((PLANE + 2 * REACH) * TOK, KV), jnp.bfloat16)] + scratch(CHUNKS) + [pltpu.SemaphoreType.DMA((PLANE + REACH,))],
         compiler_params=params(14),
         cost_estimate=cost(14),
         name="pair",
-    )(task, sel_all, q_first, q_second, rest, pltpu.with_memory_space_constraint(halo, pltpu.HBM))
+    )(task, sel_all, q_first, q_second, rest, pltpu.with_memory_space_constraint(halo, pltpu.HBM), *back[PLANE - GATES:])
     own, partner = to_first(own), to_second(lent)
 
     return pl.pallas_call(
         unpack_kernel,
         out_shape=(bf16(TOK, HEADS * HEAD_DIM), bf16(TOK, HEADS * HEAD_DIM)),
-        in_specs=[SMEM_SPEC] + [VMEM_SPEC] * 3,
+        in_specs=[SMEM_SPEC] + [VMEM_SPEC] * (PLANE + 2),
         out_specs=(VMEM_SPEC,) * 2,
         compiler_params=params(6),
         name="unpack",
-    )(row, back, own, partner)
+    )(row, *back, own, partner)
 
 
 def solution(mesh):

time: 125 us -> 133 us (1.064)
  starting transfers between devices: 35.6 us -> 41 us
  waiting for transfers between devices: 56.1 us -> 58 us
    ppermute x0 -> x7, waiting for transfers between devices: none -> 14.6 us  [body(): lax.ppermute(mine[k], 'ctx', [(i, i ^ k) for i in range(devices)])]
    ppermute x0 -> x7, starting transfers between devices: none -> 11.2 us  [body(): lax.ppermute(mine[k], 'ctx', [(i, i ^ k) for i in range(devices)])]
    all_to_all x3 -> x2, waiting for transfers between devices: 7.88 us -> 0.01 us  [exchange(): lax.all_to_all(array, 'ctx', 0, 0, axis_index_groups=planes, tiled=True)]
    ppermute x5, waiting for transfers between devices: 44.8 us -> 40.1 us  [spread(): return lax.ppermute(array, ('ctx', 'head'), pairs)]
    all_to_all x3 -> x2, starting transfers between devices: 15.8 us -> 11.8 us  [exchange(): lax.all_to_all(array, 'ctx', 0, 0, axis_index_groups=planes, tiled=True)]
    ppermute x5, starting transfers between devices: 14.2 us -> 12.3 us  [spread(): return lax.ppermute(array, ('ctx', 'head'), pairs)]
  transfers between devices with their start and end apart: 10 -> 16, of which waited for: 7 -> 10; matrix products, arithmetic and copies ran while one was open for 0% -> 0% of each run, Pallas kernels for 18% -> 14%
where the time goes in v8:
time: 133 us; the launch traced here: 132 us
  waiting for transfers between devices  58 us (44%)
  starting transfers between devices  41 us (31%)
  Pallas kernels  30.9 us (23%)
  local copies, waits for them, and re-layouts  1.66 us (1%)
    ppermute x5, waiting for transfers between devices, spread(): return lax.ppermute(array, ('ctx', 'head'), pairs)  40.1 us
    ppermute x7, waiting for transfers between devices, body(): lax.ppermute(mine[k], 'ctx', [(i, i ^ k) for i in range(devices)])  14.6 us
    ppermute x5, starting transfers between devices, spread(): return lax.ppermute(array, ('ctx', 'head'), pairs)  12.3 us
    all_to_all x2, starting transfers between devices, exchange(): lax.all_to_all(array, 'ctx', 0, 0, axis_index_groups=planes, tiled=True)  11.8 us
    ppermute x7, starting transfers between devices, body(): lax.ppermute(mine[k], 'ctx', [(i, i ^ k) for i in range(devices)])  11.2 us
    pallas_call x1, Pallas kernels, body(): pl.pallas_call(inner_kernel, out_shape=(bf16(2, TOK, 256), f32(PLANE, 3,...  9.19 us
    pallas_call x1, Pallas kernels, body(): pl.pallas_call(outer_kernel, out_shape=(pltpu.HBM((TOK, 256), jnp.bfloat1...  6.16 us
    ppermute x2, starting transfers between devices, send(): lax.ppermute(array, 'ctx', [(i, (i + by) % devices) for i in range(device...  5.58 us
  transfers between devices with their start and end apart: 16, of which 10 were waited for; matrix products, arithmetic and copies ran while one was open for 0% of the time, Pallas kernels for 14%

profile of v8, /device:TPU:1, one launch (start us, length us, event | category | flops | bytes accessed | tf_op | source)
XLA Modules:
  0.0 132.3 jit_solution(4767856492293891385)
XLA Ops:
  0.6 0.0 copy-start.1
  0.6 0.7 copy-done.1
  1.3 3.5 %cut_plane.1 = bf16[8,264,768]{2,1,0:T(8,128)(2,1)} custom-call(s32[2,14]{1,0:T(2,128)S(1)} %copy-done.1, bf16[256,1280]{1,0:T(8,128)(2,1)} %q.3, bf16[256,1280]{1,0:T(8,128)(2,1)} %qt.3, bf16[256,1280]{1,0:T(8,128)(2,1)} %k.3, bf16[256,1280]{1,0:T(8,128)(2,1)} %kt.3, bf16[256,1280]{1,0:T(8,128)(2,1)} %v.3, bf16[256,1280]{1,0:T(8,128)(2,1)} %vt.3), custom_call_target="tpu_custom_call" | custom-call | tf_op jit(solution)/shard_map/cut_plane/pallas_call | solution.py:281
  4.8 7.5 %all-to-all-start = ((bf16[8,264,768]{2,1,0:T(8,128)(2,1)}), bf16[8,264,768]{2,1,0:T(8,128)(2,1)S(1)}, u32[]{:S(2)}, u32[]{:S(2)}) async-start(bf16[8,264,768]{2,1,0:T(8,128)(2,1)} %cut_plane.1), calls=%async_computation | async-start | bytes 6488064 | tf_op jit(solution)/shard_map/all_to_all | solution.py:277
  12.3 2.7 %cut_pair.1 = (bf16[8,256,512]{2,1,0:T(8,128)(2,1)}, bf16[256,256]{1,0:T(8,128)(2,1)S(1)}, bf16[256,256]{1,0:T(8,128)(2,1)S(1)}) custom-call(s32[1]{0:T(128)} %bitcast.row_ref, bf16[256,1280]{1,0:T(8,128)(2,1)} %q.3, bf16[256,1280]{1,0:T(8,128)(2,1)} %qt.3, bf16[256,1280]{1,0:T(8,128)(2,1)} %k.3, bf16[256,1280]{1,0:T(8,128)(2,1)} %kt.3, ...), custom_call_target="tpu_custom_call" | custom-call | tf_op jit(solution)/shard_map/cut_pair/pallas_call | solution.py:291
  15.0 4.9 %collective-permute-start = (bf16[256,256]{1,0:T(8,128)(2,1)S(1)}, bf16[256,256]{1,0:T(8,128)(2,1)S(1)}, u32[]{:S(2)}, u32[]{:S(2)}) collective-permute-start(bf16[256,256]{1,0:T(8,128)(2,1)S(1)} %get-tuple-element.21), channel_id=1, source_target_pairs={{0,0},{1,17},{2,2},{3,19},{4,4},{5,21},{6,6},{7,23},{8,8},{9,25},{... | collective-permute-start | bytes 393224 | tf_op jit(solution)/shard_map/ppermute | solution.py:268
  19.9 1.3 collective-permute-start.1
  21.2 31.7 %collective-permute-done.gate_a.refs_2_.q_first = bf16[256,256]{1,0:T(8,128)(2,1)S(1)} collective-permute-done((bf16[256,256]{1,0:T(8,128)(2,1)S(1)}, bf16[256,256]{1,0:T(8,128)(2,1)S(1)}, u32[]{:S(2)}, u32[]{:S(2)}) %collective-permute-start) | collective-permute-done | bytes 131104 | tf_op jit(solution)/shard_map/ppermute | solution.py:268
  52.9 2.2 %collective-permute-done.1.gate_b.refs_3_.q_second = bf16[256,256]{1,0:T(8,128)(2,1)S(1)} collective-permute-done((bf16[256,256]{1,0:T(8,128)(2,1)S(1)}, bf16[256,256]{1,0:T(8,128)(2,1)S(1)}, u32[]{:S(2)}, u32[]{:S(2)}) %collective-permute-start.1) | collective-permute-done | bytes 131104 | tf_op jit(solution)/shard_map/ppermute | solution.py:268
  55.0 0.0 all-to-all-done.main
  55.0 1.3 edges.1
  56.3 1.6 %collective-permute-start.2 = (bf16[3,256,512]{2,1,0:T(8,128)(2,1)}, bf16[3,256,512]{2,1,0:T(8,128)(2,1)}, u32[]{:S(2)}, u32[]{:S(2)}) collective-permute-start(bf16[3,256,512]{2,1,0:T(8,128)(2,1)} %get-tuple-element.23), channel_id=1, source_target_pairs={{0,32},{4,36},{8,40},{12,44},{16,48},{20,52},{24,56},{28,60},{32,6... | collective-permute-start | bytes 2359304 | tf_op jit(solution)/shard_map/ppermute | solution.py:264
  57.9 3.9 %collective-permute-start.3 = (bf16[3,256,512]{2,1,0:T(8,128)(2,1)}, bf16[3,256,512]{2,1,0:T(8,128)(2,1)}, u32[]{:S(2)}, u32[]{:S(2)}) collective-permute-start(bf16[3,256,512]{2,1,0:T(8,128)(2,1)} %get-tuple-element.24), channel_id=1, source_target_pairs={{0,224},{4,228},{8,232},{12,236},{16,240},{20,244},{24,248},{28,25... | collective-permute-start | bytes 2359304 | tf_op jit(solution)/shard_map/ppermute | solution.py:264
  61.9 0.1 reshape.12.sel_ref.refs_1_
  62.0 4.3 %all-to-all-start.1 = ((bf16[8,256,512]{2,1,0:T(8,128)(2,1)}), bf16[8,256,512]{2,1,0:T(8,128)(2,1)}, u32[]{:S(2)}, u32[]{:S(2)}) async-start(bf16[8,256,512]{2,1,0:T(8,128)(2,1)} %after.1), calls=%async_computation.1 | async-start | bytes 4194304 | tf_op jit(solution)/shard_map/all_to_all | solution.py:277
  66.3 9.2 %inner.1 = (bf16[2,256,256]{2,1,0:T(8,128)(2,1)S(1)}, f32[8,3,256,128]{3,2,1,0:T(8,128)S(1)}, f32[8,256,256]{2,1,0:T(8,128)S(1)}, f32[8,256,128]{2,1,0:T(8,128)S(1)}) custom-call(s32[8,28]{1,0:T(8,128)S(1)} %reshape.12.sel_ref.refs_1_, bf16[8,264,768]{2,1,0:T(8,128)(2,1)S(1)} %all-to-all-done.main), custom_call_target="tpu_custom_call" | custom-call | flops 167772160 | bytes 524288 | tf_op jit(solution)/shard_map/inner/pallas_call | solution.py:317
  75.5 3.3 %collective-permute-done.2.up = bf16[3,256,512]{2,1,0:T(8,128)(2,1)} collective-permute-done((bf16[3,256,512]{2,1,0:T(8,128)(2,1)}, bf16[3,256,512]{2,1,0:T(8,128)(2,1)}, u32[]{:S(2)}, u32[]{:S(2)}) %collective-permute-start.2) | collective-permute-done | bytes 786464 | tf_op jit(solution)/shard_map/ppermute | solution.py:264
  78.9 0.0 collective-permute-done.3.dn
  78.9 6.2 %outer.1 = (bf16[256,256]{1,0:T(8,128)(2,1)}, bf16[256,256]{1,0:T(8,128)(2,1)}, bf16[256,256]{1,0:T(8,128)(2,1)}, bf16[256,256]{1,0:T(8,128)(2,1)}, bf16[256,256...) custom-call(s32[1]{0:T(128)} %bitcast.row_ref, ...), custom_call_target="tpu_custom_call" | custom-call | flops 23152558080 | bytes 72351744 | tf_op jit(solution)/shard_map/outer/pallas_call | solution.py:327
  85.0 0.0 copy-start.5
  85.0 0.0 copy-start.4
  85.1 0.0 copy-start.3
  85.1 1.3 collective-permute-start.4
  86.4 2.7 %collective-permute-start.5 = (bf16[256,256]{1,0:T(8,128)(2,1)}, bf16[256,256]{1,0:T(8,128)(2,1)S(1)}, u32[]{:S(2)}, u32[]{:S(2)}) collective-permute-start(bf16[256,256]{1,0:T(8,128)(2,1)} %get-tuple-element.31), channel_id=1, source_target_pairs={{0,8},{4,12},{8,0},{12,4},{16,24},{20,28},{24,16},{28,20},{32,40},... | collective-permute-start | bytes 393224 | tf_op jit(solution)/shard_map/ppermute | solution.py:337
  89.1 0.0 collective-permute-start.6
  89.1 1.0 collective-permute-start.7
  90.1 0.0 copy-start
  90.1 4.2 %collective-permute-done.4.rest_0_.refs_1_ = bf16[256,256]{1,0:T(8,128)(2,1)S(1)} collective-permute-done((bf16[256,256]{1,0:T(8,128)(2,1)}, bf16[256,256]{1,0:T(8,128)(2,1)S(1)}, u32[]{:S(2)}, u32[]{:S(2)}) %collective-permute-start.4) | collective-permute-done | bytes 131104 | tf_op jit(solution)/shard_map/ppermute | solution.py:337
  94.3 3.9 %collective-permute-done.5.rest_1_.refs_2_ = bf16[256,256]{1,0:T(8,128)(2,1)S(1)} collective-permute-done((bf16[256,256]{1,0:T(8,128)(2,1)}, bf16[256,256]{1,0:T(8,128)(2,1)S(1)}, u32[]{:S(2)}, u32[]{:S(2)}) %collective-permute-start.5) | collective-permute-done | bytes 131104 | tf_op jit(solution)/shard_map/ppermute | solution.py:337
  98.2 0.0 collective-permute-done.6.rest_2_.refs_3_
  98.2 0.0 collective-permute-done.7.rest_3_.refs_4_
  98.2 0.0 all-to-all-done.1.main
  98.2 1.6 %edge.1 = bf16[3,256,512]{2,1,0:T(8,128)(2,1)S(1)} custom-call(s32[1]{0:T(128)S(6)} %xor.7.task_ref, bf16[8,256,512]{2,1,0:T(8,128)(2,1)} %all-to-all-done.1.main, bf16[256,256]{1,0:T(8,128)(2,1)S(1)} %collective-permute-done.4.rest_0_.refs_1_, bf16[256,256]{1,0:T(8,128)(2,1)S(1)} %collective-permute-done.5.rest_1_.refs_2_, ...), custom_call_target="tpu_custom_call" | custom-call | tf_op jit(solution)/shard_map/edge/pallas_call | solution.py:338
  99.8 2.5 %collective-permute-start.11 = (bf16[3,256,512]{2,1,0:T(8,128)(2,1)S(1)}, bf16[3,256,512]{2,1,0:T(8,128)(2,1)S(1)}, u32[]{:S(2)}, u32[]{:S(2)}) collective-permute-start(bf16[3,256,512]{2,1,0:T(8,128)(2,1)S(1)} %edge.1), channel_id=1, source_target_pairs={{0,32},{1,225},{2,34},{3,227},{4,36},{5,229},{6,38},{7,231},{8,40}... | collective-permute-start | bytes 2359304 | tf_op jit(solution)/shard_map/ppermute | solution.py:268
  102.3 0.0 copy-done.5
  102.3 0.5 collective-permute-start.8
  102.9 0.0 copy-done.4
  102.9 3.5 %collective-permute-start.9 = (bf16[256,256]{1,0:T(8,128)(2,1)S(1)}, bf16[256,256]{1,0:T(8,128)(2,1)S(1)}, u32[]{:S(2)}, u32[]{:S(2)}) collective-permute-start(bf16[256,256]{1,0:T(8,128)(2,1)S(1)} %copy-done.4), channel_id=1, source_target_pairs={{0,24},{4,28},{8,16},{12,20},{16,8},{20,12},{24,0},{28,4},{32,56},... | collective-permute-start | bytes 393224 | tf_op jit(solution)/shard_map/ppermute | solution.py:337
  106.3 0.0 copy-done.3
  106.3 2.3 %collective-permute-start.10 = (bf16[256,256]{1,0:T(8,128)(2,1)S(1)}, bf16[256,256]{1,0:T(8,128)(2,1)S(1)}, u32[]{:S(2)}, u32[]{:S(2)}) collective-permute-start(bf16[256,256]{1,0:T(8,128)(2,1)S(1)} %copy-done.3), channel_id=1, source_target_pairs={{0,28},{4,24},{8,20},{12,16},{16,12},{20,8},{24,4},{28,0},{32,60},... | collective-permute-start | bytes 393224 | tf_op jit(solution)/shard_map/ppermute | solution.py:337
  108.6 0.6 collective-permute-done.8.rest_0_.refs_5_
  109.1 1.4 %collective-permute-done.9.rest_1_.refs_6_ = bf16[256,256]{1,0:T(8,128)(2,1)S(1)} collective-permute-done((bf16[256,256]{1,0:T(8,128)(2,1)S(1)}, bf16[256,256]{1,0:T(8,128)(2,1)S(1)}, u32[]{:S(2)}, u32[]{:S(2)}) %collective-permute-start.9) | collective-permute-done | bytes 131104 | tf_op jit(solution)/shard_map/ppermute | solution.py:337
  110.6 4.5 %collective-permute-done.10.rest_2_.refs_7_ = bf16[256,256]{1,0:T(8,128)(2,1)S(1)} collective-permute-done((bf16[256,256]{1,0:T(8,128)(2,1)S(1)}, bf16[256,256]{1,0:T(8,128)(2,1)S(1)}, u32[]{:S(2)}, u32[]{:S(2)}) %collective-permute-start.10) | collective-permute-done | bytes 131104 | tf_op jit(solution)/shard_map/ppermute | solution.py:337
  115.1 0.0 collective-permute-done.11.halo
  115.1 0.0 copy-start.2
  115.1 0.9 copy-done.2
  116.0 5.1 %pair.1 = (bf16[256,256]{1,0:T(8,128)(2,1)S(1)}, bf16[256,256]{1,0:T(8,128)(2,1)S(1)}) custom-call(s32[1]{0:T(128)S(6)} %xor.7.task_ref, s32[8,28]{1,0:T(8,128)S(1)} %reshape.12.sel_ref.refs_1_, bf16[256,256]{1,0:T(8,128)(2,1)S(1)} %collective-permute-done.gate_a.refs_2_.q_first, bf16[256,256]{1,0:T(8,128)(2,1)S(1)} %collective-permute-done.1.gate_b.refs_3_.q_second, ...), custom_call_target="tpu_custom_call" | custom-call | flops 1174405120 | bytes 3670016 | tf_op jit(solution)/shard_map/pair/pallas_call | solution.py:348
  121.1 3.6 %collective-permute-start.12 = (bf16[256,256]{1,0:T(8,128)(2,1)S(1)}, bf16[256,256]{1,0:T(8,128)(2,1)S(1)}, u32[]{:S(2)}, u32[]{:S(2)}) collective-permute-start(bf16[256,256]{1,0:T(8,128)(2,1)S(1)} %get-tuple-element.38), channel_id=1, source_target_pairs={{0,0},{1,17},{2,2},{3,19},{4,4},{5,21},{6,6},{7,23},{8,8},{9,25},{... | collective-permute-start | bytes 393224 | tf_op jit(solution)/shard_map/ppermute | solution.py:268
  124.7 0.1 collective-permute-start.13
  124.8 3.5 %collective-permute-done.12.refs_8_ = bf16[256,256]{1,0:T(8,128)(2,1)S(1)} collective-permute-done((bf16[256,256]{1,0:T(8,128)(2,1)S(1)}, bf16[256,256]{1,0:T(8,128)(2,1)S(1)}, u32[]{:S(2)}, u32[]{:S(2)}) %collective-permute-start.12) | collective-permute-done | bytes 131104 | tf_op jit(solution)/shard_map/ppermute | solution.py:268
  128.3 2.7 %collective-permute-done.13.refs_9_ = bf16[256,256]{1,0:T(8,128)(2,1)S(1)} collective-permute-done((bf16[256,256]{1,0:T(8,128)(2,1)S(1)}, bf16[256,256]{1,0:T(8,128)(2,1)S(1)}, u32[]{:S(2)}, u32[]{:S(2)}) %collective-permute-start.13) | collective-permute-done | bytes 131104 | tf_op jit(solution)/shard_map/ppermute | solution.py:268
  131.0 0.0 copy-done
  131.0 1.3 unpack.1
  (2 shorter events, 0.0 us)
Async XLA Ops:
  0.6 0.7 copy-start.1
  4.8 50.2 %all-to-all-start = ((bf16[8,264,768]{2,1,0:T(8,128)(2,1)}), bf16[8,264,768]{2,1,0:T(8,128)(2,1)S(1)}, u32[]{:S(2)}, u32[]{:S(2)}) async-start(bf16[8,264,768]{2,1,0:T(8,128)(2,1)} %cut_plane.1), calls=%async_computation | async-start | bytes 6488064 | tf_op jit(solution)/shard_map/all_to_all | solution.py:277
  15.0 37.8 %collective-permute-start = (bf16[256,256]{1,0:T(8,128)(2,1)S(1)}, bf16[256,256]{1,0:T(8,128)(2,1)S(1)}, u32[]{:S(2)}, u32[]{:S(2)}) collective-permute-start(bf16[256,256]{1,0:T(8,128)(2,1)S(1)} %get-tuple-element.21), channel_id=1, source_target_pairs={{0,0},{1,17},{2,2},{3,19},{4,4},{5,21},{6,6},{7,23},{8,8},{9,25},{... | collective-permute-start | bytes 393224 | tf_op jit(solution)/shard_map/ppermute | solution.py:268
  19.9 35.1 %collective-permute-start.1 = (bf16[256,256]{1,0:T(8,128)(2,1)S(1)}, bf16[256,256]{1,0:T(8,128)(2,1)S(1)}, u32[]{:S(2)}, u32[]{:S(2)}) collective-permute-start(bf16[256,256]{1,0:T(8,128)(2,1)S(1)} %get-tuple-element.22), channel_id=1, source_target_pairs={{0,4},{1,21},{2,6},{3,23},{4,0},{5,17},{6,2},{7,19},{8,12},{9,29},... | collective-permute-start | bytes 393224 | tf_op jit(solution)/shard_map/ppermute | solution.py:268
  56.3 22.6 %collective-permute-start.2 = (bf16[3,256,512]{2,1,0:T(8,128)(2,1)}, bf16[3,256,512]{2,1,0:T(8,128)(2,1)}, u32[]{:S(2)}, u32[]{:S(2)}) collective-permute-start(bf16[3,256,512]{2,1,0:T(8,128)(2,1)} %get-tuple-element.23), channel_id=1, source_target_pairs={{0,32},{4,36},{8,40},{12,44},{16,48},{20,52},{24,56},{28,60},{32,6... | collective-permute-start | bytes 2359304 | tf_op jit(solution)/shard_map/ppermute | solution.py:264
  57.9 20.9 %collective-permute-start.3 = (bf16[3,256,512]{2,1,0:T(8,128)(2,1)}, bf16[3,256,512]{2,1,0:T(8,128)(2,1)}, u32[]{:S(2)}, u32[]{:S(2)}) collective-permute-start(bf16[3,256,512]{2,1,0:T(8,128)(2,1)} %get-tuple-element.24), channel_id=1, source_target_pairs={{0,224},{4,228},{8,232},{12,236},{16,240},{20,244},{24,248},{28,25... | collective-permute-start | bytes 2359304 | tf_op jit(solution)/shard_map/ppermute | solution.py:264
  62.0 36.2 %all-to-all-start.1 = ((bf16[8,256,512]{2,1,0:T(8,128)(2,1)}), bf16[8,256,512]{2,1,0:T(8,128)(2,1)}, u32[]{:S(2)}, u32[]{:S(2)}) async-start(bf16[8,256,512]{2,1,0:T(8,128)(2,1)} %after.1), calls=%async_computation.1 | async-start | bytes 4194304 | tf_op jit(solution)/shard_map/all_to_all | solution.py:277
  85.0 17.3 %copy-start.5 = (bf16[256,256]{1,0:T(8,128)(2,1)S(1)}, bf16[256,256]{1,0:T(8,128)(2,1)}, u32[]{:S(2)}) copy-start(bf16[256,256]{1,0:T(8,128)(2,1)} %get-tuple-element.34) | copy-start | bytes 393220
  85.0 17.8 %copy-start.4 = (bf16[256,256]{1,0:T(8,128)(2,1)S(1)}, bf16[256,256]{1,0:T(8,128)(2,1)}, u32[]{:S(2)}) copy-start(bf16[256,256]{1,0:T(8,128)(2,1)} %get-tuple-element.35) | copy-start | bytes 393220
  85.1 21.3 %copy-start.3 = (bf16[256,256]{1,0:T(8,128)(2,1)S(1)}, bf16[256,256]{1,0:T(8,128)(2,1)}, u32[]{:S(2)}) copy-start(bf16[256,256]{1,0:T(8,128)(2,1)} %get-tuple-element.36) | copy-start | bytes 393220
  85.1 9.2 %collective-permute-start.4 = (bf16[256,256]{1,0:T(8,128)(2,1)}, bf16[256,256]{1,0:T(8,128)(2,1)S(1)}, u32[]{:S(2)}, u32[]{:S(2)}) collective-permute-start(bf16[256,256]{1,0:T(8,128)(2,1)} %get-tuple-element.30), channel_id=1, source_target_pairs={{0,4},{4,0},{8,12},{12,8},{16,20},{20,16},{24,28},{28,24},{32,36},... | collective-permute-start | bytes 393224 | tf_op jit(solution)/shard_map/ppermute | solution.py:337
  86.4 11.8 %collective-permute-start.5 = (bf16[256,256]{1,0:T(8,128)(2,1)}, bf16[256,256]{1,0:T(8,128)(2,1)S(1)}, u32[]{:S(2)}, u32[]{:S(2)}) collective-permute-start(bf16[256,256]{1,0:T(8,128)(2,1)} %get-tuple-element.31), channel_id=1, source_target_pairs={{0,8},{4,12},{8,0},{12,4},{16,24},{20,28},{24,16},{28,20},{32,40},... | collective-permute-start | bytes 393224 | tf_op jit(solution)/shard_map/ppermute | solution.py:337
  89.1 9.1 %collective-permute-start.6 = (bf16[256,256]{1,0:T(8,128)(2,1)}, bf16[256,256]{1,0:T(8,128)(2,1)S(1)}, u32[]{:S(2)}, u32[]{:S(2)}) collective-permute-start(bf16[256,256]{1,0:T(8,128)(2,1)} %get-tuple-element.32), channel_id=1, source_target_pairs={{0,12},{4,8},{8,4},{12,0},{16,28},{20,24},{24,20},{28,16},{32,44},... | collective-permute-start | bytes 393224 | tf_op jit(solution)/shard_map/ppermute | solution.py:337
  89.1 9.1 %collective-permute-start.7 = (bf16[256,256]{1,0:T(8,128)(2,1)}, bf16[256,256]{1,0:T(8,128)(2,1)S(1)}, u32[]{:S(2)}, u32[]{:S(2)}) collective-permute-start(bf16[256,256]{1,0:T(8,128)(2,1)} %get-tuple-element.33), channel_id=1, source_target_pairs={{0,16},{4,20},{8,24},{12,28},{16,0},{20,4},{24,8},{28,12},{32,48},... | collective-permute-start | bytes 393224 | tf_op jit(solution)/shard_map/ppermute | solution.py:337
  90.1 40.9 %copy-start = (bf16[256,256]{1,0:T(8,128)(2,1)S(1)}, bf16[256,256]{1,0:T(8,128)(2,1)}, u32[]{:S(2)}) copy-start(bf16[256,256]{1,0:T(8,128)(2,1)} %get-tuple-element.29.refs_0_) | copy-start | bytes 393220
  99.8 15.2 %collective-permute-start.11 = (bf16[3,256,512]{2,1,0:T(8,128)(2,1)S(1)}, bf16[3,256,512]{2,1,0:T(8,128)(2,1)S(1)}, u32[]{:S(2)}, u32[]{:S(2)}) collective-permute-start(bf16[3,256,512]{2,1,0:T(8,128)(2,1)S(1)} %edge.1), channel_id=1, source_target_pairs={{0,32},{1,225},{2,34},{3,227},{4,36},{5,229},{6,38},{7,231},{8,40}... | collective-permute-start | bytes 2359304 | tf_op jit(solution)/shard_map/ppermute | solution.py:268
  102.3 6.8 %collective-permute-start.8 = (bf16[256,256]{1,0:T(8,128)(2,1)S(1)}, bf16[256,256]{1,0:T(8,128)(2,1)S(1)}, u32[]{:S(2)}, u32[]{:S(2)}) collective-permute-start(bf16[256,256]{1,0:T(8,128)(2,1)S(1)} %copy-done.5), channel_id=1, source_target_pairs={{0,20},{4,16},{8,28},{12,24},{16,4},{20,0},{24,12},{28,8},{32,52},... | collective-permute-start | bytes 393224 | tf_op jit(solution)/shard_map/ppermute | solution.py:337
  102.9 7.7 %collective-permute-start.9 = (bf16[256,256]{1,0:T(8,128)(2,1)S(1)}, bf16[256,256]{1,0:T(8,128)(2,1)S(1)}, u32[]{:S(2)}, u32[]{:S(2)}) collective-permute-start(bf16[256,256]{1,0:T(8,128)(2,1)S(1)} %copy-done.4), channel_id=1, source_target_pairs={{0,24},{4,28},{8,16},{12,20},{16,8},{20,12},{24,0},{28,4},{32,56},... | collective-permute-start | bytes 393224 | tf_op jit(solution)/shard_map/ppermute | solution.py:337
  106.3 8.7 %collective-permute-start.10 = (bf16[256,256]{1,0:T(8,128)(2,1)S(1)}, bf16[256,256]{1,0:T(8,128)(2,1)S(1)}, u32[]{:S(2)}, u32[]{:S(2)}) collective-permute-start(bf16[256,256]{1,0:T(8,128)(2,1)S(1)} %copy-done.3), channel_id=1, source_target_pairs={{0,28},{4,24},{8,20},{12,16},{16,12},{20,8},{24,4},{28,0},{32,60},... | collective-permute-start | bytes 393224 | tf_op jit(solution)/shard_map/ppermute | solution.py:337
  115.1 0.9 copy-start.2
  121.1 7.2 %collective-permute-start.12 = (bf16[256,256]{1,0:T(8,128)(2,1)S(1)}, bf16[256,256]{1,0:T(8,128)(2,1)S(1)}, u32[]{:S(2)}, u32[]{:S(2)}) collective-permute-start(bf16[256,256]{1,0:T(8,128)(2,1)S(1)} %get-tuple-element.38), channel_id=1, source_target_pairs={{0,0},{1,17},{2,2},{3,19},{4,4},{5,21},{6,6},{7,23},{8,8},{9,25},{... | collective-permute-start | bytes 393224 | tf_op jit(solution)/shard_map/ppermute | solution.py:268
  124.7 6.3 %collective-permute-start.13 = (bf16[256,256]{1,0:T(8,128)(2,1)S(1)}, bf16[256,256]{1,0:T(8,128)(2,1)S(1)}, u32[]{:S(2)}, u32[]{:S(2)}) collective-permute-start(bf16[256,256]{1,0:T(8,128)(2,1)S(1)} %get-tuple-element.39), channel_id=1, source_target_pairs={{0,4},{1,21},{2,6},{3,23},{4,0},{5,17},{6,2},{7,19},{8,12},{9,29},... | collective-permute-start | bytes 393224 | tf_op jit(solution)/shard_map/ppermute | solution.py:268

commit v9 on v7

--- a/solution.py
+++ b/solution.py
@@ -11,6 +11,7 @@
 REACH = 3
 TOK = 256
 WIN = 14
+BPD = 2
 PLANE = 8
 CHUNKS = 2 * REACH + 1
 EXTRA = 8
@@ -40,7 +41,7 @@
     return pl.ds(n * HEAD_DIM, HEAD_DIM)
 
 
-def cut_plane_kernel(sel, q, qt, k, kt, v, vt, out, buf, in_sem, out_sem):
+def cut_plane_kernel(sel, q, qt, k, kt, v, vt, out, buf, sel_buf, sel_sem, in_sem, out_sem):
     arrays = (k, kt, v, vt, qt, q)
     ins = [[pltpu.make_async_copy(ref.at[:, lanes(j)], buf.at[j, 0:TOK, lanes(n)], in_sem.at[j, n])
             for n, ref in enumerate(arrays)] for j in range(PLANE)]
@@ -48,7 +49,8 @@
     for chunk in ins:
         for copy in chunk:
             copy.start()
-    listed = sel[...].astype(jnp.float32).astype(jnp.bfloat16)
+    run_copies([(sel, sel_buf)], sel_sem)
+    listed = sel_buf[...].astype(jnp.float32).astype(jnp.bfloat16)
     for j in range(PLANE):
         buf[j, TOK:TOK + 2, :WIN] = listed
         for copy in ins[j]:
@@ -176,18 +178,16 @@
         copy.wait()
 
 
-def edges_kernel(main, gate_a, gate_b, up, dn):
+def edges_kernel(main, gate_a, gate_b, up, dn, sem):
     del gate_a, gate_b
-    for n in range(REACH):
-        up[n] = main[PLANE - REACH + n, :TOK, :KV]
-        dn[n] = main[n, :TOK, :KV]
-
-
-def edge_kernel(task_ref, main, gate, edge):
+    run_copies([(main.at[first + n, 0:TOK, 0:KV], to.at[n]) for first, to in ((PLANE - REACH, up), (0, dn))
+                for n in range(REACH)], sem)
+
+
+def edge_kernel(task_ref, main, gate, edge, sem):
     del gate
     begin = jnp.where(task_ref[0] < PLANE // 2, PLANE - REACH, 0)
-    for n in range(REACH):
-        edge[n] = main[begin + n]
+    run_copies([(main.at[begin + n], edge.at[n]) for n in range(REACH)], sem)
 
 
 def pair_kernel(task_ref, sel_ref, q_first, q_second, main, halo, o_first, o_second, kv, s_scr, p_scr, t_scr, sem):
@@ -287,13 +287,14 @@
     plane_out = pl.pallas_call(
         cut_plane_kernel,
         out_shape=pltpu.HBM((PLANE, TOK + EXTRA, ALL), jnp.bfloat16),
-        in_specs=[VMEM_SPEC] + [HBM_SPEC] * 6,
+        in_specs=[HBM_SPEC] * 7,
         out_specs=ANY_SPEC,
         scratch_shapes=[pltpu.VMEM((PLANE, TOK + EXTRA, ALL), jnp.bfloat16),
+                        pltpu.VMEM((BPD, WIN), jnp.int32), pltpu.SemaphoreType.DMA((1,)),
                         pltpu.SemaphoreType.DMA((PLANE, 6)), pltpu.SemaphoreType.DMA((PLANE,))],
         compiler_params=params(8),
         name="cut_plane",
-    )(selection, *wide)
+    )(pltpu.with_memory_space_constraint(selection, pltpu.HBM), *wide)
     rest_out, q_same, q_opp = pl.pallas_call(
         cut_pair_kernel,
         out_shape=(pltpu.HBM((PLANE, TOK, KV), jnp.bfloat16), bf16(TOK, 256), bf16(TOK, 256)),
@@ -311,14 +312,15 @@
     sel_all = main[:, TOK:TOK + 2, :WIN].astype(jnp.int32).reshape(PLANE, 2 * WIN)
     edge_up, edge_dn = pl.pallas_call(
         edges_kernel,
-        out_shape=(bf16(REACH, TOK, KV),) * 2,
-        in_specs=[VMEM_SPEC] + [ANY_SPEC] * 2,
-        out_specs=(VMEM_SPEC,) * 2,
-        compiler_params=params(4),
+        out_shape=(pltpu.HBM((REACH, TOK, KV), jnp.bfloat16),) * 2,
+        in_specs=[ANY_SPEC] * 3,
+        out_specs=(ANY_SPEC,) * 2,
+        scratch_shapes=[pltpu.SemaphoreType.DMA((2 * REACH,))],
+        compiler_params=params(1),
         name="edges",
     )(main, q_first, q_second)
     up, dn = send(edge_up, PLANE), send(edge_dn, -PLANE)
-    rest = exchange(after(rest_out, sel_all, q_first, q_second))
+    rest = exchange(after(rest_out, sel_all, edge_up))
 
     mid, stats, first, second = pl.pallas_call(
         inner_kernel,
@@ -327,7 +329,7 @@
         out_specs=(VMEM_SPEC,) * 4,
         scratch_shapes=[pltpu.VMEM((PLANE * TOK, 2 * HEAD_DIM), jnp.bfloat16)] + scratch(CHUNKS),
         compiler_params=params(16),
-        cost_estimate=cost(2),
+        cost_estimate=cost(44),
         name="inner",
     )(sel_all, main)
     mine, done = pl.pallas_call(
@@ -337,15 +339,16 @@
         out_specs=(ANY_SPEC, VMEM_SPEC),
         scratch_shapes=[pltpu.VMEM((PLANE, TOK, 256), jnp.bfloat16), pltpu.SemaphoreType.DMA((PLANE,))] + scratch(REACH),
         compiler_params=params(16),
-        cost_estimate=cost(276),
+        cost_estimate=cost(12),
         name="outer",
     )(sel_all, main, up, dn, mid, stats, first, second)
     edge = pl.pallas_call(
         edge_kernel,
         out_shape=bf16(REACH, TOK, KV),
-        in_specs=[SMEM_SPEC, VMEM_SPEC, ANY_SPEC],
-        out_specs=VMEM_SPEC,
-        compiler_params=params(4),
+        in_specs=[SMEM_SPEC, ANY_SPEC, ANY_SPEC],
+        out_specs=ANY_SPEC,
+        scratch_shapes=[pltpu.SemaphoreType.DMA((REACH,))],
+        compiler_params=params(1),
         name="edge",
     )(task, rest, done)
     halo = spread(edge, lambda i, core: (i + (PLANE if (i ^ (4 * core)) % PLANE < PLANE // 2 else -PLANE)) % devices)

time: 125 us -> 127 us (1.016)
  starting transfers between devices: 35.6 us -> 38.3 us
  waiting for transfers between devices: 56.1 us -> 53.8 us
  Pallas kernels: 30.5 us -> 32 us
    ppermute x5, waiting for transfers between devices: 44.8 us -> 13.8 us  [spread(): return lax.ppermute(array, ('ctx', 'head'), pairs)]
    all_to_all x3, waiting for transfers between devices: 7.88 us -> 28.9 us  [exchange(): lax.all_to_all(array, 'ctx', 0, 0, axis_index_groups=planes, tiled=True)]
    ppermute x2, waiting for transfers between devices: 3.36 us -> 11 us  [send(): lax.ppermute(array, 'ctx', [(i, (i + by) % devices) for i in range(device...]
    all_to_all x3, starting transfers between devices: 15.8 us -> 18.9 us  [exchange(): lax.all_to_all(array, 'ctx', 0, 0, axis_index_groups=planes, tiled=True)]
  transfers between devices with their start and end apart: 10 -> 10, of which waited for: 7 -> 8; matrix products, arithmetic and copies ran while one was open for 0% -> 0% of each run, Pallas kernels for 18% -> 19%
where the time goes in v9:
time: 127 us; the launch traced here: 126 us
  waiting for transfers between devices  53.8 us (42%)
  starting transfers between devices  38.3 us (30%)
  Pallas kernels  32 us (25%)
    all_to_all x3, waiting for transfers between devices, exchange(): lax.all_to_all(array, 'ctx', 0, 0, axis_index_groups=planes, tiled=True)  28.9 us
    all_to_all x3, starting transfers between devices, exchange(): lax.all_to_all(array, 'ctx', 0, 0, axis_index_groups=planes, tiled=True)  18.9 us
    ppermute x5, waiting for transfers between devices, spread(): return lax.ppermute(array, ('ctx', 'head'), pairs)  13.8 us
    ppermute x5, starting transfers between devices, spread(): return lax.ppermute(array, ('ctx', 'head'), pairs)  13.7 us
    ppermute x2, waiting for transfers between devices, send(): lax.ppermute(array, 'ctx', [(i, (i + by) % devices) for i in range(device...  11 us
    pallas_call x1, Pallas kernels, body(): pl.pallas_call(inner_kernel, out_shape=(bf16(2, TOK, 256), f32(PLANE, 3,...  9.18 us
    pallas_call x1, Pallas kernels, body(): pl.pallas_call(outer_kernel, out_shape=(pltpu.HBM((PLANE, TOK, 256), jnp....  5.85 us
    pallas_call x1, Pallas kernels, body(): pl.pallas_call(pair_kernel, out_shape=(bf16(TOK, 256), bf16(TOK, 256)), i...  5.79 us
  transfers between devices with their start and end apart: 10, of which 8 were waited for; matrix products, arithmetic and copies ran while one was open for 0% of the time, Pallas kernels for 19%

profile of v9, /device:TPU:1, one launch (start us, length us, event | category | flops | bytes accessed | tf_op | source)
XLA Modules:
  0.0 125.9 jit_solution(4681978237879392457)
XLA Ops:
  0.6 4.1 %cut_plane.1 = bf16[8,264,768]{2,1,0:T(8,128)(2,1)} custom-call(s32[2,14]{1,0:T(2,128)} %sel.1, bf16[256,1280]{1,0:T(8,128)(2,1)} %q.3, bf16[256,1280]{1,0:T(8,128)(2,1)} %qt.3, bf16[256,1280]{1,0:T(8,128)(2,1)} %k.3, bf16[256,1280]{1,0:T(8,128)(2,1)} %kt.3, bf16[256,1280]{1,0:T(8,128)(2,1)} %v.3, bf16[256,1280]{1,0:T(8,128)(2,1)} %vt.3), custom_call_target="tpu_custom_call" | custom-call | tf_op jit(solution)/shard_map/cut_plane/pallas_call | solution.py:287
  4.7 7.5 %all-to-all-start = ((bf16[8,264,768]{2,1,0:T(8,128)(2,1)}), bf16[8,264,768]{2,1,0:T(8,128)(2,1)S(1)}, u32[]{:S(2)}, u32[]{:S(2)}) async-start(bf16[8,264,768]{2,1,0:T(8,128)(2,1)} %cut_plane.1), calls=%async_computation | async-start | bytes 6488064 | tf_op jit(solution)/shard_map/all_to_all | solution.py:283
  12.2 3.4 %cut_pair.1 = (bf16[8,256,512]{2,1,0:T(8,128)(2,1)}, bf16[256,256]{1,0:T(8,128)(2,1)}, bf16[256,256]{1,0:T(8,128)(2,1)}) custom-call(s32[1]{0:T(128)} %bitcast.row_ref.par_ref, bf16[256,1280]{1,0:T(8,128)(2,1)} %q.3, bf16[256,1280]{1,0:T(8,128)(2,1)} %qt.3, bf16[256,1280]{1,0:T(8,128)(2,1)} %k.3, bf16[256,1280]{1,0:T(8,128)(2,1)} %kt.3, ...), custom_call_target="tpu_custom_call" | custom-call | tf_op jit(solution)/shard_map/cut_pair/pallas_call | solution.py:298
  15.6 4.9 %collective-permute-start = (bf16[256,256]{1,0:T(8,128)(2,1)}, bf16[256,256]{1,0:T(8,128)(2,1)S(1)}, u32[]{:S(2)}, u32[]{:S(2)}) collective-permute-start(bf16[256,256]{1,0:T(8,128)(2,1)} %get-tuple-element.15), channel_id=1, source_target_pairs={{0,0},{1,17},{2,2},{3,19},{4,4},{5,21},{6,6},{7,23},{8,8},{9,25},{... | collective-permute-start | bytes 393224 | tf_op jit(solution)/shard_map/ppermute | solution.py:274
  20.5 1.3 %collective-permute-start.1 = (bf16[256,256]{1,0:T(8,128)(2,1)}, bf16[256,256]{1,0:T(8,128)(2,1)S(1)}, u32[]{:S(2)}, u32[]{:S(2)}) collective-permute-start(bf16[256,256]{1,0:T(8,128)(2,1)} %get-tuple-element.16), channel_id=1, source_target_pairs={{0,4},{1,21},{2,6},{3,23},{4,0},{5,17},{6,2},{7,19},{8,12},{9,29},... | collective-permute-start | bytes 393224 | tf_op jit(solution)/shard_map/ppermute | solution.py:274
  21.8 28.9 %all-to-all-done.main = bf16[8,264,768]{2,1,0:T(8,128)(2,1)S(1)} async-done(((bf16[8,264,768]{2,1,0:T(8,128)(2,1)}), bf16[8,264,768]{2,1,0:T(8,128)(2,1)S(1)}, u32[]{:S(2)}, u32[]{:S(2)}) %all-to-all-start) | async-done | bytes 3244064 | tf_op jit(solution)/shard_map/all_to_all | solution.py:283
  50.7 0.1 reshape.12.sel_ref.refs_1_
  50.7 2.0 %collective-permute-done.gate_a.q_first = bf16[256,256]{1,0:T(8,128)(2,1)S(1)} collective-permute-done((bf16[256,256]{1,0:T(8,128)(2,1)}, bf16[256,256]{1,0:T(8,128)(2,1)S(1)}, u32[]{:S(2)}, u32[]{:S(2)}) %collective-permute-start) | collective-permute-done | bytes 131104 | tf_op jit(solution)/shard_map/ppermute | solution.py:274
  52.8 2.2 %collective-permute-done.1.gate_b.q_second = bf16[256,256]{1,0:T(8,128)(2,1)S(1)} collective-permute-done((bf16[256,256]{1,0:T(8,128)(2,1)}, bf16[256,256]{1,0:T(8,128)(2,1)S(1)}, u32[]{:S(2)}, u32[]{:S(2)}) %collective-permute-start.1) | collective-permute-done | bytes 131104 | tf_op jit(solution)/shard_map/ppermute | solution.py:274
  54.9 1.3 edges.1
  56.2 0.0 copy-start
  56.2 1.1 copy-done
  57.3 4.3 %all-to-all-start.1 = ((bf16[8,256,512]{2,1,0:T(8,128)(2,1)}), bf16[8,256,512]{2,1,0:T(8,128)(2,1)}, u32[]{:S(2)}, u32[]{:S(2)}) async-start(bf16[8,256,512]{2,1,0:T(8,128)(2,1)} %after.2), calls=%async_computation.1 | async-start | bytes 4194304 | tf_op jit(solution)/shard_map/all_to_all | solution.py:283
  61.7 5.7 %collective-permute-start.3 = (bf16[3,256,512]{2,1,0:T(8,128)(2,1)}, bf16[3,256,512]{2,1,0:T(8,128)(2,1)}, u32[]{:S(2)}, u32[]{:S(2)}) collective-permute-start(bf16[3,256,512]{2,1,0:T(8,128)(2,1)} %get-tuple-element.18), channel_id=1, source_target_pairs={{0,224},{4,228},{8,232},{12,236},{16,240},{20,244},{24,248},{28,25... | collective-permute-start | bytes 2359304 | tf_op jit(solution)/shard_map/ppermute | solution.py:270
  67.3 0.0 collective-permute-start.2
  67.3 9.2 %inner.1 = (bf16[2,256,256]{2,1,0:T(8,128)(2,1)S(1)}, f32[8,3,256,128]{3,2,1,0:T(8,128)S(1)}, f32[8,256,256]{2,1,0:T(8,128)S(1)}, f32[8,256,128]{2,1,0:T(8,128)S(1)}) custom-call(s32[8,28]{1,0:T(8,128)S(1)} %reshape.12.sel_ref.refs_1_, bf16[8,264,768]{2,1,0:T(8,128)(2,1)S(1)} %all-to-all-done.main), custom_call_target="tpu_custom_call" | custom-call | flops 3690987520 | bytes 11534336 | tf_op jit(solution)/shard_map/inner/pallas_call | solution.py:325
  76.5 7.6 %collective-permute-done.3.dn = bf16[3,256,512]{2,1,0:T(8,128)(2,1)} collective-permute-done((bf16[3,256,512]{2,1,0:T(8,128)(2,1)}, bf16[3,256,512]{2,1,0:T(8,128)(2,1)}, u32[]{:S(2)}, u32[]{:S(2)}) %collective-permute-start.3) | collective-permute-done | bytes 786464 | tf_op jit(solution)/shard_map/ppermute | solution.py:270
  84.1 3.4 %collective-permute-done.2.up = bf16[3,256,512]{2,1,0:T(8,128)(2,1)} collective-permute-done((bf16[3,256,512]{2,1,0:T(8,128)(2,1)}, bf16[3,256,512]{2,1,0:T(8,128)(2,1)}, u32[]{:S(2)}, u32[]{:S(2)}) %collective-permute-start.2) | collective-permute-done | bytes 786464 | tf_op jit(solution)/shard_map/ppermute | solution.py:270
  87.5 5.8 %outer.1 = (bf16[8,256,256]{2,1,0:T(8,128)(2,1)}, f32[8,128]{1,0:T(8,128)S(1)}) custom-call(s32[8,28]{1,0:T(8,128)S(1)} %reshape.12.sel_ref.refs_1_, bf16[8,264,768]{2,1,0:T(8,128)(2,1)S(1)} %all-to-all-done.main, bf16[3,256,512]{2,1,0:T(8,128)(2,1)} %collective-permute-done.2.up, bf16[3,256,512]{2,1,0:T(8,128)(2,1)} %collective-permute-done.3.dn, ...), custom_call_target="tpu_custom_call" | custom-call | flops 1006632960 | bytes 3145728 | tf_op jit(solution)/shard_map/outer/pallas_call | solution.py:335
  93.4 0.0 all-to-all-done.1.main
  93.4 1.1 edge.1.refs_1_
  94.6 0.1 collective-permute-start.4
  94.7 7.1 %all-to-all-start.2 = ((bf16[8,256,256]{2,1,0:T(8,128)(2,1)}), bf16[8,256,256]{2,1,0:T(8,128)(2,1)S(1)}, u32[]{:S(2)}, u32[]{:S(2)}) async-start(bf16[8,256,256]{2,1,0:T(8,128)(2,1)} %after.3), calls=%async_computation.2 | async-start | bytes 2097152 | tf_op jit(solution)/shard_map/all_to_all | solution.py:283
  101.8 4.1 %collective-permute-done.4.halo = bf16[3,256,512]{2,1,0:T(8,128)(2,1)} collective-permute-done((bf16[3,256,512]{2,1,0:T(8,128)(2,1)S(1)}, bf16[3,256,512]{2,1,0:T(8,128)(2,1)}, u32[]{:S(2)}, u32[]{:S(2)}) %collective-permute-start.4) | collective-permute-done | bytes 786464 | tf_op jit(solution)/shard_map/ppermute | solution.py:274
  105.9 5.8 %pair.1 = (bf16[256,256]{1,0:T(8,128)(2,1)}, bf16[256,256]{1,0:T(8,128)(2,1)}) custom-call(s32[1]{0:T(128)S(6)} %xor.7.task_ref, s32[8,28]{1,0:T(8,128)S(1)} %reshape.12.sel_ref.refs_1_, bf16[256,256]{1,0:T(8,128)(2,1)S(1)} %collective-permute-done.gate_a.q_first, bf16[256,256]{1,0:T(8,128)(2,1)S(1)} %collective-permute-done.1.gate_b.q_second, ...), custom_call_target="tpu_custom_call" | custom-call | flops 1174405120 | bytes 3670016 | tf_op jit(solution)/shard_map/pair/pallas_call | solution.py:357
  111.7 6.4 %collective-permute-start.5 = (bf16[256,256]{1,0:T(8,128)(2,1)}, bf16[256,256]{1,0:T(8,128)(2,1)S(1)}, u32[]{:S(2)}, u32[]{:S(2)}) collective-permute-start(bf16[256,256]{1,0:T(8,128)(2,1)} %get-tuple-element.26), channel_id=1, source_target_pairs={{0,0},{1,17},{2,2},{3,19},{4,4},{5,21},{6,6},{7,23},{8,8},{9,25},{... | collective-permute-start | bytes 393224 | tf_op jit(solution)/shard_map/ppermute | solution.py:274
  118.1 1.0 collective-permute-start.6
  119.1 0.0 all-to-all-done.2.mine
  119.1 1.6 %collective-permute-done.5.own = bf16[256,256]{1,0:T(8,128)(2,1)S(1)} collective-permute-done((bf16[256,256]{1,0:T(8,128)(2,1)}, bf16[256,256]{1,0:T(8,128)(2,1)S(1)}, u32[]{:S(2)}, u32[]{:S(2)}) %collective-permute-start.5) | collective-permute-done | bytes 131104 | tf_op jit(solution)/shard_map/ppermute | solution.py:274
  120.7 4.0 %collective-permute-done.6.other = bf16[256,256]{1,0:T(8,128)(2,1)S(1)} collective-permute-done((bf16[256,256]{1,0:T(8,128)(2,1)}, bf16[256,256]{1,0:T(8,128)(2,1)S(1)}, u32[]{:S(2)}, u32[]{:S(2)}) %collective-permute-start.6) | collective-permute-done | bytes 131104 | tf_op jit(solution)/shard_map/ppermute | solution.py:274
  124.6 1.3 %unpack.1 = (bf16[256,1280]{1,0:T(8,128)(2,1)}, bf16[256,1280]{1,0:T(8,128)(2,1)}) custom-call(s32[1]{0:T(128)} %bitcast.row_ref.par_ref, bf16[8,256,256]{2,1,0:T(8,128)(2,1)S(1)} %all-to-all-done.2.mine, bf16[256,256]{1,0:T(8,128)(2,1)S(1)} %collective-permute-done.5.own, bf16[256,256]{1,0:T(8,128)(2,1)S(1)} %collective-permute-done.6.other), custom_call_target="tpu_custom_call" | custom-call | tf_op jit(solution)/shard_map/unpack/pallas_call | solution.py:369
  (3 shorter events, 0.0 us)
Async XLA Ops:
  4.7 45.9 %all-to-all-start = ((bf16[8,264,768]{2,1,0:T(8,128)(2,1)}), bf16[8,264,768]{2,1,0:T(8,128)(2,1)S(1)}, u32[]{:S(2)}, u32[]{:S(2)}) async-start(bf16[8,264,768]{2,1,0:T(8,128)(2,1)} %cut_plane.1), calls=%async_computation | async-start | bytes 6488064 | tf_op jit(solution)/shard_map/all_to_all | solution.py:283
  15.6 37.1 %collective-permute-start = (bf16[256,256]{1,0:T(8,128)(2,1)}, bf16[256,256]{1,0:T(8,128)(2,1)S(1)}, u32[]{:S(2)}, u32[]{:S(2)}) collective-permute-start(bf16[256,256]{1,0:T(8,128)(2,1)} %get-tuple-element.15), channel_id=1, source_target_pairs={{0,0},{1,17},{2,2},{3,19},{4,4},{5,21},{6,6},{7,23},{8,8},{9,25},{... | collective-permute-start | bytes 393224 | tf_op jit(solution)/shard_map/ppermute | solution.py:274
  20.5 34.4 %collective-permute-start.1 = (bf16[256,256]{1,0:T(8,128)(2,1)}, bf16[256,256]{1,0:T(8,128)(2,1)S(1)}, u32[]{:S(2)}, u32[]{:S(2)}) collective-permute-start(bf16[256,256]{1,0:T(8,128)(2,1)} %get-tuple-element.16), channel_id=1, source_target_pairs={{0,4},{1,21},{2,6},{3,23},{4,0},{5,17},{6,2},{7,19},{8,12},{9,29},... | collective-permute-start | bytes 393224 | tf_op jit(solution)/shard_map/ppermute | solution.py:274
  56.2 1.1 copy-start
  57.3 36.1 %all-to-all-start.1 = ((bf16[8,256,512]{2,1,0:T(8,128)(2,1)}), bf16[8,256,512]{2,1,0:T(8,128)(2,1)}, u32[]{:S(2)}, u32[]{:S(2)}) async-start(bf16[8,256,512]{2,1,0:T(8,128)(2,1)} %after.2), calls=%async_computation.1 | async-start | bytes 4194304 | tf_op jit(solution)/shard_map/all_to_all | solution.py:283
  61.7 22.5 %collective-permute-start.3 = (bf16[3,256,512]{2,1,0:T(8,128)(2,1)}, bf16[3,256,512]{2,1,0:T(8,128)(2,1)}, u32[]{:S(2)}, u32[]{:S(2)}) collective-permute-start(bf16[3,256,512]{2,1,0:T(8,128)(2,1)} %get-tuple-element.18), channel_id=1, source_target_pairs={{0,224},{4,228},{8,232},{12,236},{16,240},{20,244},{24,248},{28,25... | collective-permute-start | bytes 2359304 | tf_op jit(solution)/shard_map/ppermute | solution.py:270
  67.3 20.2 %collective-permute-start.2 = (bf16[3,256,512]{2,1,0:T(8,128)(2,1)}, bf16[3,256,512]{2,1,0:T(8,128)(2,1)}, u32[]{:S(2)}, u32[]{:S(2)}) collective-permute-start(bf16[3,256,512]{2,1,0:T(8,128)(2,1)} %get-tuple-element.17.refs_2_), channel_id=1, source_target_pairs={{0,32},{4,36},{8,40},{12,44},{16,48},{20,52},{24,56},{28,60},{32,6... | collective-permute-start | bytes 2359304 | tf_op jit(solution)/shard_map/ppermute | solution.py:270
  94.6 11.3 %collective-permute-start.4 = (bf16[3,256,512]{2,1,0:T(8,128)(2,1)S(1)}, bf16[3,256,512]{2,1,0:T(8,128)(2,1)}, u32[]{:S(2)}, u32[]{:S(2)}) collective-permute-start(bf16[3,256,512]{2,1,0:T(8,128)(2,1)S(1)} %edge.1.refs_1_), channel_id=1, source_target_pairs={{0,32},{1,225},{2,34},{3,227},{4,36},{5,229},{6,38},{7,231},{8,40}... | collective-permute-start | bytes 2359304 | tf_op jit(solution)/shard_map/ppermute | solution.py:274
  94.7 24.4 %all-to-all-start.2 = ((bf16[8,256,256]{2,1,0:T(8,128)(2,1)}), bf16[8,256,256]{2,1,0:T(8,128)(2,1)S(1)}, u32[]{:S(2)}, u32[]{:S(2)}) async-start(bf16[8,256,256]{2,1,0:T(8,128)(2,1)} %after.3), calls=%async_computation.2 | async-start | bytes 2097152 | tf_op jit(solution)/shard_map/all_to_all | solution.py:283
  111.7 9.0 %collective-permute-start.5 = (bf16[256,256]{1,0:T(8,128)(2,1)}, bf16[256,256]{1,0:T(8,128)(2,1)S(1)}, u32[]{:S(2)}, u32[]{:S(2)}) collective-permute-start(bf16[256,256]{1,0:T(8,128)(2,1)} %get-tuple-element.26), channel_id=1, source_target_pairs={{0,0},{1,17},{2,2},{3,19},{4,4},{5,21},{6,6},{7,23},{8,8},{9,25},{... | collective-permute-start | bytes 393224 | tf_op jit(solution)/shard_map/ppermute | solution.py:274
  118.1 6.5 %collective-permute-start.6 = (bf16[256,256]{1,0:T(8,128)(2,1)}, bf16[256,256]{1,0:T(8,128)(2,1)S(1)}, u32[]{:S(2)}, u32[]{:S(2)}) collective-permute-start(bf16[256,256]{1,0:T(8,128)(2,1)} %get-tuple-element.27), channel_id=1, source_target_pairs={{0,4},{1,21},{2,6},{3,23},{4,0},{5,17},{6,2},{7,19},{8,12},{9,29},... | collective-permute-start | bytes 393224 | tf_op jit(solution)/shard_map/ppermute | solution.py:274

commit v10 on v9

--- a/solution.py
+++ b/solution.py
@@ -46,10 +46,12 @@
     ins = [[pltpu.make_async_copy(ref.at[:, lanes(j)], buf.at[j, 0:TOK, lanes(n)], in_sem.at[j, n])
             for n, ref in enumerate(arrays)] for j in range(PLANE)]
     outs = [pltpu.make_async_copy(buf.at[j], out.at[j], out_sem.at[j]) for j in range(PLANE)]
+    listing = pltpu.make_async_copy(sel, sel_buf, sel_sem.at[0])
+    listing.start()
     for chunk in ins:
         for copy in chunk:
             copy.start()
-    run_copies([(sel, sel_buf)], sel_sem)
+    listing.wait()
     listed = sel_buf[...].astype(jnp.float32).astype(jnp.bfloat16)
     for j in range(PLANE):
         buf[j, TOK:TOK + 2, :WIN] = listed
@@ -78,7 +80,7 @@
         copy.wait()
 
 
-def weigh(sel_ref, row, first, count, chunk, qcat, floor, s_scr, p_scr, t_scr):
+def weigh(sel_ref, row, first, count, chunk, qcat, floor, s_scr, p_scr, t_scr, inside=None):
     dims = (((1,), (1,)), ((), ()))
     query = qcat[:, HEAD_DIM:]
     peak = [None, None]
@@ -86,7 +88,10 @@
         s = lax.dot_general(query, chunk(u)[:, :HEAD_DIM], dims, preferred_element_type=jnp.float32)
         for qb in range(2):
             for kb in range(2):
-                listed = sel_ref[row, qb * WIN + 2 * (first + u) + kb]
+                at = first + u if inside is None else jnp.clip(first + u, 0, CHUNKS - 1)
+                listed = sel_ref[row, qb * WIN + 2 * at + kb]
+                if inside is not None:
+                    listed = jnp.where(inside(first + u), listed, 0)
                 piece = s[qb * BLK:(qb + 1) * BLK, kb * BLK:(kb + 1) * BLK] + jnp.where(listed != 0, 0.0, NEG)
                 s_scr[qb * BLK:(qb + 1) * BLK, u * TOK + kb * BLK:u * TOK + (kb + 1) * BLK] = piece
                 peak[qb] = piece if peak[qb] is None else jnp.maximum(peak[qb], piece)
@@ -190,19 +195,50 @@
     run_copies([(main.at[begin + n], edge.at[n]) for n in range(REACH)], sem)
 
 
-def pair_kernel(task_ref, sel_ref, q_first, q_second, main, halo, o_first, o_second, kv, s_scr, p_scr, t_scr, sem):
+def pair_tasks(task_ref, q_first, q_second):
     task = task_ref[0]
-    begin = jnp.where(task < PLANE // 2, 0, REACH + PLANE)
-    pairs = [(main.at[c], kv.at[pl.ds((c + REACH) * TOK, TOK), :]) for c in range(PLANE)]
-    pairs += [(halo.at[n], kv.at[pl.ds(pl.multiple_of((begin + n) * TOK, TOK), TOK), :]) for n in range(REACH)]
-    run_copies(pairs, sem)
-    for ref, at, o_ref in ((q_first, task, o_first), (q_second, task + 1 - 2 * (task % 2), o_second)):
+    return ((q_first, task), (q_second, task + 1 - 2 * (task % 2)))
+
+
+def pair_inner_kernel(task_ref, sel_ref, q_first, q_second, main, gate, stats, first_ref, second_ref,
+                      kv, s_scr, p_scr, t_scr, sem):
+    del gate
+    copies = [pltpu.make_async_copy(main.at[c], kv.at[pl.ds((c + REACH) * TOK, TOK), :], sem.at[c]) for c in range(PLANE)]
+    for copy in copies:
+        copy.start()
+    for begin in (0, REACH + PLANE):
+        kv[begin * TOK:(begin + REACH) * TOK, :] = jnp.zeros((REACH * TOK, KV), jnp.bfloat16)
+    for copy in copies:
+        copy.wait()
+    for n, (ref, at) in enumerate(pair_tasks(task_ref, q_first, q_second)):
         base = pl.multiple_of(at * TOK, TOK)
-        _, total, tangent_total = weigh(
+        top, total, tangent_total = weigh(
             sel_ref, at, 0, CHUNKS, lambda u: kv[pl.ds(base + u * TOK, TOK), :2 * HEAD_DIM], ref[...], None,
-            s_scr, p_scr, t_scr)
+            s_scr, p_scr, t_scr, lambda t: jnp.logical_and(at + t >= REACH, at + t < REACH + PLANE))
         first, second = mix(p_scr, t_scr, CHUNKS * TOK, kv[pl.ds(base, CHUNKS * TOK), 2 * HEAD_DIM:])
-        o_ref[...] = finish(total, tangent_total, first, second)
+        stats[n, 0] = jnp.broadcast_to(top, (TOK, BLK))
+        stats[n, 1] = total
+        stats[n, 2] = tangent_total
+        first_ref[n] = first
+        second_ref[n] = second
+
+
+def pair_outer_kernel(task_ref, sel_ref, q_first, q_second, halo, stats, first_ref, second_ref, o_first, o_second,
+                      s_scr, p_scr, t_scr):
+    begin = jnp.where(task_ref[0] < PLANE // 2, 0, REACH + PLANE)
+    outs = (o_first, o_second)
+    for n, (ref, at) in enumerate(pair_tasks(task_ref, q_first, q_second)):
+        before = stats[n, 0][:, :1]
+        top, total, tangent_total = weigh(
+            sel_ref, at, begin - at, REACH, lambda u: halo[u, :, :2 * HEAD_DIM], ref[...], before,
+            s_scr, p_scr, t_scr, lambda t: jnp.logical_and(t >= 0, t < CHUNKS))
+        shrink = jnp.exp2(before - top)
+        first, second = first_ref[n] * shrink, second_ref[n] * shrink
+        for u in range(REACH):
+            more = mix(p_scr.at[:, u * TOK:(u + 1) * TOK], t_scr.at[:, u * TOK:(u + 1) * TOK], TOK,
+                       halo[u, :, 2 * HEAD_DIM:])
+            first, second = first + more[0], second + more[1]
+        outs[n][...] = finish(stats[n, 1] * shrink + total, stats[n, 2] * shrink + tangent_total, first, second)
 
 
 def after_kernel(*refs):
@@ -320,7 +356,7 @@
         name="edges",
     )(main, q_first, q_second)
     up, dn = send(edge_up, PLANE), send(edge_dn, -PLANE)
-    rest = exchange(after(rest_out, sel_all, edge_up))
+    rest = exchange(after(rest_out, sel_all, q_first, q_second))
 
     mid, stats, first, second = pl.pallas_call(
         inner_kernel,
@@ -354,16 +390,27 @@
     halo = spread(edge, lambda i, core: (i + (PLANE if (i ^ (4 * core)) % PLANE < PLANE // 2 else -PLANE)) % devices)
     back = exchange(after(mine, edge))
 
+    pair_sums = pl.pallas_call(
+        pair_inner_kernel,
+        out_shape=(f32(2, 3, TOK, BLK), f32(2, TOK, 256), f32(2, TOK, BLK)),
+        in_specs=[SMEM_SPEC] * 2 + [VMEM_SPEC] * 2 + [ANY_SPEC] * 2,
+        out_specs=(VMEM_SPEC,) * 3,
+        scratch_shapes=[pltpu.VMEM(((PLANE + 2 * REACH) * TOK, KV), jnp.bfloat16)] + scratch(CHUNKS)
+        + [pltpu.SemaphoreType.DMA((PLANE,))],
+        compiler_params=params(16),
+        cost_estimate=cost(14),
+        name="pair_inner",
+    )(task, sel_all, q_first, q_second, rest, edge)
     own, lent = pl.pallas_call(
-        pair_kernel,
+        pair_outer_kernel,
         out_shape=(bf16(TOK, 256), bf16(TOK, 256)),
-        in_specs=[SMEM_SPEC] * 2 + [VMEM_SPEC] * 2 + [ANY_SPEC, HBM_SPEC],
+        in_specs=[SMEM_SPEC] * 2 + [VMEM_SPEC] * 6,
         out_specs=(VMEM_SPEC,) * 2,
-        scratch_shapes=[pltpu.VMEM(((PLANE + 2 * REACH) * TOK, KV), jnp.bfloat16)] + scratch(CHUNKS) + [pltpu.SemaphoreType.DMA((PLANE + REACH,))],
-        compiler_params=params(14),
-        cost_estimate=cost(14),
-        name="pair",
-    )(task, sel_all, q_first, q_second, rest, pltpu.with_memory_space_constraint(halo, pltpu.HBM))
+        scratch_shapes=scratch(REACH),
+        compiler_params=params(8),
+        cost_estimate=cost(6),
+        name="pair_outer",
+    )(task, sel_all, q_first, q_second, halo, *pair_sums)
     own, partner = to_first(own), to_second(lent)
 
     return pl.pallas_call(

time: 127 us -> 119 us (0.937)
  waiting for transfers between devices: 53.8 us -> 47.1 us
    ppermute x5, waiting for transfers between devices: 13.8 us -> 10.1 us  [spread(): return lax.ppermute(array, ('ctx', 'head'), pairs)]
    ppermute x2, waiting for transfers between devices: 11 us -> 8.06 us  [send(): lax.ppermute(array, 'ctx', [(i, (i + by) % devices) for i in range(device...]
    all_to_all x3, starting transfers between devices: 18.9 us -> 16.4 us  [exchange(): lax.all_to_all(array, 'ctx', 0, 0, axis_index_groups=planes, tiled=True)]
    ppermute x5, starting transfers between devices: 13.7 us -> 15.4 us  [spread(): return lax.ppermute(array, ('ctx', 'head'), pairs)]
    pallas_call x1 -> x2, Pallas kernels: 5.79 us -> 7.03 us  [the longest x1 4.85 us: body(): pl.pallas_call(pair_inner_kernel, out_shape=(f32(2, 3, TOK, BLK), f32(2,...]
  transfers between devices with their start and end apart: 10 -> 10, of which waited for: 8 -> 6; matrix products, arithmetic and copies ran while one was open for 0% -> 0% of each run, Pallas kernels for 19% -> 23%
where the time goes in v10:
time: 119 us
  waiting for transfers between devices  47.1 us (40%)
  starting transfers between devices  37.5 us (32%)
  Pallas kernels  33.1 us (28%)
    all_to_all x3, waiting for transfers between devices, exchange(): lax.all_to_all(array, 'ctx', 0, 0, axis_index_groups=planes, tiled=True)  28.9 us
    all_to_all x3, starting transfers between devices, exchange(): lax.all_to_all(array, 'ctx', 0, 0, axis_index_groups=planes, tiled=True)  16.4 us
    ppermute x5, starting transfers between devices, spread(): return lax.ppermute(array, ('ctx', 'head'), pairs)  15.4 us
    ppermute x5, waiting for transfers between devices, spread(): return lax.ppermute(array, ('ctx', 'head'), pairs)  10.1 us
    pallas_call x1, Pallas kernels, body(): pl.pallas_call(inner_kernel, out_shape=(bf16(2, TOK, 256), f32(PLANE, 3,...  9.19 us
    ppermute x2, waiting for transfers between devices, send(): lax.ppermute(array, 'ctx', [(i, (i + by) % devices) for i in range(device...  8.06 us
    pallas_call x1, Pallas kernels, body(): pl.pallas_call(outer_kernel, out_shape=(pltpu.HBM((PLANE, TOK, 256), jnp....  5.86 us
    ppermute x2, starting transfers between devices, send(): lax.ppermute(array, 'ctx', [(i, (i + by) % devices) for i in range(device...  5.74 us
  transfers between devices with their start and end apart: 10, of which 6 were waited for; matrix products, arithmetic and copies ran while one was open for 0% of the time, Pallas kernels for 23%

profile of v10, /device:TPU:1, one launch (start us, length us, event | category | flops | bytes accessed | tf_op | source)
XLA Modules:
  0.0 118.5 jit_solution(15839978135097936682)
XLA Ops:
  0.6 4.1 %cut_plane.1 = bf16[8,264,768]{2,1,0:T(8,128)(2,1)} custom-call(s32[2,14]{1,0:T(2,128)} %sel.1, bf16[256,1280]{1,0:T(8,128)(2,1)} %q.3, bf16[256,1280]{1,0:T(8,128)(2,1)} %qt.3, bf16[256,1280]{1,0:T(8,128)(2,1)} %k.3, bf16[256,1280]{1,0:T(8,128)(2,1)} %kt.3, bf16[256,1280]{1,0:T(8,128)(2,1)} %v.3, bf16[256,1280]{1,0:T(8,128)(2,1)} %vt.3), custom_call_target="tpu_custom_call" | custom-call | tf_op jit(solution)/shard_map/cut_plane/pallas_call | solution.py:323
  4.7 7.5 %all-to-all-start = ((bf16[8,264,768]{2,1,0:T(8,128)(2,1)}), bf16[8,264,768]{2,1,0:T(8,128)(2,1)S(1)}, u32[]{:S(2)}, u32[]{:S(2)}) async-start(bf16[8,264,768]{2,1,0:T(8,128)(2,1)} %cut_plane.1), calls=%async_computation | async-start | bytes 6488064 | tf_op jit(solution)/shard_map/all_to_all | solution.py:319
  12.2 3.4 %cut_pair.1 = (bf16[8,256,512]{2,1,0:T(8,128)(2,1)}, bf16[256,256]{1,0:T(8,128)(2,1)}, bf16[256,256]{1,0:T(8,128)(2,1)}) custom-call(s32[1]{0:T(128)} %bitcast.row_ref.par_ref, bf16[256,1280]{1,0:T(8,128)(2,1)} %q.3, bf16[256,1280]{1,0:T(8,128)(2,1)} %qt.3, bf16[256,1280]{1,0:T(8,128)(2,1)} %k.3, bf16[256,1280]{1,0:T(8,128)(2,1)} %kt.3, ...), custom_call_target="tpu_custom_call" | custom-call | tf_op jit(solution)/shard_map/cut_pair/pallas_call | solution.py:334
  15.6 4.9 %collective-permute-start = (bf16[256,256]{1,0:T(8,128)(2,1)}, bf16[256,256]{1,0:T(8,128)(2,1)S(1)}, u32[]{:S(2)}, u32[]{:S(2)}) collective-permute-start(bf16[256,256]{1,0:T(8,128)(2,1)} %get-tuple-element.18), channel_id=1, source_target_pairs={{0,0},{1,17},{2,2},{3,19},{4,4},{5,21},{6,6},{7,23},{8,8},{9,25},{... | collective-permute-start | bytes 393224 | tf_op jit(solution)/shard_map/ppermute | solution.py:310
  20.5 1.3 %collective-permute-start.1 = (bf16[256,256]{1,0:T(8,128)(2,1)}, bf16[256,256]{1,0:T(8,128)(2,1)S(1)}, u32[]{:S(2)}, u32[]{:S(2)}) collective-permute-start(bf16[256,256]{1,0:T(8,128)(2,1)} %get-tuple-element.19), channel_id=1, source_target_pairs={{0,4},{1,21},{2,6},{3,23},{4,0},{5,17},{6,2},{7,19},{8,12},{9,29},... | collective-permute-start | bytes 393224 | tf_op jit(solution)/shard_map/ppermute | solution.py:310
  21.7 28.9 %all-to-all-done.main = bf16[8,264,768]{2,1,0:T(8,128)(2,1)S(1)} async-done(((bf16[8,264,768]{2,1,0:T(8,128)(2,1)}), bf16[8,264,768]{2,1,0:T(8,128)(2,1)S(1)}, u32[]{:S(2)}, u32[]{:S(2)}) %all-to-all-start) | async-done | bytes 3244064 | tf_op jit(solution)/shard_map/all_to_all | solution.py:319
  50.6 0.1 reshape.12.sel_ref.refs_1_
  50.7 2.0 %collective-permute-done.gate_a.refs_2_.q_first = bf16[256,256]{1,0:T(8,128)(2,1)S(1)} collective-permute-done((bf16[256,256]{1,0:T(8,128)(2,1)}, bf16[256,256]{1,0:T(8,128)(2,1)S(1)}, u32[]{:S(2)}, u32[]{:S(2)}) %collective-permute-start) | collective-permute-done | bytes 131104 | tf_op jit(solution)/shard_map/ppermute | solution.py:310
  52.7 2.2 %collective-permute-done.1.gate_b.refs_3_.q_second = bf16[256,256]{1,0:T(8,128)(2,1)S(1)} collective-permute-done((bf16[256,256]{1,0:T(8,128)(2,1)}, bf16[256,256]{1,0:T(8,128)(2,1)S(1)}, u32[]{:S(2)}, u32[]{:S(2)}) %collective-permute-start.1) | collective-permute-done | bytes 131104 | tf_op jit(solution)/shard_map/ppermute | solution.py:310
  54.9 4.3 %all-to-all-start.1 = ((bf16[8,256,512]{2,1,0:T(8,128)(2,1)}), bf16[8,256,512]{2,1,0:T(8,128)(2,1)}, u32[]{:S(2)}, u32[]{:S(2)}) async-start(bf16[8,256,512]{2,1,0:T(8,128)(2,1)} %after.2), calls=%async_computation.1 | async-start | bytes 4194304 | tf_op jit(solution)/shard_map/all_to_all | solution.py:319
  59.3 1.2 %edges.1 = (bf16[3,256,512]{2,1,0:T(8,128)(2,1)}, bf16[3,256,512]{2,1,0:T(8,128)(2,1)}) custom-call(bf16[8,264,768]{2,1,0:T(8,128)(2,1)S(1)} %all-to-all-done.main, bf16[256,256]{1,0:T(8,128)(2,1)S(1)} %collective-permute-done.gate_a.refs_2_.q_first, bf16[256,256]{1,0:T(8,128)(2,1)S(1)} %collective-permute-done.1.gate_b.refs_3_.q_second), custom_call_target="tpu_custom_call" | custom-call | tf_op jit(solution)/shard_map/edges/pallas_call | solution.py:349
  60.5 1.7 %collective-permute-start.2 = (bf16[3,256,512]{2,1,0:T(8,128)(2,1)}, bf16[3,256,512]{2,1,0:T(8,128)(2,1)}, u32[]{:S(2)}, u32[]{:S(2)}) collective-permute-start(bf16[3,256,512]{2,1,0:T(8,128)(2,1)} %get-tuple-element.20), channel_id=1, source_target_pairs={{0,32},{4,36},{8,40},{12,44},{16,48},{20,52},{24,56},{28,60},{32,6... | collective-permute-start | bytes 2359304 | tf_op jit(solution)/shard_map/ppermute | solution.py:306
  62.2 4.0 %collective-permute-start.3 = (bf16[3,256,512]{2,1,0:T(8,128)(2,1)}, bf16[3,256,512]{2,1,0:T(8,128)(2,1)}, u32[]{:S(2)}, u32[]{:S(2)}) collective-permute-start(bf16[3,256,512]{2,1,0:T(8,128)(2,1)} %get-tuple-element.21), channel_id=1, source_target_pairs={{0,224},{4,228},{8,232},{12,236},{16,240},{20,244},{24,248},{28,25... | collective-permute-start | bytes 2359304 | tf_op jit(solution)/shard_map/ppermute | solution.py:306
  66.2 9.2 %inner.1 = (bf16[2,256,256]{2,1,0:T(8,128)(2,1)S(1)}, f32[8,3,256,128]{3,2,1,0:T(8,128)S(1)}, f32[8,256,256]{2,1,0:T(8,128)S(1)}, f32[8,256,128]{2,1,0:T(8,128)S(1)}) custom-call(s32[8,28]{1,0:T(8,128)S(1)} %reshape.12.sel_ref.refs_1_, bf16[8,264,768]{2,1,0:T(8,128)(2,1)S(1)} %all-to-all-done.main), custom_call_target="tpu_custom_call" | custom-call | flops 3690987520 | bytes 11534336 | tf_op jit(solution)/shard_map/inner/pallas_call | solution.py:361
  75.4 8.1 %collective-permute-done.2.up = bf16[3,256,512]{2,1,0:T(8,128)(2,1)} collective-permute-done((bf16[3,256,512]{2,1,0:T(8,128)(2,1)}, bf16[3,256,512]{2,1,0:T(8,128)(2,1)}, u32[]{:S(2)}, u32[]{:S(2)}) %collective-permute-start.2) | collective-permute-done | bytes 786464 | tf_op jit(solution)/shard_map/ppermute | solution.py:306
  83.5 0.0 collective-permute-done.3.dn
  83.5 5.9 %outer.1 = (bf16[8,256,256]{2,1,0:T(8,128)(2,1)}, f32[8,128]{1,0:T(8,128)S(1)}) custom-call(s32[8,28]{1,0:T(8,128)S(1)} %reshape.12.sel_ref.refs_1_, bf16[8,264,768]{2,1,0:T(8,128)(2,1)S(1)} %all-to-all-done.main, bf16[3,256,512]{2,1,0:T(8,128)(2,1)} %collective-permute-done.2.up, bf16[3,256,512]{2,1,0:T(8,128)(2,1)} %collective-permute-done.3.dn, ...), custom_call_target="tpu_custom_call" | custom-call | flops 1006632960 | bytes 3145728 | tf_op jit(solution)/shard_map/outer/pallas_call | solution.py:371
  89.3 0.0 all-to-all-done.1.main
  89.3 1.1 edge.1.refs_1_.gate
  90.5 3.1 %collective-permute-start.4 = (bf16[3,256,512]{2,1,0:T(8,128)(2,1)S(1)}, bf16[3,256,512]{2,1,0:T(8,128)(2,1)S(1)}, u32[]{:S(2)}, u32[]{:S(2)}) collective-permute-start(bf16[3,256,512]{2,1,0:T(8,128)(2,1)S(1)} %edge.1.refs_1_.gate), channel_id=1, source_target_pairs={{0,32},{1,225},{2,34},{3,227},{4,36},{5,229},{6,38},{7,231},{8,40}... | collective-permute-start | bytes 2359304 | tf_op jit(solution)/shard_map/ppermute | solution.py:310
  93.6 4.5 %all-to-all-start.2 = ((bf16[8,256,256]{2,1,0:T(8,128)(2,1)}), bf16[8,256,256]{2,1,0:T(8,128)(2,1)S(1)}, u32[]{:S(2)}, u32[]{:S(2)}) async-start(bf16[8,256,256]{2,1,0:T(8,128)(2,1)} %after.3), calls=%async_computation.2 | async-start | bytes 2097152 | tf_op jit(solution)/shard_map/all_to_all | solution.py:319
  98.1 4.8 %pair_inner.1 = (f32[2,3,256,128]{3,2,1,0:T(8,128)S(1)}, f32[2,256,256]{2,1,0:T(8,128)S(1)}, f32[2,256,128]{2,1,0:T(8,128)S(1)}) custom-call(s32[1]{0:T(128)S(6)} %xor.7.task_ref, s32[8,28]{1,0:T(8,128)S(1)} %reshape.12.sel_ref.refs_1_, bf16[256,256]{1,0:T(8,128)(2,1)S(1)} %collective-permute-done.gate_a.refs_2_.q_first, ...), custom_call_target="tpu_custom_call" | custom-call | flops 1174405120 | bytes 3670016 | tf_op jit(solution)/shard_map/pair_inner/pallas_call | solution.py:393
  103.0 0.0 collective-permute-done.4.halo
  103.0 2.2 %pair_outer.1 = (bf16[256,256]{1,0:T(8,128)(2,1)S(1)}, bf16[256,256]{1,0:T(8,128)(2,1)S(1)}) custom-call(s32[1]{0:T(128)S(6)} %xor.7.task_ref, s32[8,28]{1,0:T(8,128)S(1)} %reshape.12.sel_ref.refs_1_, bf16[256,256]{1,0:T(8,128)(2,1)S(1)} %collective-permute-done.gate_a.refs_2_.q_first, bf16[256,256]{1,0:T(8,128)(2,1)S(1)} %collective-permute-done.1.gate_b.refs_3_.q_second, ...), custom_call_target="tpu_custom_call" | custom-call | flops 503316480 | bytes 1572864 | tf_op jit(solution)/shard_map/pair_outer/pallas_call | solution.py:404
  105.2 5.2 %collective-permute-start.5 = (bf16[256,256]{1,0:T(8,128)(2,1)S(1)}, bf16[256,256]{1,0:T(8,128)(2,1)S(1)}, u32[]{:S(2)}, u32[]{:S(2)}) collective-permute-start(bf16[256,256]{1,0:T(8,128)(2,1)S(1)} %get-tuple-element.32), channel_id=1, source_target_pairs={{0,0},{1,17},{2,2},{3,19},{4,4},{5,21},{6,6},{7,23},{8,8},{9,25},{... | collective-permute-start | bytes 393224 | tf_op jit(solution)/shard_map/ppermute | solution.py:310
  110.3 1.0 collective-permute-start.6
  111.3 0.0 all-to-all-done.2.mine
  111.3 3.1 %collective-permute-done.5.own = bf16[256,256]{1,0:T(8,128)(2,1)S(1)} collective-permute-done((bf16[256,256]{1,0:T(8,128)(2,1)S(1)}, bf16[256,256]{1,0:T(8,128)(2,1)S(1)}, u32[]{:S(2)}, u32[]{:S(2)}) %collective-permute-start.5) | collective-permute-done | bytes 131104 | tf_op jit(solution)/shard_map/ppermute | solution.py:310
  114.4 2.8 %collective-permute-done.6.other = bf16[256,256]{1,0:T(8,128)(2,1)S(1)} collective-permute-done((bf16[256,256]{1,0:T(8,128)(2,1)S(1)}, bf16[256,256]{1,0:T(8,128)(2,1)S(1)}, u32[]{:S(2)}, u32[]{:S(2)}) %collective-permute-start.6) | collective-permute-done | bytes 131104 | tf_op jit(solution)/shard_map/ppermute | solution.py:310
  117.2 1.3 %unpack.1 = (bf16[256,1280]{1,0:T(8,128)(2,1)}, bf16[256,1280]{1,0:T(8,128)(2,1)}) custom-call(s32[1]{0:T(128)} %bitcast.row_ref.par_ref, bf16[8,256,256]{2,1,0:T(8,128)(2,1)S(1)} %all-to-all-done.2.mine, bf16[256,256]{1,0:T(8,128)(2,1)S(1)} %collective-permute-done.5.own, bf16[256,256]{1,0:T(8,128)(2,1)S(1)} %collective-permute-done.6.other), custom_call_target="tpu_custom_call" | custom-call | tf_op jit(solution)/shard_map/unpack/pallas_call | solution.py:416
  (3 shorter events, 0.0 us)
Async XLA Ops:
  4.7 45.9 %all-to-all-start = ((bf16[8,264,768]{2,1,0:T(8,128)(2,1)}), bf16[8,264,768]{2,1,0:T(8,128)(2,1)S(1)}, u32[]{:S(2)}, u32[]{:S(2)}) async-start(bf16[8,264,768]{2,1,0:T(8,128)(2,1)} %cut_plane.1), calls=%async_computation | async-start | bytes 6488064 | tf_op jit(solution)/shard_map/all_to_all | solution.py:319
  15.6 37.1 %collective-permute-start = (bf16[256,256]{1,0:T(8,128)(2,1)}, bf16[256,256]{1,0:T(8,128)(2,1)S(1)}, u32[]{:S(2)}, u32[]{:S(2)}) collective-permute-start(bf16[256,256]{1,0:T(8,128)(2,1)} %get-tuple-element.18), channel_id=1, source_target_pairs={{0,0},{1,17},{2,2},{3,19},{4,4},{5,21},{6,6},{7,23},{8,8},{9,25},{... | collective-permute-start | bytes 393224 | tf_op jit(solution)/shard_map/ppermute | solution.py:310
  20.5 34.4 %collective-permute-start.1 = (bf16[256,256]{1,0:T(8,128)(2,1)}, bf16[256,256]{1,0:T(8,128)(2,1)S(1)}, u32[]{:S(2)}, u32[]{:S(2)}) collective-permute-start(bf16[256,256]{1,0:T(8,128)(2,1)} %get-tuple-element.19), channel_id=1, source_target_pairs={{0,4},{1,21},{2,6},{3,23},{4,0},{5,17},{6,2},{7,19},{8,12},{9,29},... | collective-permute-start | bytes 393224 | tf_op jit(solution)/shard_map/ppermute | solution.py:310
  54.9 34.4 %all-to-all-start.1 = ((bf16[8,256,512]{2,1,0:T(8,128)(2,1)}), bf16[8,256,512]{2,1,0:T(8,128)(2,1)}, u32[]{:S(2)}, u32[]{:S(2)}) async-start(bf16[8,256,512]{2,1,0:T(8,128)(2,1)} %after.2), calls=%async_computation.1 | async-start | bytes 4194304 | tf_op jit(solution)/shard_map/all_to_all | solution.py:319
  60.5 23.0 %collective-permute-start.2 = (bf16[3,256,512]{2,1,0:T(8,128)(2,1)}, bf16[3,256,512]{2,1,0:T(8,128)(2,1)}, u32[]{:S(2)}, u32[]{:S(2)}) collective-permute-start(bf16[3,256,512]{2,1,0:T(8,128)(2,1)} %get-tuple-element.20), channel_id=1, source_target_pairs={{0,32},{4,36},{8,40},{12,44},{16,48},{20,52},{24,56},{28,60},{32,6... | collective-permute-start | bytes 2359304 | tf_op jit(solution)/shard_map/ppermute | solution.py:306
  62.2 21.3 %collective-permute-start.3 = (bf16[3,256,512]{2,1,0:T(8,128)(2,1)}, bf16[3,256,512]{2,1,0:T(8,128)(2,1)}, u32[]{:S(2)}, u32[]{:S(2)}) collective-permute-start(bf16[3,256,512]{2,1,0:T(8,128)(2,1)} %get-tuple-element.21), channel_id=1, source_target_pairs={{0,224},{4,228},{8,232},{12,236},{16,240},{20,244},{24,248},{28,25... | collective-permute-start | bytes 2359304 | tf_op jit(solution)/shard_map/ppermute | solution.py:306
  90.5 12.5 %collective-permute-start.4 = (bf16[3,256,512]{2,1,0:T(8,128)(2,1)S(1)}, bf16[3,256,512]{2,1,0:T(8,128)(2,1)S(1)}, u32[]{:S(2)}, u32[]{:S(2)}) collective-permute-start(bf16[3,256,512]{2,1,0:T(8,128)(2,1)S(1)} %edge.1.refs_1_.gate), channel_id=1, source_target_pairs={{0,32},{1,225},{2,34},{3,227},{4,36},{5,229},{6,38},{7,231},{8,40}... | collective-permute-start | bytes 2359304 | tf_op jit(solution)/shard_map/ppermute | solution.py:310
  93.6 17.7 %all-to-all-start.2 = ((bf16[8,256,256]{2,1,0:T(8,128)(2,1)}), bf16[8,256,256]{2,1,0:T(8,128)(2,1)S(1)}, u32[]{:S(2)}, u32[]{:S(2)}) async-start(bf16[8,256,256]{2,1,0:T(8,128)(2,1)} %after.3), calls=%async_computation.2 | async-start | bytes 2097152 | tf_op jit(solution)/shard_map/all_to_all | solution.py:319
  105.2 9.3 %collective-permute-start.5 = (bf16[256,256]{1,0:T(8,128)(2,1)S(1)}, bf16[256,256]{1,0:T(8,128)(2,1)S(1)}, u32[]{:S(2)}, u32[]{:S(2)}) collective-permute-start(bf16[256,256]{1,0:T(8,128)(2,1)S(1)} %get-tuple-element.32), channel_id=1, source_target_pairs={{0,0},{1,17},{2,2},{3,19},{4,4},{5,21},{6,6},{7,23},{8,8},{9,25},{... | collective-permute-start | bytes 393224 | tf_op jit(solution)/shard_map/ppermute | solution.py:310
  110.3 6.9 %collective-permute-start.6 = (bf16[256,256]{1,0:T(8,128)(2,1)S(1)}, bf16[256,256]{1,0:T(8,128)(2,1)S(1)}, u32[]{:S(2)}, u32[]{:S(2)}) collective-permute-start(bf16[256,256]{1,0:T(8,128)(2,1)S(1)} %get-tuple-element.33), channel_id=1, source_target_pairs={{0,4},{1,21},{2,6},{3,23},{4,0},{5,17},{6,2},{7,19},{8,12},{9,29},... | collective-permute-start | bytes 393224 | tf_op jit(solution)/shard_map/ppermute | solution.py:310

commit v11 on v10

--- a/solution.py
+++ b/solution.py
@@ -17,6 +17,7 @@
 EXTRA = 8
 KV = 4 * HEAD_DIM
 ALL = 6 * HEAD_DIM
+AHEAD = 4
 NEG = -1.0e30
 LOG2E = 1.4426950408889634
 SCALE = HEAD_DIM ** -0.5
@@ -48,7 +49,7 @@
     outs = [pltpu.make_async_copy(buf.at[j], out.at[j], out_sem.at[j]) for j in range(PLANE)]
     listing = pltpu.make_async_copy(sel, sel_buf, sel_sem.at[0])
     listing.start()
-    for chunk in ins:
+    for chunk in ins[:AHEAD]:
         for copy in chunk:
             copy.start()
     listing.wait()
@@ -58,6 +59,8 @@
         for copy in ins[j]:
             copy.wait()
         outs[j].start()
+        for copy in ins[j + AHEAD] if j + AHEAD < PLANE else ():
+            copy.start()
     for copy in outs:
         copy.wait()
 

time: 119 us -> 120 us (level)
  transfers between devices with their start and end apart: 10 -> 10, of which waited for: 6 -> 6; matrix products, arithmetic and copies ran while one was open for 0% -> 0% of each run, Pallas kernels for 23% -> 22%
where the time goes in v11:
time: 120 us; the launch traced here: 119 us
  waiting for transfers between devices  47.1 us (39%)
  starting transfers between devices  37.5 us (31%)
  Pallas kernels  33.6 us (28%)
    all_to_all x3, waiting for transfers between devices, exchange(): lax.all_to_all(array, 'ctx', 0, 0, axis_index_groups=planes, tiled=True)  28.9 us
    all_to_all x3, starting transfers between devices, exchange(): lax.all_to_all(array, 'ctx', 0, 0, axis_index_groups=planes, tiled=True)  16.4 us
    ppermute x5, starting transfers between devices, spread(): return lax.ppermute(array, ('ctx', 'head'), pairs)  15.4 us
    ppermute x5, waiting for transfers between devices, spread(): return lax.ppermute(array, ('ctx', 'head'), pairs)  10.1 us
    pallas_call x1, Pallas kernels, body(): pl.pallas_call(inner_kernel, out_shape=(bf16(2, TOK, 256), f32(PLANE, 3,...  9.18 us
    ppermute x2, waiting for transfers between devices, send(): lax.ppermute(array, 'ctx', [(i, (i + by) % devices) for i in range(device...  8.06 us
    pallas_call x1, Pallas kernels, body(): pl.pallas_call(outer_kernel, out_shape=(pltpu.HBM((PLANE, TOK, 256), jnp....  5.85 us
    ppermute x2, starting transfers between devices, send(): lax.ppermute(array, 'ctx', [(i, (i + by) % devices) for i in range(device...  5.74 us
  transfers between devices with their start and end apart: 10, of which 6 were waited for; matrix products, arithmetic and copies ran while one was open for 0% of the time, Pallas kernels for 22%

profile of v11, /device:TPU:1, one launch (start us, length us, event | category | flops | bytes accessed | tf_op | source)
XLA Modules:
  0.0 119.0 jit_solution(6052726010647912178)
XLA Ops:
  0.6 4.5 %cut_plane.1 = bf16[8,264,768]{2,1,0:T(8,128)(2,1)} custom-call(s32[2,14]{1,0:T(2,128)} %sel.1, bf16[256,1280]{1,0:T(8,128)(2,1)} %q.3, bf16[256,1280]{1,0:T(8,128)(2,1)} %qt.3, bf16[256,1280]{1,0:T(8,128)(2,1)} %k.3, bf16[256,1280]{1,0:T(8,128)(2,1)} %kt.3, bf16[256,1280]{1,0:T(8,128)(2,1)} %v.3, bf16[256,1280]{1,0:T(8,128)(2,1)} %vt.3), custom_call_target="tpu_custom_call" | custom-call | tf_op jit(solution)/shard_map/cut_plane/pallas_call | solution.py:326
  5.2 7.5 %all-to-all-start = ((bf16[8,264,768]{2,1,0:T(8,128)(2,1)}), bf16[8,264,768]{2,1,0:T(8,128)(2,1)S(1)}, u32[]{:S(2)}, u32[]{:S(2)}) async-start(bf16[8,264,768]{2,1,0:T(8,128)(2,1)} %cut_plane.1), calls=%async_computation | async-start | bytes 6488064 | tf_op jit(solution)/shard_map/all_to_all | solution.py:322
  12.7 3.4 %cut_pair.1 = (bf16[8,256,512]{2,1,0:T(8,128)(2,1)}, bf16[256,256]{1,0:T(8,128)(2,1)}, bf16[256,256]{1,0:T(8,128)(2,1)}) custom-call(s32[1]{0:T(128)} %bitcast.row_ref.par_ref, bf16[256,1280]{1,0:T(8,128)(2,1)} %q.3, bf16[256,1280]{1,0:T(8,128)(2,1)} %qt.3, bf16[256,1280]{1,0:T(8,128)(2,1)} %k.3, bf16[256,1280]{1,0:T(8,128)(2,1)} %kt.3, ...), custom_call_target="tpu_custom_call" | custom-call | tf_op jit(solution)/shard_map/cut_pair/pallas_call | solution.py:337
  16.1 4.9 %collective-permute-start = (bf16[256,256]{1,0:T(8,128)(2,1)}, bf16[256,256]{1,0:T(8,128)(2,1)S(1)}, u32[]{:S(2)}, u32[]{:S(2)}) collective-permute-start(bf16[256,256]{1,0:T(8,128)(2,1)} %get-tuple-element.18), channel_id=1, source_target_pairs={{0,0},{1,17},{2,2},{3,19},{4,4},{5,21},{6,6},{7,23},{8,8},{9,25},{... | collective-permute-start | bytes 393224 | tf_op jit(solution)/shard_map/ppermute | solution.py:313
  21.0 1.3 %collective-permute-start.1 = (bf16[256,256]{1,0:T(8,128)(2,1)}, bf16[256,256]{1,0:T(8,128)(2,1)S(1)}, u32[]{:S(2)}, u32[]{:S(2)}) collective-permute-start(bf16[256,256]{1,0:T(8,128)(2,1)} %get-tuple-element.19), channel_id=1, source_target_pairs={{0,4},{1,21},{2,6},{3,23},{4,0},{5,17},{6,2},{7,19},{8,12},{9,29},... | collective-permute-start | bytes 393224 | tf_op jit(solution)/shard_map/ppermute | solution.py:313
  22.2 28.9 %all-to-all-done.main = bf16[8,264,768]{2,1,0:T(8,128)(2,1)S(1)} async-done(((bf16[8,264,768]{2,1,0:T(8,128)(2,1)}), bf16[8,264,768]{2,1,0:T(8,128)(2,1)S(1)}, u32[]{:S(2)}, u32[]{:S(2)}) %all-to-all-start) | async-done | bytes 3244064 | tf_op jit(solution)/shard_map/all_to_all | solution.py:322
  51.1 0.1 reshape.12.sel_ref.refs_1_
  51.2 2.0 %collective-permute-done.gate_a.refs_2_.q_first = bf16[256,256]{1,0:T(8,128)(2,1)S(1)} collective-permute-done((bf16[256,256]{1,0:T(8,128)(2,1)}, bf16[256,256]{1,0:T(8,128)(2,1)S(1)}, u32[]{:S(2)}, u32[]{:S(2)}) %collective-permute-start) | collective-permute-done | bytes 131104 | tf_op jit(solution)/shard_map/ppermute | solution.py:313
  53.2 2.2 %collective-permute-done.1.gate_b.refs_3_.q_second = bf16[256,256]{1,0:T(8,128)(2,1)S(1)} collective-permute-done((bf16[256,256]{1,0:T(8,128)(2,1)}, bf16[256,256]{1,0:T(8,128)(2,1)S(1)}, u32[]{:S(2)}, u32[]{:S(2)}) %collective-permute-start.1) | collective-permute-done | bytes 131104 | tf_op jit(solution)/shard_map/ppermute | solution.py:313
  55.4 4.3 %all-to-all-start.1 = ((bf16[8,256,512]{2,1,0:T(8,128)(2,1)}), bf16[8,256,512]{2,1,0:T(8,128)(2,1)}, u32[]{:S(2)}, u32[]{:S(2)}) async-start(bf16[8,256,512]{2,1,0:T(8,128)(2,1)} %after.2), calls=%async_computation.1 | async-start | bytes 4194304 | tf_op jit(solution)/shard_map/all_to_all | solution.py:322
  59.7 1.2 %edges.1 = (bf16[3,256,512]{2,1,0:T(8,128)(2,1)}, bf16[3,256,512]{2,1,0:T(8,128)(2,1)}) custom-call(bf16[8,264,768]{2,1,0:T(8,128)(2,1)S(1)} %all-to-all-done.main, bf16[256,256]{1,0:T(8,128)(2,1)S(1)} %collective-permute-done.gate_a.refs_2_.q_first, bf16[256,256]{1,0:T(8,128)(2,1)S(1)} %collective-permute-done.1.gate_b.refs_3_.q_second), custom_call_target="tpu_custom_call" | custom-call | tf_op jit(solution)/shard_map/edges/pallas_call | solution.py:352
  61.0 1.7 %collective-permute-start.2 = (bf16[3,256,512]{2,1,0:T(8,128)(2,1)}, bf16[3,256,512]{2,1,0:T(8,128)(2,1)}, u32[]{:S(2)}, u32[]{:S(2)}) collective-permute-start(bf16[3,256,512]{2,1,0:T(8,128)(2,1)} %get-tuple-element.20), channel_id=1, source_target_pairs={{0,32},{4,36},{8,40},{12,44},{16,48},{20,52},{24,56},{28,60},{32,6... | collective-permute-start | bytes 2359304 | tf_op jit(solution)/shard_map/ppermute | solution.py:309
  62.7 4.0 %collective-permute-start.3 = (bf16[3,256,512]{2,1,0:T(8,128)(2,1)}, bf16[3,256,512]{2,1,0:T(8,128)(2,1)}, u32[]{:S(2)}, u32[]{:S(2)}) collective-permute-start(bf16[3,256,512]{2,1,0:T(8,128)(2,1)} %get-tuple-element.21), channel_id=1, source_target_pairs={{0,224},{4,228},{8,232},{12,236},{16,240},{20,244},{24,248},{28,25... | collective-permute-start | bytes 2359304 | tf_op jit(solution)/shard_map/ppermute | solution.py:309
  66.7 9.2 %inner.1 = (bf16[2,256,256]{2,1,0:T(8,128)(2,1)S(1)}, f32[8,3,256,128]{3,2,1,0:T(8,128)S(1)}, f32[8,256,256]{2,1,0:T(8,128)S(1)}, f32[8,256,128]{2,1,0:T(8,128)S(1)}) custom-call(s32[8,28]{1,0:T(8,128)S(1)} %reshape.12.sel_ref.refs_1_, bf16[8,264,768]{2,1,0:T(8,128)(2,1)S(1)} %all-to-all-done.main), custom_call_target="tpu_custom_call" | custom-call | flops 3690987520 | bytes 11534336 | tf_op jit(solution)/shard_map/inner/pallas_call | solution.py:364
  75.9 8.1 %collective-permute-done.2.up = bf16[3,256,512]{2,1,0:T(8,128)(2,1)} collective-permute-done((bf16[3,256,512]{2,1,0:T(8,128)(2,1)}, bf16[3,256,512]{2,1,0:T(8,128)(2,1)}, u32[]{:S(2)}, u32[]{:S(2)}) %collective-permute-start.2) | collective-permute-done | bytes 786464 | tf_op jit(solution)/shard_map/ppermute | solution.py:309
  83.9 0.0 collective-permute-done.3.dn
  83.9 5.8 %outer.1 = (bf16[8,256,256]{2,1,0:T(8,128)(2,1)}, f32[8,128]{1,0:T(8,128)S(1)}) custom-call(s32[8,28]{1,0:T(8,128)S(1)} %reshape.12.sel_ref.refs_1_, bf16[8,264,768]{2,1,0:T(8,128)(2,1)S(1)} %all-to-all-done.main, bf16[3,256,512]{2,1,0:T(8,128)(2,1)} %collective-permute-done.2.up, bf16[3,256,512]{2,1,0:T(8,128)(2,1)} %collective-permute-done.3.dn, ...), custom_call_target="tpu_custom_call" | custom-call | flops 1006632960 | bytes 3145728 | tf_op jit(solution)/shard_map/outer/pallas_call | solution.py:374
  89.8 0.0 all-to-all-done.1.main
  89.8 1.1 edge.1.refs_1_.gate
  91.0 3.1 %collective-permute-start.4 = (bf16[3,256,512]{2,1,0:T(8,128)(2,1)S(1)}, bf16[3,256,512]{2,1,0:T(8,128)(2,1)S(1)}, u32[]{:S(2)}, u32[]{:S(2)}) collective-permute-start(bf16[3,256,512]{2,1,0:T(8,128)(2,1)S(1)} %edge.1.refs_1_.gate), channel_id=1, source_target_pairs={{0,32},{1,225},{2,34},{3,227},{4,36},{5,229},{6,38},{7,231},{8,40}... | collective-permute-start | bytes 2359304 | tf_op jit(solution)/shard_map/ppermute | solution.py:313
  94.1 4.5 %all-to-all-start.2 = ((bf16[8,256,256]{2,1,0:T(8,128)(2,1)}), bf16[8,256,256]{2,1,0:T(8,128)(2,1)S(1)}, u32[]{:S(2)}, u32[]{:S(2)}) async-start(bf16[8,256,256]{2,1,0:T(8,128)(2,1)} %after.3), calls=%async_computation.2 | async-start | bytes 2097152 | tf_op jit(solution)/shard_map/all_to_all | solution.py:322
  98.6 4.8 %pair_inner.1 = (f32[2,3,256,128]{3,2,1,0:T(8,128)S(1)}, f32[2,256,256]{2,1,0:T(8,128)S(1)}, f32[2,256,128]{2,1,0:T(8,128)S(1)}) custom-call(s32[1]{0:T(128)S(6)} %xor.7.task_ref, s32[8,28]{1,0:T(8,128)S(1)} %reshape.12.sel_ref.refs_1_, bf16[256,256]{1,0:T(8,128)(2,1)S(1)} %collective-permute-done.gate_a.refs_2_.q_first, ...), custom_call_target="tpu_custom_call" | custom-call | flops 1174405120 | bytes 3670016 | tf_op jit(solution)/shard_map/pair_inner/pallas_call | solution.py:396
  103.5 0.0 collective-permute-done.4.halo
  103.5 2.2 %pair_outer.1 = (bf16[256,256]{1,0:T(8,128)(2,1)S(1)}, bf16[256,256]{1,0:T(8,128)(2,1)S(1)}) custom-call(s32[1]{0:T(128)S(6)} %xor.7.task_ref, s32[8,28]{1,0:T(8,128)S(1)} %reshape.12.sel_ref.refs_1_, bf16[256,256]{1,0:T(8,128)(2,1)S(1)} %collective-permute-done.gate_a.refs_2_.q_first, bf16[256,256]{1,0:T(8,128)(2,1)S(1)} %collective-permute-done.1.gate_b.refs_3_.q_second, ...), custom_call_target="tpu_custom_call" | custom-call | flops 503316480 | bytes 1572864 | tf_op jit(solution)/shard_map/pair_outer/pallas_call | solution.py:407
  105.7 5.1 %collective-permute-start.5 = (bf16[256,256]{1,0:T(8,128)(2,1)S(1)}, bf16[256,256]{1,0:T(8,128)(2,1)S(1)}, u32[]{:S(2)}, u32[]{:S(2)}) collective-permute-start(bf16[256,256]{1,0:T(8,128)(2,1)S(1)} %get-tuple-element.32), channel_id=1, source_target_pairs={{0,0},{1,17},{2,2},{3,19},{4,4},{5,21},{6,6},{7,23},{8,8},{9,25},{... | collective-permute-start | bytes 393224 | tf_op jit(solution)/shard_map/ppermute | solution.py:313
  110.8 1.0 collective-permute-start.6
  111.8 0.0 all-to-all-done.2.mine
  111.8 3.1 %collective-permute-done.5.own = bf16[256,256]{1,0:T(8,128)(2,1)S(1)} collective-permute-done((bf16[256,256]{1,0:T(8,128)(2,1)S(1)}, bf16[256,256]{1,0:T(8,128)(2,1)S(1)}, u32[]{:S(2)}, u32[]{:S(2)}) %collective-permute-start.5) | collective-permute-done | bytes 131104 | tf_op jit(solution)/shard_map/ppermute | solution.py:313
  114.9 2.8 %collective-permute-done.6.other = bf16[256,256]{1,0:T(8,128)(2,1)S(1)} collective-permute-done((bf16[256,256]{1,0:T(8,128)(2,1)S(1)}, bf16[256,256]{1,0:T(8,128)(2,1)S(1)}, u32[]{:S(2)}, u32[]{:S(2)}) %collective-permute-start.6) | collective-permute-done | bytes 131104 | tf_op jit(solution)/shard_map/ppermute | solution.py:313
  117.7 1.3 %unpack.1 = (bf16[256,1280]{1,0:T(8,128)(2,1)}, bf16[256,1280]{1,0:T(8,128)(2,1)}) custom-call(s32[1]{0:T(128)} %bitcast.row_ref.par_ref, bf16[8,256,256]{2,1,0:T(8,128)(2,1)S(1)} %all-to-all-done.2.mine, bf16[256,256]{1,0:T(8,128)(2,1)S(1)} %collective-permute-done.5.own, bf16[256,256]{1,0:T(8,128)(2,1)S(1)} %collective-permute-done.6.other), custom_call_target="tpu_custom_call" | custom-call | tf_op jit(solution)/shard_map/unpack/pallas_call | solution.py:419
  (3 shorter events, 0.0 us)
Async XLA Ops:
  5.2 45.9 %all-to-all-start = ((bf16[8,264,768]{2,1,0:T(8,128)(2,1)}), bf16[8,264,768]{2,1,0:T(8,128)(2,1)S(1)}, u32[]{:S(2)}, u32[]{:S(2)}) async-start(bf16[8,264,768]{2,1,0:T(8,128)(2,1)} %cut_plane.1), calls=%async_computation | async-start | bytes 6488064 | tf_op jit(solution)/shard_map/all_to_all | solution.py:322
  16.1 37.1 %collective-permute-start = (bf16[256,256]{1,0:T(8,128)(2,1)}, bf16[256,256]{1,0:T(8,128)(2,1)S(1)}, u32[]{:S(2)}, u32[]{:S(2)}) collective-permute-start(bf16[256,256]{1,0:T(8,128)(2,1)} %get-tuple-element.18), channel_id=1, source_target_pairs={{0,0},{1,17},{2,2},{3,19},{4,4},{5,21},{6,6},{7,23},{8,8},{9,25},{... | collective-permute-start | bytes 393224 | tf_op jit(solution)/shard_map/ppermute | solution.py:313
  21.0 34.4 %collective-permute-start.1 = (bf16[256,256]{1,0:T(8,128)(2,1)}, bf16[256,256]{1,0:T(8,128)(2,1)S(1)}, u32[]{:S(2)}, u32[]{:S(2)}) collective-permute-start(bf16[256,256]{1,0:T(8,128)(2,1)} %get-tuple-element.19), channel_id=1, source_target_pairs={{0,4},{1,21},{2,6},{3,23},{4,0},{5,17},{6,2},{7,19},{8,12},{9,29},... | collective-permute-start | bytes 393224 | tf_op jit(solution)/shard_map/ppermute | solution.py:313
  55.4 34.4 %all-to-all-start.1 = ((bf16[8,256,512]{2,1,0:T(8,128)(2,1)}), bf16[8,256,512]{2,1,0:T(8,128)(2,1)}, u32[]{:S(2)}, u32[]{:S(2)}) async-start(bf16[8,256,512]{2,1,0:T(8,128)(2,1)} %after.2), calls=%async_computation.1 | async-start | bytes 4194304 | tf_op jit(solution)/shard_map/all_to_all | solution.py:322
  61.0 23.0 %collective-permute-start.2 = (bf16[3,256,512]{2,1,0:T(8,128)(2,1)}, bf16[3,256,512]{2,1,0:T(8,128)(2,1)}, u32[]{:S(2)}, u32[]{:S(2)}) collective-permute-start(bf16[3,256,512]{2,1,0:T(8,128)(2,1)} %get-tuple-element.20), channel_id=1, source_target_pairs={{0,32},{4,36},{8,40},{12,44},{16,48},{20,52},{24,56},{28,60},{32,6... | collective-permute-start | bytes 2359304 | tf_op jit(solution)/shard_map/ppermute | solution.py:309
  62.7 21.3 %collective-permute-start.3 = (bf16[3,256,512]{2,1,0:T(8,128)(2,1)}, bf16[3,256,512]{2,1,0:T(8,128)(2,1)}, u32[]{:S(2)}, u32[]{:S(2)}) collective-permute-start(bf16[3,256,512]{2,1,0:T(8,128)(2,1)} %get-tuple-element.21), channel_id=1, source_target_pairs={{0,224},{4,228},{8,232},{12,236},{16,240},{20,244},{24,248},{28,25... | collective-permute-start | bytes 2359304 | tf_op jit(solution)/shard_map/ppermute | solution.py:309
  91.0 12.5 %collective-permute-start.4 = (bf16[3,256,512]{2,1,0:T(8,128)(2,1)S(1)}, bf16[3,256,512]{2,1,0:T(8,128)(2,1)S(1)}, u32[]{:S(2)}, u32[]{:S(2)}) collective-permute-start(bf16[3,256,512]{2,1,0:T(8,128)(2,1)S(1)} %edge.1.refs_1_.gate), channel_id=1, source_target_pairs={{0,32},{1,225},{2,34},{3,227},{4,36},{5,229},{6,38},{7,231},{8,40}... | collective-permute-start | bytes 2359304 | tf_op jit(solution)/shard_map/ppermute | solution.py:313
  94.1 17.7 %all-to-all-start.2 = ((bf16[8,256,256]{2,1,0:T(8,128)(2,1)}), bf16[8,256,256]{2,1,0:T(8,128)(2,1)S(1)}, u32[]{:S(2)}, u32[]{:S(2)}) async-start(bf16[8,256,256]{2,1,0:T(8,128)(2,1)} %after.3), calls=%async_computation.2 | async-start | bytes 2097152 | tf_op jit(solution)/shard_map/all_to_all | solution.py:322
  105.7 9.3 %collective-permute-start.5 = (bf16[256,256]{1,0:T(8,128)(2,1)S(1)}, bf16[256,256]{1,0:T(8,128)(2,1)S(1)}, u32[]{:S(2)}, u32[]{:S(2)}) collective-permute-start(bf16[256,256]{1,0:T(8,128)(2,1)S(1)} %get-tuple-element.32), channel_id=1, source_target_pairs={{0,0},{1,17},{2,2},{3,19},{4,4},{5,21},{6,6},{7,23},{8,8},{9,25},{... | collective-permute-start | bytes 393224 | tf_op jit(solution)/shard_map/ppermute | solution.py:313
  110.8 6.9 %collective-permute-start.6 = (bf16[256,256]{1,0:T(8,128)(2,1)S(1)}, bf16[256,256]{1,0:T(8,128)(2,1)S(1)}, u32[]{:S(2)}, u32[]{:S(2)}) collective-permute-start(bf16[256,256]{1,0:T(8,128)(2,1)S(1)} %get-tuple-element.33), channel_id=1, source_target_pairs={{0,4},{1,21},{2,6},{3,23},{4,0},{5,17},{6,2},{7,19},{8,12},{9,29},... | collective-permute-start | bytes 393224 | tf_op jit(solution)/shard_map/ppermute | solution.py:313

commit v12 on v10

--- a/solution.py
+++ b/solution.py
@@ -125,7 +125,8 @@
     return first, second
 
 
-def inner_kernel(sel_ref, main, o_ref, stats, first_ref, second_ref, vv, s_scr, p_scr, t_scr):
+def inner_kernel(sel_ref, main, gate_a, gate_b, o_ref, stats, first_ref, second_ref, vv, s_scr, p_scr, t_scr):
+    del gate_a, gate_b
     for c in range(PLANE):
         vv[c * TOK:(c + 1) * TOK, :] = main[c, :TOK, 2 * HEAD_DIM:KV]
 
@@ -354,20 +355,20 @@
         scratch_shapes=[pltpu.SemaphoreType.DMA((2 * REACH,))],
         compiler_params=params(1),
         name="edges",
-    )(main, q_first, q_second)
+    )(main, q_same, q_opp)
     up, dn = send(edge_up, PLANE), send(edge_dn, -PLANE)
-    rest = exchange(after(rest_out, sel_all, q_first, q_second))
+    rest = exchange(after(rest_out, sel_all))
 
     mid, stats, first, second = pl.pallas_call(
         inner_kernel,
         out_shape=(bf16(2, TOK, 256), f32(PLANE, 3, TOK, BLK), f32(PLANE, TOK, 256), f32(PLANE, TOK, BLK)),
-        in_specs=[SMEM_SPEC, VMEM_SPEC],
+        in_specs=[SMEM_SPEC, VMEM_SPEC] + [ANY_SPEC] * 2,
         out_specs=(VMEM_SPEC,) * 4,
         scratch_shapes=[pltpu.VMEM((PLANE * TOK, 2 * HEAD_DIM), jnp.bfloat16)] + scratch(CHUNKS),
         compiler_params=params(16),
         cost_estimate=cost(44),
         name="inner",
-    )(sel_all, main)
+    )(sel_all, main, q_first, q_second)
     mine, done = pl.pallas_call(
         outer_kernel,
         out_shape=(pltpu.HBM((PLANE, TOK, 256), jnp.bfloat16), f32(8, BLK)),

time: 119 us -> 133 us (1.12)
  waiting for transfers between devices: 47.1 us -> 58 us
  starting transfers between devices: 37.5 us -> 40.3 us
    ppermute x5, waiting for transfers between devices: 10.1 us -> 20.9 us  [spread(): return lax.ppermute(array, ('ctx', 'head'), pairs)]
    all_to_all x3, waiting for transfers between devices: 28.9 us -> 37.1 us  [exchange(): lax.all_to_all(array, 'ctx', 0, 0, axis_index_groups=planes, tiled=True)]
    ppermute x2, waiting for transfers between devices: 8.06 us -> 0.01 us  [send(): lax.ppermute(array, 'ctx', [(i, (i + by) % devices) for i in range(device...]
    ppermute x5, starting transfers between devices: 15.4 us -> 17.9 us  [spread(): return lax.ppermute(array, ('ctx', 'head'), pairs)]
  transfers between devices with their start and end apart: 10 -> 10, of which waited for: 6 -> 6; matrix products, arithmetic and copies ran while one was open for 0% -> 0% of each run, Pallas kernels for 23% -> 20%
where the time goes in v12:
time: 133 us
  waiting for transfers between devices  58 us (44%)
  starting transfers between devices  40.3 us (30%)
  Pallas kernels  33.7 us (25%)
    all_to_all x3, waiting for transfers between devices, exchange(): lax.all_to_all(array, 'ctx', 0, 0, axis_index_groups=planes, tiled=True)  37.1 us
    ppermute x5, waiting for transfers between devices, spread(): return lax.ppermute(array, ('ctx', 'head'), pairs)  20.9 us
    ppermute x5, starting transfers between devices, spread(): return lax.ppermute(array, ('ctx', 'head'), pairs)  17.9 us
    all_to_all x3, starting transfers between devices, exchange(): lax.all_to_all(array, 'ctx', 0, 0, axis_index_groups=planes, tiled=True)  16.7 us
    pallas_call x1, Pallas kernels, body(): pl.pallas_call(inner_kernel, out_shape=(bf16(2, TOK, 256), f32(PLANE, 3,...  9.39 us
    pallas_call x1, Pallas kernels, body(): pl.pallas_call(outer_kernel, out_shape=(pltpu.HBM((PLANE, TOK, 256), jnp....  6.04 us
    ppermute x2, starting transfers between devices, send(): lax.ppermute(array, 'ctx', [(i, (i + by) % devices) for i in range(device...  5.74 us
    pallas_call x1, Pallas kernels, body(): pl.pallas_call(pair_inner_kernel, out_shape=(f32(2, 3, TOK, BLK), f32(2,...  4.98 us
  transfers between devices with their start and end apart: 10, of which 6 were waited for; matrix products, arithmetic and copies ran while one was open for 0% of the time, Pallas kernels for 20%

profile of v12, /device:TPU:1, one launch (start us, length us, event | category | flops | bytes accessed | tf_op | source)
XLA Modules:
  0.0 132.9 jit_solution(4662929452039604131)
XLA Ops:
  0.6 4.1 %cut_plane.1 = bf16[8,264,768]{2,1,0:T(8,128)(2,1)} custom-call(s32[2,14]{1,0:T(2,128)} %sel.1, bf16[256,1280]{1,0:T(8,128)(2,1)} %q.3, bf16[256,1280]{1,0:T(8,128)(2,1)} %qt.3, bf16[256,1280]{1,0:T(8,128)(2,1)} %k.3, bf16[256,1280]{1,0:T(8,128)(2,1)} %kt.3, bf16[256,1280]{1,0:T(8,128)(2,1)} %v.3, bf16[256,1280]{1,0:T(8,128)(2,1)} %vt.3), custom_call_target="tpu_custom_call" | custom-call | tf_op jit(solution)/shard_map/cut_plane/pallas_call | solution.py:324
  4.7 7.5 %all-to-all-start = ((bf16[8,264,768]{2,1,0:T(8,128)(2,1)}), bf16[8,264,768]{2,1,0:T(8,128)(2,1)S(1)}, u32[]{:S(2)}, u32[]{:S(2)}) async-start(bf16[8,264,768]{2,1,0:T(8,128)(2,1)} %cut_plane.1), calls=%async_computation | async-start | bytes 6488064 | tf_op jit(solution)/shard_map/all_to_all | solution.py:320
  12.2 3.3 %cut_pair.1 = (bf16[8,256,512]{2,1,0:T(8,128)(2,1)}, bf16[256,256]{1,0:T(8,128)(2,1)}, bf16[256,256]{1,0:T(8,128)(2,1)S(1)}) custom-call(s32[1]{0:T(128)} %bitcast.row_ref.par_ref, bf16[256,1280]{1,0:T(8,128)(2,1)} %q.3, bf16[256,1280]{1,0:T(8,128)(2,1)} %qt.3, bf16[256,1280]{1,0:T(8,128)(2,1)} %k.3, bf16[256,1280]{1,0:T(8,128)(2,1)} %kt.3, ...), custom_call_target="tpu_custom_call" | custom-call | tf_op jit(solution)/shard_map/cut_pair/pallas_call | solution.py:335
  15.5 0.0 copy-start
  15.5 35.1 %all-to-all-done.main = bf16[8,264,768]{2,1,0:T(8,128)(2,1)S(1)} async-done(((bf16[8,264,768]{2,1,0:T(8,128)(2,1)}), bf16[8,264,768]{2,1,0:T(8,128)(2,1)S(1)}, u32[]{:S(2)}, u32[]{:S(2)}) %all-to-all-start) | async-done | bytes 3244064 | tf_op jit(solution)/shard_map/all_to_all | solution.py:320
  50.6 0.1 reshape.12.sel_ref.refs_1_
  50.7 5.2 %all-to-all-start.1 = ((bf16[8,256,512]{2,1,0:T(8,128)(2,1)}), bf16[8,256,512]{2,1,0:T(8,128)(2,1)}, u32[]{:S(2)}, u32[]{:S(2)}) async-start(bf16[8,256,512]{2,1,0:T(8,128)(2,1)} %after.2), calls=%async_computation.1 | async-start | bytes 4194304 | tf_op jit(solution)/shard_map/all_to_all | solution.py:320
  55.9 0.0 copy-done
  55.9 1.2 edges.1
  57.1 1.7 %collective-permute-start = (bf16[3,256,512]{2,1,0:T(8,128)(2,1)}, bf16[3,256,512]{2,1,0:T(8,128)(2,1)}, u32[]{:S(2)}, u32[]{:S(2)}) collective-permute-start(bf16[3,256,512]{2,1,0:T(8,128)(2,1)} %get-tuple-element.20), channel_id=1, source_target_pairs={{0,32},{4,36},{8,40},{12,44},{16,48},{20,52},{24,56},{28,60},{32,6... | collective-permute-start | bytes 2359304 | tf_op jit(solution)/shard_map/ppermute | solution.py:307
  58.9 4.0 %collective-permute-start.1 = (bf16[3,256,512]{2,1,0:T(8,128)(2,1)}, bf16[3,256,512]{2,1,0:T(8,128)(2,1)}, u32[]{:S(2)}, u32[]{:S(2)}) collective-permute-start(bf16[3,256,512]{2,1,0:T(8,128)(2,1)} %get-tuple-element.21), channel_id=1, source_target_pairs={{0,224},{4,228},{8,232},{12,236},{16,240},{20,244},{24,248},{28,25... | collective-permute-start | bytes 2359304 | tf_op jit(solution)/shard_map/ppermute | solution.py:307
  62.9 4.9 %collective-permute-start.2 = (bf16[256,256]{1,0:T(8,128)(2,1)}, bf16[256,256]{1,0:T(8,128)(2,1)S(1)}, u32[]{:S(2)}, u32[]{:S(2)}) collective-permute-start(bf16[256,256]{1,0:T(8,128)(2,1)} %get-tuple-element.18.gate_a), channel_id=1, source_target_pairs={{0,0},{1,17},{2,2},{3,19},{4,4},{5,21},{6,6},{7,23},{8,8},{9,25},{... | collective-permute-start | bytes 393224 | tf_op jit(solution)/shard_map/ppermute | solution.py:311
  67.7 1.3 collective-permute-start.3
  69.0 15.2 %collective-permute-done.2.gate_a.q_first = bf16[256,256]{1,0:T(8,128)(2,1)S(1)} collective-permute-done((bf16[256,256]{1,0:T(8,128)(2,1)}, bf16[256,256]{1,0:T(8,128)(2,1)S(1)}, u32[]{:S(2)}, u32[]{:S(2)}) %collective-permute-start.2) | collective-permute-done | bytes 131104 | tf_op jit(solution)/shard_map/ppermute | solution.py:311
  84.2 2.2 %collective-permute-done.3.gate_b.q_second = bf16[256,256]{1,0:T(8,128)(2,1)S(1)} collective-permute-done((bf16[256,256]{1,0:T(8,128)(2,1)}, bf16[256,256]{1,0:T(8,128)(2,1)S(1)}, u32[]{:S(2)}, u32[]{:S(2)}) %collective-permute-start.3) | collective-permute-done | bytes 131104 | tf_op jit(solution)/shard_map/ppermute | solution.py:311
  86.4 9.4 %inner.1 = (bf16[2,256,256]{2,1,0:T(8,128)(2,1)S(1)}, f32[8,3,256,128]{3,2,1,0:T(8,128)S(1)}, f32[8,256,256]{2,1,0:T(8,128)S(1)}, f32[8,256,128]{2,1,0:T(8,128)S(1)}) custom-call(s32[8,28]{1,0:T(8,128)S(1)} %reshape.12.sel_ref.refs_1_, bf16[8,264,768]{2,1,0:T(8,128)(2,1)S(1)} %all-to-all-done.main, ...), custom_call_target="tpu_custom_call" | custom-call | flops 3690987520 | bytes 11534336 | tf_op jit(solution)/shard_map/inner/pallas_call | solution.py:362
  95.8 0.0 collective-permute-done.up
  95.8 0.0 collective-permute-done.1.dn
  95.8 6.0 %outer.1 = (bf16[8,256,256]{2,1,0:T(8,128)(2,1)}, f32[8,128]{1,0:T(8,128)S(1)}) custom-call(s32[8,28]{1,0:T(8,128)S(1)} %reshape.12.sel_ref.refs_1_, bf16[8,264,768]{2,1,0:T(8,128)(2,1)S(1)} %all-to-all-done.main, bf16[3,256,512]{2,1,0:T(8,128)(2,1)} %collective-permute-done.up, bf16[3,256,512]{2,1,0:T(8,128)(2,1)} %collective-permute-done.1.dn, ...), custom_call_target="tpu_custom_call" | custom-call | flops 1006632960 | bytes 3145728 | tf_op jit(solution)/shard_map/outer/pallas_call | solution.py:372
  101.8 0.0 all-to-all-done.1.main
  101.8 1.1 edge.1.refs_1_.gate
  103.0 5.7 %collective-permute-start.4 = (bf16[3,256,512]{2,1,0:T(8,128)(2,1)S(1)}, bf16[3,256,512]{2,1,0:T(8,128)(2,1)S(1)}, u32[]{:S(2)}, u32[]{:S(2)}) collective-permute-start(bf16[3,256,512]{2,1,0:T(8,128)(2,1)S(1)} %edge.1.refs_1_.gate), channel_id=1, source_target_pairs={{0,32},{1,225},{2,34},{3,227},{4,36},{5,229},{6,38},{7,231},{8,40}... | collective-permute-start | bytes 2359304 | tf_op jit(solution)/shard_map/ppermute | solution.py:311
  108.6 4.0 %all-to-all-start.2 = ((bf16[8,256,256]{2,1,0:T(8,128)(2,1)}), bf16[8,256,256]{2,1,0:T(8,128)(2,1)S(1)}, u32[]{:S(2)}, u32[]{:S(2)}) async-start(bf16[8,256,256]{2,1,0:T(8,128)(2,1)} %after.3), calls=%async_computation.2 | async-start | bytes 2097152 | tf_op jit(solution)/shard_map/all_to_all | solution.py:320
  112.6 5.0 %pair_inner.1 = (f32[2,3,256,128]{3,2,1,0:T(8,128)S(1)}, f32[2,256,256]{2,1,0:T(8,128)S(1)}, f32[2,256,128]{2,1,0:T(8,128)S(1)}) custom-call(s32[1]{0:T(128)S(6)} %xor.7.task_ref, s32[8,28]{1,0:T(8,128)S(1)} %reshape.12.sel_ref.refs_1_, bf16[256,256]{1,0:T(8,128)(2,1)S(1)} %collective-permute-done.2.gate_a.q_first, ...), custom_call_target="tpu_custom_call" | custom-call | flops 1174405120 | bytes 3670016 | tf_op jit(solution)/shard_map/pair_inner/pallas_call | solution.py:394
  117.6 0.0 collective-permute-done.4.halo
  117.6 2.2 %pair_outer.1 = (bf16[256,256]{1,0:T(8,128)(2,1)S(1)}, bf16[256,256]{1,0:T(8,128)(2,1)S(1)}) custom-call(s32[1]{0:T(128)S(6)} %xor.7.task_ref, s32[8,28]{1,0:T(8,128)S(1)} %reshape.12.sel_ref.refs_1_, bf16[256,256]{1,0:T(8,128)(2,1)S(1)} %collective-permute-done.2.gate_a.q_first, bf16[256,256]{1,0:T(8,128)(2,1)S(1)} %collective-permute-done.3.gate_b.q_second, ...), custom_call_target="tpu_custom_call" | custom-call | flops 503316480 | bytes 1572864 | tf_op jit(solution)/shard_map/pair_outer/pallas_call | solution.py:405
  119.9 4.9 %collective-permute-start.5 = (bf16[256,256]{1,0:T(8,128)(2,1)S(1)}, bf16[256,256]{1,0:T(8,128)(2,1)S(1)}, u32[]{:S(2)}, u32[]{:S(2)}) collective-permute-start(bf16[256,256]{1,0:T(8,128)(2,1)S(1)} %get-tuple-element.32), channel_id=1, source_target_pairs={{0,0},{1,17},{2,2},{3,19},{4,4},{5,21},{6,6},{7,23},{8,8},{9,25},{... | collective-permute-start | bytes 393224 | tf_op jit(solution)/shard_map/ppermute | solution.py:311
  124.7 1.3 collective-permute-start.6
  126.0 2.0 %all-to-all-done.2.mine = bf16[8,256,256]{2,1,0:T(8,128)(2,1)S(1)} async-done(((bf16[8,256,256]{2,1,0:T(8,128)(2,1)}), bf16[8,256,256]{2,1,0:T(8,128)(2,1)S(1)}, u32[]{:S(2)}, u32[]{:S(2)}) %all-to-all-start.2) | async-done | bytes 1048608 | tf_op jit(solution)/shard_map/all_to_all | solution.py:320
  128.0 1.2 collective-permute-done.5.own
  129.2 2.3 %collective-permute-done.6.other = bf16[256,256]{1,0:T(8,128)(2,1)S(1)} collective-permute-done((bf16[256,256]{1,0:T(8,128)(2,1)S(1)}, bf16[256,256]{1,0:T(8,128)(2,1)S(1)}, u32[]{:S(2)}, u32[]{:S(2)}) %collective-permute-start.6) | collective-permute-done | bytes 131104 | tf_op jit(solution)/shard_map/ppermute | solution.py:311
  131.6 1.3 unpack.1
  (3 shorter events, 0.0 us)
Async XLA Ops:
  4.7 45.9 %all-to-all-start = ((bf16[8,264,768]{2,1,0:T(8,128)(2,1)}), bf16[8,264,768]{2,1,0:T(8,128)(2,1)S(1)}, u32[]{:S(2)}, u32[]{:S(2)}) async-start(bf16[8,264,768]{2,1,0:T(8,128)(2,1)} %cut_plane.1), calls=%async_computation | async-start | bytes 6488064 | tf_op jit(solution)/shard_map/all_to_all | solution.py:320
  15.5 40.4 %copy-start = (bf16[256,256]{1,0:T(8,128)(2,1)}, bf16[256,256]{1,0:T(8,128)(2,1)S(1)}, u32[]{:S(2)}) copy-start(bf16[256,256]{1,0:T(8,128)(2,1)S(1)} %get-tuple-element.19.gate_b) | copy-start | bytes 393220
  50.7 51.1 %all-to-all-start.1 = ((bf16[8,256,512]{2,1,0:T(8,128)(2,1)}), bf16[8,256,512]{2,1,0:T(8,128)(2,1)}, u32[]{:S(2)}, u32[]{:S(2)}) async-start(bf16[8,256,512]{2,1,0:T(8,128)(2,1)} %after.2), calls=%async_computation.1 | async-start | bytes 4194304 | tf_op jit(solution)/shard_map/all_to_all | solution.py:320
  57.1 38.6 %collective-permute-start = (bf16[3,256,512]{2,1,0:T(8,128)(2,1)}, bf16[3,256,512]{2,1,0:T(8,128)(2,1)}, u32[]{:S(2)}, u32[]{:S(2)}) collective-permute-start(bf16[3,256,512]{2,1,0:T(8,128)(2,1)} %get-tuple-element.20), channel_id=1, source_target_pairs={{0,32},{4,36},{8,40},{12,44},{16,48},{20,52},{24,56},{28,60},{32,6... | collective-permute-start | bytes 2359304 | tf_op jit(solution)/shard_map/ppermute | solution.py:307
  58.9 36.9 %collective-permute-start.1 = (bf16[3,256,512]{2,1,0:T(8,128)(2,1)}, bf16[3,256,512]{2,1,0:T(8,128)(2,1)}, u32[]{:S(2)}, u32[]{:S(2)}) collective-permute-start(bf16[3,256,512]{2,1,0:T(8,128)(2,1)} %get-tuple-element.21), channel_id=1, source_target_pairs={{0,224},{4,228},{8,232},{12,236},{16,240},{20,244},{24,248},{28,25... | collective-permute-start | bytes 2359304 | tf_op jit(solution)/shard_map/ppermute | solution.py:307
  62.9 21.3 %collective-permute-start.2 = (bf16[256,256]{1,0:T(8,128)(2,1)}, bf16[256,256]{1,0:T(8,128)(2,1)S(1)}, u32[]{:S(2)}, u32[]{:S(2)}) collective-permute-start(bf16[256,256]{1,0:T(8,128)(2,1)} %get-tuple-element.18.gate_a), channel_id=1, source_target_pairs={{0,0},{1,17},{2,2},{3,19},{4,4},{5,21},{6,6},{7,23},{8,8},{9,25},{... | collective-permute-start | bytes 393224 | tf_op jit(solution)/shard_map/ppermute | solution.py:311
  67.7 18.6 %collective-permute-start.3 = (bf16[256,256]{1,0:T(8,128)(2,1)}, bf16[256,256]{1,0:T(8,128)(2,1)S(1)}, u32[]{:S(2)}, u32[]{:S(2)}) collective-permute-start(bf16[256,256]{1,0:T(8,128)(2,1)} %copy-done), channel_id=1, source_target_pairs={{0,4},{1,21},{2,6},{3,23},{4,0},{5,17},{6,2},{7,19},{8,12},{9,29},... | collective-permute-start | bytes 393224 | tf_op jit(solution)/shard_map/ppermute | solution.py:311
  103.0 14.6 %collective-permute-start.4 = (bf16[3,256,512]{2,1,0:T(8,128)(2,1)S(1)}, bf16[3,256,512]{2,1,0:T(8,128)(2,1)S(1)}, u32[]{:S(2)}, u32[]{:S(2)}) collective-permute-start(bf16[3,256,512]{2,1,0:T(8,128)(2,1)S(1)} %edge.1.refs_1_.gate), channel_id=1, source_target_pairs={{0,32},{1,225},{2,34},{3,227},{4,36},{5,229},{6,38},{7,231},{8,40}... | collective-permute-start | bytes 2359304 | tf_op jit(solution)/shard_map/ppermute | solution.py:311
  108.6 19.4 %all-to-all-start.2 = ((bf16[8,256,256]{2,1,0:T(8,128)(2,1)}), bf16[8,256,256]{2,1,0:T(8,128)(2,1)S(1)}, u32[]{:S(2)}, u32[]{:S(2)}) async-start(bf16[8,256,256]{2,1,0:T(8,128)(2,1)} %after.3), calls=%async_computation.2 | async-start | bytes 2097152 | tf_op jit(solution)/shard_map/all_to_all | solution.py:320
  119.9 9.4 %collective-permute-start.5 = (bf16[256,256]{1,0:T(8,128)(2,1)S(1)}, bf16[256,256]{1,0:T(8,128)(2,1)S(1)}, u32[]{:S(2)}, u32[]{:S(2)}) collective-permute-start(bf16[256,256]{1,0:T(8,128)(2,1)S(1)} %get-tuple-element.32), channel_id=1, source_target_pairs={{0,0},{1,17},{2,2},{3,19},{4,4},{5,21},{6,6},{7,23},{8,8},{9,25},{... | collective-permute-start | bytes 393224 | tf_op jit(solution)/shard_map/ppermute | solution.py:311
  124.7 6.9 %collective-permute-start.6 = (bf16[256,256]{1,0:T(8,128)(2,1)S(1)}, bf16[256,256]{1,0:T(8,128)(2,1)S(1)}, u32[]{:S(2)}, u32[]{:S(2)}) collective-permute-start(bf16[256,256]{1,0:T(8,128)(2,1)S(1)} %get-tuple-element.33), channel_id=1, source_target_pairs={{0,4},{1,21},{2,6},{3,23},{4,0},{5,17},{6,2},{7,19},{8,12},{9,29},... | collective-permute-start | bytes 393224 | tf_op jit(solution)/shard_map/ppermute | solution.py:311
